TPU v7x, 32 devices: a whole 2x2x4 slice. The times are simulated.
32 devices in a mesh: seq: 8 (over z, x), row: 4 (over y, core).
Axes of the slice: x: 2, y: 2, z: 4, core: 2. Of those that a mesh axis runs over, the one named last changes fastest.
Arguments:
- tokens: bfloat16 [4, 2048, 1024], P('row', 'seq'), may hold values from -6 to 6
- cotangent: bfloat16 [4, 2048, 1024], P('row', 'seq'), may hold values from -6 to 6
- segment_ids: int32 [4, 2048], P('row'), may hold values from 0 to 15, never falling along the last dimension, each value on 1 to 1536 neighbouring positions
- routes: int32 [4, 2048, 8], P('row', 'seq'), may hold values from 0 to 15, all different within a row; in each aligned block of 256 rows (0 to 255, 256 to 511, ..., all dimensions but the last counted through in order) at most 192 rows name the same one
- norm_attn: float32 [1024], P(('seq', 'row')), may hold values from 0.1 to 1.9
- w_query: float32 [1024, 1024], P(('seq', 'row')), may hold values from -0.75 to 0.75
- key_weight_matrix: float32 [1024, 512], P(('seq', 'row')), may hold values from -0.75 to 0.75
- value_weight_matrix: float32 [1024, 512], P(('seq', 'row')), may hold values from -0.1875 to 0.1875
- w_output: float32 [1024, 1024], P(('seq', 'row')), may hold values from -1.5 to 1.5
- norm_moe: float32 [1024], P(('seq', 'row')), may hold values from 0.1 to 1.9
- w_router: float32 [1024, 16], P(('seq', 'row')), may hold values from -0.09375 to 0.09375
- expert_in: float32 [16384, 1024], P(('seq', 'row')), may hold values from -0.1875 to 0.1875
- expert_out: float32 [16384, 512], P(('seq', 'row')), may hold values from -4 to 4
Outputs:
- layer_out: bfloat16 [4, 2048, 1024], P('row', 'seq')
- grad_tokens: float32 [4, 2048, 1024], P('row', 'seq')
- grad_norm_attn: float32 [1024], P(('seq', 'row'))
- grad_w_query: float32 [1024, 1024], P(('seq', 'row'))
- grad_w_key: float32 [1024, 512], P(('seq', 'row'))
- grad_w_value: float32 [1024, 512], P(('seq', 'row'))
- grad_w_output: float32 [1024, 1024], P(('seq', 'row'))
- grad_norm_moe: float32 [1024], P(('seq', 'row'))
- grad_w_router: float32 [1024, 16], P(('seq', 'row'))
- grad_expert_in: float32 [16384, 1024], P(('seq', 'row'))
- grad_expert_out: float32 [16384, 512], P(('seq', 'row'))
Inputs may be any that keep to these rules, and one draw needn't show every extreme that they name: `segment_ids`: along each row the ids never fall; each document (run of equal ids) holds 1 to 1536 tokens, and some document holds exactly 1536. `routes`: each token names 8 different experts; within the 256 tokens of one device (aligned blocks along a row) no expert is named more than 192 times, and in some blocks an expert is named exactly 192 times.
All inputs are finite; a program needn't handle non-finite values.
Results may differ from a plain program's by a relative error of at most 0.019.
The roundings to bfloat16 on the way count: a program that leaves them out, or rounds other values in their place, can miss the bound.
Values may be sent and summed in bfloat16 or wider, within the bound.
No kernel may reach another device: no remote copies, remote signals or barrier semaphores. Data moves between devices by JAX's collectives and lax.ppermute only.
A program may use at most 320 MiB of HBM per device.

v0:
```python
import functools

import jax
import jax.numpy as jnp
from jax import lax
from jax.experimental import pallas as pl
from jax.experimental.pallas import tpu as pltpu
from jax.sharding import Mesh, PartitionSpec as P

QUERY_HEADS = 16
KEY_VALUE_HEADS = 8
HEAD_SIZE = 64
F = 512
E = 16
GROUPS = 4
EXPERTS_HERE = E // GROUPS
LANES = 128
PAIR = 2 * HEAD_SIZE
HEAD_PACK = 4 * HEAD_SIZE
BLOCK = 256

NORM_EPS = 1e-06
RESIDUAL_SCALE = 0.22
SCALE_OF_SCORES = 0.015625
ROPE_BASE = 10000.0
NEGATIVE_HUGE = -1e30
HIGHEST_DOT = lax.Precision.HIGHEST
VMEM_LIMIT = 60 * 1024 * 1024

PLANE = ("b", "y", "c")
SEQ = ("a", "b")
ALL = ("a", "b", "y", "c")

f32 = jnp.float32
bf16 = jnp.bfloat16


def rotation_tables(positions):
    half = HEAD_SIZE // 2
    freq = jnp.power(ROPE_BASE, -2.0 * jnp.arange(half, dtype=f32) / HEAD_SIZE)
    angle = positions.astype(f32)[:, None] * freq[None, :]
    return jnp.cos(angle), jnp.sin(angle)


def rms_back(values, gain, grad_norm):
    mean_square = jnp.mean(values * values, axis=-1, keepdims=True)
    inverse = lax.rsqrt(mean_square + NORM_EPS)
    scaled_grad = grad_norm * gain
    grad_values = inverse * scaled_grad - values * inverse**3 * jnp.mean(
        values * scaled_grad, axis=-1, keepdims=True
    )
    grad_gain = jnp.sum(grad_norm * values * inverse, axis=0)
    return (grad_values, grad_gain)


def rms_scale(values, gain):
    mean_square = jnp.mean(values * values, axis=-1, keepdims=True)
    return values * lax.rsqrt(mean_square + NORM_EPS) * gain


def contract_rows(left_side, right_side):
    return lax.dot_general(
        left_side, right_side, (((0,), (0,)), ((), ())), preferred_element_type=f32
    )


def contract_cols(left_side, right_side):
    return lax.dot_general(
        left_side, right_side, (((1,), (1,)), ((), ())), preferred_element_type=f32
    )


def gather(x, axes):
    return lax.all_gather(x, axes, axis=0, tiled=True)


def scatter_sum(x, axes):
    return lax.psum_scatter(x, axes, scatter_dimension=0, tiled=True)


def pad_lanes(x, lanes):
    return jnp.pad(x, ((0, 0), (0, lanes - x.shape[1])))


def line_pairs(n, step):
    return [(i, i + step) for i in range(n) if 0 <= i + step < n]


def line_send(v, axis):
    n, me = lax.axis_size(axis), lax.axis_index(axis)
    v = v.reshape((n, v.shape[0] // n) + v.shape[1:])
    terms = [lax.dynamic_index_in_dim(v, me, 0, False)]
    for j in range(n - 1, 0, -1):
        for step in (j, -j):
            block = lax.dynamic_index_in_dim(v, jnp.clip(me + step, 0, n - 1), 0, False)
            terms.append(lax.ppermute(block, axis, line_pairs(n, step)))
    return tuple(terms)


def grid_gather(x):
    n = lax.axis_size("a")

    def cross(block, ends):
        return lax.ppermute(
            block, SEQ, [(2 * i + j, 2 * i + 1 - j) for i in range(n) if ends(i) for j in (0, 1)]
        )

    pieces = [(0, 0, x), (0, 1, cross(x, lambda i: True))]
    up = down = x
    for k in range(1, n):
        up = lax.ppermute(up, "a", line_pairs(n, 1))
        down = lax.ppermute(down, "a", line_pairs(n, -1))
        pieces += [(-k, 0, up), (-k, 1, cross(up, lambda i: i >= k))]
        pieces += [(k, 0, down), (k, 1, cross(down, lambda i: i + k < n))]
    return pieces


def plane_gather(x):
    swap = [(0, 1), (1, 0)]
    half = x.shape[0] // 2
    from_y = lax.ppermute(x, "y", swap)
    from_b = lax.ppermute(x, "b", swap)
    upper = lax.ppermute(from_b[:half], "y", swap)
    lower = lax.ppermute(from_y[half:], "b", swap)
    return [
        (block, lax.ppermute(block, "c", swap)) for block in (x, from_y, from_b, upper, lower)
    ]


def halve(v, axis, at):
    if lax.axis_size(axis) != 2:
        return lax.psum_scatter(v, axis, scatter_dimension=at, tiled=False)
    me = lax.axis_index(axis)
    other = lax.ppermute(lax.dynamic_index_in_dim(v, 1 - me, at, False), axis, [(0, 1), (1, 0)])
    own = lax.dynamic_index_in_dim(v, me, at, False)
    return (own.astype(f32) + other.astype(f32)).astype(v.dtype)


def sum_over_row(v):
    sizes = tuple(lax.axis_size(axis) for axis in ALL)
    v = v.reshape(sizes + (v.shape[0] // lax.axis_size(ALL), v.shape[1]))
    return halve(halve(v, "c", 3), "y", 2)


def rotate_lanes(x, cos, sin):
    width = x.shape[-1]
    lane = lax.broadcasted_iota(jnp.int32, x.shape, x.ndim - 1)
    swapped = jnp.where(
        lane % HEAD_SIZE < HEAD_SIZE // 2,
        pltpu.roll(x, width - HEAD_SIZE // 2, x.ndim - 1),
        pltpu.roll(x, HEAD_SIZE // 2, x.ndim - 1),
    )
    return x * cos + swapped * sin


def spread_tables(cos, sin):
    return jnp.concatenate([cos] * 4, axis=1), jnp.concatenate([-sin, sin, -sin, sin], axis=1)


def key_tables(cos, sin):
    low = lower_lanes(cos.shape)
    return jnp.where(low, cos, 1.0), jnp.where(low, sin, 0.0)


def project_kernel(places, place_ref, *refs):
    count = 1 if places is None else len(places)
    blocks, refs = refs[:count], refs[count:]
    small_ref, w_ref, cos_ref, sin_ref, qkv_ref, normed_ref, x_ref, gain, held, sems = refs
    i = pl.program_id(0)
    slots = held.shape[0]

    @pl.when(i == 0)
    def _():
        if places is None:
            for slot in range(slots):
                pltpu.make_async_copy(blocks[0].at[slot], held.at[slot], sems.at[slot]).start()
        else:
            for (distance, crossed), block in zip(places, blocks):
                at = place_ref[1] + distance
                member = 1 - place_ref[2] if crossed else place_ref[2]

                @pl.when((at >= 0) & (at < slots // 2))
                def _(block=block, slot=2 * at + member):
                    pltpu.make_async_copy(block, held.at[slot], sems.at[slot]).start()

        gain[...] = jnp.transpose(small_ref[...].astype(f32))[E : E + 8, :]

    arrived = blocks[0].at[0] if places is None else blocks[0]
    pltpu.make_async_copy(arrived, held.at[i], sems.at[i]).wait()
    x = held[i]
    x_ref[...] = x
    normed = rms_scale(x.astype(f32), gain[0:1, :]).astype(bf16)
    normed_ref[...] = normed
    pre = jnp.dot(normed, w_ref[...], preferred_element_type=f32)
    cos, sin = spread_tables(cos_ref[...], sin_ref[...])
    qkv_ref[:, :PAIR] = rotate_lanes(pre[:, :PAIR], cos, sin).astype(bf16)
    qkv_ref[:, PAIR:] = rotate_lanes(pre[:, PAIR:], *key_tables(cos, sin)).astype(bf16)


def project(place, places, blocks, rows, packed, cos, sin):
    width = packed.shape[0]
    small_at = packed.shape[1] // LANES - 1
    span = cos.shape[0]
    table = pl.BlockSpec((rows, HEAD_SIZE // 2), lambda i, h: (i, 0))
    token_rows = pl.BlockSpec((rows, width), lambda i, h: (i, 0))
    return pl.pallas_call(
        functools.partial(project_kernel, places),
        grid_spec=pltpu.PrefetchScalarGridSpec(
            num_scalar_prefetch=1,
            grid=(span // rows,),
            in_specs=[pl.BlockSpec(memory_space=pl.ANY)] * len(blocks)
            + [
                pl.BlockSpec((width, LANES), lambda i, h: (0, small_at)),
                pl.BlockSpec((width, HEAD_PACK), lambda i, h: (0, h[0])),
                table,
                table,
            ],
            out_specs=[
                pl.BlockSpec((rows, HEAD_PACK), lambda i, h: (i, 0)),
                token_rows,
                token_rows,
            ],
            scratch_shapes=[
                pltpu.VMEM((8, width), f32),
                pltpu.VMEM((span // rows, rows, width), bf16),
                pltpu.SemaphoreType.DMA((span // rows,)),
            ],
        ),
        out_shape=[
            jax.ShapeDtypeStruct((span, HEAD_PACK), bf16),
            jax.ShapeDtypeStruct((span, width), bf16),
            jax.ShapeDtypeStruct((span, width), bf16),
        ],
        compiler_params=pltpu.CompilerParams(vmem_limit_bytes=VMEM_LIMIT),
        cost_estimate=pl.CostEstimate(
            flops=2 * span * width * HEAD_PACK, bytes_accessed=18 * 2**20, transcendentals=0
        ),
        name="project",
    )(place, *blocks, packed, packed, cos, sin)


def head_grads_kernel(head_ref, x_ref, normed_ref, w_ref, grad_ref, out_ref, acc, gain):
    i = pl.program_id(0)

    @pl.when(i == 0)
    def _():
        acc[...] = jnp.zeros_like(acc)
        gain[...] = jnp.zeros_like(gain)

    grad = grad_ref[...]
    acc[...] += contract_rows(grad, normed_ref[...])
    x = x_ref[...].astype(f32)
    inverse = lax.rsqrt(jnp.mean(x * x, axis=-1, keepdims=True) + NORM_EPS)
    back = contract_cols(grad, w_ref[...]) * (x * inverse)
    gain[...] += jnp.sum(back.reshape(back.shape[0] // 8, 8, back.shape[1]), axis=0)

    @pl.when(i == pl.num_programs(0) - 1)
    def _():
        out_ref[:, :HEAD_PACK] = jnp.transpose(acc[...]).astype(bf16)
        total = jnp.sum(gain[...], axis=0, keepdims=True)
        rows = lax.broadcasted_iota(jnp.int32, (LANES, total.shape[1]), 0)
        out_ref[:, HEAD_PACK:] = jnp.transpose(
            jnp.where(rows == 0, jnp.broadcast_to(total, rows.shape), 0.0)
        ).astype(bf16)


def head_grads(head, x, normed, packed, grads):
    span, width = x.shape
    rows = BLOCK
    token_rows = pl.BlockSpec((rows, width), lambda i, h: (i, 0))
    return pl.pallas_call(
        head_grads_kernel,
        grid_spec=pltpu.PrefetchScalarGridSpec(
            num_scalar_prefetch=1,
            grid=(span // rows,),
            in_specs=[
                token_rows,
                token_rows,
                pl.BlockSpec((width, HEAD_PACK), lambda i, h: (0, h[0])),
                pl.BlockSpec((rows, HEAD_PACK), lambda i, h: (i, 0)),
            ],
            out_specs=pl.BlockSpec((width, HEAD_PACK + LANES), lambda i, h: (0, 0)),
            scratch_shapes=[pltpu.VMEM((HEAD_PACK, width), f32), pltpu.VMEM((8, width), f32)],
        ),
        out_shape=jax.ShapeDtypeStruct((width, HEAD_PACK + LANES), bf16),
        compiler_params=pltpu.CompilerParams(vmem_limit_bytes=VMEM_LIMIT),
        cost_estimate=pl.CostEstimate(
            flops=4 * span * width * HEAD_PACK, bytes_accessed=12 * 2**20, transcendentals=0
        ),
        name="head_grads",
    )(head, x, normed, packed, grads)


def lower_lanes(shape):
    return lax.broadcasted_iota(jnp.int32, shape, len(shape) - 1) < HEAD_SIZE


def both_heads_low(pair):
    low = lower_lanes(pair.shape)
    return jnp.concatenate(
        [jnp.where(low, pair, 0.0), jnp.where(low, pltpu.roll(pair, HEAD_SIZE, 1), 0.0)], axis=0
    )


def both_heads_high(pair):
    low = lower_lanes(pair.shape)
    return jnp.concatenate(
        [jnp.where(low, 0.0, pltpu.roll(pair, HEAD_SIZE, 1)), jnp.where(low, 0.0, pair)], axis=0
    )


def allowed_pairs(shape, query_start, key_start, doc):
    rows = lax.broadcasted_iota(jnp.int32, (shape[0] // 2, 1), 0) + query_start
    rows = jnp.concatenate([rows, rows], axis=0)
    keys = lax.broadcasted_iota(jnp.int32, shape, 1) + key_start
    return (keys >= jnp.concatenate([doc, doc], axis=0)) & (keys <= rows)


def attend_kernel(bounds_ref, q_ref, kv_ref, doc_ref, o_ref, low_ref, lse_ref, kept, top, total, acc):
    i = pl.program_id(0)
    steps = pl.num_programs(0)
    offset = bounds_ref[steps]
    first, last = bounds_ref[i], i + offset + 1
    q = both_heads_low(q_ref[...].astype(f32) * SCALE_OF_SCORES).astype(bf16)
    doc = doc_ref[...]
    top[...] = jnp.full_like(top, NEGATIVE_HUGE)
    total[...] = jnp.zeros_like(total)
    acc[...] = jnp.zeros_like(acc)

    def score(j, carried):
        start = pl.multiple_of(j * BLOCK, BLOCK)
        scores = contract_cols(q, kv_ref[pl.ds(start, BLOCK), :])
        allowed = allowed_pairs(scores.shape, (i + offset) * BLOCK, j * BLOCK, doc)
        scores = jnp.where(allowed, scores, NEGATIVE_HUGE)
        kept[:, pl.ds(start, BLOCK)] = scores
        top[...] = jnp.maximum(top[...], jnp.maximum(scores[:, :LANES], scores[:, LANES:]))
        return carried

    lax.fori_loop(first, last, score, 0)
    highest = jnp.max(top[...], axis=1, keepdims=True)

    def mix(j, carried):
        start = pl.multiple_of(j * BLOCK, BLOCK)
        probs = jnp.exp(kept[:, pl.ds(start, BLOCK)] - highest)
        total[...] += probs[:, :LANES] + probs[:, LANES:]
        acc[...] += jnp.dot(
            probs.astype(bf16), kv_ref[pl.ds(start, BLOCK), :], preferred_element_type=f32
        )
        return carried

    lax.fori_loop(first, last, mix, 0)
    row_total = jnp.sum(total[...], axis=1, keepdims=True)
    mixed = acc[...] / row_total
    first_head, second_head = mixed[:BLOCK], mixed[BLOCK:]
    out = jnp.where(
        lower_lanes(first_head.shape), pltpu.roll(first_head, HEAD_SIZE, 1), second_head
    )
    o_ref[...] = out
    low_ref[...] = out.astype(bf16)
    lse_ref[0] = highest + jnp.log(row_total)


def attend(bounds, qkv, kv, kv_at, doc):
    queries, keys = qkv.shape[0], kv.shape[0]
    steps = queries // BLOCK
    pair = pl.BlockSpec((BLOCK, PAIR), lambda i, s: (i, 0))
    return pl.pallas_call(
        attend_kernel,
        grid_spec=pltpu.PrefetchScalarGridSpec(
            num_scalar_prefetch=1,
            grid=(steps,),
            in_specs=[
                pair,
                pl.BlockSpec((keys, PAIR), lambda i, s: (0, kv_at)),
                pl.BlockSpec((BLOCK, 1), lambda i, s: (i, 0)),
            ],
            out_specs=[pair, pair, pl.BlockSpec((1, 2 * BLOCK, 1), lambda i, s: (i, 0, 0))],
            scratch_shapes=[
                pltpu.VMEM((2 * BLOCK, keys), f32),
                pltpu.VMEM((2 * BLOCK, LANES), f32),
                pltpu.VMEM((2 * BLOCK, LANES), f32),
                pltpu.VMEM((2 * BLOCK, PAIR), f32),
            ],
        ),
        out_shape=[
            jax.ShapeDtypeStruct((queries, PAIR), f32),
            jax.ShapeDtypeStruct((queries, PAIR), bf16),
            jax.ShapeDtypeStruct((steps, 2 * BLOCK, 1), f32),
        ],
        compiler_params=pltpu.CompilerParams(vmem_limit_bytes=VMEM_LIMIT),
        cost_estimate=pl.CostEstimate(
            flops=4 * queries * keys * PAIR, bytes_accessed=6 * 2**20, transcendentals=queries * keys
        ),
        name="attend",
    )(bounds, qkv, kv, doc)


def attend_back_kernel(
    fold, bounds_ref, q_ref, kv_ref, doc_ref, do_ref, o_ref, lse_ref, cos_ref, sin_ref, *refs
):
    if fold:
        out_ref, acc, dkv_ref = refs
    else:
        dq_ref, dkv_ref, acc = refs
    i = pl.program_id(0)
    steps = pl.num_programs(0)
    offset = bounds_ref[steps]

    @pl.when(i == 0)
    def _():
        dkv_ref[...] = jnp.zeros_like(dkv_ref)

    q = both_heads_low(q_ref[...].astype(f32) * SCALE_OF_SCORES).astype(bf16)
    grad = do_ref[...].astype(f32)
    product = grad * o_ref[...]
    low = lower_lanes(product.shape)
    delta = jnp.concatenate(
        [
            jnp.sum(jnp.where(low, product, 0.0), axis=1, keepdims=True),
            jnp.sum(jnp.where(low, 0.0, product), axis=1, keepdims=True),
        ],
        axis=0,
    )
    grad = both_heads_high(grad).astype(bf16)
    sources = jnp.concatenate([q, grad], axis=0)
    doc = doc_ref[...]
    lse = lse_ref[0]
    acc[...] = jnp.zeros_like(acc)

    def step(j, carried):
        start = pl.multiple_of(j * BLOCK, BLOCK)
        kv = kv_ref[pl.ds(start, BLOCK), :]
        scores = contract_cols(q, kv)
        allowed = allowed_pairs(scores.shape, (i + offset) * BLOCK, j * BLOCK, doc)
        probs = jnp.exp(jnp.where(allowed, scores - lse, NEGATIVE_HUGE))
        grad_probs = contract_cols(grad, kv)
        grad_scores = (probs * (grad_probs - delta)).astype(bf16)
        acc[...] += jnp.dot(grad_scores, kv, preferred_element_type=f32)
        both = jnp.concatenate([grad_scores, probs.astype(bf16)], axis=0)
        dkv_ref[pl.ds(start, BLOCK), :] += contract_rows(both, sources)
        return carried

    lax.fori_loop(bounds_ref[i], i + offset + 1, step, 0)
    first, second = acc[:BLOCK], acc[BLOCK:]
    dq = jnp.where(lower_lanes(first.shape), first, pltpu.roll(second, HEAD_SIZE, 1))
    if not fold:
        dq_ref[...] = dq
        return
    mine = pl.ds(pl.multiple_of(i * BLOCK, BLOCK), BLOCK)
    cos, sin = spread_tables(cos_ref[mine, :], sin_ref[mine, :])
    out_ref[mine, :PAIR] = rotate_lanes(dq * SCALE_OF_SCORES, cos, -sin).astype(bf16)

    @pl.when(i == steps - 1)
    def _():
        def finish(j, carried):
            part = pl.ds(pl.multiple_of(j * BLOCK, BLOCK), BLOCK)
            cos, sin = key_tables(*spread_tables(cos_ref[part, :], sin_ref[part, :]))
            out_ref[part, PAIR:] = rotate_lanes(dkv_ref[part, :], cos, -sin).astype(bf16)
            return carried

        lax.fori_loop(0, dkv_ref.shape[0] // BLOCK, finish, 0)


def attend_back(bounds, qkv, kv, kv_at, doc, grad, out, lse, cos, sin, fold):
    queries, keys = qkv.shape[0], kv.shape[0]
    steps = queries // BLOCK
    pair = pl.BlockSpec((BLOCK, PAIR), lambda i, s: (i, 0))
    table = pl.BlockSpec(cos.shape, lambda i, s: (0, 0))
    acc = pltpu.VMEM((2 * BLOCK, PAIR), f32)
    if fold:
        out_specs = pl.BlockSpec((queries, HEAD_PACK), lambda i, s: (0, 0))
        out_shape = jax.ShapeDtypeStruct((queries, HEAD_PACK), bf16)
        scratch = [acc, pltpu.VMEM((keys, PAIR), f32)]
    else:
        out_specs = [pair, pl.BlockSpec((keys, PAIR), lambda i, s: (0, 0))]
        out_shape = [
            jax.ShapeDtypeStruct((queries, PAIR), f32),
            jax.ShapeDtypeStruct((keys, PAIR), f32),
        ]
        scratch = [acc]
    return pl.pallas_call(
        functools.partial(attend_back_kernel, fold),
        grid_spec=pltpu.PrefetchScalarGridSpec(
            num_scalar_prefetch=1,
            grid=(steps,),
            in_specs=[
                pair,
                pl.BlockSpec((keys, PAIR), lambda i, s: (0, kv_at)),
                pl.BlockSpec((BLOCK, 1), lambda i, s: (i, 0)),
                pair,
                pair,
                pl.BlockSpec((1, 2 * BLOCK, 1), lambda i, s: (i, 0, 0)),
                table,
                table,
            ],
            out_specs=out_specs,
            scratch_shapes=scratch,
        ),
        out_shape=out_shape,
        compiler_params=pltpu.CompilerParams(vmem_limit_bytes=VMEM_LIMIT),
        cost_estimate=pl.CostEstimate(
            flops=10 * queries * keys * PAIR,
            bytes_accessed=8 * 2**20,
            transcendentals=queries * keys,
        ),
        name="attend_back",
    )(bounds, qkv, kv, doc, grad, out, lse, cos, sin)


def unrotate_kernel(dq_ref, dkv_ref, cos_ref, sin_ref, out_ref):
    cos, sin = spread_tables(cos_ref[...], sin_ref[...])
    dq = rotate_lanes(dq_ref[...] * SCALE_OF_SCORES, cos, -sin)
    cos, sin = key_tables(cos, sin)
    dkv = rotate_lanes(dkv_ref[...], cos, -sin)
    out_ref[...] = jnp.concatenate([dq, dkv], axis=1).astype(bf16)


def unrotate(dq, dkv, cos, sin):
    rows = dq.shape[0]
    pair = pl.BlockSpec((BLOCK, PAIR), lambda i: (i, 0))
    table = pl.BlockSpec((BLOCK, HEAD_SIZE // 2), lambda i: (i, 0))
    return pl.pallas_call(
        unrotate_kernel,
        grid=(rows // BLOCK,),
        in_specs=[pair, pair, table, table],
        out_specs=pl.BlockSpec((BLOCK, HEAD_PACK), lambda i: (i, 0)),
        out_shape=jax.ShapeDtypeStruct((rows, HEAD_PACK), bf16),
        cost_estimate=pl.CostEstimate(
            flops=rows * HEAD_PACK * 8, bytes_accessed=rows * HEAD_PACK * 14, transcendentals=0
        ),
        name="unrotate",
    )(dq, dkv, cos, sin)


def place_experts_kernel(place_ref, *refs):
    blocks, (ct_ref, w_ref, z_ref, sems) = refs[:10], refs[10:]
    core = place_ref[1]
    rows = w_ref.shape[1] // 2
    half = rows // 2
    sources = [[(0, 0, rows)], [(1, 0, rows)], [(2, 0, rows)], [(3, 0, half), (4, half, half)]]
    for step, parts in enumerate(sources):

        @pl.when(pl.program_id(0) == step)
        def _(parts=parts):
            copies = []
            for source, start, length in parts:
                for other in (0, 1):
                    first = jnp.where(core == other, 0, rows) + start
                    at = pl.ds(pl.multiple_of(first, half), length)
                    copies.append(
                        pltpu.make_async_copy(
                            blocks[2 * source + other], w_ref.at[0, at, :], sems.at[len(copies)]
                        )
                    )
            for copy in copies:
                copy.start()
            for copy in copies:
                copy.wait()

    z_ref[0] = jnp.dot(ct_ref[...], w_ref[0, :, 2 * F :], preferred_element_type=f32)


def place_experts(place, parts, early, width):
    rows = early.shape[0]
    blocks = [block for pair in parts for block in pair]
    return pl.pallas_call(
        place_experts_kernel,
        grid_spec=pltpu.PrefetchScalarGridSpec(
            num_scalar_prefetch=1,
            grid=(EXPERTS_HERE,),
            in_specs=[pl.BlockSpec(memory_space=pl.ANY)] * len(blocks)
            + [pl.BlockSpec((rows, width), lambda r, s: (0, 0))],
            out_specs=[
                pl.BlockSpec((1, width, 3 * F), lambda r, s: (s[0] ^ r, 0, 0)),
                pl.BlockSpec((1, rows, F), lambda r, s: (s[0] ^ r, 0, 0)),
            ],
            scratch_shapes=[pltpu.SemaphoreType.DMA((4,))],
        ),
        out_shape=[
            jax.ShapeDtypeStruct((EXPERTS_HERE, width, 3 * F), bf16),
            jax.ShapeDtypeStruct((EXPERTS_HERE, rows, F), f32),
        ],
        compiler_params=pltpu.CompilerParams(vmem_limit_bytes=VMEM_LIMIT),
        cost_estimate=pl.CostEstimate(
            flops=2 * EXPERTS_HERE * rows * width * F, bytes_accessed=36 * 2**20, transcendentals=0
        ),
        name="place_experts",
    )(place, *blocks, early)


def lane_column(x, at):
    lane = lax.broadcasted_iota(jnp.int32, x.shape, 1)
    return jnp.sum(jnp.where(lane == at, x, 0.0), axis=1, keepdims=True)


def experts_kernel(
    group_ref, n_ref, routed_ref, router_ref, w_ref, z_ref,
    back_ref, gates_ref, hidden_ref, pre_ref, acc, dots,
):
    e = pl.program_id(0)
    own = group_ref[0] * EXPERTS_HERE + e
    rows = n_ref.shape[0]

    @pl.when(e == 0)
    def _():
        logits = jnp.dot(n_ref[...], router_ref[...], preferred_element_type=f32)
        routed = routed_ref[...].astype(f32) > 0.5
        highest = jnp.max(jnp.where(routed, logits, NEGATIVE_HUGE), axis=1, keepdims=True)
        weights = jnp.where(routed, jnp.exp(jnp.where(routed, logits - highest, 0.0)), 0.0)
        gates_ref[...] = weights / jnp.sum(weights, axis=1, keepdims=True)
        acc[...] = jnp.zeros_like(acc)
        dots[...] = jnp.zeros_like(dots)

    w_in = w_ref[0, :, : 2 * F]
    for t in range(rows // BLOCK):
        part = pl.ds(t * BLOCK, BLOCK)
        pre = jnp.dot(n_ref[part, :], w_in, preferred_element_type=f32)
        gate, up = pre[:, :F], pre[:, F:]
        z = z_ref[0, part, :]
        weight = lane_column(gates_ref[part, :], own)
        sig = 1.0 / (1.0 + jnp.exp(-gate))
        act = gate * sig
        hidden = act * up
        hidden_ref[0, part, :] = (weight * hidden).astype(bf16)
        dot = RESIDUAL_SCALE * jnp.sum(hidden.astype(bf16).astype(f32) * z, axis=1, keepdims=True)
        lane = lax.broadcasted_iota(jnp.int32, (BLOCK, LANES), 1)
        dots[part, :] += jnp.where(lane == own, dot, 0.0)
        scaled = (RESIDUAL_SCALE * weight) * z
        pre_ref[0, part, :F] = (scaled * up * (sig + act * (1.0 - sig))).astype(bf16)
        pre_ref[0, part, F:] = (scaled * act).astype(bf16)
        acc[part, :] += contract_cols(pre_ref[0, part, :], w_in)

    @pl.when(e == EXPERTS_HERE - 1)
    def _():
        width = n_ref.shape[1]
        back_ref[:, :width] = acc[...].astype(bf16)
        high = dots[...].astype(bf16)
        low = dots[...] - high.astype(f32)
        back_ref[:, width:] = (high.astype(f32) + pltpu.roll(low, E, 1)).astype(bf16)


def experts(group, normed, early, packed, w_all, z):
    rows, width = normed.shape
    count = w_all.shape[0]
    whole = pl.BlockSpec((rows, width), lambda e, g: (0, 0))
    column = width // LANES
    router_at = packed.shape[1] // LANES - 1
    return pl.pallas_call(
        experts_kernel,
        grid_spec=pltpu.PrefetchScalarGridSpec(
            num_scalar_prefetch=1,
            grid=(count,),
            in_specs=[
                whole,
                pl.BlockSpec((rows, LANES), lambda e, g: (0, column)),
                pl.BlockSpec((width, LANES), lambda e, g: (0, router_at)),
                pl.BlockSpec((1, width, 3 * F), lambda e, g: (e, 0, 0)),
                pl.BlockSpec((1, rows, F), lambda e, g: (e, 0, 0)),
            ],
            out_specs=[
                pl.BlockSpec((rows, width + LANES), lambda e, g: (0, 0)),
                pl.BlockSpec((rows, LANES), lambda e, g: (0, 0)),
                pl.BlockSpec((1, rows, F), lambda e, g: (e, 0, 0)),
                pl.BlockSpec((1, rows, 2 * F), lambda e, g: (e, 0, 0)),
            ],
            scratch_shapes=[pltpu.VMEM((rows, width), f32), pltpu.VMEM((rows, LANES), f32)],
        ),
        out_shape=[
            jax.ShapeDtypeStruct((rows, width + LANES), bf16),
            jax.ShapeDtypeStruct((rows, LANES), f32),
            jax.ShapeDtypeStruct((count, rows, F), bf16),
            jax.ShapeDtypeStruct((count, rows, 2 * F), bf16),
        ],
        compiler_params=pltpu.CompilerParams(vmem_limit_bytes=VMEM_LIMIT),
        cost_estimate=pl.CostEstimate(
            flops=2 * count * rows * width * 4 * F, bytes_accessed=40 * 2**20, transcendentals=0
        ),
        name="experts",
    )(group, normed, early, packed, w_all, z)


def expert_grads_kernel(n_ref, ct_ref, w_ref, hidden_ref, pre_ref, y_ref, grad_ref, n_t, ct_t, acc):
    e = pl.program_id(0)

    @pl.when(e == 0)
    def _():
        n_t[...] = jnp.transpose(n_ref[...])
        ct_t[...] = jnp.transpose(ct_ref[...])
        acc[...] = jnp.zeros_like(acc)

    grad_ref[0, :, : 2 * F] = jnp.dot(
        n_t[...], pre_ref[0], preferred_element_type=f32
    ).astype(bf16)
    grad_ref[0, :, 2 * F :] = (
        RESIDUAL_SCALE * jnp.dot(ct_t[...], hidden_ref[0], preferred_element_type=f32)
    ).astype(bf16)
    acc[...] += contract_cols(hidden_ref[0], w_ref[0, :, 2 * F :])

    @pl.when(e == EXPERTS_HERE - 1)
    def _():
        y_ref[...] = acc[...].astype(bf16)


def expert_grads(normed, early, w_all, hidden, pre):
    rows, width = normed.shape
    count = w_all.shape[0]
    whole = pl.BlockSpec((rows, width), lambda e: (0, 0))
    return pl.pallas_call(
        expert_grads_kernel,
        grid=(count,),
        in_specs=[
            whole,
            whole,
            pl.BlockSpec((1, width, 3 * F), lambda e: (e, 0, 0)),
            pl.BlockSpec((1, rows, F), lambda e: (e, 0, 0)),
            pl.BlockSpec((1, rows, 2 * F), lambda e: (e, 0, 0)),
        ],
        out_specs=[whole, pl.BlockSpec((1, width, 3 * F), lambda e: (e, 0, 0))],
        out_shape=[
            jax.ShapeDtypeStruct((rows, width), bf16),
            jax.ShapeDtypeStruct((count, width, 3 * F), bf16),
        ],
        scratch_shapes=[
            pltpu.VMEM((width, rows), bf16),
            pltpu.VMEM((width, rows), bf16),
            pltpu.VMEM((rows, width), f32),
        ],
        compiler_params=pltpu.CompilerParams(vmem_limit_bytes=VMEM_LIMIT),
        cost_estimate=pl.CostEstimate(
            flops=2 * count * rows * width * 4 * F, bytes_accessed=40 * 2**20, transcendentals=0
        ),
        name="expert_grads",
    )(normed, early, w_all, hidden, pre)


def exchange(x, axes):
    return lax.all_to_all(x, axes, 0, 0, tiled=True)


def body(
    tokens,
    cotangent,
    segment_ids,
    routes,
    norm_attn,
    w_query,
    key_weight_matrix,
    value_weight_matrix,
    w_output,
    norm_moe,
    w_router,
    expert_in,
    expert_out,
):
    x_local = tokens[0].astype(f32)
    token_count, width = x_local.shape
    seg_row = segment_ids[0]
    group = lax.axis_index("a")
    head_axes = SEQ if lax.axis_size(SEQ) == KEY_VALUE_HEADS else ("b",)
    whole_rows = head_axes == SEQ
    span = token_count * KEY_VALUE_HEADS
    span_start = 0 if whole_rows else group * span

    def start_of_doc(ids):
        return jnp.sum((seg_row[None, :] < ids[:, None]).astype(jnp.int32), axis=1)

    seg_span = lax.dynamic_slice_in_dim(seg_row, span_start, span)
    doc_span = start_of_doc(seg_span)
    cos_span, sin_span = rotation_tables(
        span_start + jnp.arange(span, dtype=jnp.int32) - doc_span
    )
    bounds = jnp.concatenate(
        [
            doc_span.reshape(-1, BLOCK)[:, 0] // BLOCK,
            jnp.full((1,), span_start // BLOCK, jnp.int32),
        ]
    )
    doc_column = doc_span[:, None]

    own_rows = w_query.shape[0]
    by_head = jnp.concatenate(
        [
            w_query.astype(bf16).reshape(own_rows, KEY_VALUE_HEADS, PAIR),
            key_weight_matrix.astype(bf16).reshape(own_rows, KEY_VALUE_HEADS, HEAD_SIZE),
            value_weight_matrix.astype(bf16).reshape(own_rows, KEY_VALUE_HEADS, HEAD_SIZE),
        ],
        axis=2,
    ).reshape(own_rows, KEY_VALUE_HEADS * HEAD_PACK)
    qkv_width = KEY_VALUE_HEADS * HEAD_PACK
    first_all = gather(
        jnp.concatenate(
            [
                by_head,
                w_output.astype(bf16),
                pad_lanes(
                    jnp.concatenate(
                        [
                            w_router.astype(bf16),
                            norm_attn.astype(bf16)[:, None],
                            norm_moe.astype(bf16)[:, None],
                        ],
                        axis=1,
                    ),
                    LANES,
                ),
            ],
            axis=1,
        ),
        ALL,
    )
    experts_low = jnp.concatenate([expert_in.astype(bf16), expert_out.astype(bf16)], axis=1)
    if whole_rows:
        pieces = grid_gather(tokens[0])
        places = [piece[:2] for piece in pieces]
        blocks = tuple(piece[2] for piece in pieces)
    else:
        places = None
        blocks = (gather(tokens[0], "b").reshape((-1,) + tokens.shape[1:]),)
    first_all, experts_low, blocks, cos_span, sin_span, bounds, doc_column = (
        lax.optimization_barrier(
            (first_all, experts_low, blocks, cos_span, sin_span, bounds, doc_column)
        )
    )
    output_w = first_all[:, qkv_width : qkv_width + width]
    small_at = qkv_width + width
    router_w = first_all[:, small_at : small_at + E]
    gain_one_f = first_all[:, small_at + E].astype(f32)
    gain_two_f = first_all[:, small_at + E + 1].astype(f32)

    expert_ids = jnp.arange(E, dtype=jnp.int32)
    routed_own = jnp.any(routes[0][:, :, None] == expert_ids[None, None, :], axis=1)
    early = jnp.concatenate([cotangent[0], pad_lanes(routed_own.astype(bf16), LANES)], axis=1)
    early, first_all = lax.optimization_barrier((early, first_all))
    early_all = gather(early, "a")
    small_plane = lax.axis_size("b") == 2 and lax.axis_size("y") == 2
    if small_plane:
        parts = plane_gather(experts_low)
    else:
        parts = gather(experts_low, PLANE)

    place = jnp.stack([lax.axis_index(head_axes), group, lax.axis_index("b")])
    qkv, normed_span, x_span = project(
        place, places, blocks, token_count, first_all, cos_span, sin_span
    )
    if whole_rows:
        kv, kv_at = qkv, 1
    else:
        kv, kv_at = gather(qkv[:, PAIR:], "a"), 0
    attention_result, attended, log_total = attend(bounds, qkv, kv, kv_at, doc_column)
    attended_low = (
        exchange(attended.reshape(KEY_VALUE_HEADS, token_count, PAIR), head_axes)
        .transpose(1, 0, 2)
        .reshape(token_count, QUERY_HEADS * HEAD_SIZE)
    )
    attn_out = jnp.dot(attended_low, output_w, preferred_element_type=f32)
    resid = x_local + RESIDUAL_SCALE * attn_out
    normed_two = rms_scale(resid, gain_two_f).astype(bf16)

    normed_two, parts, early_all = lax.optimization_barrier((normed_two, parts, early_all))
    normed_all = gather(normed_two, "a")
    if small_plane:
        home = jnp.stack([lax.axis_index("b") * 2 + lax.axis_index("y"), lax.axis_index("c")])
        experts_all, grad_hidden = place_experts(home, parts, early_all, width)
    else:
        experts_all = parts.reshape(EXPERTS_HERE, width, 3 * F)
        grad_hidden = jnp.einsum(
            "td,edf->etf",
            early_all[:, :width],
            experts_all[:, :, 2 * F :],
            preferred_element_type=f32,
        )
    back_part, gates_all, gated_hidden, grad_pre = experts(
        group.reshape(1), normed_all, early_all, first_all, experts_all, grad_hidden
    )
    back_own = scatter_sum(back_part, "a").astype(f32)
    moe_part, grad_experts = expert_grads(
        normed_all, early_all, experts_all, gated_hidden, grad_pre
    )
    back_own, moe_part, grad_experts = lax.optimization_barrier(
        (back_own, moe_part, grad_experts)
    )
    grad_experts = scatter_sum(grad_experts.reshape(EXPERTS_HERE * width, 3 * F), PLANE)
    moe_terms = line_send(moe_part, "a")

    grad_out = cotangent[0].astype(f32)
    gates = lax.dynamic_slice_in_dim(gates_all, group * token_count, token_count)[:, :E]
    gate_grads_own = back_own[:, width : width + E] + back_own[:, width + E : width + 2 * E]
    grad_logits = gates * (gate_grads_own - jnp.sum(gates * gate_grads_own, axis=-1, keepdims=True))
    grad_normed_two = back_own[:, :width] + jnp.dot(
        grad_logits, router_w.astype(f32).T, precision=HIGHEST_DOT
    )
    grad_router = jnp.dot(normed_two.astype(f32).T, grad_logits, precision=HIGHEST_DOT)
    grad_resid_norm, grad_gain_two = rms_back(resid, gain_two_f, grad_normed_two)
    grad_resid = grad_out + grad_resid_norm
    grad_attn_low = (RESIDUAL_SCALE * grad_resid).astype(bf16)
    grad_heads = contract_cols(grad_attn_low, output_w).astype(bf16)
    grad_mixed = exchange(
        grad_heads.reshape(token_count, KEY_VALUE_HEADS, PAIR).transpose(1, 0, 2), head_axes
    ).reshape(span, PAIR)
    small = jnp.concatenate([grad_router, grad_gain_two[:, None]], axis=1)
    second_part = sum_over_row(
        jnp.concatenate(
            [contract_rows(attended_low, grad_attn_low), pad_lanes(small, LANES)], axis=1
        ).astype(bf16)
    )
    second_part = halve(second_part, "b", 1)
    rest = line_send(second_part.reshape(-1, second_part.shape[2]), "a")
    grads = attend_back(
        bounds, qkv, kv, kv_at, doc_column, grad_mixed, attention_result, log_total,
        cos_span, sin_span, whole_rows,
    )
    if whole_rows:
        grad_pack = grads
    else:
        grad_kv = scatter_sum(grads[1].astype(bf16), "a").astype(f32)
        grad_pack = unrotate(grads[0], grad_kv, cos_span, sin_span)
    moe_terms, resid, grad_pack = lax.optimization_barrier((moe_terms, resid, grad_pack))
    first_part = head_grads(place, x_span, normed_span, first_all, grad_pack)
    by_tokens = exchange(grad_pack.reshape(KEY_VALUE_HEADS, token_count, HEAD_PACK), head_axes)
    by_tokens, first_part = lax.optimization_barrier((by_tokens, first_part))
    sums = exchange(first_part.reshape(-1, own_rows, first_part.shape[1]), ALL).astype(f32)
    sums = sums.reshape(lax.axis_size(SEQ), -1, own_rows, first_part.shape[1]).sum(axis=1)
    by_heads = sums[:, :, :HEAD_PACK].reshape(-1, KEY_VALUE_HEADS, own_rows, HEAD_PACK).sum(axis=0)
    rest = sum(term.astype(f32) for term in rest)
    grad_qkv = by_tokens.transpose(1, 0, 2).reshape(token_count, qkv_width)
    grad_normed_one = contract_cols(grad_qkv, first_all[:, :qkv_width])
    grad_x_norm, _ = rms_back(x_local, gain_one_f, grad_normed_one)
    grad_input = grad_resid + grad_x_norm
    layer_sum = resid + RESIDUAL_SCALE * sum(term.astype(f32) for term in moe_terms)
    grad_experts = grad_experts.astype(f32)
    by_rows = by_heads.transpose(1, 0, 2)
    return (
        layer_sum.astype(bf16)[None],
        grad_input[None],
        sums[:, :, HEAD_PACK].sum(axis=0),
        by_rows[:, :, :PAIR].reshape(own_rows, -1),
        by_rows[:, :, PAIR : PAIR + HEAD_SIZE].reshape(own_rows, -1),
        by_rows[:, :, PAIR + HEAD_SIZE :].reshape(own_rows, -1),
        rest[:, :width],
        rest[:, width + E],
        rest[:, width : width + E],
        grad_experts[:, : 2 * F],
        grad_experts[:, 2 * F :],
    )


def solution(mesh):
    seq, row = mesh.shape["seq"], mesh.shape["row"]
    cut = Mesh(mesh.devices.reshape(GROUPS, seq // GROUPS, row // 2, 2), ALL)
    token_spec = P(("y", "c"), SEQ, None)
    row_spec = P(ALL, None)
    flat_spec = P(ALL)
    in_specs = (
        token_spec,
        token_spec,
        P(("y", "c"), None),
        token_spec,
        flat_spec,
        row_spec,
        row_spec,
        row_spec,
        row_spec,
        flat_spec,
        row_spec,
        row_spec,
        row_spec,
    )
    out_specs = (
        token_spec,
        token_spec,
        flat_spec,
        row_spec,
        row_spec,
        row_spec,
        row_spec,
        flat_spec,
        row_spec,
        row_spec,
        row_spec,
    )
    return jax.shard_map(body, mesh=cut, in_specs=in_specs, out_specs=out_specs, check_vma=False)
```

profile of v0, /device:TPU:0, one launch (start us, length us, event | category | flops | bytes accessed | tf_op | source)
XLA Modules:
  0.0 493.1 jit_solution(13528220815213505573)
XLA Ops:
  14.5 3.0 collective-permute-start
  17.5 4.3 collective-permute-start.1
  26.2 9.1 %collective-permute-done.1.refs_2_ = bf16[256,1024]{1,0:T(8,128)(2,1)} collective-permute-done((bf16[256,1024]{1,0:T(8,128)(2,1)}, bf16[256,1024]{1,0:T(8,128)(2,1)}, u32[]{:S(2)}, u32[]{:S(2)}) %collective-permute-start.1) | collective-permute-done | bytes 524320 | tf_op jit(solution)/shard_map/ppermute | solution.py:111
  35.3 4.4 collective-permute-start.5
  44.2 14.3 %collective-permute-done.5.refs_6_ = bf16[256,1024]{1,0:T(8,128)(2,1)S(1)} collective-permute-done((bf16[256,1024]{1,0:T(8,128)(2,1)}, bf16[256,1024]{1,0:T(8,128)(2,1)S(1)}, u32[]{:S(2)}, u32[]{:S(2)}) %collective-permute-start.5) | collective-permute-done | bytes 524320 | tf_op jit(solution)/shard_map/ppermute | solution.py:111
  58.5 5.1 %collective-permute-start.9 = (bf16[256,1024]{1,0:T(8,128)(2,1)S(1)}, bf16[256,1024]{1,0:T(8,128)(2,1)}, u32[]{:S(2)}, u32[]{:S(2)}) collective-permute-start(bf16[256,1024]{1,0:T(8,128)(2,1)S(1)} %collective-permute-done.5.refs_6_), channel_id=1, source_target_pairs={{0,8},{8,16},{16,24},{1,9},{9,17},{17,25},{2,10},{10,18},{18,26},{... | collective-permute-start | bytes 1572872 | tf_op jit(solution)/shard_map/ppermute | solution.py:111
  69.1 1.9 collective-permute-start.4
  71.7 3.9 collective-permute-start.8
  77.1 7.8 %collective-permute-done.11.refs_12_ = bf16[256,1024]{1,0:T(8,128)(2,1)} collective-permute-done((bf16[256,1024]{1,0:T(8,128)(2,1)}, bf16[256,1024]{1,0:T(8,128)(2,1)}, u32[]{:S(2)}, u32[]{:S(2)}) %collective-permute-start.11) | collective-permute-done | bytes 524320 | tf_op jit(solution)/shard_map/ppermute | solution.py:112
  87.5 5.5 %multiply_sine_fusion = (f32[2048,32]{1,0:T(8,128)}, f32[2048,32]{1,0:T(8,128)}) fusion(f32[32]{0:T(128)S(1)} %multiply_power_fusion, f32[2048]{0:T(1024)S(1)} %subtract_convert_fusion), kind=kLoop, calls=%fused_computation.20 | loop fusion | flops 65536 | bytes 532608 | tf_op jit(solution)/shard_map/sin | solution.py:42
  93.0 3.1 collective-permute-done.4.refs_5_
  96.0 11.3 %collective-permute-done.8.refs_9_ = bf16[256,1024]{1,0:T(8,128)(2,1)} collective-permute-done((bf16[256,1024]{1,0:T(8,128)(2,1)}, bf16[256,1024]{1,0:T(8,128)(2,1)}, u32[]{:S(2)}, u32[]{:S(2)}) %collective-permute-start.8) | collective-permute-done | bytes 524320 | tf_op jit(solution)/shard_map/ppermute | solution.py:104
  107.4 8.3 %collective-permute-done.12.refs_13_ = bf16[256,1024]{1,0:T(8,128)(2,1)} collective-permute-done((bf16[256,1024]{1,0:T(8,128)(2,1)}, bf16[256,1024]{1,0:T(8,128)(2,1)}, u32[]{:S(2)}, u32[]{:S(2)}) %collective-permute-start.12) | collective-permute-done | bytes 524320 | tf_op jit(solution)/shard_map/ppermute | solution.py:104
  119.5 10.3 %project.1 = (bf16[2048,256]{1,0:T(8,128)(2,1)}, bf16[2048,1024]{1,0:T(8,128)(2,1)}, bf16[2048,1024]{1,0:T(8,128)(2,1)}) custom-call(s32[3]{0:T(128)} %pad_add_fusion.1.place_ref.head_ref, bf16[256,1024]{1,0:T(8,128)(2,1)} %bitcast.1.refs_0_, bf16[256,1024]{1,0:T(8,128)(2,1)} %collective-permute-done.refs_1_, ...), custom_call_target="tpu_custom_call" | custom-call | flops 1073741824 | bytes 18874368 | tf_op jit(solution)/shard_map/project/pallas_call | solution.py:206
  129.8 21.4 %attend.1 = (f32[2048,128]{1,0:T(8,128)}, bf16[2048,128]{1,0:T(8,128)(2,1)}, f32[8,512,1]{2,1,0:T(8,128)}) custom-call(s32[9]{0:T(128)} %pad_add_fusion.bounds_ref, bf16[2048,256]{1,0:T(8,128)(2,1)} %get-tuple-element.92.q_ref.kv_ref, bf16[2048,256]{1,0:T(8,128)(2,1)} %get-tuple-element.92.q_ref.kv_ref, s32[2048,1]{1,0:T(8,128)} %copy.96.doc_ref), custom_call_target="tpu_custom_call" | custom-call | flops 2147483648 | bytes 6291456 | tf_op jit(solution)/shard_map/attend/pallas_call | solution.py:367
  151.2 2.0 copy.97
  153.3 3.5 all-to-all-start
  159.3 1.9 collective-permute-start.20
  163.2 7.0 %collective-permute-done.18.refs_6_ = bf16[256,1536]{1,0:T(8,128)(2,1)} collective-permute-done((bf16[256,1536]{1,0:T(8,128)(2,1)S(1)}, bf16[256,1536]{1,0:T(8,128)(2,1)}, u32[]{:S(2)}, u32[]{:S(2)}) %collective-permute-start.18) | collective-permute-done | bytes 786464 | tf_op jit(solution)/shard_map/ppermute | solution.py:123
  170.2 4.8 collective-permute-done.20.refs_8_
  175.0 2.7 multiply_reduce_fusion.2
  179.6 18.7 %place_experts.1 = (bf16[4,1024,1536]{2,1,0:T(8,128)(2,1)}, f32[4,1024,512]{2,1,0:T(8,128)}) custom-call(s32[2]{0:T(128)} %pad_add_fusion.2.place_ref, bf16[512,1536]{1,0:T(8,128)(2,1)} %copy-done.10, bf16[512,1536]{1,0:T(8,128)(2,1)} %collective-permute-done.13.refs_1_, bf16[512,1536]{1,0:T(8,128)(2,1)} %collective-permute-done.14.refs_2_, ...), custom_call_target="tpu_custom_call" | custom-call | flops 4294967296 | bytes 37748736 | tf_op jit(solution)/shard_map/place_experts/pallas_call | solution.py:566
  198.3 26.3 %all-gather.8.cloned.1.call-done.n_ref = bf16[1024,1024]{1,0:T(8,128)(2,1)} async-done(((bf16[256,1024]{1,0:T(8,128)(2,1)}), bf16[1024,1024]{1,0:T(8,128)(2,1)}) %all-gather.8.cloned.1.call-update) | async-done | bytes 2097168 | tf_op jit(solution)/shard_map/all_gather | solution.py:74
  224.6 29.0 %experts.1 = (bf16[1024,1152]{1,0:T(8,128)(2,1)}, f32[1024,128]{1,0:T(8,128)}, bf16[4,1024,512]{2,1,0:T(8,128)(2,1)}, bf16[4,1024,1024]{2,1,0:T(8,128)(2,1)}) custom-call(s32[1]{0:T(128)} %bitcast.group_ref, bf16[1024,1024]{1,0:T(8,128)(2,1)} %all-gather.8.cloned.1.call-done.n_ref, ...), custom_call_target="tpu_custom_call" | custom-call | flops 17179869184 | bytes 41943040 | tf_op jit(solution)/shard_map/experts/pallas_call | solution.py:648
  253.9 26.6 %expert_grads.1 = (bf16[1024,1024]{1,0:T(8,128)(2,1)}, bf16[4,1024,1536]{2,1,0:T(8,128)(2,1)}) custom-call(bf16[1024,1024]{1,0:T(8,128)(2,1)} %all-gather.8.cloned.1.call-done.n_ref, bf16[1024,1152]{1,0:T(8,128)(2,1)} %all-gather.6.cloned.1.call-done.refs_10_.routed_ref.ct_ref, bf16[4,1024,1536]{2,1,0:T(8,128)(2,1)} %get-tuple-element.109.w_ref, ...), custom_call_target="tpu_custom_call" | custom-call | flops 17179869184 | bytes 41943040 | tf_op jit(solution)/shard_map/expert_grads/pallas_call | solution.py:708
  280.5 20.1 %reduce-scatter.3.cloned.1.call-done = bf16[256,1152]{1,0:T(8,128)(2,1)} async-done(((bf16[1024,1152]{1,0:T(8,128)(2,1)}), bf16[256,1152]{1,0:T(8,128)(2,1)}) %reduce-scatter.3.cloned.1.call-update) | async-done | bytes 589840 | tf_op jit(solution)/shard_map/reduce_scatter | solution.py:78
  303.1 2.4 multiply_reduce_fusion
  310.1 3.0 fusion.18
  314.0 4.3 all-to-all-start.1
  318.4 4.5 dynamic-slice_bitcast_fusion.1
  322.9 6.5 %collective-permute-start.22 = (bf16[256,1024]{1,0:T(8,128)(2,1)S(1)}, bf16[256,1024]{1,0:T(8,128)(2,1)}, u32[]{:S(2)}, u32[]{:S(2)}) collective-permute-start(bf16[256,1024]{1,0:T(8,128)(2,1)S(1)} %get-tuple-element.223), channel_id=1, source_target_pairs={{0,24},{1,25},{2,26},{3,27},{4,28},{5,29},{6,30},{7,31}} | collective-permute-start | bytes 1572872 | tf_op jit(solution)/shard_map/ppermute | solution.py:96
  337.4 3.5 collective-permute-done.22
  340.8 5.2 %collective-permute-start.26 = (bf16[256,1024]{1,0:T(8,128)(2,1)}, bf16[256,1024]{1,0:T(8,128)(2,1)S(1)}, u32[]{:S(2)}, u32[]{:S(2)}) collective-permute-start(bf16[256,1024]{1,0:T(8,128)(2,1)} %get-tuple-element.219), channel_id=1, source_target_pairs={{0,8},{8,16},{16,24},{1,9},{9,17},{17,25},{2,10},{10,18},{18,26},{... | collective-permute-start | bytes 1572872 | tf_op jit(solution)/shard_map/ppermute | solution.py:96
  348.5 31.8 %attend_back.1.grad_ref = bf16[2048,256]{1,0:T(8,128)(2,1)} custom-call(s32[9]{0:T(128)} %pad_add_fusion.bounds_ref, bf16[2048,256]{1,0:T(8,128)(2,1)} %get-tuple-element.92.q_ref.kv_ref, bf16[2048,256]{1,0:T(8,128)(2,1)} %get-tuple-element.92.q_ref.kv_ref, s32[2048,1]{1,0:T(8,128)} %copy.96.doc_ref, bf16[2048,128]{1,0:T(8,128)(2,1)} %bitcast.24.do_ref, ...), custom_call_target="tpu_custom_call" | custom-call | flops 5368709120 | bytes 8388608 | tf_op jit(solution)/shard_map/attend_back/pallas_call | solution.py:481
  381.2 2.4 copy.100
  383.6 11.7 %all-to-all-start.2 = ((bf16[8,256,256]{1,2,0:T(8,128)(2,1)}), bf16[8,256,256]{1,2,0:T(8,128)(2,1)}, u32[]{:S(2)}, u32[]{:S(2)}) async-start(bf16[8,256,256]{1,2,0:T(8,128)(2,1)} %copy.100), calls=%async_computation.3 | async-start | bytes 2097152 | tf_op jit(solution)/shard_map/all_to_all | solution.py:737
  396.6 2.1 collective-permute-start.30
  398.7 23.3 %collective-permute-done.30 = bf16[4,32,1152]{2,1,0:T(8,128)(2,1)S(1)} collective-permute-done((bf16[4,32,1152]{2,1,0:T(8,128)(2,1)S(1)}, bf16[4,32,1152]{2,1,0:T(8,128)(2,1)S(1)}, u32[]{:S(2)}, u32[]{:S(2)}) %collective-permute-start.30) | collective-permute-done | bytes 294944 | tf_op jit(solution)/shard_map/ppermute | solution.py:134
  423.7 3.3 fusion.33
  427.0 5.0 %collective-permute-start.35 = (bf16[32,1152]{1,0:T(8,128)(2,1)S(1)}, bf16[32,1152]{1,0:T(8,128)(2,1)S(1)}, u32[]{:S(2)}, u32[]{:S(2)}) collective-permute-start(bf16[32,1152]{1,0:T(8,128)(2,1)S(1)} %get-tuple-element.227), channel_id=1, source_target_pairs={{0,8},{8,16},{16,24},{1,9},{9,17},{17,25},{2,10},{10,18},{18,26},{... | collective-permute-start | bytes 221192 | tf_op jit(solution)/shard_map/ppermute | solution.py:96
  433.3 5.4 %collective-permute-start.33 = (bf16[32,1152]{1,0:T(8,128)(2,1)S(1)}, bf16[32,1152]{1,0:T(8,128)(2,1)S(1)}, u32[]{:S(2)}, u32[]{:S(2)}) collective-permute-start(bf16[32,1152]{1,0:T(8,128)(2,1)S(1)} %get-tuple-element.229), channel_id=1, source_target_pairs={{0,16},{8,24},{1,17},{9,25},{2,18},{10,26},{3,19},{11,27},{4,20},{... | collective-permute-start | bytes 221192 | tf_op jit(solution)/shard_map/ppermute | solution.py:96
  440.1 6.3 %collective-permute-start.31 = (bf16[32,1152]{1,0:T(8,128)(2,1)S(1)}, bf16[32,1152]{1,0:T(8,128)(2,1)S(1)}, u32[]{:S(2)}, u32[]{:S(2)}) collective-permute-start(bf16[32,1152]{1,0:T(8,128)(2,1)S(1)} %get-tuple-element.225), channel_id=1, source_target_pairs={{0,24},{1,25},{2,26},{3,27},{4,28},{5,29},{6,30},{7,31}} | collective-permute-start | bytes 221192 | tf_op jit(solution)/shard_map/ppermute | solution.py:96
  446.5 9.7 %head_grads.1 = bf16[1024,384]{1,0:T(8,128)(2,1)} custom-call(s32[3]{0:T(128)} %pad_add_fusion.1.place_ref.head_ref, bf16[2048,1024]{1,0:T(8,128)(2,1)} %get-tuple-element.130.x_ref, bf16[2048,1024]{1,0:T(8,128)(2,1)} %get-tuple-element.131.normed_ref, bf16[1024,3200]{1,0:T(8,128)(2,1)} %all-gather.4.cloned.1.call-done.refs_14_.refs_15_.router_ref.w_ref, ...), custom_call_target="tpu_custom_call" | custom-call | flops 2147483648 | bytes 12582912 | tf_op jit(solution)/shard_map/head_grads/pallas_call | solution.py:271
  456.2 2.6 all-to-all-start.3
  461.0 4.1 fusion.26
  465.1 2.3 fusion.30
  467.4 12.0 %all-to-all-done.3 = bf16[32,32,384]{2,1,0:T(8,128)(2,1)S(1)} async-done(((bf16[32,32,384]{2,1,0:T(8,128)(2,1)}), bf16[32,32,384]{2,1,0:T(8,128)(2,1)S(1)}, u32[]{:S(2)}, u32[]{:S(2)}) %all-to-all-start.3) | async-done | bytes 786464 | tf_op jit(solution)/shard_map/all_to_all | solution.py:737
  482.6 2.9 slice.99
  (186 shorter events, 67.8 us)
Async XLA Ops:
  7.2 108.4 %all-gather.4.cloned.1.call-start = ((), (), s32[]{:S(2)}) async-start(), calls=%async_computation.6 | async-start | bytes 6758400 | tf_op jit(solution)/shard_map/all_gather | solution.py:74
  14.4 164.3 %all-gather.6.cloned.1.call-start = ((), (), s32[]{:S(2)}) async-start(), calls=%async_computation.7 | async-start | bytes 2949120 | tf_op jit(solution)/shard_map/all_gather | solution.py:74
  14.5 56.5 %collective-permute-start = (bf16[256,1024]{1,0:T(8,128)(2,1)}, bf16[256,1024]{1,0:T(8,128)(2,1)}, u32[]{:S(2)}, u32[]{:S(2)}) collective-permute-start(bf16[256,1024]{1,0:T(8,128)(2,1)} %bitcast.1.refs_0_), channel_id=1, source_target_pairs={{0,4},{4,0},{8,12},{12,8},{16,20},{20,16},{24,28},{28,24},{1,5},{5... | collective-permute-start | bytes 1572872 | tf_op jit(solution)/shard_map/ppermute | solution.py:104
  17.5 17.9 %collective-permute-start.1 = (bf16[256,1024]{1,0:T(8,128)(2,1)}, bf16[256,1024]{1,0:T(8,128)(2,1)}, u32[]{:S(2)}, u32[]{:S(2)}) collective-permute-start(bf16[256,1024]{1,0:T(8,128)(2,1)} %bitcast.1.refs_0_), channel_id=1, source_target_pairs={{0,8},{8,16},{16,24},{1,9},{9,17},{17,25},{2,10},{10,18},{18,26},{... | collective-permute-start | bytes 1572872 | tf_op jit(solution)/shard_map/ppermute | solution.py:111
  21.8 19.6 %collective-permute-start.3 = (bf16[256,1024]{1,0:T(8,128)(2,1)}, bf16[256,1024]{1,0:T(8,128)(2,1)}, u32[]{:S(2)}, u32[]{:S(2)}) collective-permute-start(bf16[256,1024]{1,0:T(8,128)(2,1)} %bitcast.1.refs_0_), channel_id=1, source_target_pairs={{8,0},{16,8},{24,16},{9,1},{17,9},{25,17},{10,2},{18,10},{26,18},{... | collective-permute-start | bytes 1572872 | tf_op jit(solution)/shard_map/ppermute | solution.py:112
  35.3 23.1 %collective-permute-start.5 = (bf16[256,1024]{1,0:T(8,128)(2,1)}, bf16[256,1024]{1,0:T(8,128)(2,1)S(1)}, u32[]{:S(2)}, u32[]{:S(2)}) collective-permute-start(bf16[256,1024]{1,0:T(8,128)(2,1)} %collective-permute-done.1.refs_2_), channel_id=1, source_target_pairs={{0,8},{8,16},{16,24},{1,9},{9,17},{17,25},{2,10},{10,18},{18,26},{... | collective-permute-start | bytes 1572872 | tf_op jit(solution)/shard_map/ppermute | solution.py:111
  41.4 23.3 %collective-permute-start.7 = (bf16[256,1024]{1,0:T(8,128)(2,1)}, bf16[256,1024]{1,0:T(8,128)(2,1)}, u32[]{:S(2)}, u32[]{:S(2)}) collective-permute-start(bf16[256,1024]{1,0:T(8,128)(2,1)} %collective-permute-done.3.refs_4_), channel_id=1, source_target_pairs={{8,0},{16,8},{24,16},{9,1},{17,9},{25,17},{10,2},{18,10},{26,18},{... | collective-permute-start | bytes 1572872 | tf_op jit(solution)/shard_map/ppermute | solution.py:112
  42.7 29.0 %collective-permute-start.2 = (bf16[256,1024]{1,0:T(8,128)(2,1)}, bf16[256,1024]{1,0:T(8,128)(2,1)}, u32[]{:S(2)}, u32[]{:S(2)}) collective-permute-start(bf16[256,1024]{1,0:T(8,128)(2,1)} %collective-permute-done.1.refs_2_), channel_id=1, source_target_pairs={{8,12},{12,8},{16,20},{20,16},{24,28},{28,24},{9,13},{13,9},{17,21... | collective-permute-start | bytes 1572872 | tf_op jit(solution)/shard_map/ppermute | solution.py:104
  58.5 17.2 %collective-permute-start.9 = (bf16[256,1024]{1,0:T(8,128)(2,1)S(1)}, bf16[256,1024]{1,0:T(8,128)(2,1)}, u32[]{:S(2)}, u32[]{:S(2)}) collective-permute-start(bf16[256,1024]{1,0:T(8,128)(2,1)S(1)} %collective-permute-done.5.refs_6_), channel_id=1, source_target_pairs={{0,8},{8,16},{16,24},{1,9},{9,17},{17,25},{2,10},{10,18},{18,26},{... | collective-permute-start | bytes 1572872 | tf_op jit(solution)/shard_map/ppermute | solution.py:111
  64.7 20.2 %collective-permute-start.11 = (bf16[256,1024]{1,0:T(8,128)(2,1)}, bf16[256,1024]{1,0:T(8,128)(2,1)}, u32[]{:S(2)}, u32[]{:S(2)}) collective-permute-start(bf16[256,1024]{1,0:T(8,128)(2,1)} %collective-permute-done.7.refs_8_), channel_id=1, source_target_pairs={{8,0},{16,8},{24,16},{9,1},{17,9},{25,17},{10,2},{18,10},{26,18},{... | collective-permute-start | bytes 1572872 | tf_op jit(solution)/shard_map/ppermute | solution.py:112
  69.1 92.2 %copy-start.10 = (bf16[512,1536]{1,0:T(8,128)(2,1)}, bf16[512,1536]{1,0:T(8,128)(2,1)S(1)}, u32[]{:S(2)}) copy-start(bf16[512,1536]{1,0:T(8,128)(2,1)S(1)} %pad_maximum_fusion.refs_0_) | copy-start | bytes 4718596
  69.1 27.0 %collective-permute-start.4 = (bf16[256,1024]{1,0:T(8,128)(2,1)}, bf16[256,1024]{1,0:T(8,128)(2,1)S(1)}, u32[]{:S(2)}, u32[]{:S(2)}) collective-permute-start(bf16[256,1024]{1,0:T(8,128)(2,1)} %collective-permute-done.3.refs_4_), channel_id=1, source_target_pairs={{0,4},{4,0},{8,12},{12,8},{16,20},{20,16},{1,5},{5,1},{9,13},{13,9... | collective-permute-start | bytes 1572872 | tf_op jit(solution)/shard_map/ppermute | solution.py:104
  71.0 25.0 %collective-permute-start.6 = (bf16[256,1024]{1,0:T(8,128)(2,1)S(1)}, bf16[256,1024]{1,0:T(8,128)(2,1)S(1)}, u32[]{:S(2)}, u32[]{:S(2)}) collective-permute-start(bf16[256,1024]{1,0:T(8,128)(2,1)S(1)} %collective-permute-done.5.refs_6_), channel_id=1, source_target_pairs={{16,20},{20,16},{24,28},{28,24},{17,21},{21,17},{25,29},{29,25},{1... | collective-permute-start | bytes 1572872 | tf_op jit(solution)/shard_map/ppermute | solution.py:104
  71.7 35.6 %collective-permute-start.8 = (bf16[256,1024]{1,0:T(8,128)(2,1)}, bf16[256,1024]{1,0:T(8,128)(2,1)}, u32[]{:S(2)}, u32[]{:S(2)}) collective-permute-start(bf16[256,1024]{1,0:T(8,128)(2,1)} %collective-permute-done.7.refs_8_), channel_id=1, source_target_pairs={{0,4},{4,0},{8,12},{12,8},{1,5},{5,1},{9,13},{13,9},{2,6},{6,2},{1... | collective-permute-start | bytes 1572872 | tf_op jit(solution)/shard_map/ppermute | solution.py:104
  75.7 31.7 %collective-permute-start.10 = (bf16[256,1024]{1,0:T(8,128)(2,1)}, bf16[256,1024]{1,0:T(8,128)(2,1)}, u32[]{:S(2)}, u32[]{:S(2)}) collective-permute-start(bf16[256,1024]{1,0:T(8,128)(2,1)} %collective-permute-done.9.refs_10_), channel_id=1, source_target_pairs={{24,28},{28,24},{25,29},{29,25},{26,30},{30,26},{27,31},{31,27}} | collective-permute-start | bytes 1572872 | tf_op jit(solution)/shard_map/ppermute | solution.py:104
  85.0 30.7 %collective-permute-start.12 = (bf16[256,1024]{1,0:T(8,128)(2,1)}, bf16[256,1024]{1,0:T(8,128)(2,1)}, u32[]{:S(2)}, u32[]{:S(2)}) collective-permute-start(bf16[256,1024]{1,0:T(8,128)(2,1)} %collective-permute-done.11.refs_12_), channel_id=1, source_target_pairs={{0,4},{4,0},{1,5},{5,1},{2,6},{6,2},{3,7},{7,3}} | collective-permute-start | bytes 1572872 | tf_op jit(solution)/shard_map/ppermute | solution.py:104
  115.7 41.2 %collective-permute-start.16 = (bf16[512,1536]{1,0:T(8,128)(2,1)S(1)}, bf16[512,1536]{1,0:T(8,128)(2,1)}, u32[]{:S(2)}, u32[]{:S(2)}) collective-permute-start(bf16[512,1536]{1,0:T(8,128)(2,1)S(1)} %pad_maximum_fusion.refs_0_), channel_id=1, source_target_pairs={{0,4},{4,0},{1,5},{5,1},{2,6},{6,2},{3,7},{7,3},{8,12},{12,8},{9,1... | collective-permute-start | bytes 4718600 | tf_op jit(solution)/shard_map/ppermute | solution.py:122
  115.9 42.2 %collective-permute-start.14 = (bf16[512,1536]{1,0:T(8,128)(2,1)S(1)}, bf16[512,1536]{1,0:T(8,128)(2,1)}, u32[]{:S(2)}, u32[]{:S(2)}) collective-permute-start(bf16[512,1536]{1,0:T(8,128)(2,1)S(1)} %pad_maximum_fusion.refs_0_), channel_id=1, source_target_pairs={{0,2},{2,0},{1,3},{3,1},{4,6},{6,4},{5,7},{7,5},{8,10},{10,8},{9,1... | collective-permute-start | bytes 4718600 | tf_op jit(solution)/shard_map/ppermute | solution.py:121
  153.3 21.7 %all-to-all-start = ((bf16[8,256,128]{1,2,0:T(8,128)(2,1)}), bf16[8,256,128]{1,2,0:T(8,128)(2,1)S(1)}, u32[]{:S(2)}, u32[]{:S(2)}) async-start(bf16[8,256,128]{1,2,0:T(8,128)(2,1)} %copy.97), calls=%async_computation | async-start | bytes 1048576 | tf_op jit(solution)/shard_map/all_to_all | solution.py:737
  156.8 67.8 %all-gather.8.cloned.1.call-start = ((), (), s32[]{:S(2)}) async-start(), calls=%async_computation.8 | async-start | bytes 2621440 | tf_op jit(solution)/shard_map/all_gather | solution.py:74
  158.0 12.2 %collective-permute-start.18 = (bf16[256,1536]{1,0:T(8,128)(2,1)S(1)}, bf16[256,1536]{1,0:T(8,128)(2,1)}, u32[]{:S(2)}, u32[]{:S(2)}) collective-permute-start(bf16[256,1536]{1,0:T(8,128)(2,1)S(1)} %slice.89), channel_id=1, source_target_pairs={{0,2},{2,0},{1,3},{3,1},{4,6},{6,4},{5,7},{7,5},{8,10},{10,8},{9,1... | collective-permute-start | bytes 2359304 | tf_op jit(solution)/shard_map/ppermute | solution.py:123
  159.3 15.7 %collective-permute-start.20 = (bf16[256,1536]{1,0:T(8,128)(2,1)S(1)}, bf16[256,1536]{1,0:T(8,128)(2,1)}, u32[]{:S(2)}, u32[]{:S(2)}) collective-permute-start(bf16[256,1536]{1,0:T(8,128)(2,1)S(1)} %slice.90), channel_id=1, source_target_pairs={{0,4},{4,0},{1,5},{5,1},{2,6},{6,2},{3,7},{7,3},{8,12},{12,8},{9,1... | collective-permute-start | bytes 2359304 | tf_op jit(solution)/shard_map/ppermute | solution.py:124
  161.2 17.5 %collective-permute-start.13 = (bf16[512,1536]{1,0:T(8,128)(2,1)S(1)}, bf16[512,1536]{1,0:T(8,128)(2,1)}, u32[]{:S(2)}, u32[]{:S(2)}) collective-permute-start(bf16[512,1536]{1,0:T(8,128)(2,1)S(1)} %pad_maximum_fusion.refs_0_), channel_id=1, source_target_pairs={{0,1},{1,0},{2,3},{3,2},{4,5},{5,4},{6,7},{7,6},{8,9},{9,8},{10,11... | collective-permute-start | bytes 4718600 | tf_op jit(solution)/shard_map/ppermute | solution.py:126
  161.2 17.5 %collective-permute-start.15 = (bf16[512,1536]{1,0:T(8,128)(2,1)}, bf16[512,1536]{1,0:T(8,128)(2,1)}, u32[]{:S(2)}, u32[]{:S(2)}) collective-permute-start(bf16[512,1536]{1,0:T(8,128)(2,1)} %collective-permute-done.14.refs_2_), channel_id=1, source_target_pairs={{0,1},{1,0},{2,3},{3,2},{4,5},{5,4},{6,7},{7,6},{8,9},{9,8},{10,11... | collective-permute-start | bytes 4718600 | tf_op jit(solution)/shard_map/ppermute | solution.py:126
  161.7 17.0 %collective-permute-start.17 = (bf16[512,1536]{1,0:T(8,128)(2,1)}, bf16[512,1536]{1,0:T(8,128)(2,1)}, u32[]{:S(2)}, u32[]{:S(2)}) collective-permute-start(bf16[512,1536]{1,0:T(8,128)(2,1)} %collective-permute-done.16.refs_4_), channel_id=1, source_target_pairs={{0,1},{1,0},{2,3},{3,2},{4,5},{5,4},{6,7},{7,6},{8,9},{9,8},{10,11... | collective-permute-start | bytes 4718600 | tf_op jit(solution)/shard_map/ppermute | solution.py:126
  170.2 8.5 %collective-permute-start.19 = (bf16[256,1536]{1,0:T(8,128)(2,1)}, bf16[256,1536]{1,0:T(8,128)(2,1)}, u32[]{:S(2)}, u32[]{:S(2)}) collective-permute-start(bf16[256,1536]{1,0:T(8,128)(2,1)} %collective-permute-done.18.refs_6_), channel_id=1, source_target_pairs={{0,1},{1,0},{2,3},{3,2},{4,5},{5,4},{6,7},{7,6},{8,9},{9,8},{10,11... | collective-permute-start | bytes 2359304 | tf_op jit(solution)/shard_map/ppermute | solution.py:126
  175.0 3.7 collective-permute-start.21
  178.8 121.8 %reduce-scatter.3.cloned.1.call-start = ((), (), s32[]{:S(2)}) async-start(), calls=%async_computation.9 | async-start | bytes 2949120 | tf_op jit(solution)/shard_map/reduce_scatter | solution.py:78
  253.6 228.9 %reduce-scatter.5.cloned.1.call-start = ((), (), s32[]{:S(2)}) async-start(), calls=%async_computation.10 | async-start | bytes 14155776 | tf_op jit(solution)/shard_map/reduce_scatter | solution.py:78
  310.1 20.5 %collective-permute-start.28 = (bf16[4,2,2,32,1152]{4,3,2,1,0:T(8,128)(2,1)}, bf16[4,2,2,32,1152]{4,3,2,1,0:T(8,128)(2,1)}, u32[]{:S(2)}, u32[]{:S(2)}) collective-permute-start(bf16[4,2,2,32,1152]{4,3,2,1,0:T(8,128)(2,1)} %fusion.22), channel_id=1, source_target_pairs={{0,1},{1,0},{2,3},{3,2},{4,5},{5,4},{6,7},{7,6},{8,9},{9,8},{10,11... | collective-permute-start | bytes 3538952 | tf_op jit(solution)/shard_map/ppermute | solution.py:134
  314.0 34.4 %all-to-all-start.1 = ((bf16[8,256,128]{2,1,0:T(8,128)(2,1)}), bf16[8,256,128]{2,1,0:T(8,128)(2,1)}, u32[]{:S(2)}, u32[]{:S(2)}) async-start(bf16[8,256,128]{2,1,0:T(8,128)(2,1)} %bitcast.128), calls=%async_computation.2 | async-start | bytes 1048576 | tf_op jit(solution)/shard_map/all_to_all | solution.py:737
  322.9 18.0 %collective-permute-start.22 = (bf16[256,1024]{1,0:T(8,128)(2,1)S(1)}, bf16[256,1024]{1,0:T(8,128)(2,1)}, u32[]{:S(2)}, u32[]{:S(2)}) collective-permute-start(bf16[256,1024]{1,0:T(8,128)(2,1)S(1)} %get-tuple-element.223), channel_id=1, source_target_pairs={{0,24},{1,25},{2,26},{3,27},{4,28},{5,29},{6,30},{7,31}} | collective-permute-start | bytes 1572872 | tf_op jit(solution)/shard_map/ppermute | solution.py:96
  329.3 17.9 %collective-permute-start.23 = (bf16[256,1024]{1,0:T(8,128)(2,1)S(1)}, bf16[256,1024]{1,0:T(8,128)(2,1)}, u32[]{:S(2)}, u32[]{:S(2)}) collective-permute-start(bf16[256,1024]{1,0:T(8,128)(2,1)S(1)} %get-tuple-element.222), channel_id=1, source_target_pairs={{24,0},{25,1},{26,2},{27,3},{28,4},{29,5},{30,6},{31,7}} | collective-permute-start | bytes 1572872 | tf_op jit(solution)/shard_map/ppermute | solution.py:96
  333.3 62.0 %collective-permute-start.29 = (bf16[4,2,32,1152]{3,2,1,0:T(8,128)(2,1)S(1)}, bf16[4,2,32,1152]{3,2,1,0:T(8,128)(2,1)}, u32[]{:S(2)}, u32[]{:S(2)}) collective-permute-start(bf16[4,2,32,1152]{3,2,1,0:T(8,128)(2,1)S(1)} %dynamic-slice_bitcast_fusion), channel_id=1, source_target_pairs={{0,2},{2,0},{1,3},{3,1},{4,6},{6,4},{5,7},{7,5},{8,10},{10,8},{9,1... | collective-permute-start | bytes 1769480 | tf_op jit(solution)/shard_map/ppermute | solution.py:134
  334.7 45.5 %collective-permute-start.24 = (bf16[256,1024]{1,0:T(8,128)(2,1)}, bf16[256,1024]{1,0:T(8,128)(2,1)S(1)}, u32[]{:S(2)}, u32[]{:S(2)}) collective-permute-start(bf16[256,1024]{1,0:T(8,128)(2,1)} %get-tuple-element.221), channel_id=1, source_target_pairs={{0,16},{8,24},{1,17},{9,25},{2,18},{10,26},{3,19},{11,27},{4,20},{... | collective-permute-start | bytes 1572872 | tf_op jit(solution)/shard_map/ppermute | solution.py:96
  336.1 44.2 %collective-permute-start.25 = (bf16[256,1024]{1,0:T(8,128)(2,1)}, bf16[256,1024]{1,0:T(8,128)(2,1)S(1)}, u32[]{:S(2)}, u32[]{:S(2)}) collective-permute-start(bf16[256,1024]{1,0:T(8,128)(2,1)} %get-tuple-element.220), channel_id=1, source_target_pairs={{16,0},{24,8},{17,1},{25,9},{18,2},{26,10},{19,3},{27,11},{20,4},{... | collective-permute-start | bytes 1572872 | tf_op jit(solution)/shard_map/ppermute | solution.py:96
  340.8 39.5 %collective-permute-start.26 = (bf16[256,1024]{1,0:T(8,128)(2,1)}, bf16[256,1024]{1,0:T(8,128)(2,1)S(1)}, u32[]{:S(2)}, u32[]{:S(2)}) collective-permute-start(bf16[256,1024]{1,0:T(8,128)(2,1)} %get-tuple-element.219), channel_id=1, source_target_pairs={{0,8},{8,16},{16,24},{1,9},{9,17},{17,25},{2,10},{10,18},{18,26},{... | collective-permute-start | bytes 1572872 | tf_op jit(solution)/shard_map/ppermute | solution.py:96
  347.2 33.1 %collective-permute-start.27 = (bf16[256,1024]{1,0:T(8,128)(2,1)}, bf16[256,1024]{1,0:T(8,128)(2,1)}, u32[]{:S(2)}, u32[]{:S(2)}) collective-permute-start(bf16[256,1024]{1,0:T(8,128)(2,1)} %get-tuple-element.218), channel_id=1, source_target_pairs={{8,0},{16,8},{24,16},{9,1},{17,9},{25,17},{10,2},{18,10},{26,18},{... | collective-permute-start | bytes 1572872 | tf_op jit(solution)/shard_map/ppermute | solution.py:96
  383.6 72.6 %all-to-all-start.2 = ((bf16[8,256,256]{1,2,0:T(8,128)(2,1)}), bf16[8,256,256]{1,2,0:T(8,128)(2,1)}, u32[]{:S(2)}, u32[]{:S(2)}) async-start(bf16[8,256,256]{1,2,0:T(8,128)(2,1)} %copy.100), calls=%async_computation.3 | async-start | bytes 2097152 | tf_op jit(solution)/shard_map/all_to_all | solution.py:737
  395.3 28.4 %copy-start.6 = (bf16[256,1024]{1,0:T(8,128)(2,1)S(1)}, bf16[256,1024]{1,0:T(8,128)(2,1)}, u32[]{:S(2)}) copy-start(bf16[256,1024]{1,0:T(8,128)(2,1)} %get-tuple-element.122) | copy-start | bytes 1572868
  396.6 25.4 %collective-permute-start.30 = (bf16[4,32,1152]{2,1,0:T(8,128)(2,1)S(1)}, bf16[4,32,1152]{2,1,0:T(8,128)(2,1)S(1)}, u32[]{:S(2)}, u32[]{:S(2)}) collective-permute-start(bf16[4,32,1152]{2,1,0:T(8,128)(2,1)S(1)} %dynamic-slice_bitcast_fusion.8), channel_id=1, source_target_pairs={{0,4},{4,0},{1,5},{5,1},{2,6},{6,2},{3,7},{7,3},{8,12},{12,8},{9,1... | collective-permute-start | bytes 884744 | tf_op jit(solution)/shard_map/ppermute | solution.py:134
  422.1 18.0 %collective-permute-start.36 = (bf16[32,1152]{1,0:T(8,128)(2,1)S(1)}, bf16[32,1152]{1,0:T(8,128)(2,1)S(1)}, u32[]{:S(2)}, u32[]{:S(2)}) collective-permute-start(bf16[32,1152]{1,0:T(8,128)(2,1)S(1)} %get-tuple-element.226), channel_id=1, source_target_pairs={{8,0},{16,8},{24,16},{9,1},{17,9},{25,17},{10,2},{18,10},{26,18},{... | collective-permute-start | bytes 221192 | tf_op jit(solution)/shard_map/ppermute | solution.py:96
  427.0 31.8 %collective-permute-start.35 = (bf16[32,1152]{1,0:T(8,128)(2,1)S(1)}, bf16[32,1152]{1,0:T(8,128)(2,1)S(1)}, u32[]{:S(2)}, u32[]{:S(2)}) collective-permute-start(bf16[32,1152]{1,0:T(8,128)(2,1)S(1)} %get-tuple-element.227), channel_id=1, source_target_pairs={{0,8},{8,16},{16,24},{1,9},{9,17},{17,25},{2,10},{10,18},{18,26},{... | collective-permute-start | bytes 221192 | tf_op jit(solution)/shard_map/ppermute | solution.py:96
  432.0 26.8 %collective-permute-start.34 = (bf16[32,1152]{1,0:T(8,128)(2,1)S(1)}, bf16[32,1152]{1,0:T(8,128)(2,1)S(1)}, u32[]{:S(2)}, u32[]{:S(2)}) collective-permute-start(bf16[32,1152]{1,0:T(8,128)(2,1)S(1)} %get-tuple-element.228), channel_id=1, source_target_pairs={{16,0},{24,8},{17,1},{25,9},{18,2},{26,10},{19,3},{27,11},{20,4},{... | collective-permute-start | bytes 221192 | tf_op jit(solution)/shard_map/ppermute | solution.py:96
  433.3 25.5 %collective-permute-start.33 = (bf16[32,1152]{1,0:T(8,128)(2,1)S(1)}, bf16[32,1152]{1,0:T(8,128)(2,1)S(1)}, u32[]{:S(2)}, u32[]{:S(2)}) collective-permute-start(bf16[32,1152]{1,0:T(8,128)(2,1)S(1)} %get-tuple-element.229), channel_id=1, source_target_pairs={{0,16},{8,24},{1,17},{9,25},{2,18},{10,26},{3,19},{11,27},{4,20},{... | collective-permute-start | bytes 221192 | tf_op jit(solution)/shard_map/ppermute | solution.py:96
  438.8 20.0 %collective-permute-start.32 = (bf16[32,1152]{1,0:T(8,128)(2,1)S(1)}, bf16[32,1152]{1,0:T(8,128)(2,1)S(1)}, u32[]{:S(2)}, u32[]{:S(2)}) collective-permute-start(bf16[32,1152]{1,0:T(8,128)(2,1)S(1)} %get-tuple-element.230), channel_id=1, source_target_pairs={{24,0},{25,1},{26,2},{27,3},{28,4},{29,5},{30,6},{31,7}} | collective-permute-start | bytes 221192 | tf_op jit(solution)/shard_map/ppermute | solution.py:96
  440.1 18.7 %collective-permute-start.31 = (bf16[32,1152]{1,0:T(8,128)(2,1)S(1)}, bf16[32,1152]{1,0:T(8,128)(2,1)S(1)}, u32[]{:S(2)}, u32[]{:S(2)}) collective-permute-start(bf16[32,1152]{1,0:T(8,128)(2,1)S(1)} %get-tuple-element.225), channel_id=1, source_target_pairs={{0,24},{1,25},{2,26},{3,27},{4,28},{5,29},{6,30},{7,31}} | collective-permute-start | bytes 221192 | tf_op jit(solution)/shard_map/ppermute | solution.py:96
  456.2 23.2 %all-to-all-start.3 = ((bf16[32,32,384]{2,1,0:T(8,128)(2,1)}), bf16[32,32,384]{2,1,0:T(8,128)(2,1)S(1)}, u32[]{:S(2)}, u32[]{:S(2)}) async-start(bf16[32,32,384]{2,1,0:T(8,128)(2,1)} %bitcast.123), calls=%async_computation.4 | async-start | bytes 1572864 | tf_op jit(solution)/shard_map/all_to_all | solution.py:737
  (20 other events, 177.8 us)
Sparse Core Ops, SparseCore 0:
  14.5 92.2 all-gather.3
  115.8 57.7 all-gather.5
  178.9 45.6 all-gather.7
  253.7 46.8 reduce-scatter.2
  303.9 122.4 reduce-scatter.4
where the time goes:
time: 497 us; the launch traced here: 493 us
  waiting for transfers between devices  155 us (31%)
  Pallas kernels  147 us (30%)
  starting transfers between devices  101 us (20%)
  other arithmetic  36.1 us (7%)
  local copies, waits for them, and re-layouts  26.1 us (5%)
  between operations  14.6 us (3%)
  matrix products  13.3 us (3%)
    ppermute x12, starting transfers between devices, line_send(): terms.append(lax.ppermute(block, axis, line_pairs(n, step)))  37.9 us
    pallas_call x1, Pallas kernels, attend_back(): pl.pallas_call(functools.partial(attend_back_kernel, fold), grid_spec=plt...  31.8 us
    pallas_call x1, Pallas kernels, experts(): pl.pallas_call(experts_kernel, grid_spec=pltpu.PrefetchScalarGridSpec(num...  29 us
    pallas_call x1, Pallas kernels, expert_grads(): pl.pallas_call(expert_grads_kernel, grid=(count,), in_specs=[whole, whole...  26.6 us
    all_gather x3, waiting for transfers between devices, gather(): return lax.all_gather(x, axes, axis=0, tiled=True)  26.3 us
    ppermute x3, waiting for transfers between devices, grid_gather(): up = lax.ppermute(up, 'a', line_pairs(n, 1))  23.4 us
    ppermute x3, waiting for transfers between devices, halve(): lax.ppermute(lax.dynamic_index_in_dim(v, 1 - me, at, False), axis, [(0, 1...  23.3 us
    ppermute x7, waiting for transfers between devices, cross(): lax.ppermute(block, SEQ, [(2 * i + j, 2 * i + 1 - j) for i in range(n) if...  22.7 us
  transfers between devices with their start and end apart: 46, of which 16 were waited for; matrix products, arithmetic and copies ran while one was open for 12% of the time, Pallas kernels for 24%

commit v1 on v0

--- a/solution.py
+++ b/solution.py
@@ -86,17 +86,6 @@
     return [(i, i + step) for i in range(n) if 0 <= i + step < n]
 
 
-def line_send(v, axis):
-    n, me = lax.axis_size(axis), lax.axis_index(axis)
-    v = v.reshape((n, v.shape[0] // n) + v.shape[1:])
-    terms = [lax.dynamic_index_in_dim(v, me, 0, False)]
-    for j in range(n - 1, 0, -1):
-        for step in (j, -j):
-            block = lax.dynamic_index_in_dim(v, jnp.clip(me + step, 0, n - 1), 0, False)
-            terms.append(lax.ppermute(block, axis, line_pairs(n, step)))
-    return tuple(terms)
-
-
 def grid_gather(x):
     n = lax.axis_size("a")
 
@@ -127,19 +116,15 @@
     ]
 
 
-def halve(v, axis, at):
-    if lax.axis_size(axis) != 2:
-        return lax.psum_scatter(v, axis, scatter_dimension=at, tiled=False)
+def halve_send(v, axis, at):
     me = lax.axis_index(axis)
     other = lax.ppermute(lax.dynamic_index_in_dim(v, 1 - me, at, False), axis, [(0, 1), (1, 0)])
-    own = lax.dynamic_index_in_dim(v, me, at, False)
-    return (own.astype(f32) + other.astype(f32)).astype(v.dtype)
-
-
-def sum_over_row(v):
-    sizes = tuple(lax.axis_size(axis) for axis in ALL)
-    v = v.reshape(sizes + (v.shape[0] // lax.axis_size(ALL), v.shape[1]))
-    return halve(halve(v, "c", 3), "y", 2)
+    return lax.dynamic_index_in_dim(v, me, at, False), other
+
+
+def halve_add(terms):
+    own, other = terms
+    return (own.astype(f32) + other.astype(f32)).astype(own.dtype)
 
 
 def rotate_lanes(x, cos, sin):
@@ -679,58 +664,126 @@
     )(group, normed, early, packed, w_all, z)
 
 
-def expert_grads_kernel(n_ref, ct_ref, w_ref, hidden_ref, pre_ref, y_ref, grad_ref, n_t, ct_t, acc):
+def expert_grads_kernel(with_y, half_ref, n_ref, ct_ref, w_ref, hidden_ref, pre_ref, *refs):
+    if with_y:
+        y_ref, grad_ref, n_t, ct_t, acc = refs
+    else:
+        grad_ref, n_t, ct_t = refs
     e = pl.program_id(0)
 
     @pl.when(e == 0)
     def _():
         n_t[...] = jnp.transpose(n_ref[...])
         ct_t[...] = jnp.transpose(ct_ref[...])
-        acc[...] = jnp.zeros_like(acc)
-
-    grad_ref[0, :, : 2 * F] = jnp.dot(
-        n_t[...], pre_ref[0], preferred_element_type=f32
-    ).astype(bf16)
+        if with_y:
+            acc[...] = jnp.zeros_like(acc)
+
+    grad_ref[0, :, : 2 * F] = jnp.dot(n_t[...], pre_ref[0], preferred_element_type=f32).astype(bf16)
     grad_ref[0, :, 2 * F :] = (
         RESIDUAL_SCALE * jnp.dot(ct_t[...], hidden_ref[0], preferred_element_type=f32)
     ).astype(bf16)
+    if not with_y:
+        return
     acc[...] += contract_cols(hidden_ref[0], w_ref[0, :, 2 * F :])
 
-    @pl.when(e == EXPERTS_HERE - 1)
+    @pl.when(e == pl.num_programs(0) - 1)
     def _():
         y_ref[...] = acc[...].astype(bf16)
 
 
-def expert_grads(normed, early, w_all, hidden, pre):
+def expert_grads(half, halves, normed, early, w_all, hidden, pre, with_y):
     rows, width = normed.shape
     count = w_all.shape[0]
-    whole = pl.BlockSpec((rows, width), lambda e: (0, 0))
+    own = width // halves
+    feature = pl.BlockSpec((rows, own), lambda e, h: (0, h[0]))
+    out_specs = [pl.BlockSpec((1, own, 3 * F), lambda e, h: (e, 0, 0))]
+    out_shape = [jax.ShapeDtypeStruct((count, own, 3 * F), bf16)]
+    scratch = [pltpu.VMEM((own, rows), bf16), pltpu.VMEM((own, rows), bf16)]
+    if with_y:
+        out_specs.insert(0, pl.BlockSpec((rows, width), lambda e, h: (0, 0)))
+        out_shape.insert(0, jax.ShapeDtypeStruct((rows, width), bf16))
+        scratch.append(pltpu.VMEM((rows, width), f32))
     return pl.pallas_call(
-        expert_grads_kernel,
-        grid=(count,),
-        in_specs=[
-            whole,
-            whole,
-            pl.BlockSpec((1, width, 3 * F), lambda e: (e, 0, 0)),
-            pl.BlockSpec((1, rows, F), lambda e: (e, 0, 0)),
-            pl.BlockSpec((1, rows, 2 * F), lambda e: (e, 0, 0)),
-        ],
-        out_specs=[whole, pl.BlockSpec((1, width, 3 * F), lambda e: (e, 0, 0))],
+        functools.partial(expert_grads_kernel, with_y),
+        grid_spec=pltpu.PrefetchScalarGridSpec(
+            num_scalar_prefetch=1,
+            grid=(count,),
+            in_specs=[
+                feature,
+                feature,
+                pl.BlockSpec((1, width, 3 * F), lambda e, h: (e, 0, 0)),
+                pl.BlockSpec((1, rows, F), lambda e, h: (e, 0, 0)),
+                pl.BlockSpec((1, rows, 2 * F), lambda e, h: (e, 0, 0)),
+            ],
+            out_specs=out_specs,
+            scratch_shapes=scratch,
+        ),
+        out_shape=out_shape,
+        compiler_params=pltpu.CompilerParams(vmem_limit_bytes=VMEM_LIMIT),
+        cost_estimate=pl.CostEstimate(
+            flops=2 * count * rows * width * 3 * F // halves + 2 * with_y * count * rows * width * F,
+            bytes_accessed=30 * 2**20,
+            transcendentals=0,
+        ),
+        name="expert_grads",
+    )(half, normed, early, w_all, hidden, pre)
+
+
+def join_kernel(place_ref, o_ref, w_ref, small_ref, x_ref, normed_ref, resid_ref, own_ref, gain):
+    t = pl.program_id(0)
+    b = place_ref[2]
+
+    @pl.when(t == 0)
+    def _():
+        gain[...] = jnp.transpose(small_ref[...].astype(f32))[E : E + 8, :]
+
+    pairs = []
+    for a in range(o_ref.shape[0]):
+        same, other = o_ref[a, 0, 0], o_ref[a, 1, 0]
+        pairs.append(jnp.where(b == 0, same, other))
+        pairs.append(jnp.where(b == 0, other, same))
+    attended = jnp.concatenate(pairs, axis=1)
+    resid = x_ref[...].astype(f32) + RESIDUAL_SCALE * jnp.dot(
+        attended, w_ref[...], preferred_element_type=f32
+    )
+    normed_ref[...] = rms_scale(resid, gain[1:2, :]).astype(bf16)
+
+    @pl.when(t == place_ref[1])
+    def _():
+        resid_ref[...] = resid
+        own_ref[...] = attended
+
+
+def join(place, outs, packed, weights_at, x):
+    width = packed.shape[0]
+    lines, _, _, rows, pair = outs.shape
+    small_at = packed.shape[1] // LANES - 1
+    own = pl.BlockSpec((rows, width), lambda t, s: (0, 0))
+    return pl.pallas_call(
+        join_kernel,
+        grid_spec=pltpu.PrefetchScalarGridSpec(
+            num_scalar_prefetch=1,
+            grid=(lines,),
+            in_specs=[
+                pl.BlockSpec((lines, 2, 1, rows, pair), lambda t, s: (0, 0, t, 0, 0)),
+                pl.BlockSpec((width, width), lambda t, s: (0, weights_at)),
+                pl.BlockSpec((width, LANES), lambda t, s: (0, small_at)),
+                pl.BlockSpec((rows, width), lambda t, s: (2 * t + s[2], 0)),
+            ],
+            out_specs=[pl.BlockSpec((rows, width), lambda t, s: (t, 0)), own, own],
+            scratch_shapes=[pltpu.VMEM((8, width), f32)],
+        ),
         out_shape=[
+            jax.ShapeDtypeStruct((lines * rows, width), bf16),
+            jax.ShapeDtypeStruct((rows, width), f32),
             jax.ShapeDtypeStruct((rows, width), bf16),
-            jax.ShapeDtypeStruct((count, width, 3 * F), bf16),
-        ],
-        scratch_shapes=[
-            pltpu.VMEM((width, rows), bf16),
-            pltpu.VMEM((width, rows), bf16),
-            pltpu.VMEM((rows, width), f32),
         ],
         compiler_params=pltpu.CompilerParams(vmem_limit_bytes=VMEM_LIMIT),
         cost_estimate=pl.CostEstimate(
-            flops=2 * count * rows * width * 4 * F, bytes_accessed=40 * 2**20, transcendentals=0
-        ),
-        name="expert_grads",
-    )(normed, early, w_all, hidden, pre)
+            flops=2 * lines * rows * width * width, bytes_accessed=12 * 2**20, transcendentals=0
+        ),
+        name="join",
+    )(place, outs, packed, packed, x)
 
 
 def exchange(x, axes):
@@ -847,21 +900,29 @@
     else:
         kv, kv_at = gather(qkv[:, PAIR:], "a"), 0
     attention_result, attended, log_total = attend(bounds, qkv, kv, kv_at, doc_column)
-    attended_low = (
-        exchange(attended.reshape(KEY_VALUE_HEADS, token_count, PAIR), head_axes)
-        .transpose(1, 0, 2)
-        .reshape(token_count, QUERY_HEADS * HEAD_SIZE)
-    )
-    attn_out = jnp.dot(attended_low, output_w, preferred_element_type=f32)
-    resid = x_local + RESIDUAL_SCALE * attn_out
-    normed_two = rms_scale(resid, gain_two_f).astype(bf16)
-
-    normed_two, parts, early_all = lax.optimization_barrier((normed_two, parts, early_all))
-    normed_all = gather(normed_two, "a")
     if small_plane:
-        home = jnp.stack([lax.axis_index("b") * 2 + lax.axis_index("y"), lax.axis_index("c")])
+        member = lax.axis_index("b")
+        by_column = attended.reshape(GROUPS, 2, token_count, PAIR)
+        other = lax.ppermute(
+            lax.dynamic_index_in_dim(by_column, 1 - member, 1, False), "b", [(0, 1), (1, 0)]
+        )
+        own = lax.dynamic_index_in_dim(by_column, member, 1, False)
+        pair, early_all = lax.optimization_barrier((jnp.stack([own, other]), early_all))
+        outs = lax.all_gather(pair, "a", axis=0, tiled=False)
+        normed_all, resid, attended_low = join(place, outs, first_all, qkv_width // width, x_span)
+        normed_two = lax.dynamic_slice_in_dim(normed_all, group * token_count, token_count)
+        home = jnp.stack([member * 2 + lax.axis_index("y"), lax.axis_index("c")])
         experts_all, grad_hidden = place_experts(home, parts, early_all, width)
     else:
+        attended_low = (
+            exchange(attended.reshape(KEY_VALUE_HEADS, token_count, PAIR), head_axes)
+            .transpose(1, 0, 2)
+            .reshape(token_count, QUERY_HEADS * HEAD_SIZE)
+        )
+        attn_out = jnp.dot(attended_low, output_w, preferred_element_type=f32)
+        resid = x_local + RESIDUAL_SCALE * attn_out
+        normed_two = rms_scale(resid, gain_two_f).astype(bf16)
+        normed_all = gather(normed_two, "a")
         experts_all = parts.reshape(EXPERTS_HERE, width, 3 * F)
         grad_hidden = jnp.einsum(
             "td,edf->etf",
@@ -873,14 +934,20 @@
         group.reshape(1), normed_all, early_all, first_all, experts_all, grad_hidden
     )
     back_own = scatter_sum(back_part, "a").astype(f32)
-    moe_part, grad_experts = expert_grads(
-        normed_all, early_all, experts_all, gated_hidden, grad_pre
-    )
-    back_own, moe_part, grad_experts = lax.optimization_barrier(
-        (back_own, moe_part, grad_experts)
-    )
-    grad_experts = scatter_sum(grad_experts.reshape(EXPERTS_HERE * width, 3 * F), PLANE)
-    moe_terms = line_send(moe_part, "a")
+    inputs = (normed_all, early_all, experts_all, gated_hidden, grad_pre)
+    if small_plane:
+        core = lax.axis_index("c")
+        (send,) = expert_grads((1 - core).reshape(1), 2, *inputs, False)
+        arrived = lax.ppermute(send, "c", [(0, 1), (1, 0)])
+        moe_part, keep = expert_grads(core.reshape(1), 2, *inputs, True)
+        back_own, moe_part, keep = lax.optimization_barrier((back_own, moe_part, keep))
+    else:
+        moe_part, grad_experts = expert_grads(jnp.zeros((1,), jnp.int32), 1, *inputs, True)
+        back_own, moe_part, grad_experts = lax.optimization_barrier(
+            (back_own, moe_part, grad_experts)
+        )
+        grad_experts = scatter_sum(grad_experts.reshape(EXPERTS_HERE * width, 3 * F), PLANE)
+    moe_sum = scatter_sum(moe_part, "a")
 
     grad_out = cotangent[0].astype(f32)
     gates = lax.dynamic_slice_in_dim(gates_all, group * token_count, token_count)[:, :E]
@@ -897,14 +964,23 @@
     grad_mixed = exchange(
         grad_heads.reshape(token_count, KEY_VALUE_HEADS, PAIR).transpose(1, 0, 2), head_axes
     ).reshape(span, PAIR)
+    if small_plane:
+        keep, arrived, grad_heads = lax.optimization_barrier((keep, arrived, grad_heads))
+        total = keep.astype(f32) + arrived.astype(f32)
+        total = total.astype(bf16).reshape((2, 2) + keep.shape[1:])
+        total, attended_low, grad_router = lax.optimization_barrier(
+            (total, attended_low, grad_router)
+        )
+        wide = 3 * F // 2
+        left, right = halve_send(total[..., :wide], "y", 1), halve_send(total[..., wide:], "b", 0)
     small = jnp.concatenate([grad_router, grad_gain_two[:, None]], axis=1)
-    second_part = sum_over_row(
-        jnp.concatenate(
-            [contract_rows(attended_low, grad_attn_low), pad_lanes(small, LANES)], axis=1
-        ).astype(bf16)
-    )
-    second_part = halve(second_part, "b", 1)
-    rest = line_send(second_part.reshape(-1, second_part.shape[2]), "a")
+    second_part = jnp.concatenate(
+        [contract_rows(attended_low, grad_attn_low), pad_lanes(small, LANES)], axis=1
+    ).astype(bf16)
+    cols = second_part.shape[1]
+    second_part = second_part.reshape(GROUPS, -1, own_rows, cols).transpose(1, 0, 2, 3)
+    second_part, grad_mixed = lax.optimization_barrier((second_part, grad_mixed))
+    rest = scatter_sum(second_part.reshape(-1, cols), PLANE)
     grads = attend_back(
         bounds, qkv, kv, kv_at, doc_column, grad_mixed, attention_result, log_total,
         cos_span, sin_span, whole_rows,
@@ -914,20 +990,33 @@
     else:
         grad_kv = scatter_sum(grads[1].astype(bf16), "a").astype(f32)
         grad_pack = unrotate(grads[0], grad_kv, cos_span, sin_span)
-    moe_terms, resid, grad_pack = lax.optimization_barrier((moe_terms, resid, grad_pack))
+    if small_plane:
+        left, right, moe_sum, grad_pack = lax.optimization_barrier(
+            (left, right, moe_sum, grad_pack)
+        )
+        left, right = halve_add(left), halve_add(right)
+        left, right = halve_send(left, "b", 0), halve_send(right, "y", 0)
     first_part = head_grads(place, x_span, normed_span, first_all, grad_pack)
+    rest, first_part = lax.optimization_barrier((rest, first_part))
+    rest = scatter_sum(rest, "a")
     by_tokens = exchange(grad_pack.reshape(KEY_VALUE_HEADS, token_count, HEAD_PACK), head_axes)
     by_tokens, first_part = lax.optimization_barrier((by_tokens, first_part))
-    sums = exchange(first_part.reshape(-1, own_rows, first_part.shape[1]), ALL).astype(f32)
-    sums = sums.reshape(lax.axis_size(SEQ), -1, own_rows, first_part.shape[1]).sum(axis=1)
+    sums = exchange(first_part.reshape(-1, own_rows, first_part.shape[1]), ALL)
+    sums, moe_sum, resid = lax.optimization_barrier((sums, moe_sum, resid))
+    sums = sums.astype(f32).reshape(lax.axis_size(SEQ), -1, own_rows, first_part.shape[1]).sum(axis=1)
     by_heads = sums[:, :, :HEAD_PACK].reshape(-1, KEY_VALUE_HEADS, own_rows, HEAD_PACK).sum(axis=0)
-    rest = sum(term.astype(f32) for term in rest)
+    rest = rest.astype(f32)
     grad_qkv = by_tokens.transpose(1, 0, 2).reshape(token_count, qkv_width)
     grad_normed_one = contract_cols(grad_qkv, first_all[:, :qkv_width])
     grad_x_norm, _ = rms_back(x_local, gain_one_f, grad_normed_one)
     grad_input = grad_resid + grad_x_norm
-    layer_sum = resid + RESIDUAL_SCALE * sum(term.astype(f32) for term in moe_terms)
-    grad_experts = grad_experts.astype(f32)
+    layer_sum = resid + RESIDUAL_SCALE * moe_sum.astype(f32)
+    if small_plane:
+        grad_experts = jnp.concatenate(
+            [own.astype(f32) + other.astype(f32) for own, other in (left, right)], axis=1
+        )
+    else:
+        grad_experts = grad_experts.astype(f32)
     by_rows = by_heads.transpose(1, 0, 2)
     return (
         layer_sum.astype(bf16)[None],

time: 497 us -> 455 us (0.915)
  starting transfers between devices: 101 us -> 62.6 us
  waiting for transfers between devices: 155 us -> 132 us
  Pallas kernels: 147 us -> 163 us
  other arithmetic: 36.1 us -> 45.8 us
    ppermute x15 -> x6, starting transfers between devices: 41.4 us -> 6.94 us  [the longest x4 4.98 us: halve_send(): lax.ppermute(lax.dynamic_index_in_dim(v, 1 - me, at, False), axis, [(0, 1...]
    all_gather x3 -> x2, waiting for transfers between devices: 26.3 us -> 4 us  [gather(): return lax.all_gather(x, axes, axis=0, tiled=True)]
    ppermute x15 -> x6, waiting for transfers between devices: 27.9 us -> 7.62 us  [the longest x1 4.48 us: body(): lax.ppermute(lax.dynamic_index_in_dim(by_column, 1 - member, 1, False), '...]
    pallas_call x1 -> x3, Pallas kernels: 26.6 us -> 41.9 us  [the longest x2 33.7 us: expert_grads(): pl.pallas_call(functools.partial(expert_grads_kernel, with_y), grid_spec=...]
    reduce_scatter x2 -> x4, waiting for transfers between devices: 20.1 us -> 34 us  [scatter_sum(): return lax.psum_scatter(x, axes, scatter_dimension=0, tiled=True)]
    ppermute x1, waiting for transfers between devices: 7 us -> 15.2 us  [plane_gather(): upper = lax.ppermute(from_b[:half], 'y', swap)]
    all_to_all x4 -> x3, starting transfers between devices: 22.1 us -> 14.1 us  [exchange(): return lax.all_to_all(x, axes, 0, 0, tiled=True)]
    convert_element_type x4, other arithmetic: 3.88 us -> 11.2 us  [the longest x1 6.53 us: body(): total = total.astype(bf16).reshape((2, 2) + keep.shape[1:])]
  transfers between devices with their start and end apart: 46 -> 38, of which waited for: 16 -> 19; matrix products, arithmetic and copies ran while one was open for 12% -> 15% of each run, Pallas kernels for 24% -> 28%
where the time goes in v1:
time: 455 us; the launch traced here: 453 us
  Pallas kernels  163 us (36%)
  waiting for transfers between devices  132 us (29%)
  starting transfers between devices  62.6 us (14%)
  other arithmetic  45.8 us (10%)
  local copies, waits for them, and re-layouts  24 us (5%)
  between operations  14.8 us (3%)
  matrix products  11.5 us (3%)
    reduce_scatter x4, waiting for transfers between devices, scatter_sum(): return lax.psum_scatter(x, axes, scatter_dimension=0, tiled=True)  34 us
    pallas_call x2, Pallas kernels, expert_grads(): pl.pallas_call(functools.partial(expert_grads_kernel, with_y), grid_spec=...  33.7 us
    pallas_call x1, Pallas kernels, attend_back(): pl.pallas_call(functools.partial(attend_back_kernel, fold), grid_spec=plt...  31.8 us
    pallas_call x1, Pallas kernels, experts(): pl.pallas_call(experts_kernel, grid_spec=pltpu.PrefetchScalarGridSpec(num...  29 us
    ppermute x3, waiting for transfers between devices, grid_gather(): up = lax.ppermute(up, 'a', line_pairs(n, 1))  21.7 us
    pallas_call x1, Pallas kernels, attend(): pl.pallas_call(attend_kernel, grid_spec=pltpu.PrefetchScalarGridSpec(num_...  21.4 us
    ppermute x7, waiting for transfers between devices, cross(): lax.ppermute(block, SEQ, [(2 * i + j, 2 * i + 1 - j) for i in range(n) if...  19 us
    pallas_call x1, Pallas kernels, place_experts(): pl.pallas_call(place_experts_kernel, grid_spec=pltpu.PrefetchScalarGridSp...  18.5 us
  transfers between devices with their start and end apart: 38, of which 19 were waited for; matrix products, arithmetic and copies ran while one was open for 15% of the time, Pallas kernels for 28%

profile of v1, /device:TPU:0, one launch (start us, length us, event | category | flops | bytes accessed | tf_op | source)
XLA Modules:
  0.0 452.9 jit_solution(9171237357250653666)
XLA Ops:
  14.5 3.0 collective-permute-start
  17.5 4.3 collective-permute-start.1
  27.0 7.9 %collective-permute-done.1.refs_2_ = bf16[256,1024]{1,0:T(8,128)(2,1)} collective-permute-done((bf16[256,1024]{1,0:T(8,128)(2,1)S(1)}, bf16[256,1024]{1,0:T(8,128)(2,1)}, u32[]{:S(2)}, u32[]{:S(2)}) %collective-permute-start.1) | collective-permute-done | bytes 524320 | tf_op jit(solution)/shard_map/ppermute | solution.py:100
  34.9 5.3 %collective-permute-start.5 = (bf16[256,1024]{1,0:T(8,128)(2,1)}, bf16[256,1024]{1,0:T(8,128)(2,1)}, u32[]{:S(2)}, u32[]{:S(2)}) collective-permute-start(bf16[256,1024]{1,0:T(8,128)(2,1)} %collective-permute-done.1.refs_2_), channel_id=1, source_target_pairs={{0,8},{8,16},{16,24},{1,9},{9,17},{17,25},{2,10},{10,18},{18,26},{... | collective-permute-start | bytes 1572872 | tf_op jit(solution)/shard_map/ppermute | solution.py:100
  44.0 13.8 %collective-permute-done.5.refs_6_ = bf16[256,1024]{1,0:T(8,128)(2,1)} collective-permute-done((bf16[256,1024]{1,0:T(8,128)(2,1)}, bf16[256,1024]{1,0:T(8,128)(2,1)}, u32[]{:S(2)}, u32[]{:S(2)}) %collective-permute-start.5) | collective-permute-done | bytes 524320 | tf_op jit(solution)/shard_map/ppermute | solution.py:100
  57.8 5.2 %collective-permute-start.9 = (bf16[256,1024]{1,0:T(8,128)(2,1)}, bf16[256,1024]{1,0:T(8,128)(2,1)}, u32[]{:S(2)}, u32[]{:S(2)}) collective-permute-start(bf16[256,1024]{1,0:T(8,128)(2,1)} %collective-permute-done.5.refs_6_), channel_id=1, source_target_pairs={{0,8},{8,16},{16,24},{1,9},{9,17},{17,25},{2,10},{10,18},{18,26},{... | collective-permute-start | bytes 1572872 | tf_op jit(solution)/shard_map/ppermute | solution.py:100
  68.0 1.9 collective-permute-start.4
  71.6 3.9 collective-permute-start.8
  77.0 7.8 %collective-permute-done.11.refs_12_ = bf16[256,1024]{1,0:T(8,128)(2,1)} collective-permute-done((bf16[256,1024]{1,0:T(8,128)(2,1)}, bf16[256,1024]{1,0:T(8,128)(2,1)}, u32[]{:S(2)}, u32[]{:S(2)}) %collective-permute-start.11) | collective-permute-done | bytes 524320 | tf_op jit(solution)/shard_map/ppermute | solution.py:101
  84.8 1.9 collective-permute-start.12
  87.3 5.5 %multiply_sine_fusion = (f32[2048,32]{1,0:T(8,128)}, f32[2048,32]{1,0:T(8,128)}) fusion(f32[32]{0:T(128)S(1)} %multiply_power_fusion, f32[2048]{0:T(1024)S(1)} %subtract_convert_fusion), kind=kLoop, calls=%fused_computation.23 | loop fusion | flops 65536 | bytes 532608 | tf_op jit(solution)/shard_map/sin | solution.py:42
  92.8 2.7 collective-permute-done.4.refs_5_
  95.5 10.6 %collective-permute-done.8.refs_9_ = bf16[256,1024]{1,0:T(8,128)(2,1)} collective-permute-done((bf16[256,1024]{1,0:T(8,128)(2,1)}, bf16[256,1024]{1,0:T(8,128)(2,1)}, u32[]{:S(2)}, u32[]{:S(2)}) %collective-permute-start.8) | collective-permute-done | bytes 524320 | tf_op jit(solution)/shard_map/ppermute | solution.py:93
  106.1 5.6 %collective-permute-done.12.refs_13_ = bf16[256,1024]{1,0:T(8,128)(2,1)} collective-permute-done((bf16[256,1024]{1,0:T(8,128)(2,1)}, bf16[256,1024]{1,0:T(8,128)(2,1)}, u32[]{:S(2)}, u32[]{:S(2)}) %collective-permute-start.12) | collective-permute-done | bytes 524320 | tf_op jit(solution)/shard_map/ppermute | solution.py:93
  112.4 2.7 collective-permute-start.15
  116.8 10.3 %project.1 = (bf16[2048,256]{1,0:T(8,128)(2,1)}, bf16[2048,1024]{1,0:T(8,128)(2,1)}, bf16[2048,1024]{1,0:T(8,128)(2,1)}) custom-call(s32[3]{0:T(128)} %pad_add_fusion.place_ref.head_ref, bf16[256,1024]{1,0:T(8,128)(2,1)} %bitcast.91, bf16[256,1024]{1,0:T(8,128)(2,1)} %copy-done.14, bf16[256,1024]{1,0:T(8,128)(2,1)} %collective-permute-done.1.refs_2_, ...), custom_call_target="tpu_custom_call" | custom-call | flops 1073741824 | bytes 18874368 | tf_op jit(solution)/shard_map/project/pallas_call | solution.py:191
  127.1 21.4 %attend.1 = (f32[2048,128]{1,0:T(8,128)}, bf16[2048,128]{1,0:T(8,128)(2,1)}, f32[8,512,1]{2,1,0:T(8,128)}) custom-call(s32[9]{0:T(128)} %pad_add_fusion.1.bounds_ref, bf16[2048,256]{1,0:T(8,128)(2,1)} %get-tuple-element.94.q_ref.kv_ref, bf16[2048,256]{1,0:T(8,128)(2,1)} %get-tuple-element.94.q_ref.kv_ref, s32[2048,1]{1,0:T(8,128)} %copy.102.doc_ref), custom_call_target="tpu_custom_call" | custom-call | flops 2147483648 | bytes 6291456 | tf_op jit(solution)/shard_map/attend/pallas_call | solution.py:352
  149.6 2.0 collective-permute-start.13
  151.6 4.5 collective-permute-done.13
  156.9 4.0 all-gather.7.cloned.1.call-done.refs_10_.routed_ref.ct_ref
  167.2 15.2 %collective-permute-done.19.refs_6_ = bf16[256,1536]{1,0:T(8,128)(2,1)S(1)} collective-permute-done((bf16[256,1536]{1,0:T(8,128)(2,1)S(1)}, bf16[256,1536]{1,0:T(8,128)(2,1)S(1)}, u32[]{:S(2)}, u32[]{:S(2)}) %collective-permute-start.19) | collective-permute-done | bytes 786464 | tf_op jit(solution)/shard_map/ppermute | solution.py:112
  182.4 3.1 collective-permute-done.21.refs_8_
  186.1 2.0 collective-permute-done.22.refs_9_
  188.1 18.5 %place_experts.1 = (bf16[4,1024,1536]{2,1,0:T(8,128)(2,1)}, f32[4,1024,512]{2,1,0:T(8,128)}) custom-call(s32[2]{0:T(128)} %pad_add_fusion.2.place_ref, bf16[512,1536]{1,0:T(8,128)(2,1)} %pad_maximum_fusion.2.refs_0_, bf16[512,1536]{1,0:T(8,128)(2,1)} %collective-permute-done.14.refs_1_, bf16[512,1536]{1,0:T(8,128)(2,1)} %collective-permute-done.15.refs_2_, ...), custom_call_target="tpu_custom_call" | custom-call | flops 4294967296 | bytes 37748736 | tf_op jit(solution)/shard_map/place_experts/pallas_call | solution.py:551
  207.8 8.2 %join.1 = (bf16[1024,1024]{1,0:T(8,128)(2,1)}, f32[256,1024]{1,0:T(8,128)}, bf16[256,1024]{1,0:T(8,128)(2,1)}) custom-call(s32[3]{0:T(128)} %pad_add_fusion.place_ref.head_ref, bf16[4,2,4,256,128]{4,3,2,1,0:T(8,128)(2,1)} %bitcast.96, bf16[1024,3200]{1,0:T(8,128)(2,1)} %all-gather.5.cloned.1.call-done.refs_14_.refs_15_.w_ref.small_ref.router_ref, ...), custom_call_target="tpu_custom_call" | custom-call | flops 2147483648 | bytes 12582912 | tf_op jit(solution)/shard_map/join/pallas_call | solution.py:762
  216.1 29.0 %experts.1 = (bf16[1024,1152]{1,0:T(8,128)(2,1)}, f32[1024,128]{1,0:T(8,128)}, bf16[4,1024,512]{2,1,0:T(8,128)(2,1)}, bf16[4,1024,1024]{2,1,0:T(8,128)(2,1)}) custom-call(s32[1]{0:T(128)} %bitcast.group_ref, bf16[1024,1024]{1,0:T(8,128)(2,1)} %get-tuple-element.100.n_ref, bf16[1024,1152]{1,0:T(8,128)(2,1)} %all-gather.7.cloned.1.call-done.refs_10_.routed_ref.ct_ref, ...), custom_call_target="tpu_custom_call" | custom-call | flops 17179869184 | bytes 41943040 | tf_op jit(solution)/shard_map/experts/pallas_call | solution.py:633
  245.4 15.0 %expert_grads.3 = bf16[4,512,1536]{2,1,0:T(8,128)(2,1)} custom-call(s32[1]{0:T(128)} %bitcast.17.half_ref, bf16[1024,1024]{1,0:T(8,128)(2,1)} %get-tuple-element.100.n_ref, bf16[1024,1152]{1,0:T(8,128)(2,1)} %all-gather.7.cloned.1.call-done.refs_10_.routed_ref.ct_ref, bf16[4,1024,1536]{2,1,0:T(8,128)(2,1)} %get-tuple-element.103.w_ref, ...), custom_call_target="tpu_custom_call" | custom-call | flops 6442450944 | bytes 31457280 | tf_op jit(solution)/shard_map/expert_grads/pallas_call | solution.py:706
  262.0 18.7 %expert_grads.2 = (bf16[1024,1024]{1,0:T(8,128)(2,1)}, bf16[4,512,1536]{2,1,0:T(8,128)(2,1)}) custom-call(s32[1]{0:T(128)} %bitcast.16.half_ref, bf16[1024,1024]{1,0:T(8,128)(2,1)} %get-tuple-element.100.n_ref, bf16[1024,1152]{1,0:T(8,128)(2,1)} %all-gather.7.cloned.1.call-done.refs_10_.routed_ref.ct_ref, bf16[4,1024,1536]{2,1,0:T(8,128)(2,1)} %get-tuple-element.103.w_ref, ...), custom_call_target="tpu_custom_call" | custom-call | flops 10737418240 | bytes 31457280 | tf_op jit(solution)/shard_map/expert_grads/pallas_call | solution.py:706
  280.7 11.3 %reduce-scatter.5.cloned.1.call-done = bf16[256,1152]{1,0:T(8,128)(2,1)} async-done(((bf16[1024,1152]{1,0:T(8,128)(2,1)}), bf16[256,1152]{1,0:T(8,128)(2,1)}) %reduce-scatter.5.cloned.1.call-update) | async-done | bytes 589840 | tf_op jit(solution)/shard_map/reduce_scatter | solution.py:78
  295.7 2.7 fusion.7
  299.4 4.1 all-to-all-start
  305.2 6.5 %add_convert_fusion = bf16[4,512,1536]{2,1,0:T(8,128)(2,1)S(1)} fusion(bf16[4,512,1536]{2,1,0:T(8,128)(2,1)} %collective-permute-done.23, bf16[4,512,1536]{2,1,0:T(8,128)(2,1)} %get-tuple-element.114), kind=kLoop, calls=%fused_computation.1 | loop fusion | flops 12582912 | bytes 18874368 | tf_op jit(solution)/shard_map/convert_element_type | solution.py:970
  311.8 2.1 fusion.29
  313.9 1.8 dynamic-slice_bitcast_fusion.2
  319.9 13.4 %all-to-all-done = bf16[8,256,128]{2,1,0:T(8,128)(2,1)} async-done(((bf16[8,256,128]{2,1,0:T(8,128)(2,1)}), bf16[8,256,128]{2,1,0:T(8,128)(2,1)}, u32[]{:S(2)}, u32[]{:S(2)}) %all-to-all-start) | async-done | bytes 524320 | tf_op jit(solution)/shard_map/all_to_all | solution.py:790
  333.4 1.9 dynamic-slice_bitcast_fusion
  335.5 31.8 %attend_back.1.grad_ref = bf16[2048,256]{1,0:T(8,128)(2,1)} custom-call(s32[9]{0:T(128)} %pad_add_fusion.1.bounds_ref, bf16[2048,256]{1,0:T(8,128)(2,1)} %get-tuple-element.94.q_ref.kv_ref, bf16[2048,256]{1,0:T(8,128)(2,1)} %get-tuple-element.94.q_ref.kv_ref, s32[2048,1]{1,0:T(8,128)} %copy.102.doc_ref, bf16[2048,128]{1,0:T(8,128)(2,1)} %bitcast.27.do_ref, ...), custom_call_target="tpu_custom_call" | custom-call | flops 5368709120 | bytes 8388608 | tf_op jit(solution)/shard_map/attend_back/pallas_call | solution.py:466
  367.3 3.1 collective-permute-done.25
  370.4 2.4 copy.108
  372.9 4.2 all-to-all-start.1
  377.2 1.9 add_convert_fusion.1
  381.5 1.8 add_convert_fusion.2
  386.1 9.7 %head_grads.1 = bf16[1024,384]{1,0:T(8,128)(2,1)} custom-call(s32[3]{0:T(128)} %pad_add_fusion.place_ref.head_ref, bf16[2048,1024]{1,0:T(8,128)(2,1)} %get-tuple-element.99.x_ref, bf16[2048,1024]{1,0:T(8,128)(2,1)} %get-tuple-element.126.normed_ref, bf16[1024,3200]{1,0:T(8,128)(2,1)} %all-gather.5.cloned.1.call-done.refs_14_.refs_15_.w_ref.small_ref.router_ref, ...), custom_call_target="tpu_custom_call" | custom-call | flops 2147483648 | bytes 12582912 | tf_op jit(solution)/shard_map/head_grads/pallas_call | solution.py:256
  395.8 8.4 %reduce-scatter.9.cloned.1.call-done = bf16[128,1152]{1,0:T(8,128)(2,1)} async-done(((bf16[1024,1152]{1,0:T(8,128)(2,1)}), bf16[128,1152]{1,0:T(8,128)(2,1)}) %reduce-scatter.9.cloned.1.call-update) | async-done | bytes 294928 | tf_op jit(solution)/shard_map/reduce_scatter | solution.py:78
  404.2 5.7 %all-to-all-start.2 = ((bf16[32,32,384]{2,1,0:T(8,128)(2,1)}), bf16[32,32,384]{2,1,0:T(8,128)(2,1)}, u32[]{:S(2)}, u32[]{:S(2)}) async-start(bf16[32,32,384]{2,1,0:T(8,128)(2,1)} %bitcast.90), calls=%async_computation.5 | async-start | bytes 1572864 | tf_op jit(solution)/shard_map/all_to_all | solution.py:790
  415.4 14.2 %reduce-scatter.11.cloned.1.call-done = bf16[32,1152]{1,0:T(8,128)(2,1)} async-done(((bf16[128,1152]{1,0:T(8,128)(2,1)}), bf16[32,1152]{1,0:T(8,128)(2,1)}) %reduce-scatter.11.cloned.1.call-update) | async-done | bytes 73744 | tf_op jit(solution)/shard_map/reduce_scatter | solution.py:78
  434.1 4.8 %fusion.10 = (f32[256]{0:T(256)S(1)}, f32[256]{0:T(256)S(1)}, f32[256,1024]{1,0:T(8,128)}) fusion(bf16[1,256,1024]{2,1,0:T(8,128)(2,1)S(1)} %copy-done.9, f32[1024]{0:T(1024)S(1)} %get-tuple-element.216, bf16[256,2048]{0,1:T(8,128)(2,1)} %bitcast.33, bf16[1024,3200]{1,0:T(8,128)(2,1)} %all-gather.5.cloned.1.call-done.refs_14_.refs_15_.w_ref.small_ref.router_ref), kind=kOutput, calls=%fused_computation.28 | convolution fusion | flops 1075314176 | bytes 6821888 | tf_op jit(solution)/shard_map/dot_general | solution.py:68
  443.4 2.7 fusion.14
  (174 shorter events, 69.1 us)
Async XLA Ops:
  7.2 15.9 %copy-start.12 = (f32[512,512]{1,0:T(8,128)S(1)}, f32[512,512]{1,0:T(8,128)}, u32[]{:S(2)}) copy-start(f32[512,512]{1,0:T(8,128)} %param.25) | copy-start | bytes 3145732
  7.2 104.6 %all-gather.5.cloned.1.call-start = ((), (), s32[]{:S(2)}) async-start(), calls=%async_computation.7 | async-start | bytes 6758400 | tf_op jit(solution)/shard_map/all_gather | solution.py:74
  14.4 146.5 %all-gather.7.cloned.1.call-start = ((), (), s32[]{:S(2)}) async-start(), calls=%async_computation.8 | async-start | bytes 2949120 | tf_op jit(solution)/shard_map/all_gather | solution.py:74
  14.4 12.3 %copy-start.18 = (s32[1,256,8]{1,2,0:T(8,128)S(1)}, s32[1,256,8]{1,2,0:T(8,128)}, u32[]{:S(2)}) copy-start(s32[1,256,8]{1,2,0:T(8,128)} %param.16) | copy-start | bytes 24580
  14.5 51.4 %copy-start.10 = (bf16[1,256,1024]{2,1,0:T(8,128)(2,1)S(1)}, bf16[1,256,1024]{2,1,0:T(8,128)(2,1)}, u32[]{:S(2)}) copy-start(bf16[1,256,1024]{2,1,0:T(8,128)(2,1)} %param.14) | copy-start | bytes 1572868
  14.5 55.5 %collective-permute-start = (bf16[256,1024]{1,0:T(8,128)(2,1)S(1)}, bf16[256,1024]{1,0:T(8,128)(2,1)S(1)}, u32[]{:S(2)}, u32[]{:S(2)}) collective-permute-start(bf16[256,1024]{1,0:T(8,128)(2,1)S(1)} %bitcast.92), channel_id=1, source_target_pairs={{0,4},{4,0},{8,12},{12,8},{16,20},{20,16},{24,28},{28,24},{1,5},{5... | collective-permute-start | bytes 1572872 | tf_op jit(solution)/shard_map/ppermute | solution.py:93
  17.5 17.4 %collective-permute-start.1 = (bf16[256,1024]{1,0:T(8,128)(2,1)S(1)}, bf16[256,1024]{1,0:T(8,128)(2,1)}, u32[]{:S(2)}, u32[]{:S(2)}) collective-permute-start(bf16[256,1024]{1,0:T(8,128)(2,1)S(1)} %bitcast.93), channel_id=1, source_target_pairs={{0,8},{8,16},{16,24},{1,9},{9,17},{17,25},{2,10},{10,18},{18,26},{... | collective-permute-start | bytes 1572872 | tf_op jit(solution)/shard_map/ppermute | solution.py:100
  21.8 19.4 %collective-permute-start.3 = (bf16[256,1024]{1,0:T(8,128)(2,1)S(1)}, bf16[256,1024]{1,0:T(8,128)(2,1)}, u32[]{:S(2)}, u32[]{:S(2)}) collective-permute-start(bf16[256,1024]{1,0:T(8,128)(2,1)S(1)} %bitcast.94), channel_id=1, source_target_pairs={{8,0},{16,8},{24,16},{9,1},{17,9},{25,17},{10,2},{18,10},{26,18},{... | collective-permute-start | bytes 1572872 | tf_op jit(solution)/shard_map/ppermute | solution.py:101
  34.9 22.9 %collective-permute-start.5 = (bf16[256,1024]{1,0:T(8,128)(2,1)}, bf16[256,1024]{1,0:T(8,128)(2,1)}, u32[]{:S(2)}, u32[]{:S(2)}) collective-permute-start(bf16[256,1024]{1,0:T(8,128)(2,1)} %collective-permute-done.1.refs_2_), channel_id=1, source_target_pairs={{0,8},{8,16},{16,24},{1,9},{9,17},{17,25},{2,10},{10,18},{18,26},{... | collective-permute-start | bytes 1572872 | tf_op jit(solution)/shard_map/ppermute | solution.py:100
  41.2 23.3 %collective-permute-start.7 = (bf16[256,1024]{1,0:T(8,128)(2,1)}, bf16[256,1024]{1,0:T(8,128)(2,1)}, u32[]{:S(2)}, u32[]{:S(2)}) collective-permute-start(bf16[256,1024]{1,0:T(8,128)(2,1)} %collective-permute-done.3.refs_4_), channel_id=1, source_target_pairs={{8,0},{16,8},{24,16},{9,1},{17,9},{25,17},{10,2},{18,10},{26,18},{... | collective-permute-start | bytes 1572872 | tf_op jit(solution)/shard_map/ppermute | solution.py:101
  42.5 29.0 %collective-permute-start.2 = (bf16[256,1024]{1,0:T(8,128)(2,1)}, bf16[256,1024]{1,0:T(8,128)(2,1)}, u32[]{:S(2)}, u32[]{:S(2)}) collective-permute-start(bf16[256,1024]{1,0:T(8,128)(2,1)} %collective-permute-done.1.refs_2_), channel_id=1, source_target_pairs={{8,12},{12,8},{16,20},{20,16},{24,28},{28,24},{9,13},{13,9},{17,21... | collective-permute-start | bytes 1572872 | tf_op jit(solution)/shard_map/ppermute | solution.py:93
  57.8 17.7 %collective-permute-start.9 = (bf16[256,1024]{1,0:T(8,128)(2,1)}, bf16[256,1024]{1,0:T(8,128)(2,1)}, u32[]{:S(2)}, u32[]{:S(2)}) collective-permute-start(bf16[256,1024]{1,0:T(8,128)(2,1)} %collective-permute-done.5.refs_6_), channel_id=1, source_target_pairs={{0,8},{8,16},{16,24},{1,9},{9,17},{17,25},{2,10},{10,18},{18,26},{... | collective-permute-start | bytes 1572872 | tf_op jit(solution)/shard_map/ppermute | solution.py:100
  64.6 20.2 %collective-permute-start.11 = (bf16[256,1024]{1,0:T(8,128)(2,1)}, bf16[256,1024]{1,0:T(8,128)(2,1)}, u32[]{:S(2)}, u32[]{:S(2)}) collective-permute-start(bf16[256,1024]{1,0:T(8,128)(2,1)} %collective-permute-done.7.refs_8_), channel_id=1, source_target_pairs={{8,0},{16,8},{24,16},{9,1},{17,9},{25,17},{10,2},{18,10},{26,18},{... | collective-permute-start | bytes 1572872 | tf_op jit(solution)/shard_map/ppermute | solution.py:101
  68.0 27.5 %collective-permute-start.4 = (bf16[256,1024]{1,0:T(8,128)(2,1)}, bf16[256,1024]{1,0:T(8,128)(2,1)S(1)}, u32[]{:S(2)}, u32[]{:S(2)}) collective-permute-start(bf16[256,1024]{1,0:T(8,128)(2,1)} %collective-permute-done.3.refs_4_), channel_id=1, source_target_pairs={{0,4},{4,0},{8,12},{12,8},{16,20},{20,16},{1,5},{5,1},{9,13},{13,9... | collective-permute-start | bytes 1572872 | tf_op jit(solution)/shard_map/ppermute | solution.py:93
  70.0 46.8 %copy-start.14 = (bf16[256,1024]{1,0:T(8,128)(2,1)}, bf16[256,1024]{1,0:T(8,128)(2,1)S(1)}, u32[]{:S(2)}) copy-start(bf16[256,1024]{1,0:T(8,128)(2,1)S(1)} %collective-permute-done.refs_1_) | copy-start | bytes 1572868
  70.0 42.5 %copy-start.11 = (bf16[512,1536]{1,0:T(8,128)(2,1)S(1)}, bf16[512,1536]{1,0:T(8,128)(2,1)}, u32[]{:S(2)}) copy-start(bf16[512,1536]{1,0:T(8,128)(2,1)} %pad_maximum_fusion.2.refs_0_) | copy-start | bytes 4718596
  70.0 25.5 %collective-permute-start.6 = (bf16[256,1024]{1,0:T(8,128)(2,1)}, bf16[256,1024]{1,0:T(8,128)(2,1)}, u32[]{:S(2)}, u32[]{:S(2)}) collective-permute-start(bf16[256,1024]{1,0:T(8,128)(2,1)} %collective-permute-done.5.refs_6_), channel_id=1, source_target_pairs={{16,20},{20,16},{24,28},{28,24},{17,21},{21,17},{25,29},{29,25},{1... | collective-permute-start | bytes 1572872 | tf_op jit(solution)/shard_map/ppermute | solution.py:93
  71.6 34.5 %collective-permute-start.8 = (bf16[256,1024]{1,0:T(8,128)(2,1)}, bf16[256,1024]{1,0:T(8,128)(2,1)}, u32[]{:S(2)}, u32[]{:S(2)}) collective-permute-start(bf16[256,1024]{1,0:T(8,128)(2,1)} %collective-permute-done.7.refs_8_), channel_id=1, source_target_pairs={{0,4},{4,0},{8,12},{12,8},{1,5},{5,1},{9,13},{13,9},{2,6},{6,2},{1... | collective-permute-start | bytes 1572872 | tf_op jit(solution)/shard_map/ppermute | solution.py:93
  75.5 30.6 %collective-permute-start.10 = (bf16[256,1024]{1,0:T(8,128)(2,1)}, bf16[256,1024]{1,0:T(8,128)(2,1)}, u32[]{:S(2)}, u32[]{:S(2)}) collective-permute-start(bf16[256,1024]{1,0:T(8,128)(2,1)} %collective-permute-done.9.refs_10_), channel_id=1, source_target_pairs={{24,28},{28,24},{25,29},{29,25},{26,30},{30,26},{27,31},{31,27}} | collective-permute-start | bytes 1572872 | tf_op jit(solution)/shard_map/ppermute | solution.py:93
  84.8 27.0 %collective-permute-start.12 = (bf16[256,1024]{1,0:T(8,128)(2,1)}, bf16[256,1024]{1,0:T(8,128)(2,1)}, u32[]{:S(2)}, u32[]{:S(2)}) collective-permute-start(bf16[256,1024]{1,0:T(8,128)(2,1)} %collective-permute-done.11.refs_12_), channel_id=1, source_target_pairs={{0,4},{4,0},{1,5},{5,1},{2,6},{6,2},{3,7},{7,3}} | collective-permute-start | bytes 1572872 | tf_op jit(solution)/shard_map/ppermute | solution.py:93
  95.5 21.3 %copy-start.16 = (bf16[256,1024]{1,0:T(8,128)(2,1)}, bf16[256,1024]{1,0:T(8,128)(2,1)S(1)}, u32[]{:S(2)}) copy-start(bf16[256,1024]{1,0:T(8,128)(2,1)S(1)} %collective-permute-done.4.refs_5_) | copy-start | bytes 1572868
  111.8 96.0 %all-gather.9.cloned.1.call-start = ((), (), s32[]{:S(2)}) async-start(), calls=%async_computation.13 | async-start | bytes 2621440 | tf_op jit(solution)/shard_map/all_gather | solution.py:911
  112.4 51.7 %collective-permute-start.15 = (bf16[512,1536]{1,0:T(8,128)(2,1)S(1)}, bf16[512,1536]{1,0:T(8,128)(2,1)}, u32[]{:S(2)}, u32[]{:S(2)}) collective-permute-start(bf16[512,1536]{1,0:T(8,128)(2,1)S(1)} %copy-done.11), channel_id=1, source_target_pairs={{0,2},{2,0},{1,3},{3,1},{4,6},{6,4},{5,7},{7,5},{8,10},{10,8},{9,1... | collective-permute-start | bytes 4718600 | tf_op jit(solution)/shard_map/ppermute | solution.py:110
  115.1 46.1 %collective-permute-start.17 = (bf16[512,1536]{1,0:T(8,128)(2,1)S(1)}, bf16[512,1536]{1,0:T(8,128)(2,1)}, u32[]{:S(2)}, u32[]{:S(2)}) collective-permute-start(bf16[512,1536]{1,0:T(8,128)(2,1)S(1)} %copy-done.11), channel_id=1, source_target_pairs={{0,4},{4,0},{1,5},{5,1},{2,6},{6,2},{3,7},{7,3},{8,12},{12,8},{9,1... | collective-permute-start | bytes 4718600 | tf_op jit(solution)/shard_map/ppermute | solution.py:111
  149.6 6.4 %collective-permute-start.13 = (bf16[4,256,128]{2,1,0:T(8,128)(2,1)S(1)}, bf16[4,256,128]{2,1,0:T(8,128)(2,1)S(1)}, u32[]{:S(2)}, u32[]{:S(2)}) collective-permute-start(bf16[4,256,128]{2,1,0:T(8,128)(2,1)S(1)} %get-tuple-element.229), channel_id=1, source_target_pairs={{0,4},{4,0},{1,5},{5,1},{2,6},{6,2},{3,7},{7,3},{8,12},{12,8},{9,1... | collective-permute-start | bytes 786440 | tf_op jit(solution)/shard_map/ppermute | solution.py:906
  160.9 131.1 %reduce-scatter.5.cloned.1.call-start = ((), (), s32[]{:S(2)}) async-start(), calls=%async_computation.9 | async-start | bytes 2949120 | tf_op jit(solution)/shard_map/reduce_scatter | solution.py:78
  161.1 24.9 %collective-permute-start.14 = (bf16[512,1536]{1,0:T(8,128)(2,1)S(1)}, bf16[512,1536]{1,0:T(8,128)(2,1)}, u32[]{:S(2)}, u32[]{:S(2)}) collective-permute-start(bf16[512,1536]{1,0:T(8,128)(2,1)S(1)} %copy-done.11), channel_id=1, source_target_pairs={{0,1},{1,0},{2,3},{3,2},{4,5},{5,4},{6,7},{7,6},{8,9},{9,8},{10,11... | collective-permute-start | bytes 4718600 | tf_op jit(solution)/shard_map/ppermute | solution.py:115
  162.4 20.0 %collective-permute-start.19 = (bf16[256,1536]{1,0:T(8,128)(2,1)S(1)}, bf16[256,1536]{1,0:T(8,128)(2,1)S(1)}, u32[]{:S(2)}, u32[]{:S(2)}) collective-permute-start(bf16[256,1536]{1,0:T(8,128)(2,1)S(1)} %slice.97), channel_id=1, source_target_pairs={{0,2},{2,0},{1,3},{3,1},{4,6},{6,4},{5,7},{7,5},{8,10},{10,8},{9,1... | collective-permute-start | bytes 2359304 | tf_op jit(solution)/shard_map/ppermute | solution.py:112
  164.0 22.1 %collective-permute-start.18 = (bf16[512,1536]{1,0:T(8,128)(2,1)}, bf16[512,1536]{1,0:T(8,128)(2,1)}, u32[]{:S(2)}, u32[]{:S(2)}) collective-permute-start(bf16[512,1536]{1,0:T(8,128)(2,1)} %collective-permute-done.17.refs_4_), channel_id=1, source_target_pairs={{0,1},{1,0},{2,3},{3,2},{4,5},{5,4},{6,7},{7,6},{8,9},{9,8},{10,11... | collective-permute-start | bytes 4718600 | tf_op jit(solution)/shard_map/ppermute | solution.py:115
  164.2 21.9 %collective-permute-start.16 = (bf16[512,1536]{1,0:T(8,128)(2,1)}, bf16[512,1536]{1,0:T(8,128)(2,1)}, u32[]{:S(2)}, u32[]{:S(2)}) collective-permute-start(bf16[512,1536]{1,0:T(8,128)(2,1)} %collective-permute-done.15.refs_2_), channel_id=1, source_target_pairs={{0,1},{1,0},{2,3},{3,2},{4,5},{5,4},{6,7},{7,6},{8,9},{9,8},{10,11... | collective-permute-start | bytes 4718600 | tf_op jit(solution)/shard_map/ppermute | solution.py:115
  165.7 19.8 %collective-permute-start.21 = (bf16[256,1536]{1,0:T(8,128)(2,1)S(1)}, bf16[256,1536]{1,0:T(8,128)(2,1)}, u32[]{:S(2)}, u32[]{:S(2)}) collective-permute-start(bf16[256,1536]{1,0:T(8,128)(2,1)S(1)} %slice.98), channel_id=1, source_target_pairs={{0,4},{4,0},{1,5},{5,1},{2,6},{6,2},{3,7},{7,3},{8,12},{12,8},{9,1... | collective-permute-start | bytes 2359304 | tf_op jit(solution)/shard_map/ppermute | solution.py:113
  182.4 3.7 collective-permute-start.20
  185.5 2.6 collective-permute-start.22
  245.1 125.3 %reduce-scatter.7.cloned.1.call-start = ((), (), s32[]{:S(2)}) async-start(), calls=%async_computation.10 | async-start | bytes 2621440 | tf_op jit(solution)/shard_map/reduce_scatter | solution.py:78
  245.4 16.4 %copy-start = (f32[256,1024]{1,0:T(8,128)S(1)}, f32[256,1024]{1,0:T(8,128)}, u32[]{:S(2)}) copy-start(f32[256,1024]{1,0:T(8,128)} %get-tuple-element.130) | copy-start | bytes 3145732
  260.4 44.8 %collective-permute-start.23 = (bf16[4,512,1536]{2,1,0:T(8,128)(2,1)}, bf16[4,512,1536]{2,1,0:T(8,128)(2,1)}, u32[]{:S(2)}, u32[]{:S(2)}) collective-permute-start(bf16[4,512,1536]{2,1,0:T(8,128)(2,1)} %expert_grads.3), channel_id=1, source_target_pairs={{0,1},{1,0},{2,3},{3,2},{4,5},{5,4},{6,7},{7,6},{8,9},{9,8},{10,11... | collective-permute-start | bytes 18874376 | tf_op jit(solution)/shard_map/ppermute | solution.py:941
  280.7 12.5 %copy-start.17 = (f32[1024,128]{1,0:T(8,128)S(1)}, f32[1024,128]{1,0:T(8,128)}, u32[]{:S(2)}) copy-start(f32[1024,128]{1,0:T(8,128)} %get-tuple-element.113) | copy-start | bytes 1572868
  299.4 33.9 %all-to-all-start = ((bf16[8,256,128]{2,1,0:T(8,128)(2,1)}), bf16[8,256,128]{2,1,0:T(8,128)(2,1)}, u32[]{:S(2)}, u32[]{:S(2)}) async-start(bf16[8,256,128]{2,1,0:T(8,128)(2,1)} %bitcast_bitcast_fusion), calls=%async_computation.2 | async-start | bytes 1048576 | tf_op jit(solution)/shard_map/all_to_all | solution.py:790
  303.5 100.7 %reduce-scatter.9.cloned.1.call-start = ((), (), s32[]{:S(2)}) async-start(), calls=%async_computation.11 | async-start | bytes 2654208 | tf_op jit(solution)/shard_map/reduce_scatter | solution.py:78
  315.7 51.6 %collective-permute-start.24 = (bf16[2,512,768]{2,1,0:T(8,128)(2,1)}, bf16[2,512,768]{2,1,0:T(8,128)(2,1)}, u32[]{:S(2)}, u32[]{:S(2)}) collective-permute-start(bf16[2,512,768]{2,1,0:T(8,128)(2,1)} %get-tuple-element.226), channel_id=1, source_target_pairs={{0,2},{2,0},{1,3},{3,1},{4,6},{6,4},{5,7},{7,5},{8,10},{10,8},{9,1... | collective-permute-start | bytes 4718600 | tf_op jit(solution)/shard_map/ppermute | solution.py:121
  318.2 15.1 %copy-start.2 = (bf16[2,2,512,768]{3,2,1,0:T(8,128)(2,1)S(1)}, bf16[2,2,512,768]{3,2,1,0:T(8,128)(2,1)}, u32[]{:S(2)}) copy-start(bf16[2,2,512,768]{3,2,1,0:T(8,128)(2,1)} %get-tuple-element.222) | copy-start | bytes 9437188
  335.2 35.2 %collective-permute-start.25 = (bf16[2,512,768]{2,1,0:T(8,128)(2,1)}, bf16[2,512,768]{2,1,0:T(8,128)(2,1)}, u32[]{:S(2)}, u32[]{:S(2)}) collective-permute-start(bf16[2,512,768]{2,1,0:T(8,128)(2,1)} %get-tuple-element.224), channel_id=1, source_target_pairs={{0,4},{4,0},{1,5},{5,1},{2,6},{6,2},{3,7},{7,3},{8,12},{12,8},{9,1... | collective-permute-start | bytes 4718600 | tf_op jit(solution)/shard_map/ppermute | solution.py:121
  372.9 31.3 %all-to-all-start.1 = ((bf16[8,256,256]{1,2,0:T(8,128)(2,1)}), bf16[8,256,256]{1,2,0:T(8,128)(2,1)}, u32[]{:S(2)}, u32[]{:S(2)}) async-start(bf16[8,256,256]{1,2,0:T(8,128)(2,1)} %copy.108), calls=%async_computation.3 | async-start | bytes 2097152 | tf_op jit(solution)/shard_map/all_to_all | solution.py:790
  377.1 52.5 %reduce-scatter.11.cloned.1.call-start = ((), (), s32[]{:S(2)}) async-start(), calls=%async_computation.12 | async-start | bytes 368640 | tf_op jit(solution)/shard_map/reduce_scatter | solution.py:78
  380.1 29.9 %collective-permute-start.27 = (bf16[512,768]{1,0:T(8,128)(2,1)}, bf16[512,768]{1,0:T(8,128)(2,1)}, u32[]{:S(2)}, u32[]{:S(2)}) collective-permute-start(bf16[512,768]{1,0:T(8,128)(2,1)} %dynamic-slice_bitcast_fusion.4), channel_id=1, source_target_pairs={{0,2},{2,0},{1,3},{3,1},{4,6},{6,4},{5,7},{7,5},{8,10},{10,8},{9,1... | collective-permute-start | bytes 2359304 | tf_op jit(solution)/shard_map/ppermute | solution.py:121
  384.3 28.1 %collective-permute-start.26 = (bf16[512,768]{1,0:T(8,128)(2,1)}, bf16[512,768]{1,0:T(8,128)(2,1)}, u32[]{:S(2)}, u32[]{:S(2)}) collective-permute-start(bf16[512,768]{1,0:T(8,128)(2,1)} %dynamic-slice_bitcast_fusion.5), channel_id=1, source_target_pairs={{0,4},{4,0},{1,5},{5,1},{2,6},{6,2},{3,7},{7,3},{8,12},{12,8},{9,1... | collective-permute-start | bytes 2359304 | tf_op jit(solution)/shard_map/ppermute | solution.py:121
  404.2 34.7 %all-to-all-start.2 = ((bf16[32,32,384]{2,1,0:T(8,128)(2,1)}), bf16[32,32,384]{2,1,0:T(8,128)(2,1)}, u32[]{:S(2)}, u32[]{:S(2)}) async-start(bf16[32,32,384]{2,1,0:T(8,128)(2,1)} %bitcast.90), calls=%async_computation.5 | async-start | bytes 1572864 | tf_op jit(solution)/shard_map/all_to_all | solution.py:790
  413.7 20.3 %copy-start.9 = (bf16[1,256,1024]{2,1,0:T(8,128)(2,1)S(1)}, bf16[1,256,1024]{2,1,0:T(8,128)(2,1)}, u32[]{:S(2)}) copy-start(bf16[1,256,1024]{2,1,0:T(8,128)(2,1)} %param.13) | copy-start | bytes 1572868
  (11 other events, 57.9 us)
Sparse Core Ops, SparseCore 0:
  14.5 92.0 all-gather.4
  111.9 48.9 all-gather.6
  163.0 44.7 all-gather.8
  245.2 46.7 reduce-scatter.4
  294.2 51.7 reduce-scatter.6
  349.5 54.6 reduce-scatter.8
  406.4 23.1 reduce-scatter.10

commit v2 on v1

--- a/solution.py
+++ b/solution.py
@@ -18,6 +18,7 @@
 PAIR = 2 * HEAD_SIZE
 HEAD_PACK = 4 * HEAD_SIZE
 BLOCK = 256
+QUERY_BLOCK = 512
 
 NORM_EPS = 1e-06
 RESIDUAL_SCALE = 0.22
@@ -30,6 +31,7 @@
 PLANE = ("b", "y", "c")
 SEQ = ("a", "b")
 ALL = ("a", "b", "y", "c")
+SWAP = [(0, 1), (1, 0)]
 
 f32 = jnp.float32
 bf16 = jnp.bfloat16
@@ -104,21 +106,20 @@
     return pieces
 
 
-def plane_gather(x):
-    swap = [(0, 1), (1, 0)]
+def neighbours(x):
+    return lax.ppermute(x, "y", SWAP), lax.ppermute(x, "b", SWAP)
+
+
+def plane_gather(x, from_y, from_b):
     half = x.shape[0] // 2
-    from_y = lax.ppermute(x, "y", swap)
-    from_b = lax.ppermute(x, "b", swap)
-    upper = lax.ppermute(from_b[:half], "y", swap)
-    lower = lax.ppermute(from_y[half:], "b", swap)
-    return [
-        (block, lax.ppermute(block, "c", swap)) for block in (x, from_y, from_b, upper, lower)
-    ]
+    upper = lax.ppermute(from_b[:half], "y", SWAP)
+    lower = lax.ppermute(from_y[half:], "b", SWAP)
+    return [(block, lax.ppermute(block, "c", SWAP)) for block in (x, from_y, from_b, upper, lower)]
 
 
 def halve_send(v, axis, at):
     me = lax.axis_index(axis)
-    other = lax.ppermute(lax.dynamic_index_in_dim(v, 1 - me, at, False), axis, [(0, 1), (1, 0)])
+    other = lax.ppermute(lax.dynamic_index_in_dim(v, 1 - me, at, False), axis, SWAP)
     return lax.dynamic_index_in_dim(v, me, at, False), other
 
 
@@ -147,15 +148,29 @@
     return jnp.where(low, cos, 1.0), jnp.where(low, sin, 0.0)
 
 
-def project_kernel(places, place_ref, *refs):
+def project_kernel(places, spots, place_ref, *refs):
     count = 1 if places is None else len(places)
     blocks, refs = refs[:count], refs[count:]
-    small_ref, w_ref, cos_ref, sin_ref, qkv_ref, normed_ref, x_ref, gain, held, sems = refs
+    count = 1 if spots is None else len(spots)
+    weights, refs = refs[:count], refs[count:]
+    cos_ref, sin_ref, qkv_ref, normed_ref, x_ref, w_ref, wide_cos_ref, wide_sin_ref = refs[:8]
+    gain, held, sems = refs[8:]
     i = pl.program_id(0)
     slots = held.shape[0]
 
     @pl.when(i == 0)
     def _():
+        copies = []
+        if spots is None:
+            copies.append(pltpu.make_async_copy(weights[0], w_ref, sems.at[slots]))
+        else:
+            for at, ((y, c), block) in enumerate(zip(spots, weights)):
+                row = 2 * (place_ref[3] ^ y) + (place_ref[4] ^ c)
+                copies.append(
+                    pltpu.make_async_copy(block, w_ref.at[:, row], sems.at[slots + at])
+                )
+        for copy in copies:
+            copy.start()
         if places is None:
             for slot in range(slots):
                 pltpu.make_async_copy(blocks[0].at[slot], held.at[slot], sems.at[slot]).start()
@@ -168,7 +183,10 @@
                 def _(block=block, slot=2 * at + member):
                     pltpu.make_async_copy(block, held.at[slot], sems.at[slot]).start()
 
-        gain[...] = jnp.transpose(small_ref[...].astype(f32))[E : E + 8, :]
+        for copy in copies:
+            copy.wait()
+        small = w_ref[..., HEAD_PACK:].reshape(held.shape[2], LANES)
+        gain[...] = jnp.transpose(small.astype(f32))[:8, :]
 
     arrived = blocks[0].at[0] if places is None else blocks[0]
     pltpu.make_async_copy(arrived, held.at[i], sems.at[i]).wait()
@@ -176,55 +194,61 @@
     x_ref[...] = x
     normed = rms_scale(x.astype(f32), gain[0:1, :]).astype(bf16)
     normed_ref[...] = normed
-    pre = jnp.dot(normed, w_ref[...], preferred_element_type=f32)
+    w = w_ref[..., :HEAD_PACK].reshape(held.shape[2], HEAD_PACK)
+    pre = jnp.dot(normed, w, preferred_element_type=f32)
     cos, sin = spread_tables(cos_ref[...], sin_ref[...])
+    wide_cos_ref[...] = cos
+    wide_sin_ref[...] = sin
     qkv_ref[:, :PAIR] = rotate_lanes(pre[:, :PAIR], cos, sin).astype(bf16)
     qkv_ref[:, PAIR:] = rotate_lanes(pre[:, PAIR:], *key_tables(cos, sin)).astype(bf16)
 
 
-def project(place, places, blocks, rows, packed, cos, sin):
-    width = packed.shape[0]
-    small_at = packed.shape[1] // LANES - 1
+def project(place, places, blocks, spots, weights, rows, width, cos, sin):
     span = cos.shape[0]
     table = pl.BlockSpec((rows, HEAD_SIZE // 2), lambda i, h: (i, 0))
     token_rows = pl.BlockSpec((rows, width), lambda i, h: (i, 0))
+    cols = HEAD_PACK + LANES
+    shape = weights[0].shape if spots is None else (
+        weights[0].shape[0], len(spots), weights[0].shape[1], cols
+    )
     return pl.pallas_call(
-        functools.partial(project_kernel, places),
+        functools.partial(project_kernel, places, spots),
         grid_spec=pltpu.PrefetchScalarGridSpec(
             num_scalar_prefetch=1,
             grid=(span // rows,),
-            in_specs=[pl.BlockSpec(memory_space=pl.ANY)] * len(blocks)
-            + [
-                pl.BlockSpec((width, LANES), lambda i, h: (0, small_at)),
-                pl.BlockSpec((width, HEAD_PACK), lambda i, h: (0, h[0])),
-                table,
-                table,
-            ],
+            in_specs=[pl.BlockSpec(memory_space=pl.ANY)] * (len(blocks) + len(weights))
+            + [table, table],
             out_specs=[
                 pl.BlockSpec((rows, HEAD_PACK), lambda i, h: (i, 0)),
                 token_rows,
                 token_rows,
+                pl.BlockSpec(shape, lambda i, h: (0,) * len(shape)),
+                pl.BlockSpec((rows, PAIR), lambda i, h: (i, 0)),
+                pl.BlockSpec((rows, PAIR), lambda i, h: (i, 0)),
             ],
             scratch_shapes=[
                 pltpu.VMEM((8, width), f32),
                 pltpu.VMEM((span // rows, rows, width), bf16),
-                pltpu.SemaphoreType.DMA((span // rows,)),
+                pltpu.SemaphoreType.DMA((span // rows + len(weights),)),
             ],
         ),
         out_shape=[
             jax.ShapeDtypeStruct((span, HEAD_PACK), bf16),
             jax.ShapeDtypeStruct((span, width), bf16),
             jax.ShapeDtypeStruct((span, width), bf16),
+            jax.ShapeDtypeStruct(shape, bf16),
+            jax.ShapeDtypeStruct((span, PAIR), f32),
+            jax.ShapeDtypeStruct((span, PAIR), f32),
         ],
         compiler_params=pltpu.CompilerParams(vmem_limit_bytes=VMEM_LIMIT),
         cost_estimate=pl.CostEstimate(
             flops=2 * span * width * HEAD_PACK, bytes_accessed=18 * 2**20, transcendentals=0
         ),
         name="project",
-    )(place, *blocks, packed, packed, cos, sin)
-
-
-def head_grads_kernel(head_ref, x_ref, normed_ref, w_ref, grad_ref, out_ref, acc, gain):
+    )(place, *blocks, *weights, cos, sin)
+
+
+def head_grads_kernel(x_ref, normed_ref, w_ref, grad_ref, out_ref, acc, gain):
     i = pl.program_id(0)
 
     @pl.when(i == 0)
@@ -249,31 +273,28 @@
         ).astype(bf16)
 
 
-def head_grads(head, x, normed, packed, grads):
+def head_grads(x, normed, weights, grads):
     span, width = x.shape
-    rows = BLOCK
-    token_rows = pl.BlockSpec((rows, width), lambda i, h: (i, 0))
+    rows = 2 * BLOCK
+    token_rows = pl.BlockSpec((rows, width), lambda i: (i, 0))
     return pl.pallas_call(
         head_grads_kernel,
-        grid_spec=pltpu.PrefetchScalarGridSpec(
-            num_scalar_prefetch=1,
-            grid=(span // rows,),
-            in_specs=[
-                token_rows,
-                token_rows,
-                pl.BlockSpec((width, HEAD_PACK), lambda i, h: (0, h[0])),
-                pl.BlockSpec((rows, HEAD_PACK), lambda i, h: (i, 0)),
-            ],
-            out_specs=pl.BlockSpec((width, HEAD_PACK + LANES), lambda i, h: (0, 0)),
-            scratch_shapes=[pltpu.VMEM((HEAD_PACK, width), f32), pltpu.VMEM((8, width), f32)],
-        ),
+        grid=(span // rows,),
+        in_specs=[
+            token_rows,
+            token_rows,
+            pl.BlockSpec((width, HEAD_PACK), lambda i: (0, 0)),
+            pl.BlockSpec((rows, HEAD_PACK), lambda i: (i, 0)),
+        ],
+        out_specs=pl.BlockSpec((width, HEAD_PACK + LANES), lambda i: (0, 0)),
+        scratch_shapes=[pltpu.VMEM((HEAD_PACK, width), f32), pltpu.VMEM((8, width), f32)],
         out_shape=jax.ShapeDtypeStruct((width, HEAD_PACK + LANES), bf16),
         compiler_params=pltpu.CompilerParams(vmem_limit_bytes=VMEM_LIMIT),
         cost_estimate=pl.CostEstimate(
             flops=4 * span * width * HEAD_PACK, bytes_accessed=12 * 2**20, transcendentals=0
         ),
         name="head_grads",
-    )(head, x, normed, packed, grads)
+    )(x, normed, weights, grads)
 
 
 def lower_lanes(shape):
@@ -294,83 +315,84 @@
     )
 
 
-def allowed_pairs(shape, query_start, key_start, doc):
-    rows = lax.broadcasted_iota(jnp.int32, (shape[0] // 2, 1), 0) + query_start
-    rows = jnp.concatenate([rows, rows], axis=0)
-    keys = lax.broadcasted_iota(jnp.int32, shape, 1) + key_start
-    return (keys >= jnp.concatenate([doc, doc], axis=0)) & (keys <= rows)
-
-
-def attend_kernel(bounds_ref, q_ref, kv_ref, doc_ref, o_ref, low_ref, lse_ref, kept, top, total, acc):
-    i = pl.program_id(0)
-    steps = pl.num_programs(0)
-    offset = bounds_ref[steps]
-    first, last = bounds_ref[i], i + offset + 1
+def block_bounds(bounds_ref):
+    i, steps = pl.program_id(0), pl.num_programs(0)
+    query_start = (i + bounds_ref[2 * steps]) * QUERY_BLOCK
+    diagonal = query_start // BLOCK
+    full = jnp.minimum(bounds_ref[steps + i], diagonal)
+    return query_start, bounds_ref[i], full, diagonal, diagonal + QUERY_BLOCK // BLOCK
+
+
+def pair_mask(doc, query_start):
+    doc = jnp.concatenate([doc, doc], axis=1)
+    queries = lax.broadcasted_iota(jnp.int32, doc.shape, 1) % QUERY_BLOCK + query_start
+
+    def masked(scores, start):
+        keys = lax.broadcasted_iota(jnp.int32, scores.shape, 0) + start
+        return jnp.where((keys >= doc) & (keys <= queries), scores, NEGATIVE_HUGE)
+
+    return masked
+
+
+def attend_kernel(bounds_ref, q_ref, kv_ref, doc_ref, o_ref, low_ref, lse_ref, acc):
+    query_start, first, full, diagonal, end = block_bounds(bounds_ref)
     q = both_heads_low(q_ref[...].astype(f32) * SCALE_OF_SCORES).astype(bf16)
-    doc = doc_ref[...]
-    top[...] = jnp.full_like(top, NEGATIVE_HUGE)
-    total[...] = jnp.zeros_like(total)
+    masked = pair_mask(doc_ref[0], query_start)
     acc[...] = jnp.zeros_like(acc)
 
-    def score(j, carried):
+    def step(mask, j, carried):
+        top, total = carried
         start = pl.multiple_of(j * BLOCK, BLOCK)
-        scores = contract_cols(q, kv_ref[pl.ds(start, BLOCK), :])
-        allowed = allowed_pairs(scores.shape, (i + offset) * BLOCK, j * BLOCK, doc)
-        scores = jnp.where(allowed, scores, NEGATIVE_HUGE)
-        kept[:, pl.ds(start, BLOCK)] = scores
-        top[...] = jnp.maximum(top[...], jnp.maximum(scores[:, :LANES], scores[:, LANES:]))
-        return carried
-
-    lax.fori_loop(first, last, score, 0)
-    highest = jnp.max(top[...], axis=1, keepdims=True)
-
-    def mix(j, carried):
-        start = pl.multiple_of(j * BLOCK, BLOCK)
-        probs = jnp.exp(kept[:, pl.ds(start, BLOCK)] - highest)
-        total[...] += probs[:, :LANES] + probs[:, LANES:]
-        acc[...] += jnp.dot(
-            probs.astype(bf16), kv_ref[pl.ds(start, BLOCK), :], preferred_element_type=f32
-        )
-        return carried
-
-    lax.fori_loop(first, last, mix, 0)
-    row_total = jnp.sum(total[...], axis=1, keepdims=True)
-    mixed = acc[...] / row_total
-    first_head, second_head = mixed[:BLOCK], mixed[BLOCK:]
-    out = jnp.where(
-        lower_lanes(first_head.shape), pltpu.roll(first_head, HEAD_SIZE, 1), second_head
-    )
+        kv = kv_ref[pl.ds(start, BLOCK), :]
+        scores = contract_cols(kv, q)
+        if mask:
+            scores = masked(scores, start)
+        new = jnp.maximum(top, jnp.max(scores, axis=0, keepdims=True))
+        probs = jnp.exp(scores - new)
+        keep = jnp.exp(top - new)
+        acc[...] = acc[...] * keep + contract_rows(kv, probs.astype(bf16))
+        return new, total * keep + jnp.sum(probs, axis=0, keepdims=True)
+
+    row = (1, 2 * QUERY_BLOCK)
+    carried = (jnp.full(row, NEGATIVE_HUGE, f32), jnp.zeros(row, f32))
+    carried = lax.fori_loop(first, full, functools.partial(step, True), carried)
+    carried = lax.fori_loop(full, diagonal, functools.partial(step, False), carried)
+    top, total = lax.fori_loop(diagonal, end, functools.partial(step, True), carried)
+    mixed = jnp.transpose(acc[...] / total)
+    one, two = mixed[:QUERY_BLOCK], mixed[QUERY_BLOCK:]
+    out = jnp.where(lower_lanes(one.shape), pltpu.roll(one, HEAD_SIZE, 1), two)
     o_ref[...] = out
     low_ref[...] = out.astype(bf16)
-    lse_ref[0] = highest + jnp.log(row_total)
+    lse_ref[0] = top + jnp.log(total)
+
+
+def attention_specs(kv_at, keys):
+    pair = pl.BlockSpec((QUERY_BLOCK, PAIR), lambda i, s: (i, 0))
+    return (
+        pair,
+        pl.BlockSpec((keys, PAIR), lambda i, s: (0, kv_at)),
+        pl.BlockSpec((1, 1, QUERY_BLOCK), lambda i, s: (i, 0, 0)),
+        pl.BlockSpec((1, 1, 2 * QUERY_BLOCK), lambda i, s: (i, 0, 0)),
+    )
 
 
 def attend(bounds, qkv, kv, kv_at, doc):
     queries, keys = qkv.shape[0], kv.shape[0]
-    steps = queries // BLOCK
-    pair = pl.BlockSpec((BLOCK, PAIR), lambda i, s: (i, 0))
+    steps = queries // QUERY_BLOCK
+    pair, whole, doc_row, lse_row = attention_specs(kv_at, keys)
     return pl.pallas_call(
         attend_kernel,
         grid_spec=pltpu.PrefetchScalarGridSpec(
             num_scalar_prefetch=1,
             grid=(steps,),
-            in_specs=[
-                pair,
-                pl.BlockSpec((keys, PAIR), lambda i, s: (0, kv_at)),
-                pl.BlockSpec((BLOCK, 1), lambda i, s: (i, 0)),
-            ],
-            out_specs=[pair, pair, pl.BlockSpec((1, 2 * BLOCK, 1), lambda i, s: (i, 0, 0))],
-            scratch_shapes=[
-                pltpu.VMEM((2 * BLOCK, keys), f32),
-                pltpu.VMEM((2 * BLOCK, LANES), f32),
-                pltpu.VMEM((2 * BLOCK, LANES), f32),
-                pltpu.VMEM((2 * BLOCK, PAIR), f32),
-            ],
+            in_specs=[pair, whole, doc_row],
+            out_specs=[pair, pair, lse_row],
+            scratch_shapes=[pltpu.VMEM((PAIR, 2 * QUERY_BLOCK), f32)],
         ),
         out_shape=[
             jax.ShapeDtypeStruct((queries, PAIR), f32),
             jax.ShapeDtypeStruct((queries, PAIR), bf16),
-            jax.ShapeDtypeStruct((steps, 2 * BLOCK, 1), f32),
+            jax.ShapeDtypeStruct((steps, 1, 2 * QUERY_BLOCK), f32),
         ],
         compiler_params=pltpu.CompilerParams(vmem_limit_bytes=VMEM_LIMIT),
         cost_estimate=pl.CostEstimate(
@@ -388,8 +410,7 @@
     else:
         dq_ref, dkv_ref, acc = refs
     i = pl.program_id(0)
-    steps = pl.num_programs(0)
-    offset = bounds_ref[steps]
+    query_start, first, full, diagonal, end = block_bounds(bounds_ref)
 
     @pl.when(i == 0)
     def _():
@@ -397,49 +418,52 @@
 
     q = both_heads_low(q_ref[...].astype(f32) * SCALE_OF_SCORES).astype(bf16)
     grad = do_ref[...].astype(f32)
-    product = grad * o_ref[...]
-    low = lower_lanes(product.shape)
+    product = jnp.transpose(grad * o_ref[...])
     delta = jnp.concatenate(
         [
-            jnp.sum(jnp.where(low, product, 0.0), axis=1, keepdims=True),
-            jnp.sum(jnp.where(low, 0.0, product), axis=1, keepdims=True),
+            jnp.sum(product[:HEAD_SIZE], axis=0, keepdims=True),
+            jnp.sum(product[HEAD_SIZE:], axis=0, keepdims=True),
         ],
-        axis=0,
+        axis=1,
     )
     grad = both_heads_high(grad).astype(bf16)
     sources = jnp.concatenate([q, grad], axis=0)
-    doc = doc_ref[...]
+    masked = pair_mask(doc_ref[0], query_start)
     lse = lse_ref[0]
     acc[...] = jnp.zeros_like(acc)
 
-    def step(j, carried):
+    def step(mask, j, carried):
         start = pl.multiple_of(j * BLOCK, BLOCK)
         kv = kv_ref[pl.ds(start, BLOCK), :]
-        scores = contract_cols(q, kv)
-        allowed = allowed_pairs(scores.shape, (i + offset) * BLOCK, j * BLOCK, doc)
-        probs = jnp.exp(jnp.where(allowed, scores - lse, NEGATIVE_HUGE))
-        grad_probs = contract_cols(grad, kv)
-        grad_scores = (probs * (grad_probs - delta)).astype(bf16)
-        acc[...] += jnp.dot(grad_scores, kv, preferred_element_type=f32)
-        both = jnp.concatenate([grad_scores, probs.astype(bf16)], axis=0)
-        dkv_ref[pl.ds(start, BLOCK), :] += contract_rows(both, sources)
+        scores = contract_cols(kv, q) - lse
+        if mask:
+            scores = masked(scores, start)
+        probs = jnp.exp(scores)
+        grad_scores = (probs * (contract_cols(kv, grad) - delta)).astype(bf16)
+        acc[...] += contract_rows(kv, grad_scores)
+        both = jnp.concatenate([grad_scores, probs.astype(bf16)], axis=1)
+        dkv_ref[pl.ds(start, BLOCK), :] += jnp.dot(both, sources, preferred_element_type=f32)
         return carried
 
-    lax.fori_loop(bounds_ref[i], i + offset + 1, step, 0)
-    first, second = acc[:BLOCK], acc[BLOCK:]
-    dq = jnp.where(lower_lanes(first.shape), first, pltpu.roll(second, HEAD_SIZE, 1))
+    lax.fori_loop(first, full, functools.partial(step, True), 0)
+    lax.fori_loop(full, diagonal, functools.partial(step, False), 0)
+    lax.fori_loop(diagonal, end, functools.partial(step, True), 0)
+    dq = jnp.transpose(acc[...])
+    one, two = dq[:QUERY_BLOCK], dq[QUERY_BLOCK:]
+    dq = jnp.where(lower_lanes(one.shape), one, pltpu.roll(two, HEAD_SIZE, 1))
     if not fold:
         dq_ref[...] = dq
         return
-    mine = pl.ds(pl.multiple_of(i * BLOCK, BLOCK), BLOCK)
-    cos, sin = spread_tables(cos_ref[mine, :], sin_ref[mine, :])
-    out_ref[mine, :PAIR] = rotate_lanes(dq * SCALE_OF_SCORES, cos, -sin).astype(bf16)
-
-    @pl.when(i == steps - 1)
+    mine = pl.ds(pl.multiple_of(i * QUERY_BLOCK, QUERY_BLOCK), QUERY_BLOCK)
+    out_ref[mine, :PAIR] = rotate_lanes(
+        dq * SCALE_OF_SCORES, cos_ref[mine, :], -sin_ref[mine, :]
+    ).astype(bf16)
+
+    @pl.when(i == pl.num_programs(0) - 1)
     def _():
         def finish(j, carried):
             part = pl.ds(pl.multiple_of(j * BLOCK, BLOCK), BLOCK)
-            cos, sin = key_tables(*spread_tables(cos_ref[part, :], sin_ref[part, :]))
+            cos, sin = key_tables(cos_ref[part, :], sin_ref[part, :])
             out_ref[part, PAIR:] = rotate_lanes(dkv_ref[part, :], cos, -sin).astype(bf16)
             return carried
 
@@ -448,10 +472,10 @@
 
 def attend_back(bounds, qkv, kv, kv_at, doc, grad, out, lse, cos, sin, fold):
     queries, keys = qkv.shape[0], kv.shape[0]
-    steps = queries // BLOCK
-    pair = pl.BlockSpec((BLOCK, PAIR), lambda i, s: (i, 0))
+    steps = queries // QUERY_BLOCK
+    pair, whole, doc_row, lse_row = attention_specs(kv_at, keys)
     table = pl.BlockSpec(cos.shape, lambda i, s: (0, 0))
-    acc = pltpu.VMEM((2 * BLOCK, PAIR), f32)
+    acc = pltpu.VMEM((PAIR, 2 * QUERY_BLOCK), f32)
     if fold:
         out_specs = pl.BlockSpec((queries, HEAD_PACK), lambda i, s: (0, 0))
         out_shape = jax.ShapeDtypeStruct((queries, HEAD_PACK), bf16)
@@ -468,16 +492,7 @@
         grid_spec=pltpu.PrefetchScalarGridSpec(
             num_scalar_prefetch=1,
             grid=(steps,),
-            in_specs=[
-                pair,
-                pl.BlockSpec((keys, PAIR), lambda i, s: (0, kv_at)),
-                pl.BlockSpec((BLOCK, 1), lambda i, s: (i, 0)),
-                pair,
-                pair,
-                pl.BlockSpec((1, 2 * BLOCK, 1), lambda i, s: (i, 0, 0)),
-                table,
-                table,
-            ],
+            in_specs=[pair, whole, doc_row, pair, pair, lse_row, table, table],
             out_specs=out_specs,
             scratch_shapes=scratch,
         ),
@@ -493,7 +508,7 @@
 
 
 def unrotate_kernel(dq_ref, dkv_ref, cos_ref, sin_ref, out_ref):
-    cos, sin = spread_tables(cos_ref[...], sin_ref[...])
+    cos, sin = cos_ref[...], sin_ref[...]
     dq = rotate_lanes(dq_ref[...] * SCALE_OF_SCORES, cos, -sin)
     cos, sin = key_tables(cos, sin)
     dkv = rotate_lanes(dkv_ref[...], cos, -sin)
@@ -503,11 +518,10 @@
 def unrotate(dq, dkv, cos, sin):
     rows = dq.shape[0]
     pair = pl.BlockSpec((BLOCK, PAIR), lambda i: (i, 0))
-    table = pl.BlockSpec((BLOCK, HEAD_SIZE // 2), lambda i: (i, 0))
     return pl.pallas_call(
         unrotate_kernel,
         grid=(rows // BLOCK,),
-        in_specs=[pair, pair, table, table],
+        in_specs=[pair, pair, pair, pair],
         out_specs=pl.BlockSpec((BLOCK, HEAD_PACK), lambda i: (i, 0)),
         out_shape=jax.ShapeDtypeStruct((rows, HEAD_PACK), bf16),
         cost_estimate=pl.CostEstimate(
@@ -786,6 +800,91 @@
     )(place, outs, packed, packed, x)
 
 
+def token_grads_kernel(grad_ref, w_ref, small_ref, x_ref, resid_ref, out_ref, acc):
+    h = pl.program_id(0)
+    part = contract_cols(grad_ref[0], w_ref[...])
+
+    @pl.when(h == 0)
+    def _():
+        acc[...] = part
+
+    @pl.when(h > 0)
+    def _():
+        acc[...] += part
+
+    @pl.when(h == pl.num_programs(0) - 1)
+    def _():
+        gain = jnp.transpose(small_ref[...].astype(f32))[E : E + 1, :]
+        x = x_ref[...].astype(f32)
+        inverse = lax.rsqrt(jnp.mean(x * x, axis=-1, keepdims=True) + NORM_EPS)
+        scaled = acc[...] * gain
+        mean = jnp.mean(x * scaled, axis=-1, keepdims=True)
+        out_ref[...] = resid_ref[...] + (inverse * scaled - x * inverse**3 * mean)
+
+
+def token_grads(grads, packed, x, resid):
+    heads, rows, pack = grads.shape
+    width = x.shape[1]
+    small_at = packed.shape[1] // LANES - 1
+    whole = pl.BlockSpec((rows, width), lambda h: (0, 0))
+    return pl.pallas_call(
+        token_grads_kernel,
+        grid=(heads,),
+        in_specs=[
+            pl.BlockSpec((1, rows, pack), lambda h: (h, 0, 0)),
+            pl.BlockSpec((width, pack), lambda h: (0, h)),
+            pl.BlockSpec((width, LANES), lambda h: (0, small_at)),
+            whole,
+            whole,
+        ],
+        out_specs=whole,
+        out_shape=jax.ShapeDtypeStruct((rows, width), f32),
+        scratch_shapes=[pltpu.VMEM((rows, width), f32)],
+        compiler_params=pltpu.CompilerParams(vmem_limit_bytes=VMEM_LIMIT),
+        cost_estimate=pl.CostEstimate(
+            flops=2 * rows * width * heads * pack, bytes_accessed=8 * 2**20, transcendentals=0
+        ),
+        name="token_grads",
+    )(grads, packed, packed, x, resid)
+
+
+def weight_sums_kernel(sums_ref, q_ref, k_ref, v_ref, gain_ref):
+    groups, heads, members = sums_ref.shape[:3]
+    gain = jnp.zeros(gain_ref.shape, f32)
+    values = []
+    for h in range(heads):
+        total = jnp.zeros(sums_ref.shape[3:], f32)
+        for g in range(groups):
+            for member in range(members):
+                total += sums_ref[g, h, member].astype(f32)
+        values.append(total)
+        gain += total[:, HEAD_PACK:]
+        q_ref[:, h * PAIR : (h + 1) * PAIR] = total[:, :PAIR]
+    gain_ref[...] = gain
+    for h in range(0, heads, 2):
+        one, two = values[h][:, PAIR:HEAD_PACK], values[h + 1][:, PAIR:HEAD_PACK]
+        low = lower_lanes(one.shape)
+        at = slice(h // 2 * PAIR, (h // 2 + 1) * PAIR)
+        k_ref[:, at] = jnp.where(low, one, pltpu.roll(two, HEAD_SIZE, 1))
+        v_ref[:, at] = jnp.where(low, pltpu.roll(one, HEAD_SIZE, 1), two)
+
+
+def weight_sums(sums):
+    rows, heads = sums.shape[3], sums.shape[1]
+    return pl.pallas_call(
+        weight_sums_kernel,
+        out_shape=[
+            jax.ShapeDtypeStruct((rows, heads * PAIR), f32),
+            jax.ShapeDtypeStruct((rows, heads * HEAD_SIZE), f32),
+            jax.ShapeDtypeStruct((rows, heads * HEAD_SIZE), f32),
+            jax.ShapeDtypeStruct((rows, LANES), f32),
+        ],
+        compiler_params=pltpu.CompilerParams(vmem_limit_bytes=VMEM_LIMIT),
+        cost_estimate=pl.CostEstimate(flops=2**20, bytes_accessed=2 * 2**20, transcendentals=0),
+        name="weight_sums",
+    )(sums)
+
+
 def exchange(x, axes):
     return lax.all_to_all(x, axes, 0, 0, tiled=True)
 
@@ -822,13 +921,15 @@
     cos_span, sin_span = rotation_tables(
         span_start + jnp.arange(span, dtype=jnp.int32) - doc_span
     )
+    by_block = doc_span.reshape(-1, QUERY_BLOCK)
     bounds = jnp.concatenate(
         [
-            doc_span.reshape(-1, BLOCK)[:, 0] // BLOCK,
-            jnp.full((1,), span_start // BLOCK, jnp.int32),
+            by_block[:, 0] // BLOCK,
+            (by_block[:, -1] + BLOCK - 1) // BLOCK,
+            jnp.full((1,), span_start // QUERY_BLOCK, jnp.int32),
         ]
     )
-    doc_column = doc_span[:, None]
+    doc_rows = by_block[:, None, :]
 
     own_rows = w_query.shape[0]
     by_head = jnp.concatenate(
@@ -862,6 +963,36 @@
         ALL,
     )
     experts_low = jnp.concatenate([expert_in.astype(bf16), expert_out.astype(bf16)], axis=1)
+    small_plane = lax.axis_size("b") == 2 and lax.axis_size("y") == 2 and lax.axis_size("c") == 2
+    if small_plane:
+        gains = jnp.broadcast_to(
+            pad_lanes(norm_attn.astype(bf16)[:, None], LANES), (KEY_VALUE_HEADS, own_rows, LANES)
+        )
+        columns = exchange(
+            jnp.concatenate(
+                [by_head.reshape(own_rows, KEY_VALUE_HEADS, HEAD_PACK).transpose(1, 0, 2), gains],
+                axis=2,
+            ),
+            SEQ,
+        )
+        from_y = lax.ppermute(columns, "y", SWAP)
+        spots = ((0, 0), (0, 1), (1, 0), (1, 1))
+        weights = (
+            columns, lax.ppermute(columns, "c", SWAP), from_y, lax.ppermute(from_y, "c", SWAP)
+        )
+    else:
+        spots = None
+        at = lax.axis_index(head_axes) * HEAD_PACK
+        gain_at = qkv_width + width + E
+        weights = (
+            jnp.concatenate(
+                [
+                    lax.dynamic_slice_in_dim(first_all, at, HEAD_PACK, 1),
+                    pad_lanes(first_all[:, gain_at : gain_at + 1], LANES),
+                ],
+                axis=1,
+            ),
+        )
     if whole_rows:
         pieces = grid_gather(tokens[0])
         places = [piece[:2] for piece in pieces]
@@ -869,42 +1000,44 @@
     else:
         places = None
         blocks = (gather(tokens[0], "b").reshape((-1,) + tokens.shape[1:]),)
-    first_all, experts_low, blocks, cos_span, sin_span, bounds, doc_column = (
+    experts_low, blocks, weights, cos_span, sin_span, bounds, doc_rows = (
         lax.optimization_barrier(
-            (first_all, experts_low, blocks, cos_span, sin_span, bounds, doc_column)
+            (experts_low, blocks, weights, cos_span, sin_span, bounds, doc_rows)
         )
     )
     output_w = first_all[:, qkv_width : qkv_width + width]
     small_at = qkv_width + width
     router_w = first_all[:, small_at : small_at + E]
-    gain_one_f = first_all[:, small_at + E].astype(f32)
     gain_two_f = first_all[:, small_at + E + 1].astype(f32)
 
     expert_ids = jnp.arange(E, dtype=jnp.int32)
     routed_own = jnp.any(routes[0][:, :, None] == expert_ids[None, None, :], axis=1)
     early = jnp.concatenate([cotangent[0], pad_lanes(routed_own.astype(bf16), LANES)], axis=1)
-    early, first_all = lax.optimization_barrier((early, first_all))
     early_all = gather(early, "a")
-    small_plane = lax.axis_size("b") == 2 and lax.axis_size("y") == 2
     if small_plane:
-        parts = plane_gather(experts_low)
+        beside = neighbours(experts_low)
     else:
         parts = gather(experts_low, PLANE)
 
-    place = jnp.stack([lax.axis_index(head_axes), group, lax.axis_index("b")])
-    qkv, normed_span, x_span = project(
-        place, places, blocks, token_count, first_all, cos_span, sin_span
-    )
+    place = jnp.stack(
+        [lax.axis_index(axis) for axis in (head_axes, "a", "b", "y", "c")]
+    )
+    qkv, normed_span, x_span, own_weights, wide_cos, wide_sin = project(
+        place, places, blocks, spots, weights, token_count, width, cos_span, sin_span
+    )
+    own_weights = own_weights.reshape(width, HEAD_PACK + LANES)
     if whole_rows:
         kv, kv_at = qkv, 1
     else:
         kv, kv_at = gather(qkv[:, PAIR:], "a"), 0
-    attention_result, attended, log_total = attend(bounds, qkv, kv, kv_at, doc_column)
+    attention_result, attended, log_total = attend(bounds, qkv, kv, kv_at, doc_rows)
     if small_plane:
         member = lax.axis_index("b")
+        attended, beside, first_all = lax.optimization_barrier((attended, beside, first_all))
+        parts = plane_gather(experts_low, *beside)
         by_column = attended.reshape(GROUPS, 2, token_count, PAIR)
         other = lax.ppermute(
-            lax.dynamic_index_in_dim(by_column, 1 - member, 1, False), "b", [(0, 1), (1, 0)]
+            lax.dynamic_index_in_dim(by_column, 1 - member, 1, False), "b", SWAP
         )
         own = lax.dynamic_index_in_dim(by_column, member, 1, False)
         pair, early_all = lax.optimization_barrier((jnp.stack([own, other]), early_all))
@@ -938,7 +1071,7 @@
     if small_plane:
         core = lax.axis_index("c")
         (send,) = expert_grads((1 - core).reshape(1), 2, *inputs, False)
-        arrived = lax.ppermute(send, "c", [(0, 1), (1, 0)])
+        arrived = lax.ppermute(send, "c", SWAP)
         moe_part, keep = expert_grads(core.reshape(1), 2, *inputs, True)
         back_own, moe_part, keep = lax.optimization_barrier((back_own, moe_part, keep))
     else:
@@ -982,34 +1115,32 @@
     second_part, grad_mixed = lax.optimization_barrier((second_part, grad_mixed))
     rest = scatter_sum(second_part.reshape(-1, cols), PLANE)
     grads = attend_back(
-        bounds, qkv, kv, kv_at, doc_column, grad_mixed, attention_result, log_total,
-        cos_span, sin_span, whole_rows,
+        bounds, qkv, kv, kv_at, doc_rows, grad_mixed, attention_result, log_total,
+        wide_cos, wide_sin, whole_rows,
     )
     if whole_rows:
         grad_pack = grads
     else:
         grad_kv = scatter_sum(grads[1].astype(bf16), "a").astype(f32)
-        grad_pack = unrotate(grads[0], grad_kv, cos_span, sin_span)
+        grad_pack = unrotate(grads[0], grad_kv, wide_cos, wide_sin)
     if small_plane:
         left, right, moe_sum, grad_pack = lax.optimization_barrier(
             (left, right, moe_sum, grad_pack)
         )
         left, right = halve_add(left), halve_add(right)
         left, right = halve_send(left, "b", 0), halve_send(right, "y", 0)
-    first_part = head_grads(place, x_span, normed_span, first_all, grad_pack)
+    first_part = head_grads(x_span, normed_span, own_weights, grad_pack)
     rest, first_part = lax.optimization_barrier((rest, first_part))
     rest = scatter_sum(rest, "a")
     by_tokens = exchange(grad_pack.reshape(KEY_VALUE_HEADS, token_count, HEAD_PACK), head_axes)
     by_tokens, first_part = lax.optimization_barrier((by_tokens, first_part))
     sums = exchange(first_part.reshape(-1, own_rows, first_part.shape[1]), ALL)
     sums, moe_sum, resid = lax.optimization_barrier((sums, moe_sum, resid))
-    sums = sums.astype(f32).reshape(lax.axis_size(SEQ), -1, own_rows, first_part.shape[1]).sum(axis=1)
-    by_heads = sums[:, :, :HEAD_PACK].reshape(-1, KEY_VALUE_HEADS, own_rows, HEAD_PACK).sum(axis=0)
+    grad_q_w, grad_k_w, grad_v_w, grad_gain_one = weight_sums(
+        sums.reshape(-1, KEY_VALUE_HEADS, lax.axis_size(("y", "c")), own_rows, first_part.shape[1])
+    )
     rest = rest.astype(f32)
-    grad_qkv = by_tokens.transpose(1, 0, 2).reshape(token_count, qkv_width)
-    grad_normed_one = contract_cols(grad_qkv, first_all[:, :qkv_width])
-    grad_x_norm, _ = rms_back(x_local, gain_one_f, grad_normed_one)
-    grad_input = grad_resid + grad_x_norm
+    grad_input = token_grads(by_tokens, first_all, tokens[0], grad_resid)
     layer_sum = resid + RESIDUAL_SCALE * moe_sum.astype(f32)
     if small_plane:
         grad_experts = jnp.concatenate(
@@ -1017,14 +1148,13 @@
         )
     else:
         grad_experts = grad_experts.astype(f32)
-    by_rows = by_heads.transpose(1, 0, 2)
     return (
         layer_sum.astype(bf16)[None],
         grad_input[None],
-        sums[:, :, HEAD_PACK].sum(axis=0),
-        by_rows[:, :, :PAIR].reshape(own_rows, -1),
-        by_rows[:, :, PAIR : PAIR + HEAD_SIZE].reshape(own_rows, -1),
-        by_rows[:, :, PAIR + HEAD_SIZE :].reshape(own_rows, -1),
+        grad_gain_one[:, 0],
+        grad_q_w,
+        grad_k_w,
+        grad_v_w,
         rest[:, :width],
         rest[:, width + E],
         rest[:, width : width + E],

time: 455 us -> 486 us (1.068); the launches traced: 453 us -> 478 us
  waiting for transfers between devices: 132 us -> 152 us
  starting transfers between devices: 62.6 us -> 69.9 us
    ppermute x14 -> x17, waiting for transfers between devices: 23.5 us -> 70.6 us  [the longest x4 37.4 us: halve_send(): lax.ppermute(lax.dynamic_index_in_dim(v, 1 - me, at, False), axis, SWAP)]
    reduce_scatter x4, waiting for transfers between devices: 34 us -> 9.7 us  [scatter_sum(): return lax.psum_scatter(x, axes, scatter_dimension=0, tiled=True)]
    all_to_all x3 -> x4, waiting for transfers between devices: 13.4 us -> 24.8 us  [exchange(): return lax.all_to_all(x, axes, 0, 0, tiled=True)]
    pallas_call x2 -> x4, Pallas kernels: 20 us -> 29.1 us  [the longest x1 11 us: project(): pl.pallas_call(functools.partial(project_kernel, places, spots), grid_spe...]
    pallas_call x1, Pallas kernels: 31.8 us -> 25 us  [attend_back(): pl.pallas_call(functools.partial(attend_back_kernel, fold), grid_spec=plt...]
    ppermute x3, waiting for transfers between devices: 10.3 us -> 4.49 us  [grid_gather(): down = lax.ppermute(down, 'a', line_pairs(n, -1))]
    pallas_call x1, Pallas kernels: 21.4 us -> 16.4 us  [attend(): pl.pallas_call(attend_kernel, grid_spec=pltpu.PrefetchScalarGridSpec(num_...]
    ppermute x3, waiting for transfers between devices: 21.7 us -> 16.7 us  [grid_gather(): up = lax.ppermute(up, 'a', line_pairs(n, 1))]
  transfers between devices with their start and end apart: 38 -> 42, of which waited for: 19 -> 20; matrix products, arithmetic and copies ran while one was open for 15% -> 15% of each run, Pallas kernels for 28% -> 25%
where the time goes in v2:
time: 486 us; the launch traced here: 478 us
  Pallas kernels  160 us (33%)
  waiting for transfers between devices  152 us (31%)
  starting transfers between devices  69.9 us (14%)
  other arithmetic  46.7 us (10%)
  local copies, waits for them, and re-layouts  26.7 us (5%)
  between operations  15.2 us (3%)
  matrix products  6.71 us (1%)
    ppermute x4, waiting for transfers between devices, halve_send(): lax.ppermute(lax.dynamic_index_in_dim(v, 1 - me, at, False), axis, SWAP)  37.4 us
    pallas_call x2, Pallas kernels, expert_grads(): pl.pallas_call(functools.partial(expert_grads_kernel, with_y), grid_spec=...  34 us
    pallas_call x1, Pallas kernels, experts(): pl.pallas_call(experts_kernel, grid_spec=pltpu.PrefetchScalarGridSpec(num...  29.1 us
    pallas_call x1, Pallas kernels, attend_back(): pl.pallas_call(functools.partial(attend_back_kernel, fold), grid_spec=plt...  25 us
    all_to_all x4, waiting for transfers between devices, exchange(): return lax.all_to_all(x, axes, 0, 0, tiled=True)  24.8 us
    ppermute x7, waiting for transfers between devices, cross(): lax.ppermute(block, SEQ, [(2 * i + j, 2 * i + 1 - j) for i in range(n) if...  19 us
    pallas_call x1, Pallas kernels, place_experts(): pl.pallas_call(place_experts_kernel, grid_spec=pltpu.PrefetchScalarGridSp...  18.5 us
    ppermute x3, starting transfers between devices, grid_gather(): up = lax.ppermute(up, 'a', line_pairs(n, 1))  18.1 us
  transfers between devices with their start and end apart: 42, of which 20 were waited for; matrix products, arithmetic and copies ran while one was open for 15% of the time, Pallas kernels for 25%

profile of v2, /device:TPU:0, one launch (start us, length us, event | category | flops | bytes accessed | tf_op | source)
XLA Modules:
  0.0 477.9 jit_solution(13802484574906491317)
XLA Ops:
  14.5 5.7 %collective-permute-start.1 = (bf16[256,1024]{1,0:T(8,128)(2,1)S(1)}, bf16[256,1024]{1,0:T(8,128)(2,1)}, u32[]{:S(2)}, u32[]{:S(2)}) collective-permute-start(bf16[256,1024]{1,0:T(8,128)(2,1)S(1)} %bitcast.84), channel_id=1, source_target_pairs={{0,8},{8,16},{16,24},{1,9},{9,17},{17,25},{2,10},{10,18},{18,26},{... | collective-permute-start | bytes 1572872 | tf_op jit(solution)/shard_map/ppermute | solution.py:102
  23.8 5.9 %all-to-all-start = ((bf16[8,32,384]{2,1,0:T(8,128)(2,1)}), bf16[8,32,384]{2,1,0:T(8,128)(2,1)S(1)}, u32[]{:S(2)}, u32[]{:S(2)}) async-start(bf16[8,32,384]{2,1,0:T(8,128)(2,1)} %pad_maximum_fusion.6), calls=%async_computation | async-start | bytes 393216 | tf_op jit(solution)/shard_map/all_to_all | solution.py:889
  30.9 3.9 collective-permute-done.1.refs_2_
  34.8 6.0 %collective-permute-start.5 = (bf16[256,1024]{1,0:T(8,128)(2,1)}, bf16[256,1024]{1,0:T(8,128)(2,1)}, u32[]{:S(2)}, u32[]{:S(2)}) collective-permute-start(bf16[256,1024]{1,0:T(8,128)(2,1)} %collective-permute-done.1.refs_2_), channel_id=1, source_target_pairs={{0,8},{8,16},{16,24},{1,9},{9,17},{17,25},{2,10},{10,18},{18,26},{... | collective-permute-start | bytes 1572872 | tf_op jit(solution)/shard_map/ppermute | solution.py:102
  42.6 1.8 convert_reduce_fusion
  45.7 12.8 %collective-permute-done.5.refs_6_ = bf16[256,1024]{1,0:T(8,128)(2,1)} collective-permute-done((bf16[256,1024]{1,0:T(8,128)(2,1)}, bf16[256,1024]{1,0:T(8,128)(2,1)}, u32[]{:S(2)}, u32[]{:S(2)}) %collective-permute-start.5) | collective-permute-done | bytes 524320 | tf_op jit(solution)/shard_map/ppermute | solution.py:102
  58.4 6.3 %collective-permute-start.9 = (bf16[256,1024]{1,0:T(8,128)(2,1)}, bf16[256,1024]{1,0:T(8,128)(2,1)}, u32[]{:S(2)}, u32[]{:S(2)}) collective-permute-start(bf16[256,1024]{1,0:T(8,128)(2,1)} %collective-permute-done.5.refs_6_), channel_id=1, source_target_pairs={{0,8},{8,16},{16,24},{1,9},{9,17},{17,25},{2,10},{10,18},{18,26},{... | collective-permute-start | bytes 1572872 | tf_op jit(solution)/shard_map/ppermute | solution.py:102
  68.1 4.4 collective-permute-done.14.refs_16_
  72.6 7.9 %collective-permute-start.4 = (bf16[256,1024]{1,0:T(8,128)(2,1)}, bf16[256,1024]{1,0:T(8,128)(2,1)S(1)}, u32[]{:S(2)}, u32[]{:S(2)}) collective-permute-start(bf16[256,1024]{1,0:T(8,128)(2,1)} %collective-permute-done.3.refs_4_), channel_id=1, source_target_pairs={{0,4},{4,0},{8,12},{12,8},{16,20},{20,16},{1,5},{5,1},{9,13},{13,9... | collective-permute-start | bytes 1572872 | tf_op jit(solution)/shard_map/ppermute | solution.py:95
  81.2 1.9 collective-permute-start.8
  83.9 4.0 collective-permute-done.11.refs_12_
  87.9 4.4 collective-permute-start.12
  92.9 6.2 %multiply_sine_fusion = (f32[2048,32]{1,0:T(8,128)}, f32[2048,32]{1,0:T(8,128)}) fusion(f32[32]{0:T(128)} %multiply_power_fusion, f32[2048]{0:T(1024)S(1)} %subtract_convert_fusion), kind=kLoop, calls=%fused_computation.17 | loop fusion | flops 65536 | bytes 532608 | tf_op jit(solution)/shard_map/sin | solution.py:44
  99.1 7.8 %collective-permute-done.8.refs_9_ = bf16[256,1024]{1,0:T(8,128)(2,1)S(1)} collective-permute-done((bf16[256,1024]{1,0:T(8,128)(2,1)}, bf16[256,1024]{1,0:T(8,128)(2,1)S(1)}, u32[]{:S(2)}, u32[]{:S(2)}) %collective-permute-start.8) | collective-permute-done | bytes 524320 | tf_op jit(solution)/shard_map/ppermute | solution.py:95
  106.9 11.2 %collective-permute-done.12.refs_13_ = bf16[256,1024]{1,0:T(8,128)(2,1)S(1)} collective-permute-done((bf16[256,1024]{1,0:T(8,128)(2,1)}, bf16[256,1024]{1,0:T(8,128)(2,1)S(1)}, u32[]{:S(2)}, u32[]{:S(2)}) %collective-permute-start.12) | collective-permute-done | bytes 524320 | tf_op jit(solution)/shard_map/ppermute | solution.py:95
  120.8 11.0 %project.1 = (bf16[2048,256]{1,0:T(8,128)(2,1)}, bf16[2048,1024]{1,0:T(8,128)(2,1)}, bf16[2048,1024]{1,0:T(8,128)(2,1)}, bf16[8,4,32,384]{3,2,1,0:T(8,128)(2,1)}...) custom-call(s32[5]{0:T(128)} %stack.36.place_ref, bf16[256,1024]{1,0:T(8,128)(2,1)} %bitcast.82, ...), custom_call_target="tpu_custom_call" | custom-call | flops 1073741824 | bytes 18874368 | tf_op jit(solution)/shard_map/project/pallas_call | solution.py:214
  131.8 16.4 %attend.1 = (f32[2048,128]{1,0:T(8,128)}, bf16[2048,128]{1,0:T(8,128)(2,1)}, f32[4,1,1024]{2,1,0:T(1,128)}) custom-call(s32[9]{0:T(128)} %pad_add_fusion.bounds_ref, bf16[2048,256]{1,0:T(8,128)(2,1)} %get-tuple-element.108.q_ref.kv_ref, bf16[2048,256]{1,0:T(8,128)(2,1)} %get-tuple-element.108.q_ref.kv_ref, s32[4,1,512]{2,1,0:T(1,128)} %bitcast.96), custom_call_target="tpu_custom_call" | custom-call | flops 2147483648 | bytes 6291456 | tf_op jit(solution)/shard_map/attend/pallas_call | solution.py:383
  148.2 6.5 %collective-permute-done.16.refs_2_ = bf16[512,1536]{1,0:T(8,128)(2,1)} collective-permute-done((bf16[512,1536]{1,0:T(8,128)(2,1)S(1)}, bf16[512,1536]{1,0:T(8,128)(2,1)}, u32[]{:S(2)}, u32[]{:S(2)}) %collective-permute-start.16) | collective-permute-done | bytes 1572896 | tf_op jit(solution)/shard_map/ppermute | solution.py:110
  157.4 6.9 %collective-permute-done.18 = bf16[4,256,128]{2,1,0:T(8,128)(2,1)S(1)} collective-permute-done((bf16[4,256,128]{2,1,0:T(8,128)(2,1)S(1)}, bf16[4,256,128]{2,1,0:T(8,128)(2,1)S(1)}, u32[]{:S(2)}, u32[]{:S(2)}) %collective-permute-start.18) | collective-permute-done | bytes 262176 | tf_op jit(solution)/shard_map/ppermute | solution.py:1039
  169.3 17.4 %collective-permute-done.22.refs_6_ = bf16[256,1536]{1,0:T(8,128)(2,1)} collective-permute-done((bf16[256,1536]{1,0:T(8,128)(2,1)S(1)}, bf16[256,1536]{1,0:T(8,128)(2,1)}, u32[]{:S(2)}, u32[]{:S(2)}) %collective-permute-start.22) | collective-permute-done | bytes 786464 | tf_op jit(solution)/shard_map/ppermute | solution.py:115
  191.0 18.5 %place_experts.1 = (bf16[4,1024,1536]{2,1,0:T(8,128)(2,1)}, f32[4,1024,512]{2,1,0:T(8,128)}) custom-call(s32[2]{0:T(128)} %pad_add_fusion.1.place_ref, bf16[512,1536]{1,0:T(8,128)(2,1)} %copy-done.8, bf16[512,1536]{1,0:T(8,128)(2,1)} %collective-permute-done.19.refs_1_, bf16[512,1536]{1,0:T(8,128)(2,1)} %collective-permute-done.16.refs_2_, ...), custom_call_target="tpu_custom_call" | custom-call | flops 4294967296 | bytes 37748736 | tf_op jit(solution)/shard_map/place_experts/pallas_call | solution.py:565
  209.5 8.2 %join.1 = (bf16[1024,1024]{1,0:T(8,128)(2,1)}, f32[256,1024]{1,0:T(8,128)}, bf16[256,1024]{1,0:T(8,128)(2,1)}) custom-call(s32[5]{0:T(128)} %stack.36.place_ref, bf16[4,2,4,256,128]{4,3,2,1,0:T(8,128)(2,1)} %bitcast.88, bf16[1024,3200]{1,0:T(8,128)(2,1)} %all-gather.5.cloned.1.call-done.w_ref.small_ref.router_ref, ...), custom_call_target="tpu_custom_call" | custom-call | flops 2147483648 | bytes 12582912 | tf_op jit(solution)/shard_map/join/pallas_call | solution.py:776
  217.8 29.1 %experts.1 = (bf16[1024,1152]{1,0:T(8,128)(2,1)}, f32[1024,128]{1,0:T(8,128)}, bf16[4,1024,512]{2,1,0:T(8,128)(2,1)}, bf16[4,1024,1024]{2,1,0:T(8,128)(2,1)}) custom-call(s32[1]{0:T(128)} %bitcast.group_ref, bf16[1024,1024]{1,0:T(8,128)(2,1)} %get-tuple-element.116.n_ref, bf16[1024,1152]{1,0:T(8,128)(2,1)} %all-gather.7.cloned.1.call-done.refs_10_.routed_ref.ct_ref, ...), custom_call_target="tpu_custom_call" | custom-call | flops 17179869184 | bytes 41943040 | tf_op jit(solution)/shard_map/experts/pallas_call | solution.py:647
  247.1 15.4 %expert_grads.3 = bf16[4,512,1536]{2,1,0:T(8,128)(2,1)} custom-call(s32[1]{0:T(128)} %bitcast.19.half_ref, bf16[1024,1024]{1,0:T(8,128)(2,1)} %get-tuple-element.116.n_ref, bf16[1024,1152]{1,0:T(8,128)(2,1)} %all-gather.7.cloned.1.call-done.refs_10_.routed_ref.ct_ref, bf16[4,1024,1536]{2,1,0:T(8,128)(2,1)} %get-tuple-element.120.w_ref, ...), custom_call_target="tpu_custom_call" | custom-call | flops 6442450944 | bytes 31457280 | tf_op jit(solution)/shard_map/expert_grads/pallas_call | solution.py:720
  263.9 18.6 %expert_grads.2 = (bf16[1024,1024]{1,0:T(8,128)(2,1)}, bf16[4,512,1536]{2,1,0:T(8,128)(2,1)}) custom-call(s32[1]{0:T(128)} %bitcast.4.half_ref, bf16[1024,1024]{1,0:T(8,128)(2,1)} %get-tuple-element.116.n_ref, bf16[1024,1152]{1,0:T(8,128)(2,1)} %all-gather.7.cloned.1.call-done.refs_10_.routed_ref.ct_ref, bf16[4,1024,1536]{2,1,0:T(8,128)(2,1)} %get-tuple-element.120.w_ref, ...), custom_call_target="tpu_custom_call" | custom-call | flops 10737418240 | bytes 31457280 | tf_op jit(solution)/shard_map/expert_grads/pallas_call | solution.py:720
  282.5 9.7 %reduce-scatter.5.cloned.1.call-done = bf16[256,1152]{1,0:T(8,128)(2,1)} async-done(((bf16[1024,1152]{1,0:T(8,128)(2,1)}), bf16[256,1152]{1,0:T(8,128)(2,1)}) %reduce-scatter.5.cloned.1.call-update) | async-done | bytes 589840 | tf_op jit(solution)/shard_map/reduce_scatter | solution.py:80
  295.5 1.8 multiply_reduce_fusion
  297.7 2.7 fusion.2
  301.4 4.1 all-to-all-start.1
  307.2 9.2 %add_convert_fusion = bf16[4,512,1536]{2,1,0:T(8,128)(2,1)} fusion(bf16[4,512,1536]{2,1,0:T(8,128)(2,1)} %collective-permute-done.26, bf16[4,512,1536]{2,1,0:T(8,128)(2,1)} %get-tuple-element.131), kind=kLoop, calls=%fused_computation.1 | loop fusion | flops 12582912 | bytes 18874368 | tf_op jit(solution)/shard_map/convert_element_type | solution.py:1103
  319.1 15.4 %all-to-all-done.1 = bf16[8,256,128]{2,1,0:T(8,128)(2,1)S(1)} async-done(((bf16[8,256,128]{2,1,0:T(8,128)(2,1)}), bf16[8,256,128]{2,1,0:T(8,128)(2,1)S(1)}, u32[]{:S(2)}, u32[]{:S(2)}) %all-to-all-start.1) | async-done | bytes 524320 | tf_op jit(solution)/shard_map/all_to_all | solution.py:889
  334.6 5.1 %fusion.21 = (bf16[2,2,512,768]{3,2,1,0:T(8,128)(2,1)S(1)}, bf16[2,2,512,768]{3,2,1,0:T(8,128)(2,1)}) fusion(bf16[2,2,512,1536]{3,2,1,0:T(8,128)(2,1)} %bitcast.76), kind=kLoop, calls=%fused_computation.84 | loop fusion | bytes 12582912 | tf_op jit(solution)/shard_map/slice | solution.py:1108
  339.6 1.9 dynamic-slice_bitcast_fusion
  343.0 3.8 dynamic-slice_bitcast_fusion.2
  348.2 25.0 %attend_back.1.grad_ref = bf16[2048,256]{1,0:T(8,128)(2,1)} custom-call(s32[9]{0:T(128)} %pad_add_fusion.bounds_ref, bf16[2048,256]{1,0:T(8,128)(2,1)} %get-tuple-element.108.q_ref.kv_ref, bf16[2048,256]{1,0:T(8,128)(2,1)} %get-tuple-element.108.q_ref.kv_ref, s32[4,1,512]{2,1,0:T(1,128)} %bitcast.97, bf16[2048,128]{1,0:T(8,128)(2,1)} %bitcast.94, ...), custom_call_target="tpu_custom_call" | custom-call | flops 5368709120 | bytes 8388608 | tf_op jit(solution)/shard_map/attend_back/pallas_call | solution.py:490
  373.2 9.4 %collective-permute-done.28 = bf16[2,512,768]{2,1,0:T(8,128)(2,1)S(1)} collective-permute-done((bf16[2,512,768]{2,1,0:T(8,128)(2,1)}, bf16[2,512,768]{2,1,0:T(8,128)(2,1)S(1)}, u32[]{:S(2)}, u32[]{:S(2)}) %collective-permute-start.28) | collective-permute-done | bytes 1572896 | tf_op jit(solution)/shard_map/ppermute | solution.py:122
  382.6 6.2 %collective-permute-done.27 = bf16[2,512,768]{2,1,0:T(8,128)(2,1)} collective-permute-done((bf16[2,512,768]{2,1,0:T(8,128)(2,1)}, bf16[2,512,768]{2,1,0:T(8,128)(2,1)}, u32[]{:S(2)}, u32[]{:S(2)}) %collective-permute-start.27) | collective-permute-done | bytes 1572896 | tf_op jit(solution)/shard_map/ppermute | solution.py:122
  388.8 4.2 all-to-all-start.2
  393.1 2.4 add_convert_fusion.1
  397.9 3.0 add_convert_fusion.2
  400.9 7.5 %head_grads.1 = bf16[1024,384]{1,0:T(8,128)(2,1)} custom-call(bf16[2048,1024]{1,0:T(8,128)(2,1)} %get-tuple-element.115.x_ref, bf16[2048,1024]{1,0:T(8,128)(2,1)} %get-tuple-element.145.normed_ref, bf16[1024,384]{1,0:T(8,128)(2,1)} %bitcast.91, bf16[2048,256]{1,0:T(8,128)(2,1)} %attend_back.1.grad_ref), custom_call_target="tpu_custom_call" | custom-call | flops 2147483648 | bytes 12582912 | tf_op jit(solution)/shard_map/head_grads/pallas_call | solution.py:280
  408.3 9.4 %all-to-all-done.2.grad_ref = bf16[8,256,256]{2,1,0:T(8,128)(2,1)} async-done(((bf16[8,256,256]{2,1,0:T(8,128)(2,1)}), bf16[8,256,256]{2,1,0:T(8,128)(2,1)}, u32[]{:S(2)}, u32[]{:S(2)}) %all-to-all-start.2) | async-done | bytes 1048608 | tf_op jit(solution)/shard_map/all_to_all | solution.py:889
  417.7 3.4 all-to-all-start.3
  421.1 2.1 dynamic-slice_bitcast_fusion.5
  423.2 1.8 collective-permute-start.29
  427.5 21.8 %collective-permute-done.29 = bf16[512,768]{1,0:T(8,128)(2,1)} collective-permute-done((bf16[512,768]{1,0:T(8,128)(2,1)}, bf16[512,768]{1,0:T(8,128)(2,1)}, u32[]{:S(2)}, u32[]{:S(2)}) %collective-permute-start.29) | collective-permute-done | bytes 786464 | tf_op jit(solution)/shard_map/ppermute | solution.py:122
  456.7 8.8 %token_grads.1 = f32[256,1024]{1,0:T(8,128)} custom-call(bf16[8,256,256]{2,1,0:T(8,128)(2,1)} %all-to-all-done.2.grad_ref, bf16[1024,3200]{1,0:T(8,128)(2,1)} %all-gather.5.cloned.1.call-done.w_ref.small_ref.router_ref, bf16[1024,3200]{1,0:T(8,128)(2,1)} %all-gather.5.cloned.1.call-done.w_ref.small_ref.router_ref, bf16[256,1024]{1,0:T(8,128)(2,1)} %bitcast.83, ...), custom_call_target="tpu_custom_call" | custom-call | flops 1073741824 | bytes 8388608 | tf_op jit(solution)/shard_map/token_grads/pallas_call | solution.py:830
  466.4 1.9 weight_sums.1
  (184 shorter events, 64.0 us)
Async XLA Ops:
  7.2 148.7 %all-gather.5.cloned.1.call-start = ((), (), s32[]{:S(2)}) async-start(), calls=%async_computation.8 | async-start | bytes 6758400 | tf_op jit(solution)/shard_map/all_gather | solution.py:76
  12.5 30.1 %copy-start.25 = (s32[1,2048]{1,0:T(1,128)S(1)}, s32[1,2048]{1,0:T(1,128)}, u32[]{:S(2)}) copy-start(s32[1,2048]{1,0:T(1,128)} %param.15) | copy-start | bytes 24580
  12.5 31.9 %copy-start.6 = (f32[512,1024]{1,0:T(8,128)S(1)}, f32[512,1024]{1,0:T(8,128)}, u32[]{:S(2)}) copy-start(f32[512,1024]{1,0:T(8,128)} %param.24) | copy-start | bytes 6291460
  14.5 20.3 %collective-permute-start.1 = (bf16[256,1024]{1,0:T(8,128)(2,1)S(1)}, bf16[256,1024]{1,0:T(8,128)(2,1)}, u32[]{:S(2)}, u32[]{:S(2)}) collective-permute-start(bf16[256,1024]{1,0:T(8,128)(2,1)S(1)} %bitcast.84), channel_id=1, source_target_pairs={{0,8},{8,16},{16,24},{1,9},{9,17},{17,25},{2,10},{10,18},{18,26},{... | collective-permute-start | bytes 1572872 | tf_op jit(solution)/shard_map/ppermute | solution.py:102
  20.3 21.0 %collective-permute-start.3 = (bf16[256,1024]{1,0:T(8,128)(2,1)S(1)}, bf16[256,1024]{1,0:T(8,128)(2,1)}, u32[]{:S(2)}, u32[]{:S(2)}) collective-permute-start(bf16[256,1024]{1,0:T(8,128)(2,1)S(1)} %bitcast.85), channel_id=1, source_target_pairs={{8,0},{16,8},{24,16},{9,1},{17,9},{25,17},{10,2},{18,10},{26,18},{... | collective-permute-start | bytes 1572872 | tf_op jit(solution)/shard_map/ppermute | solution.py:103
  21.5 46.5 %collective-permute-start = (bf16[256,1024]{1,0:T(8,128)(2,1)S(1)}, bf16[256,1024]{1,0:T(8,128)(2,1)}, u32[]{:S(2)}, u32[]{:S(2)}) collective-permute-start(bf16[256,1024]{1,0:T(8,128)(2,1)S(1)} %bitcast.86), channel_id=1, source_target_pairs={{0,4},{4,0},{8,12},{12,8},{16,20},{20,16},{24,28},{28,24},{1,5},{5... | collective-permute-start | bytes 1572872 | tf_op jit(solution)/shard_map/ppermute | solution.py:95
  23.8 42.8 %all-to-all-start = ((bf16[8,32,384]{2,1,0:T(8,128)(2,1)}), bf16[8,32,384]{2,1,0:T(8,128)(2,1)S(1)}, u32[]{:S(2)}, u32[]{:S(2)}) async-start(bf16[8,32,384]{2,1,0:T(8,128)(2,1)} %pad_maximum_fusion.6), calls=%async_computation | async-start | bytes 393216 | tf_op jit(solution)/shard_map/all_to_all | solution.py:889
  29.7 135.4 %all-gather.7.cloned.1.call-start = ((), (), s32[]{:S(2)}) async-start(), calls=%async_computation.9 | async-start | bytes 2949120 | tf_op jit(solution)/shard_map/all_gather | solution.py:76
  30.8 178.7 %all-gather.9.cloned.1.call-start = ((), (), s32[]{:S(2)}) async-start(), calls=%async_computation.14 | async-start | bytes 2621440 | tf_op jit(solution)/shard_map/all_gather | solution.py:1044
  34.8 23.6 %collective-permute-start.5 = (bf16[256,1024]{1,0:T(8,128)(2,1)}, bf16[256,1024]{1,0:T(8,128)(2,1)}, u32[]{:S(2)}, u32[]{:S(2)}) collective-permute-start(bf16[256,1024]{1,0:T(8,128)(2,1)} %collective-permute-done.1.refs_2_), channel_id=1, source_target_pairs={{0,8},{8,16},{16,24},{1,9},{9,17},{17,25},{2,10},{10,18},{18,26},{... | collective-permute-start | bytes 1572872 | tf_op jit(solution)/shard_map/ppermute | solution.py:102
  41.3 23.5 %collective-permute-start.7 = (bf16[256,1024]{1,0:T(8,128)(2,1)}, bf16[256,1024]{1,0:T(8,128)(2,1)}, u32[]{:S(2)}, u32[]{:S(2)}) collective-permute-start(bf16[256,1024]{1,0:T(8,128)(2,1)} %collective-permute-done.3.refs_4_), channel_id=1, source_target_pairs={{8,0},{16,8},{24,16},{9,1},{17,9},{25,17},{10,2},{18,10},{26,18},{... | collective-permute-start | bytes 1572872 | tf_op jit(solution)/shard_map/ppermute | solution.py:103
  44.8 120.6 %copy-start.8 = (bf16[512,1536]{1,0:T(8,128)(2,1)}, bf16[512,1536]{1,0:T(8,128)(2,1)S(1)}, u32[]{:S(2)}) copy-start(bf16[512,1536]{1,0:T(8,128)(2,1)S(1)} %pad_maximum_fusion.2.refs_0_) | copy-start | bytes 4718596
  45.0 36.2 %collective-permute-start.2 = (bf16[256,1024]{1,0:T(8,128)(2,1)}, bf16[256,1024]{1,0:T(8,128)(2,1)S(1)}, u32[]{:S(2)}, u32[]{:S(2)}) collective-permute-start(bf16[256,1024]{1,0:T(8,128)(2,1)} %collective-permute-done.1.refs_2_), channel_id=1, source_target_pairs={{8,12},{12,8},{16,20},{20,16},{24,28},{28,24},{9,13},{13,9},{17,21... | collective-permute-start | bytes 1572872 | tf_op jit(solution)/shard_map/ppermute | solution.py:95
  58.4 24.7 %collective-permute-start.9 = (bf16[256,1024]{1,0:T(8,128)(2,1)}, bf16[256,1024]{1,0:T(8,128)(2,1)}, u32[]{:S(2)}, u32[]{:S(2)}) collective-permute-start(bf16[256,1024]{1,0:T(8,128)(2,1)} %collective-permute-done.5.refs_6_), channel_id=1, source_target_pairs={{0,8},{8,16},{16,24},{1,9},{9,17},{17,25},{2,10},{10,18},{18,26},{... | collective-permute-start | bytes 1572872 | tf_op jit(solution)/shard_map/ppermute | solution.py:102
  64.7 23.1 %collective-permute-start.11 = (bf16[256,1024]{1,0:T(8,128)(2,1)}, bf16[256,1024]{1,0:T(8,128)(2,1)}, u32[]{:S(2)}, u32[]{:S(2)}) collective-permute-start(bf16[256,1024]{1,0:T(8,128)(2,1)} %collective-permute-done.7.refs_8_), channel_id=1, source_target_pairs={{8,0},{16,8},{24,16},{9,1},{17,9},{25,17},{10,2},{18,10},{26,18},{... | collective-permute-start | bytes 1572872 | tf_op jit(solution)/shard_map/ppermute | solution.py:103
  66.6 54.2 %copy-start.11 = (bf16[8,32,384]{2,1,0:T(8,128)(2,1)}, bf16[8,32,384]{2,1,0:T(8,128)(2,1)S(1)}, u32[]{:S(2)}) copy-start(bf16[8,32,384]{2,1,0:T(8,128)(2,1)S(1)} %all-to-all-done.refs_14_) | copy-start | bytes 589828
  66.6 6.0 %collective-permute-start.14 = (bf16[8,32,384]{2,1,0:T(8,128)(2,1)S(1)}, bf16[8,32,384]{2,1,0:T(8,128)(2,1)S(1)}, u32[]{:S(2)}, u32[]{:S(2)}) collective-permute-start(bf16[8,32,384]{2,1,0:T(8,128)(2,1)S(1)} %all-to-all-done.refs_14_), channel_id=1, source_target_pairs={{0,2},{2,0},{1,3},{3,1},{4,6},{6,4},{5,7},{7,5},{8,10},{10,8},{9,1... | collective-permute-start | bytes 589832 | tf_op jit(solution)/shard_map/ppermute | solution.py:978
  68.1 4.5 collective-permute-start.13
  72.5 48.2 %copy-start.21 = (bf16[8,32,384]{2,1,0:T(8,128)(2,1)}, bf16[8,32,384]{2,1,0:T(8,128)(2,1)S(1)}, u32[]{:S(2)}) copy-start(bf16[8,32,384]{2,1,0:T(8,128)(2,1)S(1)} %collective-permute-done.14.refs_16_) | copy-start | bytes 589828
  72.5 7.9 %collective-permute-start.15 = (bf16[8,32,384]{2,1,0:T(8,128)(2,1)S(1)}, bf16[8,32,384]{2,1,0:T(8,128)(2,1)}, u32[]{:S(2)}, u32[]{:S(2)}) collective-permute-start(bf16[8,32,384]{2,1,0:T(8,128)(2,1)S(1)} %collective-permute-done.14.refs_16_), channel_id=1, source_target_pairs={{0,1},{1,0},{2,3},{3,2},{4,5},{5,4},{6,7},{7,6},{8,9},{9,8},{10,11... | collective-permute-start | bytes 589832 | tf_op jit(solution)/shard_map/ppermute | solution.py:981
  72.6 26.5 %collective-permute-start.4 = (bf16[256,1024]{1,0:T(8,128)(2,1)}, bf16[256,1024]{1,0:T(8,128)(2,1)S(1)}, u32[]{:S(2)}, u32[]{:S(2)}) collective-permute-start(bf16[256,1024]{1,0:T(8,128)(2,1)} %collective-permute-done.3.refs_4_), channel_id=1, source_target_pairs={{0,4},{4,0},{8,12},{12,8},{16,20},{20,16},{1,5},{5,1},{9,13},{13,9... | collective-permute-start | bytes 1572872 | tf_op jit(solution)/shard_map/ppermute | solution.py:95
  80.5 18.6 %collective-permute-start.6 = (bf16[256,1024]{1,0:T(8,128)(2,1)}, bf16[256,1024]{1,0:T(8,128)(2,1)S(1)}, u32[]{:S(2)}, u32[]{:S(2)}) collective-permute-start(bf16[256,1024]{1,0:T(8,128)(2,1)} %collective-permute-done.5.refs_6_), channel_id=1, source_target_pairs={{16,20},{20,16},{24,28},{28,24},{17,21},{21,17},{25,29},{29,25},{1... | collective-permute-start | bytes 1572872 | tf_op jit(solution)/shard_map/ppermute | solution.py:95
  81.2 39.6 %copy-start.12 = (bf16[256,1024]{1,0:T(8,128)(2,1)}, bf16[256,1024]{1,0:T(8,128)(2,1)S(1)}, u32[]{:S(2)}) copy-start(bf16[256,1024]{1,0:T(8,128)(2,1)S(1)} %collective-permute-done.2.refs_3_) | copy-start | bytes 1572868
  81.2 25.7 %collective-permute-start.8 = (bf16[256,1024]{1,0:T(8,128)(2,1)}, bf16[256,1024]{1,0:T(8,128)(2,1)S(1)}, u32[]{:S(2)}, u32[]{:S(2)}) collective-permute-start(bf16[256,1024]{1,0:T(8,128)(2,1)} %collective-permute-done.7.refs_8_), channel_id=1, source_target_pairs={{0,4},{4,0},{8,12},{12,8},{1,5},{5,1},{9,13},{13,9},{2,6},{6,2},{1... | collective-permute-start | bytes 1572872 | tf_op jit(solution)/shard_map/ppermute | solution.py:95
  83.2 23.8 %collective-permute-start.10 = (bf16[256,1024]{1,0:T(8,128)(2,1)}, bf16[256,1024]{1,0:T(8,128)(2,1)S(1)}, u32[]{:S(2)}, u32[]{:S(2)}) collective-permute-start(bf16[256,1024]{1,0:T(8,128)(2,1)} %collective-permute-done.9.refs_10_), channel_id=1, source_target_pairs={{24,28},{28,24},{25,29},{29,25},{26,30},{30,26},{27,31},{31,27}} | collective-permute-start | bytes 1572872 | tf_op jit(solution)/shard_map/ppermute | solution.py:95
  87.9 30.2 %collective-permute-start.12 = (bf16[256,1024]{1,0:T(8,128)(2,1)}, bf16[256,1024]{1,0:T(8,128)(2,1)S(1)}, u32[]{:S(2)}, u32[]{:S(2)}) collective-permute-start(bf16[256,1024]{1,0:T(8,128)(2,1)} %collective-permute-done.11.refs_12_), channel_id=1, source_target_pairs={{0,4},{4,0},{1,5},{5,1},{2,6},{6,2},{3,7},{7,3}} | collective-permute-start | bytes 1572872 | tf_op jit(solution)/shard_map/ppermute | solution.py:95
  118.1 36.6 %collective-permute-start.16 = (bf16[512,1536]{1,0:T(8,128)(2,1)S(1)}, bf16[512,1536]{1,0:T(8,128)(2,1)}, u32[]{:S(2)}, u32[]{:S(2)}) collective-permute-start(bf16[512,1536]{1,0:T(8,128)(2,1)S(1)} %pad_maximum_fusion.2.refs_0_), channel_id=1, source_target_pairs={{0,2},{2,0},{1,3},{3,1},{4,6},{6,4},{5,7},{7,5},{8,10},{10,8},{9,1... | collective-permute-start | bytes 4718600 | tf_op jit(solution)/shard_map/ppermute | solution.py:110
  119.6 36.3 %collective-permute-start.17 = (bf16[512,1536]{1,0:T(8,128)(2,1)S(1)}, bf16[512,1536]{1,0:T(8,128)(2,1)}, u32[]{:S(2)}, u32[]{:S(2)}) collective-permute-start(bf16[512,1536]{1,0:T(8,128)(2,1)S(1)} %pad_maximum_fusion.2.refs_0_), channel_id=1, source_target_pairs={{0,4},{4,0},{1,5},{5,1},{2,6},{6,2},{3,7},{7,3},{8,12},{12,8},{9,1... | collective-permute-start | bytes 4718600 | tf_op jit(solution)/shard_map/ppermute | solution.py:110
  157.0 7.3 %collective-permute-start.18 = (bf16[4,256,128]{2,1,0:T(8,128)(2,1)S(1)}, bf16[4,256,128]{2,1,0:T(8,128)(2,1)S(1)}, u32[]{:S(2)}, u32[]{:S(2)}) collective-permute-start(bf16[4,256,128]{2,1,0:T(8,128)(2,1)S(1)} %get-tuple-element.240), channel_id=1, source_target_pairs={{0,4},{4,0},{1,5},{5,1},{2,6},{6,2},{3,7},{7,3},{8,12},{12,8},{9,1... | collective-permute-start | bytes 786440 | tf_op jit(solution)/shard_map/ppermute | solution.py:1039
  165.1 127.1 %reduce-scatter.5.cloned.1.call-start = ((), (), s32[]{:S(2)}) async-start(), calls=%async_computation.10 | async-start | bytes 2949120 | tf_op jit(solution)/shard_map/reduce_scatter | solution.py:80
  165.3 23.6 %collective-permute-start.19 = (bf16[512,1536]{1,0:T(8,128)(2,1)S(1)}, bf16[512,1536]{1,0:T(8,128)(2,1)}, u32[]{:S(2)}, u32[]{:S(2)}) collective-permute-start(bf16[512,1536]{1,0:T(8,128)(2,1)S(1)} %pad_maximum_fusion.2.refs_0_), channel_id=1, source_target_pairs={{0,1},{1,0},{2,3},{3,2},{4,5},{5,4},{6,7},{7,6},{8,9},{9,8},{10,11... | collective-permute-start | bytes 4718600 | tf_op jit(solution)/shard_map/ppermute | solution.py:117
  166.6 20.1 %collective-permute-start.22 = (bf16[256,1536]{1,0:T(8,128)(2,1)S(1)}, bf16[256,1536]{1,0:T(8,128)(2,1)}, u32[]{:S(2)}, u32[]{:S(2)}) collective-permute-start(bf16[256,1536]{1,0:T(8,128)(2,1)S(1)} %slice.59), channel_id=1, source_target_pairs={{0,2},{2,0},{1,3},{3,1},{4,6},{6,4},{5,7},{7,5},{8,10},{10,8},{9,1... | collective-permute-start | bytes 2359304 | tf_op jit(solution)/shard_map/ppermute | solution.py:115
  168.5 19.8 %collective-permute-start.24 = (bf16[256,1536]{1,0:T(8,128)(2,1)S(1)}, bf16[256,1536]{1,0:T(8,128)(2,1)}, u32[]{:S(2)}, u32[]{:S(2)}) collective-permute-start(bf16[256,1536]{1,0:T(8,128)(2,1)S(1)} %slice.60), channel_id=1, source_target_pairs={{0,4},{4,0},{1,5},{5,1},{2,6},{6,2},{3,7},{7,3},{8,12},{12,8},{9,1... | collective-permute-start | bytes 2359304 | tf_op jit(solution)/shard_map/ppermute | solution.py:116
  168.8 22.2 %collective-permute-start.20 = (bf16[512,1536]{1,0:T(8,128)(2,1)}, bf16[512,1536]{1,0:T(8,128)(2,1)}, u32[]{:S(2)}, u32[]{:S(2)}) collective-permute-start(bf16[512,1536]{1,0:T(8,128)(2,1)} %collective-permute-done.16.refs_2_), channel_id=1, source_target_pairs={{0,1},{1,0},{2,3},{3,2},{4,5},{5,4},{6,7},{7,6},{8,9},{9,8},{10,11... | collective-permute-start | bytes 4718600 | tf_op jit(solution)/shard_map/ppermute | solution.py:117
  168.9 22.1 %collective-permute-start.21 = (bf16[512,1536]{1,0:T(8,128)(2,1)}, bf16[512,1536]{1,0:T(8,128)(2,1)}, u32[]{:S(2)}, u32[]{:S(2)}) collective-permute-start(bf16[512,1536]{1,0:T(8,128)(2,1)} %collective-permute-done.17.refs_4_), channel_id=1, source_target_pairs={{0,1},{1,0},{2,3},{3,2},{4,5},{5,4},{6,7},{7,6},{8,9},{9,8},{10,11... | collective-permute-start | bytes 4718600 | tf_op jit(solution)/shard_map/ppermute | solution.py:117
  186.7 2.6 collective-permute-start.23
  188.3 2.6 collective-permute-start.25
  246.9 142.0 %reduce-scatter.7.cloned.1.call-start = ((), (), s32[]{:S(2)}) async-start(), calls=%async_computation.11 | async-start | bytes 2621440 | tf_op jit(solution)/shard_map/reduce_scatter | solution.py:80
  262.5 44.6 %collective-permute-start.26 = (bf16[4,512,1536]{2,1,0:T(8,128)(2,1)}, bf16[4,512,1536]{2,1,0:T(8,128)(2,1)}, u32[]{:S(2)}, u32[]{:S(2)}) collective-permute-start(bf16[4,512,1536]{2,1,0:T(8,128)(2,1)} %expert_grads.3), channel_id=1, source_target_pairs={{0,1},{1,0},{2,3},{3,2},{4,5},{5,4},{6,7},{7,6},{8,9},{9,8},{10,11... | collective-permute-start | bytes 18874376 | tf_op jit(solution)/shard_map/ppermute | solution.py:1074
  301.4 33.2 %all-to-all-start.1 = ((bf16[8,256,128]{2,1,0:T(8,128)(2,1)}), bf16[8,256,128]{2,1,0:T(8,128)(2,1)S(1)}, u32[]{:S(2)}, u32[]{:S(2)}) async-start(bf16[8,256,128]{2,1,0:T(8,128)(2,1)} %bitcast_bitcast_fusion), calls=%async_computation.3 | async-start | bytes 1048576 | tf_op jit(solution)/shard_map/all_to_all | solution.py:889
  305.5 102.9 %reduce-scatter.9.cloned.1.call-start = ((), (), s32[]{:S(2)}) async-start(), calls=%async_computation.12 | async-start | bytes 2654208 | tf_op jit(solution)/shard_map/reduce_scatter | solution.py:80
  341.5 41.1 %collective-permute-start.28 = (bf16[2,512,768]{2,1,0:T(8,128)(2,1)}, bf16[2,512,768]{2,1,0:T(8,128)(2,1)S(1)}, u32[]{:S(2)}, u32[]{:S(2)}) collective-permute-start(bf16[2,512,768]{2,1,0:T(8,128)(2,1)} %get-tuple-element.235), channel_id=1, source_target_pairs={{0,4},{4,0},{1,5},{5,1},{2,6},{6,2},{3,7},{7,3},{8,12},{12,8},{9,1... | collective-permute-start | bytes 4718600 | tf_op jit(solution)/shard_map/ppermute | solution.py:122
  346.8 42.1 %collective-permute-start.27 = (bf16[2,512,768]{2,1,0:T(8,128)(2,1)}, bf16[2,512,768]{2,1,0:T(8,128)(2,1)}, u32[]{:S(2)}, u32[]{:S(2)}) collective-permute-start(bf16[2,512,768]{2,1,0:T(8,128)(2,1)} %get-tuple-element.237), channel_id=1, source_target_pairs={{0,2},{2,0},{1,3},{3,1},{4,6},{6,4},{5,7},{7,5},{8,10},{10,8},{9,1... | collective-permute-start | bytes 4718600 | tf_op jit(solution)/shard_map/ppermute | solution.py:122
  388.8 28.9 %all-to-all-start.2 = ((bf16[8,256,256]{2,1,0:T(8,128)(2,1)}), bf16[8,256,256]{2,1,0:T(8,128)(2,1)}, u32[]{:S(2)}, u32[]{:S(2)}) async-start(bf16[8,256,256]{2,1,0:T(8,128)(2,1)} %bitcast.79), calls=%async_computation.4 | async-start | bytes 2097152 | tf_op jit(solution)/shard_map/all_to_all | solution.py:889
  396.4 28.6 %collective-permute-start.30 = (bf16[512,768]{1,0:T(8,128)(2,1)}, bf16[512,768]{1,0:T(8,128)(2,1)}, u32[]{:S(2)}, u32[]{:S(2)}) collective-permute-start(bf16[512,768]{1,0:T(8,128)(2,1)} %dynamic-slice_bitcast_fusion.4), channel_id=1, source_target_pairs={{0,2},{2,0},{1,3},{3,1},{4,6},{6,4},{5,7},{7,5},{8,10},{10,8},{9,1... | collective-permute-start | bytes 2359304 | tf_op jit(solution)/shard_map/ppermute | solution.py:122
  417.7 47.8 %all-to-all-start.3 = ((bf16[32,32,384]{2,1,0:T(8,128)(2,1)}), bf16[32,32,384]{2,1,0:T(8,128)(2,1)S(1)}, u32[]{:S(2)}, u32[]{:S(2)}) async-start(bf16[32,32,384]{2,1,0:T(8,128)(2,1)} %bitcast.81), calls=%async_computation.6 | async-start | bytes 1572864 | tf_op jit(solution)/shard_map/all_to_all | solution.py:889
  421.1 31.2 %reduce-scatter.11.cloned.1.call-start = ((), (), s32[]{:S(2)}) async-start(), calls=%async_computation.13 | async-start | bytes 368640 | tf_op jit(solution)/shard_map/reduce_scatter | solution.py:80
  423.2 26.1 %collective-permute-start.29 = (bf16[512,768]{1,0:T(8,128)(2,1)}, bf16[512,768]{1,0:T(8,128)(2,1)}, u32[]{:S(2)}, u32[]{:S(2)}) collective-permute-start(bf16[512,768]{1,0:T(8,128)(2,1)} %dynamic-slice_bitcast_fusion.5), channel_id=1, source_target_pairs={{0,4},{4,0},{1,5},{5,1},{2,6},{6,2},{3,7},{7,3},{8,12},{12,8},{9,1... | collective-permute-start | bytes 2359304 | tf_op jit(solution)/shard_map/ppermute | solution.py:122
  (20 other events, 265.7 us)
Sparse Core Ops, SparseCore 0:
  14.6 82.7 all-gather.4
  99.0 49.7 all-gather.6
  165.2 42.2 all-gather.8
  247.0 45.1 reduce-scatter.4
  294.4 51.6 reduce-scatter.6
  349.6 56.3 reduce-scatter.8
  425.1 21.7 reduce-scatter.10

commit v3 on v2

--- a/solution.py
+++ b/solution.py
@@ -88,22 +88,20 @@
     return [(i, i + step) for i in range(n) if 0 <= i + step < n]
 
 
-def grid_gather(x):
-    n = lax.axis_size("a")
-
-    def cross(block, ends):
-        return lax.ppermute(
-            block, SEQ, [(2 * i + j, 2 * i + 1 - j) for i in range(n) if ends(i) for j in (0, 1)]
-        )
-
-    pieces = [(0, 0, x), (0, 1, cross(x, lambda i: True))]
+def line_gather(x, axis):
+    n = lax.axis_size(axis)
+    pieces = [(0, x)]
     up = down = x
     for k in range(1, n):
-        up = lax.ppermute(up, "a", line_pairs(n, 1))
-        down = lax.ppermute(down, "a", line_pairs(n, -1))
-        pieces += [(-k, 0, up), (-k, 1, cross(up, lambda i: i >= k))]
-        pieces += [(k, 0, down), (k, 1, cross(down, lambda i: i + k < n))]
+        up = lax.ppermute(up, axis, line_pairs(n, 1))
+        down = lax.ppermute(down, axis, line_pairs(n, -1))
+        pieces += [(-k, up), (k, down)]
     return pieces
+
+
+def by_columns(own, other, member):
+    first, second = jnp.where(member == 0, own, other), jnp.where(member == 0, other, own)
+    return jnp.stack([first, second], axis=1)
 
 
 def neighbours(x):
@@ -153,10 +151,10 @@
     blocks, refs = refs[:count], refs[count:]
     count = 1 if spots is None else len(spots)
     weights, refs = refs[:count], refs[count:]
-    cos_ref, sin_ref, qkv_ref, normed_ref, x_ref, w_ref, wide_cos_ref, wide_sin_ref = refs[:8]
-    gain, held, sems = refs[8:]
+    cos_ref, sin_ref, q_ref, kv_ref, x_ref, w_ref, gain, held, sems = refs
     i = pl.program_id(0)
-    slots = held.shape[0]
+    slots, _, width = held.shape
+    heads = q_ref.shape[1] // PAIR
 
     @pl.when(i == 0)
     def _():
@@ -165,7 +163,7 @@
             copies.append(pltpu.make_async_copy(weights[0], w_ref, sems.at[slots]))
         else:
             for at, ((y, c), block) in enumerate(zip(spots, weights)):
-                row = 2 * (place_ref[3] ^ y) + (place_ref[4] ^ c)
+                row = 2 * (place_ref[2] ^ y) + (place_ref[3] ^ c)
                 copies.append(
                     pltpu.make_async_copy(block, w_ref.at[:, row], sems.at[slots + at])
                 )
@@ -175,17 +173,16 @@
             for slot in range(slots):
                 pltpu.make_async_copy(blocks[0].at[slot], held.at[slot], sems.at[slot]).start()
         else:
-            for (distance, crossed), block in zip(places, blocks):
-                at = place_ref[1] + distance
-                member = 1 - place_ref[2] if crossed else place_ref[2]
-
-                @pl.when((at >= 0) & (at < slots // 2))
-                def _(block=block, slot=2 * at + member):
+            for distance, block in zip(places, blocks):
+                slot = place_ref[0] + distance
+
+                @pl.when((slot >= 0) & (slot < slots))
+                def _(block=block, slot=slot):
                     pltpu.make_async_copy(block, held.at[slot], sems.at[slot]).start()
 
         for copy in copies:
             copy.wait()
-        small = w_ref[..., HEAD_PACK:].reshape(held.shape[2], LANES)
+        small = w_ref[..., heads * HEAD_PACK :].reshape(width, LANES)
         gain[...] = jnp.transpose(small.astype(f32))[:8, :]
 
     arrived = blocks[0].at[0] if places is None else blocks[0]
@@ -193,21 +190,25 @@
     x = held[i]
     x_ref[...] = x
     normed = rms_scale(x.astype(f32), gain[0:1, :]).astype(bf16)
-    normed_ref[...] = normed
-    w = w_ref[..., :HEAD_PACK].reshape(held.shape[2], HEAD_PACK)
+    w = w_ref[..., : heads * HEAD_PACK].reshape(width, heads * HEAD_PACK)
     pre = jnp.dot(normed, w, preferred_element_type=f32)
     cos, sin = spread_tables(cos_ref[...], sin_ref[...])
-    wide_cos_ref[...] = cos
-    wide_sin_ref[...] = sin
-    qkv_ref[:, :PAIR] = rotate_lanes(pre[:, :PAIR], cos, sin).astype(bf16)
-    qkv_ref[:, PAIR:] = rotate_lanes(pre[:, PAIR:], *key_tables(cos, sin)).astype(bf16)
+    key_cos, key_sin = key_tables(cos, sin)
+    for h in range(heads):
+        out, at = slice(h * PAIR, (h + 1) * PAIR), h * HEAD_PACK
+        q_ref[:, out] = rotate_lanes(pre[:, at : at + PAIR], cos, sin).astype(bf16)
+        kv_ref[:, out] = rotate_lanes(
+            pre[:, at + PAIR : at + HEAD_PACK], key_cos, key_sin
+        ).astype(bf16)
 
 
 def project(place, places, blocks, spots, weights, rows, width, cos, sin):
     span = cos.shape[0]
+    cols = weights[0].shape[-1]
+    heads = (cols - LANES) // HEAD_PACK
     table = pl.BlockSpec((rows, HEAD_SIZE // 2), lambda i, h: (i, 0))
     token_rows = pl.BlockSpec((rows, width), lambda i, h: (i, 0))
-    cols = HEAD_PACK + LANES
+    head_rows = pl.BlockSpec((rows, heads * PAIR), lambda i, h: (i, 0))
     shape = weights[0].shape if spots is None else (
         weights[0].shape[0], len(spots), weights[0].shape[1], cols
     )
@@ -219,12 +220,10 @@
             in_specs=[pl.BlockSpec(memory_space=pl.ANY)] * (len(blocks) + len(weights))
             + [table, table],
             out_specs=[
-                pl.BlockSpec((rows, HEAD_PACK), lambda i, h: (i, 0)),
-                token_rows,
+                head_rows,
+                head_rows,
                 token_rows,
                 pl.BlockSpec(shape, lambda i, h: (0,) * len(shape)),
-                pl.BlockSpec((rows, PAIR), lambda i, h: (i, 0)),
-                pl.BlockSpec((rows, PAIR), lambda i, h: (i, 0)),
             ],
             scratch_shapes=[
                 pltpu.VMEM((8, width), f32),
@@ -233,68 +232,101 @@
             ],
         ),
         out_shape=[
-            jax.ShapeDtypeStruct((span, HEAD_PACK), bf16),
-            jax.ShapeDtypeStruct((span, width), bf16),
+            jax.ShapeDtypeStruct((span, heads * PAIR), bf16),
+            jax.ShapeDtypeStruct((span, heads * PAIR), bf16),
             jax.ShapeDtypeStruct((span, width), bf16),
             jax.ShapeDtypeStruct(shape, bf16),
-            jax.ShapeDtypeStruct((span, PAIR), f32),
-            jax.ShapeDtypeStruct((span, PAIR), f32),
         ],
         compiler_params=pltpu.CompilerParams(vmem_limit_bytes=VMEM_LIMIT),
         cost_estimate=pl.CostEstimate(
-            flops=2 * span * width * HEAD_PACK, bytes_accessed=18 * 2**20, transcendentals=0
+            flops=2 * span * width * heads * HEAD_PACK, bytes_accessed=8 * 2**20, transcendentals=0
         ),
         name="project",
     )(place, *blocks, *weights, cos, sin)
 
 
-def head_grads_kernel(x_ref, normed_ref, w_ref, grad_ref, out_ref, acc, gain):
+def spread_kernel(cos_ref, sin_ref, wide_cos_ref, wide_sin_ref):
+    wide_cos_ref[...], wide_sin_ref[...] = spread_tables(cos_ref[...], sin_ref[...])
+
+
+def spread(cos, sin):
+    rows = cos.shape[0]
+    wide = jax.ShapeDtypeStruct((rows, PAIR), f32)
+    return pl.pallas_call(
+        spread_kernel,
+        grid=(4,),
+        in_specs=[pl.BlockSpec((rows // 4, HEAD_SIZE // 2), lambda i: (i, 0))] * 2,
+        out_specs=[pl.BlockSpec((rows // 4, PAIR), lambda i: (i, 0))] * 2,
+        out_shape=[wide, wide],
+        cost_estimate=pl.CostEstimate(flops=2**20, bytes_accessed=4 * 2**20, transcendentals=0),
+        name="spread",
+    )(cos, sin)
+
+
+def head_grads_kernel(place_ref, own_ref, other_ref, w_ref, small_ref, grad_ref, out_ref, acc, sums, gain):
     i = pl.program_id(0)
+    half = pl.num_programs(0) // 2
 
     @pl.when(i == 0)
     def _():
         acc[...] = jnp.zeros_like(acc)
-        gain[...] = jnp.zeros_like(gain)
+        sums[...] = jnp.zeros_like(sums)
+        gain[...] = jnp.transpose(small_ref[...].astype(f32))[:8, :]
 
     grad = grad_ref[...]
-    acc[...] += contract_rows(grad, normed_ref[...])
-    x = x_ref[...].astype(f32)
+    x = jnp.where(i < half, own_ref[...], other_ref[...]).astype(f32)
     inverse = lax.rsqrt(jnp.mean(x * x, axis=-1, keepdims=True) + NORM_EPS)
-    back = contract_cols(grad, w_ref[...]) * (x * inverse)
-    gain[...] += jnp.sum(back.reshape(back.shape[0] // 8, 8, back.shape[1]), axis=0)
+    x = x * inverse
+    acc[...] += contract_rows(grad, (x * gain[0:1, :]).astype(bf16))
+    back = contract_cols(grad, w_ref[...]) * x
+    sums[...] += jnp.sum(back.reshape(back.shape[0] // 8, 8, back.shape[1]), axis=0)
 
     @pl.when(i == pl.num_programs(0) - 1)
     def _():
         out_ref[:, :HEAD_PACK] = jnp.transpose(acc[...]).astype(bf16)
-        total = jnp.sum(gain[...], axis=0, keepdims=True)
+        total = jnp.sum(sums[...], axis=0, keepdims=True)
         rows = lax.broadcasted_iota(jnp.int32, (LANES, total.shape[1]), 0)
         out_ref[:, HEAD_PACK:] = jnp.transpose(
             jnp.where(rows == 0, jnp.broadcast_to(total, rows.shape), 0.0)
         ).astype(bf16)
 
 
-def head_grads(x, normed, weights, grads):
-    span, width = x.shape
-    rows = 2 * BLOCK
-    token_rows = pl.BlockSpec((rows, width), lambda i: (i, 0))
+def head_grads(own, other, first, second, stride, head_at, weights, grads):
+    span, pack = grads.shape
+    width = own.shape[1]
+    rows = BLOCK
+    half = span // rows // 2
+    small_at = weights.shape[1] // LANES - 1
+
+    def grads_at(i, s):
+        return (jnp.where(i < half, s[0] + stride * i, s[1] + stride * (i - half)), 0)
+
     return pl.pallas_call(
         head_grads_kernel,
-        grid=(span // rows,),
-        in_specs=[
-            token_rows,
-            token_rows,
-            pl.BlockSpec((width, HEAD_PACK), lambda i: (0, 0)),
-            pl.BlockSpec((rows, HEAD_PACK), lambda i: (i, 0)),
-        ],
-        out_specs=pl.BlockSpec((width, HEAD_PACK + LANES), lambda i: (0, 0)),
-        scratch_shapes=[pltpu.VMEM((HEAD_PACK, width), f32), pltpu.VMEM((8, width), f32)],
-        out_shape=jax.ShapeDtypeStruct((width, HEAD_PACK + LANES), bf16),
+        grid_spec=pltpu.PrefetchScalarGridSpec(
+            num_scalar_prefetch=1,
+            grid=(span // rows,),
+            in_specs=[
+                pl.BlockSpec((rows, width), lambda i, s: (jnp.minimum(i, half - 1), 0)),
+                pl.BlockSpec((rows, width), lambda i, s: (jnp.maximum(i - half, 0), 0)),
+                pl.BlockSpec((width, pack), lambda i, s: (0, s[2])),
+                pl.BlockSpec((width, LANES), lambda i, s: (0, small_at)),
+                pl.BlockSpec((rows, pack), grads_at),
+            ],
+            out_specs=pl.BlockSpec((width, pack + LANES), lambda i, s: (0, 0)),
+            scratch_shapes=[
+                pltpu.VMEM((pack, width), f32),
+                pltpu.VMEM((8, width), f32),
+                pltpu.VMEM((8, width), f32),
+            ],
+        ),
+        out_shape=jax.ShapeDtypeStruct((width, pack + LANES), bf16),
         compiler_params=pltpu.CompilerParams(vmem_limit_bytes=VMEM_LIMIT),
         cost_estimate=pl.CostEstimate(
-            flops=4 * span * width * HEAD_PACK, bytes_accessed=12 * 2**20, transcendentals=0
+            flops=4 * span * width * pack, bytes_accessed=8 * 2**20, transcendentals=0
         ),
         name="head_grads",
-    )(x, normed, weights, grads)
+    )(jnp.stack([first, second, head_at]), own, other, weights, weights, grads)
 
 
 def lower_lanes(shape):
@@ -315,17 +347,16 @@
     )
 
 
-def block_bounds(bounds_ref):
-    i, steps = pl.program_id(0), pl.num_programs(0)
-    query_start = (i + bounds_ref[2 * steps]) * QUERY_BLOCK
-    diagonal = query_start // BLOCK
-    full = jnp.minimum(bounds_ref[steps + i], diagonal)
-    return query_start, bounds_ref[i], full, diagonal, diagonal + QUERY_BLOCK // BLOCK
-
-
-def pair_mask(doc, query_start):
+def block_bounds(bounds_ref, tile, tiles, stride):
+    place = bounds_ref[2 * tiles] + stride * (QUERY_BLOCK // BLOCK) * tile
+    full = jnp.minimum(bounds_ref[tiles + tile], place)
+    return place, bounds_ref[tile], full, place + stride * (QUERY_BLOCK // BLOCK - 1) + 1
+
+
+def pair_mask(doc, place, stride):
     doc = jnp.concatenate([doc, doc], axis=1)
-    queries = lax.broadcasted_iota(jnp.int32, doc.shape, 1) % QUERY_BLOCK + query_start
+    lane = lax.broadcasted_iota(jnp.int32, doc.shape, 1) % QUERY_BLOCK
+    queries = (place + stride * (lane // BLOCK)) * BLOCK + lane % BLOCK
 
     def masked(scores, start):
         keys = lax.broadcasted_iota(jnp.int32, scores.shape, 0) + start
@@ -334,10 +365,12 @@
     return masked
 
 
-def attend_kernel(bounds_ref, q_ref, kv_ref, doc_ref, o_ref, low_ref, lse_ref, acc):
-    query_start, first, full, diagonal, end = block_bounds(bounds_ref)
+def attend_kernel(stride, bounds_ref, q_ref, kv_ref, doc_ref, o_ref, low_ref, lse_ref, acc):
+    place, first, full, end = block_bounds(
+        bounds_ref, pl.program_id(1), pl.num_programs(1), stride
+    )
     q = both_heads_low(q_ref[...].astype(f32) * SCALE_OF_SCORES).astype(bf16)
-    masked = pair_mask(doc_ref[0], query_start)
+    masked = pair_mask(doc_ref[0], place, stride)
     acc[...] = jnp.zeros_like(acc)
 
     def step(mask, j, carried):
@@ -356,50 +389,50 @@
     row = (1, 2 * QUERY_BLOCK)
     carried = (jnp.full(row, NEGATIVE_HUGE, f32), jnp.zeros(row, f32))
     carried = lax.fori_loop(first, full, functools.partial(step, True), carried)
-    carried = lax.fori_loop(full, diagonal, functools.partial(step, False), carried)
-    top, total = lax.fori_loop(diagonal, end, functools.partial(step, True), carried)
+    carried = lax.fori_loop(full, place, functools.partial(step, False), carried)
+    top, total = lax.fori_loop(place, end, functools.partial(step, True), carried)
     mixed = jnp.transpose(acc[...] / total)
     one, two = mixed[:QUERY_BLOCK], mixed[QUERY_BLOCK:]
     out = jnp.where(lower_lanes(one.shape), pltpu.roll(one, HEAD_SIZE, 1), two)
     o_ref[...] = out
     low_ref[...] = out.astype(bf16)
-    lse_ref[0] = top + jnp.log(total)
-
-
-def attention_specs(kv_at, keys):
-    pair = pl.BlockSpec((QUERY_BLOCK, PAIR), lambda i, s: (i, 0))
-    return (
-        pair,
-        pl.BlockSpec((keys, PAIR), lambda i, s: (0, kv_at)),
-        pl.BlockSpec((1, 1, QUERY_BLOCK), lambda i, s: (i, 0, 0)),
-        pl.BlockSpec((1, 1, 2 * QUERY_BLOCK), lambda i, s: (i, 0, 0)),
-    )
-
-
-def attend(bounds, qkv, kv, kv_at, doc):
-    queries, keys = qkv.shape[0], kv.shape[0]
-    steps = queries // QUERY_BLOCK
-    pair, whole, doc_row, lse_row = attention_specs(kv_at, keys)
+    lse_ref[0, 0] = top + jnp.log(total)
+
+
+def attend(bounds, q, kv, doc, stride):
+    (queries, cols), keys = q.shape, kv.shape[0]
+    heads, tiles = cols // PAIR, queries // QUERY_BLOCK
+    pair = pl.BlockSpec((QUERY_BLOCK, PAIR), lambda h, i, s: (i, h))
     return pl.pallas_call(
-        attend_kernel,
+        functools.partial(attend_kernel, stride),
         grid_spec=pltpu.PrefetchScalarGridSpec(
             num_scalar_prefetch=1,
-            grid=(steps,),
-            in_specs=[pair, whole, doc_row],
-            out_specs=[pair, pair, lse_row],
+            grid=(heads, tiles),
+            in_specs=[
+                pair,
+                pl.BlockSpec((keys, PAIR), lambda h, i, s: (0, h)),
+                pl.BlockSpec((1, 1, QUERY_BLOCK), lambda h, i, s: (i, 0, 0)),
+            ],
+            out_specs=[
+                pair,
+                pair,
+                pl.BlockSpec((1, 1, 1, 2 * QUERY_BLOCK), lambda h, i, s: (h, i, 0, 0)),
+            ],
             scratch_shapes=[pltpu.VMEM((PAIR, 2 * QUERY_BLOCK), f32)],
         ),
         out_shape=[
-            jax.ShapeDtypeStruct((queries, PAIR), f32),
-            jax.ShapeDtypeStruct((queries, PAIR), bf16),
-            jax.ShapeDtypeStruct((steps, 1, 2 * QUERY_BLOCK), f32),
+            jax.ShapeDtypeStruct((queries, cols), f32),
+            jax.ShapeDtypeStruct((queries, cols), bf16),
+            jax.ShapeDtypeStruct((heads, tiles, 1, 2 * QUERY_BLOCK), f32),
         ],
         compiler_params=pltpu.CompilerParams(vmem_limit_bytes=VMEM_LIMIT),
         cost_estimate=pl.CostEstimate(
-            flops=4 * queries * keys * PAIR, bytes_accessed=6 * 2**20, transcendentals=queries * keys
+            flops=4 * queries * keys * cols,
+            bytes_accessed=6 * 2**20,
+            transcendentals=queries * keys * heads,
         ),
         name="attend",
-    )(bounds, qkv, kv, doc)
+    )(bounds, q, kv, doc)
 
 
 def attend_back_kernel(
@@ -410,7 +443,7 @@
     else:
         dq_ref, dkv_ref, acc = refs
     i = pl.program_id(0)
-    query_start, first, full, diagonal, end = block_bounds(bounds_ref)
+    place, first, full, end = block_bounds(bounds_ref, i, pl.num_programs(0), 1)
 
     @pl.when(i == 0)
     def _():
@@ -428,7 +461,7 @@
     )
     grad = both_heads_high(grad).astype(bf16)
     sources = jnp.concatenate([q, grad], axis=0)
-    masked = pair_mask(doc_ref[0], query_start)
+    masked = pair_mask(doc_ref[0], place, 1)
     lse = lse_ref[0]
     acc[...] = jnp.zeros_like(acc)
 
@@ -446,8 +479,8 @@
         return carried
 
     lax.fori_loop(first, full, functools.partial(step, True), 0)
-    lax.fori_loop(full, diagonal, functools.partial(step, False), 0)
-    lax.fori_loop(diagonal, end, functools.partial(step, True), 0)
+    lax.fori_loop(full, place, functools.partial(step, False), 0)
+    lax.fori_loop(place, end, functools.partial(step, True), 0)
     dq = jnp.transpose(acc[...])
     one, two = dq[:QUERY_BLOCK], dq[QUERY_BLOCK:]
     dq = jnp.where(lower_lanes(one.shape), one, pltpu.roll(two, HEAD_SIZE, 1))
@@ -470,10 +503,13 @@
         lax.fori_loop(0, dkv_ref.shape[0] // BLOCK, finish, 0)
 
 
-def attend_back(bounds, qkv, kv, kv_at, doc, grad, out, lse, cos, sin, fold):
-    queries, keys = qkv.shape[0], kv.shape[0]
+def attend_back(bounds, q, kv, doc, grad, out, lse, cos, sin, fold):
+    queries, keys = q.shape[0], kv.shape[0]
     steps = queries // QUERY_BLOCK
-    pair, whole, doc_row, lse_row = attention_specs(kv_at, keys)
+    pair = pl.BlockSpec((QUERY_BLOCK, PAIR), lambda i, s: (i, 0))
+    whole = pl.BlockSpec((keys, PAIR), lambda i, s: (0, s[2 * steps + 1]))
+    doc_row = pl.BlockSpec((1, 1, QUERY_BLOCK), lambda i, s: (i, 0, 0))
+    lse_row = pl.BlockSpec((1, 1, 2 * QUERY_BLOCK), lambda i, s: (i, 0, 0))
     table = pl.BlockSpec(cos.shape, lambda i, s: (0, 0))
     acc = pltpu.VMEM((PAIR, 2 * QUERY_BLOCK), f32)
     if fold:
@@ -504,7 +540,7 @@
             transcendentals=queries * keys,
         ),
         name="attend_back",
-    )(bounds, qkv, kv, doc, grad, out, lse, cos, sin)
+    )(bounds, q, kv, doc, grad, out, lse, cos, sin)
 
 
 def unrotate_kernel(dq_ref, dkv_ref, cos_ref, sin_ref, out_ref):
@@ -678,26 +714,26 @@
     )(group, normed, early, packed, w_all, z)
 
 
-def expert_grads_kernel(with_y, half_ref, n_ref, ct_ref, w_ref, hidden_ref, pre_ref, *refs):
-    if with_y:
-        y_ref, grad_ref, n_t, ct_t, acc = refs
-    else:
-        grad_ref, n_t, ct_t = refs
+def expert_grads_kernel(half_ref, n_ref, ct_ref, w_ref, hidden_ref, pre_ref, y_ref, *refs):
+    grad_refs, (n_t, ct_t, acc) = refs[:-3], refs[-3:]
     e = pl.program_id(0)
 
     @pl.when(e == 0)
     def _():
         n_t[...] = jnp.transpose(n_ref[...])
         ct_t[...] = jnp.transpose(ct_ref[...])
-        if with_y:
-            acc[...] = jnp.zeros_like(acc)
-
-    grad_ref[0, :, : 2 * F] = jnp.dot(n_t[...], pre_ref[0], preferred_element_type=f32).astype(bf16)
-    grad_ref[0, :, 2 * F :] = (
-        RESIDUAL_SCALE * jnp.dot(ct_t[...], hidden_ref[0], preferred_element_type=f32)
-    ).astype(bf16)
-    if not with_y:
-        return
+        acc[...] = jnp.zeros_like(acc)
+
+    for part in range(len(grad_refs) // 2):
+        left_ref, right_ref = grad_refs[2 * part : 2 * part + 2]
+        rows, cut = left_ref.shape[1:]
+        at = pl.ds(pl.multiple_of((half_ref[0] ^ part) * rows, rows), rows)
+        grads = jnp.dot(n_t[at, :], pre_ref[0], preferred_element_type=f32).astype(bf16)
+        left_ref[0] = grads[:, :cut]
+        right_ref[0, :, : 2 * F - cut] = grads[:, cut:]
+        right_ref[0, :, 2 * F - cut :] = (
+            RESIDUAL_SCALE * jnp.dot(ct_t[at, :], hidden_ref[0], preferred_element_type=f32)
+        ).astype(bf16)
     acc[...] += contract_cols(hidden_ref[0], w_ref[0, :, 2 * F :])
 
     @pl.when(e == pl.num_programs(0) - 1)
@@ -705,39 +741,35 @@
         y_ref[...] = acc[...].astype(bf16)
 
 
-def expert_grads(half, halves, normed, early, w_all, hidden, pre, with_y):
+def expert_grads(half, parts, normed, early, w_all, hidden, pre):
     rows, width = normed.shape
     count = w_all.shape[0]
-    own = width // halves
-    feature = pl.BlockSpec((rows, own), lambda e, h: (0, h[0]))
-    out_specs = [pl.BlockSpec((1, own, 3 * F), lambda e, h: (e, 0, 0))]
-    out_shape = [jax.ShapeDtypeStruct((count, own, 3 * F), bf16)]
-    scratch = [pltpu.VMEM((own, rows), bf16), pltpu.VMEM((own, rows), bf16)]
-    if with_y:
-        out_specs.insert(0, pl.BlockSpec((rows, width), lambda e, h: (0, 0)))
-        out_shape.insert(0, jax.ShapeDtypeStruct((rows, width), bf16))
-        scratch.append(pltpu.VMEM((rows, width), f32))
+    own, cut = width // parts, 3 * F // 2
+    whole = pl.BlockSpec((rows, width), lambda e, h: (0, 0))
     return pl.pallas_call(
-        functools.partial(expert_grads_kernel, with_y),
+        expert_grads_kernel,
         grid_spec=pltpu.PrefetchScalarGridSpec(
             num_scalar_prefetch=1,
             grid=(count,),
             in_specs=[
-                feature,
-                feature,
+                whole,
+                whole,
                 pl.BlockSpec((1, width, 3 * F), lambda e, h: (e, 0, 0)),
                 pl.BlockSpec((1, rows, F), lambda e, h: (e, 0, 0)),
                 pl.BlockSpec((1, rows, 2 * F), lambda e, h: (e, 0, 0)),
             ],
-            out_specs=out_specs,
-            scratch_shapes=scratch,
-        ),
-        out_shape=out_shape,
+            out_specs=[whole] + [pl.BlockSpec((1, own, cut), lambda e, h: (e, 0, 0))] * (2 * parts),
+            scratch_shapes=[
+                pltpu.VMEM((width, rows), bf16),
+                pltpu.VMEM((width, rows), bf16),
+                pltpu.VMEM((rows, width), f32),
+            ],
+        ),
+        out_shape=[jax.ShapeDtypeStruct((rows, width), bf16)]
+        + [jax.ShapeDtypeStruct((count, own, cut), bf16)] * (2 * parts),
         compiler_params=pltpu.CompilerParams(vmem_limit_bytes=VMEM_LIMIT),
         cost_estimate=pl.CostEstimate(
-            flops=2 * count * rows * width * 3 * F // halves + 2 * with_y * count * rows * width * F,
-            bytes_accessed=30 * 2**20,
-            transcendentals=0,
+            flops=2 * count * rows * width * 4 * F, bytes_accessed=40 * 2**20, transcendentals=0
         ),
         name="expert_grads",
     )(half, normed, early, w_all, hidden, pre)
@@ -745,24 +777,18 @@
 
 def join_kernel(place_ref, o_ref, w_ref, small_ref, x_ref, normed_ref, resid_ref, own_ref, gain):
     t = pl.program_id(0)
-    b = place_ref[2]
 
     @pl.when(t == 0)
     def _():
         gain[...] = jnp.transpose(small_ref[...].astype(f32))[E : E + 8, :]
 
-    pairs = []
-    for a in range(o_ref.shape[0]):
-        same, other = o_ref[a, 0, 0], o_ref[a, 1, 0]
-        pairs.append(jnp.where(b == 0, same, other))
-        pairs.append(jnp.where(b == 0, other, same))
-    attended = jnp.concatenate(pairs, axis=1)
+    attended = jnp.concatenate([o_ref[a] for a in range(o_ref.shape[0])], axis=1)
     resid = x_ref[...].astype(f32) + RESIDUAL_SCALE * jnp.dot(
         attended, w_ref[...], preferred_element_type=f32
     )
     normed_ref[...] = rms_scale(resid, gain[1:2, :]).astype(bf16)
 
-    @pl.when(t == place_ref[1])
+    @pl.when(t == place_ref[0])
     def _():
         resid_ref[...] = resid
         own_ref[...] = attended
@@ -770,7 +796,8 @@
 
 def join(place, outs, packed, weights_at, x):
     width = packed.shape[0]
-    lines, _, _, rows, pair = outs.shape
+    lines, tokens, cols = outs.shape
+    rows = tokens // lines
     small_at = packed.shape[1] // LANES - 1
     own = pl.BlockSpec((rows, width), lambda t, s: (0, 0))
     return pl.pallas_call(
@@ -779,10 +806,10 @@
             num_scalar_prefetch=1,
             grid=(lines,),
             in_specs=[
-                pl.BlockSpec((lines, 2, 1, rows, pair), lambda t, s: (0, 0, t, 0, 0)),
+                pl.BlockSpec((lines, rows, cols), lambda t, s: (0, t, 0)),
                 pl.BlockSpec((width, width), lambda t, s: (0, weights_at)),
                 pl.BlockSpec((width, LANES), lambda t, s: (0, small_at)),
-                pl.BlockSpec((rows, width), lambda t, s: (2 * t + s[2], 0)),
+                pl.BlockSpec((rows, width), lambda t, s: (t, 0)),
             ],
             out_specs=[pl.BlockSpec((rows, width), lambda t, s: (t, 0)), own, own],
             scratch_shapes=[pltpu.VMEM((8, width), f32)],
@@ -907,29 +934,37 @@
     x_local = tokens[0].astype(f32)
     token_count, width = x_local.shape
     seg_row = segment_ids[0]
-    group = lax.axis_index("a")
-    head_axes = SEQ if lax.axis_size(SEQ) == KEY_VALUE_HEADS else ("b",)
-    whole_rows = head_axes == SEQ
+    group, member = lax.axis_index("a"), lax.axis_index("b")
+    by_column = all(lax.axis_size(axis) == 2 for axis in PLANE)
+    by_column = by_column and lax.axis_size(SEQ) == KEY_VALUE_HEADS
+    head_axes = SEQ if by_column else ("b",)
     span = token_count * KEY_VALUE_HEADS
-    span_start = 0 if whole_rows else group * span
+    span_start = 0 if by_column else group * span
 
     def start_of_doc(ids):
         return jnp.sum((seg_row[None, :] < ids[:, None]).astype(jnp.int32), axis=1)
 
-    seg_span = lax.dynamic_slice_in_dim(seg_row, span_start, span)
-    doc_span = start_of_doc(seg_span)
-    cos_span, sin_span = rotation_tables(
-        span_start + jnp.arange(span, dtype=jnp.int32) - doc_span
-    )
-    by_block = doc_span.reshape(-1, QUERY_BLOCK)
-    bounds = jnp.concatenate(
-        [
-            by_block[:, 0] // BLOCK,
-            (by_block[:, -1] + BLOCK - 1) // BLOCK,
-            jnp.full((1,), span_start // QUERY_BLOCK, jnp.int32),
-        ]
-    )
-    doc_rows = by_block[:, None, :]
+    def tile_bounds(docs, place):
+        tiles = docs.reshape(-1, QUERY_BLOCK)
+        ends = (tiles[:, 0] // BLOCK, (tiles[:, -1] + BLOCK - 1) // BLOCK, jnp.stack(place))
+        return jnp.concatenate(ends).astype(jnp.int32), tiles[:, None, :]
+
+    def own_column(x):
+        x = x.reshape((GROUPS, 2, token_count) + x.shape[1:])
+        x = lax.dynamic_index_in_dim(x, member, 1, False)
+        return x.reshape((GROUPS * token_count,) + x.shape[2:])
+
+    doc_span = start_of_doc(lax.dynamic_slice_in_dim(seg_row, span_start, span))
+    cos_span, sin_span = rotation_tables(span_start + jnp.arange(span, dtype=jnp.int32) - doc_span)
+    zero = jnp.zeros_like(member)
+    head_of_two = member if by_column else zero
+    bounds, doc_rows = tile_bounds(doc_span, (zero + span_start // BLOCK, head_of_two))
+    wide_cos, wide_sin = spread(cos_span, sin_span)
+    if by_column:
+        cos_ahead, sin_ahead = own_column(cos_span), own_column(sin_span)
+        bounds_ahead, docs_ahead = tile_bounds(own_column(doc_span), (member,))
+    else:
+        cos_ahead, sin_ahead, bounds_ahead, docs_ahead = cos_span, sin_span, bounds, doc_rows
 
     own_rows = w_query.shape[0]
     by_head = jnp.concatenate(
@@ -963,46 +998,36 @@
         ALL,
     )
     experts_low = jnp.concatenate([expert_in.astype(bf16), expert_out.astype(bf16)], axis=1)
-    small_plane = lax.axis_size("b") == 2 and lax.axis_size("y") == 2 and lax.axis_size("c") == 2
-    if small_plane:
-        gains = jnp.broadcast_to(
-            pad_lanes(norm_attn.astype(bf16)[:, None], LANES), (KEY_VALUE_HEADS, own_rows, LANES)
-        )
-        columns = exchange(
-            jnp.concatenate(
-                [by_head.reshape(own_rows, KEY_VALUE_HEADS, HEAD_PACK).transpose(1, 0, 2), gains],
-                axis=2,
-            ),
-            SEQ,
-        )
+    if by_column:
+        two = by_head.reshape(own_rows, GROUPS, 2 * HEAD_PACK).transpose(1, 0, 2)
+        gains = pad_lanes(norm_attn.astype(bf16)[:, None], LANES)
+        gains = jnp.broadcast_to(gains, (GROUPS, own_rows, LANES))
+        columns = exchange(jnp.repeat(jnp.concatenate([two, gains], axis=2), 2, axis=0), SEQ)
         from_y = lax.ppermute(columns, "y", SWAP)
         spots = ((0, 0), (0, 1), (1, 0), (1, 1))
         weights = (
             columns, lax.ppermute(columns, "c", SWAP), from_y, lax.ppermute(from_y, "c", SWAP)
         )
+        pieces = line_gather(tokens[0], "a")
+        places = [piece[0] for piece in pieces]
+        blocks = tuple(piece[1] for piece in pieces)
     else:
-        spots = None
         at = lax.axis_index(head_axes) * HEAD_PACK
         gain_at = qkv_width + width + E
+        gains = pad_lanes(first_all[:, gain_at : gain_at + 1], LANES)
+        spots, places = None, None
         weights = (
             jnp.concatenate(
-                [
-                    lax.dynamic_slice_in_dim(first_all, at, HEAD_PACK, 1),
-                    pad_lanes(first_all[:, gain_at : gain_at + 1], LANES),
-                ],
-                axis=1,
+                [lax.dynamic_slice_in_dim(first_all, at, HEAD_PACK, 1), gains], axis=1
             ),
         )
-    if whole_rows:
-        pieces = grid_gather(tokens[0])
-        places = [piece[:2] for piece in pieces]
-        blocks = tuple(piece[2] for piece in pieces)
-    else:
-        places = None
         blocks = (gather(tokens[0], "b").reshape((-1,) + tokens.shape[1:]),)
-    experts_low, blocks, weights, cos_span, sin_span, bounds, doc_rows = (
+    experts_low, blocks, weights, cos_ahead, sin_ahead, bounds_ahead, docs_ahead, wide_cos, wide_sin = (
         lax.optimization_barrier(
-            (experts_low, blocks, weights, cos_span, sin_span, bounds, doc_rows)
+            (
+                experts_low, blocks, weights, cos_ahead, sin_ahead, bounds_ahead, docs_ahead,
+                wide_cos, wide_sin,
+            )
         )
     )
     output_w = first_all[:, qkv_width : qkv_width + width]
@@ -1014,38 +1039,54 @@
     routed_own = jnp.any(routes[0][:, :, None] == expert_ids[None, None, :], axis=1)
     early = jnp.concatenate([cotangent[0], pad_lanes(routed_own.astype(bf16), LANES)], axis=1)
     early_all = gather(early, "a")
-    if small_plane:
+    if by_column:
         beside = neighbours(experts_low)
     else:
         parts = gather(experts_low, PLANE)
 
-    place = jnp.stack(
-        [lax.axis_index(axis) for axis in (head_axes, "a", "b", "y", "c")]
-    )
-    qkv, normed_span, x_span, own_weights, wide_cos, wide_sin = project(
-        place, places, blocks, spots, weights, token_count, width, cos_span, sin_span
-    )
-    own_weights = own_weights.reshape(width, HEAD_PACK + LANES)
-    if whole_rows:
-        kv, kv_at = qkv, 1
+    place = jnp.stack([lax.axis_index(axis) for axis in ALL])
+    q, kv, x_span, own_weights = project(
+        place, places, blocks, spots, weights, token_count, width, cos_ahead, sin_ahead
+    )
+    own_weights = own_weights.reshape(width, own_weights.shape[-1])
+    if by_column:
+        columns = (GROUPS, token_count)
+
+        def in_row(own, other, shape):
+            return by_columns(own.reshape(shape), other.reshape(shape), member)
+
+        kv_other = lax.ppermute(kv, "b", SWAP)
+        kv = in_row(kv, kv_other, columns + (2 * PAIR,)).reshape(span, 2 * PAIR)
     else:
-        kv, kv_at = gather(qkv[:, PAIR:], "a"), 0
-    attention_result, attended, log_total = attend(bounds, qkv, kv, kv_at, doc_rows)
-    if small_plane:
-        member = lax.axis_index("b")
-        attended, beside, first_all = lax.optimization_barrier((attended, beside, first_all))
+        kv = gather(kv, "a")
+    attention_result, attended, log_total = attend(
+        bounds_ahead, q, kv, docs_ahead, 2 if by_column else 1
+    )
+    if by_column:
+        attended, first_all = lax.optimization_barrier((attended, first_all))
+        attended, early_all = lax.optimization_barrier((attended, early_all))
+        outs = lax.all_gather(attended, "a", axis=0, tiled=False)
         parts = plane_gather(experts_low, *beside)
-        by_column = attended.reshape(GROUPS, 2, token_count, PAIR)
-        other = lax.ppermute(
-            lax.dynamic_index_in_dim(by_column, 1 - member, 1, False), "b", SWAP
-        )
-        own = lax.dynamic_index_in_dim(by_column, member, 1, False)
-        pair, early_all = lax.optimization_barrier((jnp.stack([own, other]), early_all))
-        outs = lax.all_gather(pair, "a", axis=0, tiled=False)
+
+        def heads_apart(x, axis):
+            mine = lax.dynamic_index_in_dim(x, member, axis, False)
+            return mine, lax.dynamic_index_in_dim(x, 1 - member, axis, False)
+
+        q, q_sent = heads_apart(q.reshape(-1, 2, PAIR), 1)
+        attention_result, out_sent = heads_apart(attention_result.reshape(-1, 2, PAIR), 1)
+        log_total, log_sent = heads_apart(log_total, 0)
+        q_other, out_other, log_other = (
+            lax.ppermute(x, "b", SWAP) for x in (q_sent, out_sent, log_sent)
+        )
+        cut = 2 * token_count
+        x_other = [lax.ppermute(x_span[:cut], "b", SWAP)]
+        home = jnp.stack([member * 2 + lax.axis_index("y"), lax.axis_index("c")])
+        experts_all, grad_hidden = place_experts(home, parts, early_all, width)
+        outs, experts_all, x_other[0], q_other, out_other, log_other = lax.optimization_barrier(
+            (outs, experts_all, x_other[0], q_other, out_other, log_other)
+        )
         normed_all, resid, attended_low = join(place, outs, first_all, qkv_width // width, x_span)
         normed_two = lax.dynamic_slice_in_dim(normed_all, group * token_count, token_count)
-        home = jnp.stack([member * 2 + lax.axis_index("y"), lax.axis_index("c")])
-        experts_all, grad_hidden = place_experts(home, parts, early_all, width)
     else:
         attended_low = (
             exchange(attended.reshape(KEY_VALUE_HEADS, token_count, PAIR), head_axes)
@@ -1066,20 +1107,33 @@
     back_part, gates_all, gated_hidden, grad_pre = experts(
         group.reshape(1), normed_all, early_all, first_all, experts_all, grad_hidden
     )
-    back_own = scatter_sum(back_part, "a").astype(f32)
+    if by_column:
+        q = in_row(q, q_other, columns + (PAIR,)).reshape(span, PAIR)
+        attention_result = in_row(attention_result, out_other, columns + (PAIR,)).reshape(span, PAIR)
+
+        def by_block(x):
+            x = x.reshape(-1, 2, QUERY_BLOCK // BLOCK, BLOCK).transpose(0, 2, 1, 3)
+            return x.reshape(GROUPS, 2, BLOCK)
+
+        log_total = in_row(by_block(log_total), by_block(log_other), (GROUPS, 2, BLOCK))
+        log_total = log_total.transpose(0, 2, 1, 3)
+    log_total = log_total.reshape(-1, 1, 2 * QUERY_BLOCK)
+    back_own = scatter_sum(back_part, "a")
     inputs = (normed_all, early_all, experts_all, gated_hidden, grad_pre)
-    if small_plane:
+    if by_column:
         core = lax.axis_index("c")
-        (send,) = expert_grads((1 - core).reshape(1), 2, *inputs, False)
-        arrived = lax.ppermute(send, "c", SWAP)
-        moe_part, keep = expert_grads(core.reshape(1), 2, *inputs, True)
+        x_other.append(lax.ppermute(x_span[cut:], "b", SWAP))
+        moe_part, *keep, send_left, send_right = expert_grads(core.reshape(1), 2, *inputs)
+        arrived = [lax.ppermute(x, "c", SWAP) for x in (send_left, send_right)]
         back_own, moe_part, keep = lax.optimization_barrier((back_own, moe_part, keep))
     else:
-        moe_part, grad_experts = expert_grads(jnp.zeros((1,), jnp.int32), 1, *inputs, True)
+        moe_part, *grads = expert_grads(jnp.zeros((1,), jnp.int32), 1, *inputs)
+        grad_experts = jnp.concatenate(grads, axis=2)
         back_own, moe_part, grad_experts = lax.optimization_barrier(
             (back_own, moe_part, grad_experts)
         )
         grad_experts = scatter_sum(grad_experts.reshape(EXPERTS_HERE * width, 3 * F), PLANE)
+    back_own = back_own.astype(f32)
     moe_sum = scatter_sum(moe_part, "a")
 
     grad_out = cotangent[0].astype(f32)
@@ -1097,39 +1151,44 @@
     grad_mixed = exchange(
         grad_heads.reshape(token_count, KEY_VALUE_HEADS, PAIR).transpose(1, 0, 2), head_axes
     ).reshape(span, PAIR)
-    if small_plane:
-        keep, arrived, grad_heads = lax.optimization_barrier((keep, arrived, grad_heads))
-        total = keep.astype(f32) + arrived.astype(f32)
-        total = total.astype(bf16).reshape((2, 2) + keep.shape[1:])
-        total, attended_low, grad_router = lax.optimization_barrier(
-            (total, attended_low, grad_router)
-        )
-        wide = 3 * F // 2
-        left, right = halve_send(total[..., :wide], "y", 1), halve_send(total[..., wide:], "b", 0)
+    if by_column:
+        keep, arrived, x_other, grad_heads = lax.optimization_barrier(
+            (keep, arrived, tuple(x_other), grad_heads)
+        )
+        x_other = jnp.concatenate(x_other)
+        left, right = (
+            halve_add(terms).reshape((2, 2) + terms[0].shape[1:]) for terms in zip(keep, arrived)
+        )
+        left, right = halve_send(left, "y", 1), halve_send(right, "b", 0)
     small = jnp.concatenate([grad_router, grad_gain_two[:, None]], axis=1)
     second_part = jnp.concatenate(
         [contract_rows(attended_low, grad_attn_low), pad_lanes(small, LANES)], axis=1
     ).astype(bf16)
     cols = second_part.shape[1]
     second_part = second_part.reshape(GROUPS, -1, own_rows, cols).transpose(1, 0, 2, 3)
-    second_part, grad_mixed = lax.optimization_barrier((second_part, grad_mixed))
+    if by_column:
+        left, right = halve_add(left), halve_add(right)
+        second_part, left, right, grad_mixed = lax.optimization_barrier(
+            (second_part, left, right, grad_mixed)
+        )
+        left, right = halve_send(left, "b", 0), halve_send(right, "y", 0)
     rest = scatter_sum(second_part.reshape(-1, cols), PLANE)
     grads = attend_back(
-        bounds, qkv, kv, kv_at, doc_rows, grad_mixed, attention_result, log_total,
-        wide_cos, wide_sin, whole_rows,
-    )
-    if whole_rows:
-        grad_pack = grads
+        bounds, q, kv, doc_rows, grad_mixed, attention_result, log_total, wide_cos, wide_sin,
+        by_column,
+    )
+    if by_column:
+        left, right, moe_sum, grad_pack = lax.optimization_barrier((left, right, moe_sum, grads))
+        first_part = head_grads(
+            x_span, x_other, member, 1 - member, 2, member, own_weights, grad_pack
+        )
     else:
         grad_kv = scatter_sum(grads[1].astype(bf16), "a").astype(f32)
         grad_pack = unrotate(grads[0], grad_kv, wide_cos, wide_sin)
-    if small_plane:
-        left, right, moe_sum, grad_pack = lax.optimization_barrier(
-            (left, right, moe_sum, grad_pack)
-        )
-        left, right = halve_add(left), halve_add(right)
-        left, right = halve_send(left, "b", 0), halve_send(right, "y", 0)
-    first_part = head_grads(x_span, normed_span, own_weights, grad_pack)
+        half = span // 2
+        first_part = head_grads(
+            x_span[:half], x_span[half:], zero, zero + half // BLOCK, 1, zero, own_weights, grad_pack
+        )
     rest, first_part = lax.optimization_barrier((rest, first_part))
     rest = scatter_sum(rest, "a")
     by_tokens = exchange(grad_pack.reshape(KEY_VALUE_HEADS, token_count, HEAD_PACK), head_axes)
@@ -1142,7 +1201,7 @@
     rest = rest.astype(f32)
     grad_input = token_grads(by_tokens, first_all, tokens[0], grad_resid)
     layer_sum = resid + RESIDUAL_SCALE * moe_sum.astype(f32)
-    if small_plane:
+    if by_column:
         grad_experts = jnp.concatenate(
             [own.astype(f32) + other.astype(f32) for own, other in (left, right)], axis=1
         )

time: 486 us -> 494 us (1.016)
  starting transfers between devices: 69.9 us -> 58.5 us
  local copies, waits for them, and re-layouts: 26.7 us -> 36.1 us
  waiting for transfers between devices: 152 us -> 161 us
  Pallas kernels: 160 us -> 153 us
    reduce_scatter x4, waiting for transfers between devices: 9.7 us -> 36.7 us  [scatter_sum(): return lax.psum_scatter(x, axes, scatter_dimension=0, tiled=True)]
    ppermute x4, waiting for transfers between devices: 37.4 us -> 20.5 us  [halve_send(): lax.ppermute(lax.dynamic_index_in_dim(v, 1 - me, at, False), axis, SWAP)]
    ppermute x15 -> x14, starting transfers between devices: 40.1 us -> 27 us  [the longest x3 15.6 us: line_gather(): up = lax.ppermute(up, axis, line_pairs(n, 1))]
    ppermute x15 -> x14, waiting for transfers between devices: 47.1 us -> 59.6 us  [the longest x3 20.2 us: line_gather(): down = lax.ppermute(down, axis, line_pairs(n, -1))]
    all_gather x2, waiting for transfers between devices: 0.01 us -> 10.4 us  [gather(): return lax.all_gather(x, axes, axis=0, tiled=True)]
    all_to_all x4, waiting for transfers between devices: 24.8 us -> 14.8 us  [exchange(): return lax.all_to_all(x, axes, 0, 0, tiled=True)]
    convert_element_type x2 -> x1, other arithmetic: 10.3 us -> 1.14 us  [body(): back_own = back_own.astype(f32)]
    ppermute x2, waiting for transfers between devices: 7.72 us -> 0.38 us  [neighbours(): return (lax.ppermute(x, 'y', SWAP), lax.ppermute(x, 'b', SWAP))]
  transfers between devices with their start and end apart: 42 -> 41, of which waited for: 20 -> 18; matrix products, arithmetic and copies ran while one was open for 15% -> 17% of each run, Pallas kernels for 25% -> 24%
where the time goes in v3:
time: 494 us; the launch traced here: 484 us
  waiting for transfers between devices  161 us (33%)
  Pallas kernels  153 us (31%)
  starting transfers between devices  58.5 us (12%)
  other arithmetic  51 us (10%)
  local copies, waits for them, and re-layouts  36.1 us (7%)
  between operations  15.4 us (3%)
  matrix products  9.46 us (2%)
    reduce_scatter x4, waiting for transfers between devices, scatter_sum(): return lax.psum_scatter(x, axes, scatter_dimension=0, tiled=True)  36.7 us
    pallas_call x1, Pallas kernels, experts(): pl.pallas_call(experts_kernel, grid_spec=pltpu.PrefetchScalarGridSpec(num...  29.1 us
    pallas_call x1, Pallas kernels, expert_grads(): pl.pallas_call(expert_grads_kernel, grid_spec=pltpu.PrefetchScalarGridSpe...  27.1 us
    pallas_call x1, Pallas kernels, attend_back(): pl.pallas_call(functools.partial(attend_back_kernel, fold), grid_spec=plt...  21.5 us
    ppermute x4, waiting for transfers between devices, halve_send(): lax.ppermute(lax.dynamic_index_in_dim(v, 1 - me, at, False), axis, SWAP)  20.5 us
    ppermute x3, waiting for transfers between devices, line_gather(): down = lax.ppermute(down, axis, line_pairs(n, -1))  20.2 us
    pallas_call x1, Pallas kernels, place_experts(): pl.pallas_call(place_experts_kernel, grid_spec=pltpu.PrefetchScalarGridSp...  18.5 us
    all_to_all x4, starting transfers between devices, exchange(): return lax.all_to_all(x, axes, 0, 0, tiled=True)  17.4 us
  transfers between devices with their start and end apart: 41, of which 18 were waited for; matrix products, arithmetic and copies ran while one was open for 17% of the time, Pallas kernels for 24%

profile of v3, /device:TPU:0, one launch (start us, length us, event | category | flops | bytes accessed | tf_op | source)
XLA Modules:
  0.0 484.1 jit_solution(13818595051047847281)
XLA Ops:
  14.4 5.8 %collective-permute-start = (bf16[256,1024]{1,0:T(8,128)(2,1)S(1)}, bf16[256,1024]{1,0:T(8,128)(2,1)}, u32[]{:S(2)}, u32[]{:S(2)}) collective-permute-start(bf16[256,1024]{1,0:T(8,128)(2,1)S(1)} %bitcast.114), channel_id=1, source_target_pairs={{0,8},{8,16},{16,24},{1,9},{9,17},{17,25},{2,10},{10,18},{18,26},{... | collective-permute-start | bytes 1572872 | tf_op jit(solution)/shard_map/ppermute | solution.py:96
  22.4 6.9 %all-to-all-start = ((bf16[8,32,640]{2,1,0:T(8,128)(2,1)}), bf16[8,32,640]{2,1,0:T(8,128)(2,1)}, u32[]{:S(2)}, u32[]{:S(2)}) async-start(bf16[8,32,640]{2,1,0:T(8,128)(2,1)} %bitcast.7), calls=%async_computation | async-start | bytes 655360 | tf_op jit(solution)/shard_map/all_to_all | solution.py:916
  30.5 1.8 convert_reduce_fusion
  32.3 5.5 %multiply_sine_fusion = (f32[2048,32]{1,0:T(8,128)}, f32[2048,32]{1,0:T(8,128)}) fusion(f32[2048]{0:T(1024)S(1)} %subtract_convert_fusion, f32[32]{0:T(128)S(1)} %multiply_power_fusion), kind=kLoop, calls=%fused_computation.19 | loop fusion | flops 65536 | bytes 532608 | tf_op jit(solution)/shard_map/sin | solution.py:44
  38.7 4.7 collective-permute-start.2
  45.3 2.1 all-to-all-done.refs_7_
  49.3 12.9 %collective-permute-done.2.refs_3_ = bf16[256,1024]{1,0:T(8,128)(2,1)} collective-permute-done((bf16[256,1024]{1,0:T(8,128)(2,1)}, bf16[256,1024]{1,0:T(8,128)(2,1)}, u32[]{:S(2)}, u32[]{:S(2)}) %collective-permute-start.2) | collective-permute-done | bytes 524320 | tf_op jit(solution)/shard_map/ppermute | solution.py:96
  62.2 5.2 %collective-permute-start.4 = (bf16[256,1024]{1,0:T(8,128)(2,1)}, bf16[256,1024]{1,0:T(8,128)(2,1)}, u32[]{:S(2)}, u32[]{:S(2)}) collective-permute-start(bf16[256,1024]{1,0:T(8,128)(2,1)} %collective-permute-done.2.refs_3_), channel_id=1, source_target_pairs={{0,8},{8,16},{16,24},{1,9},{9,17},{17,25},{2,10},{10,18},{18,26},{... | collective-permute-start | bytes 1572872 | tf_op jit(solution)/shard_map/ppermute | solution.py:96
  68.7 2.7 dynamic-slice_sine_fusion
  73.6 4.5 spread.1
  79.6 20.2 %collective-permute-done.5.refs_6_ = bf16[256,1024]{1,0:T(8,128)(2,1)} collective-permute-done((bf16[256,1024]{1,0:T(8,128)(2,1)}, bf16[256,1024]{1,0:T(8,128)(2,1)}, u32[]{:S(2)}, u32[]{:S(2)}) %collective-permute-start.5) | collective-permute-done | bytes 524320 | tf_op jit(solution)/shard_map/ppermute | solution.py:97
  99.8 7.8 %project.1 = (bf16[1024,256]{1,0:T(8,128)(2,1)}, bf16[1024,256]{1,0:T(8,128)(2,1)}, bf16[1024,1024]{1,0:T(8,128)(2,1)}, bf16[8,4,32,640]{3,2,1,0:T(8,128)(2,1)}) custom-call(s32[4]{0:T(128)} %pad_add_fusion.place_ref, bf16[256,1024]{1,0:T(8,128)(2,1)} %bitcast.112, bf16[256,1024]{1,0:T(8,128)(2,1)} %collective-permute-done.refs_1_, ...), custom_call_target="tpu_custom_call" | custom-call | flops 1073741824 | bytes 8388608 | tf_op jit(solution)/shard_map/project/pallas_call | solution.py:215
  111.2 11.5 %collective-permute-done.9 = bf16[1024,256]{1,0:T(8,128)(2,1)S(1)} collective-permute-done((bf16[1024,256]{1,0:T(8,128)(2,1)}, bf16[1024,256]{1,0:T(8,128)(2,1)S(1)}, u32[]{:S(2)}, u32[]{:S(2)}) %collective-permute-start.9) | collective-permute-done | bytes 524320 | tf_op jit(solution)/shard_map/ppermute | solution.py:1058
  124.9 15.5 %attend.1 = (f32[1024,256]{1,0:T(8,128)}, bf16[1024,256]{1,0:T(8,128)(2,1)}, f32[2,2,1,1024]{3,2,1,0:T(1,128)}) custom-call(s32[5]{0:T(128)} %pad_add_fusion.1.bounds_ref, bf16[1024,256]{1,0:T(8,128)(2,1)} %get-tuple-element.109.q_ref, bf16[2048,256]{1,0:T(8,128)(2,1)} %bitcast.125, s32[2,1,512]{2,1,0:T(1,128)} %bitcast.141), custom_call_target="tpu_custom_call" | custom-call | flops 2147483648 | bytes 6291456 | tf_op jit(solution)/shard_map/attend/pallas_call | solution.py:406
  140.5 10.4 %all-gather.7.cloned.1.call-done.refs_10_.routed_ref.ct_ref = bf16[1024,1152]{1,0:T(8,128)(2,1)} async-done(((bf16[256,1152]{1,0:T(8,128)(2,1)}), bf16[1024,1152]{1,0:T(8,128)(2,1)}) %all-gather.7.cloned.1.call-update) | async-done | bytes 2359312 | tf_op jit(solution)/shard_map/all_gather | solution.py:76
  153.2 1.9 collective-permute-start.15
  157.5 15.1 %collective-permute-done.15.refs_6_ = bf16[256,1536]{1,0:T(8,128)(2,1)} collective-permute-done((bf16[256,1536]{1,0:T(8,128)(2,1)S(1)}, bf16[256,1536]{1,0:T(8,128)(2,1)}, u32[]{:S(2)}, u32[]{:S(2)}) %collective-permute-start.15) | collective-permute-done | bytes 786464 | tf_op jit(solution)/shard_map/ppermute | solution.py:113
  172.6 2.4 collective-permute-done.17.refs_8_
  181.9 1.9 constant_dynamic-slice_fusion.1
  186.0 18.5 %place_experts.1 = (bf16[4,1024,1536]{2,1,0:T(8,128)(2,1)}, f32[4,1024,512]{2,1,0:T(8,128)}) custom-call(s32[2]{0:T(128)} %pad_add_fusion.2.place_ref, bf16[512,1536]{1,0:T(8,128)(2,1)} %pad_maximum_fusion.3.refs_0_, bf16[512,1536]{1,0:T(8,128)(2,1)} %collective-permute-done.10.refs_1_, bf16[512,1536]{1,0:T(8,128)(2,1)} %collective-permute-done.11.refs_2_, ...), custom_call_target="tpu_custom_call" | custom-call | flops 4294967296 | bytes 37748736 | tf_op jit(solution)/shard_map/place_experts/pallas_call | solution.py:601
  204.5 14.7 %collective-permute-done.20 = bf16[1024,128]{1,0:T(8,128)(2,1)S(1)} collective-permute-done((bf16[1024,128]{1,0:T(8,128)(2,1)S(1)}, bf16[1024,128]{1,0:T(8,128)(2,1)S(1)}, u32[]{:S(2)}, u32[]{:S(2)}) %collective-permute-start.20) | collective-permute-done | bytes 262176 | tf_op jit(solution)/shard_map/ppermute | solution.py:1079
  219.3 8.2 %join.1 = (bf16[1024,1024]{1,0:T(8,128)(2,1)}, f32[256,1024]{1,0:T(8,128)}, bf16[256,1024]{1,0:T(8,128)(2,1)}) custom-call(s32[4]{0:T(128)} %pad_add_fusion.place_ref, bf16[4,1024,256]{2,1,0:T(8,128)(2,1)} %bitcast.111, bf16[1024,3200]{1,0:T(8,128)(2,1)} %all-gather.5.cloned.1.call-done.w_ref.small_ref.router_ref, ...), custom_call_target="tpu_custom_call" | custom-call | flops 2147483648 | bytes 12582912 | tf_op jit(solution)/shard_map/join/pallas_call | solution.py:803
  227.6 29.1 %experts.1 = (bf16[1024,1152]{1,0:T(8,128)(2,1)}, f32[1024,128]{1,0:T(8,128)}, bf16[4,1024,512]{2,1,0:T(8,128)(2,1)}, bf16[4,1024,1024]{2,1,0:T(8,128)(2,1)}) custom-call(s32[1]{0:T(128)} %bitcast.group_ref, bf16[1024,1024]{1,0:T(8,128)(2,1)} %get-tuple-element.125.n_ref, bf16[1024,1152]{1,0:T(8,128)(2,1)} %all-gather.7.cloned.1.call-done.refs_10_.routed_ref.ct_ref, ...), custom_call_target="tpu_custom_call" | custom-call | flops 17179869184 | bytes 41943040 | tf_op jit(solution)/shard_map/experts/pallas_call | solution.py:683
  257.0 27.1 %expert_grads.1 = (bf16[1024,1024]{1,0:T(8,128)(2,1)}, bf16[4,512,768]{2,1,0:T(8,128)(2,1)}, bf16[4,512,768]{2,1,0:T(8,128)(2,1)}, bf16[4,512,768]{2,1,0:T(8,128)(2,1)}, bf16[4,512,768]{2,1,0:T(8,128)(2,1)}) custom-call(s32[1]{0:T(128)} %bitcast.3.half_ref, bf16[1024,1024]{1,0:T(8,128)(2,1)} %get-tuple-element.125.n_ref, ...), custom_call_target="tpu_custom_call" | custom-call | flops 17179869184 | bytes 41943040 | tf_op jit(solution)/shard_map/expert_grads/pallas_call | solution.py:749
  287.6 15.1 %reduce-scatter.5.cloned.1.call-done = bf16[256,1152]{1,0:T(8,128)(2,1)} async-done(((bf16[1024,1152]{1,0:T(8,128)(2,1)}), bf16[256,1152]{1,0:T(8,128)(2,1)}) %reduce-scatter.5.cloned.1.call-update) | async-done | bytes 589840 | tf_op jit(solution)/shard_map/reduce_scatter | solution.py:80
  306.1 2.4 multiply_reduce_fusion.1
  308.8 3.9 fusion.4
  312.7 2.7 add_convert_fusion
  319.1 2.8 add_convert_fusion.1
  321.9 1.7 copy-done.4
  329.1 1.9 bitcast_bitcast_fusion
  331.0 4.1 all-to-all-start.1
  335.5 1.8 convolution_convert_fusion
  337.3 1.8 copy_bitcast_fusion
  339.1 18.6 %collective-permute-done.27 = bf16[2,512,768]{2,1,0:T(8,128)(2,1)} collective-permute-done((bf16[2,512,768]{2,1,0:T(8,128)(2,1)}, bf16[2,512,768]{2,1,0:T(8,128)(2,1)}, u32[]{:S(2)}, u32[]{:S(2)}) %collective-permute-start.27) | collective-permute-done | bytes 1572896 | tf_op jit(solution)/shard_map/ppermute | solution.py:120
  357.7 1.8 fusion
  360.8 3.0 fusion.1
  368.0 2.8 dynamic-slice_bitcast_fusion.4
  375.6 21.5 %attend_back.1.grad_ref = bf16[2048,256]{1,0:T(8,128)(2,1)} custom-call(s32[10]{0:T(128)} %pad_add_fusion.3.bounds_ref, bf16[2048,128]{1,0:T(8,128)(2,1)} %bitcast.130, bf16[2048,256]{1,0:T(8,128)(2,1)} %bitcast.126, s32[4,1,512]{2,1,0:T(1,128)} %bitcast.136, bf16[2048,128]{1,0:T(8,128)(2,1)} %bitcast.34.do_ref, f32[2048,128]{1,0:T(8,128)} %bitcast.127, ...), custom_call_target="tpu_custom_call" | custom-call | flops 5368709120 | bytes 8388608 | tf_op jit(solution)/shard_map/attend_back/pallas_call | solution.py:526
  398.6 3.8 all-to-all-start.2
  403.0 3.1 pad_maximum_fusion.2.other_ref
  406.1 10.1 %head_grads.1 = bf16[1024,384]{1,0:T(8,128)(2,1)} custom-call(s32[3]{0:T(128)} %pad_add_fusion.4.place_ref, bf16[1024,1024]{1,0:T(8,128)(2,1)} %get-tuple-element.118.x_ref.own_ref, bf16[1024,1024]{1,0:T(8,128)(2,1)} %pad_maximum_fusion.2.other_ref, bf16[1024,640]{1,0:T(8,128)(2,1)} %bitcast.106, bf16[1024,640]{1,0:T(8,128)(2,1)} %bitcast.107, ...), custom_call_target="tpu_custom_call" | custom-call | flops 2147483648 | bytes 8388608 | tf_op jit(solution)/shard_map/head_grads/pallas_call | solution.py:304
  417.3 12.7 %all-to-all-done.2.grad_ref = bf16[8,256,256]{2,1,0:T(8,128)(2,1)S(1)} async-done(((bf16[8,256,256]{2,1,0:T(8,128)(2,1)}), bf16[8,256,256]{2,1,0:T(8,128)(2,1)S(1)}, u32[]{:S(2)}, u32[]{:S(2)}) %all-to-all-start.2) | async-done | bytes 1048608 | tf_op jit(solution)/shard_map/all_to_all | solution.py:916
  430.0 2.6 all-to-all-start.3
  433.4 1.6 convert_add_fusion.2
  437.9 20.5 %reduce-scatter.11.cloned.1.call-done = bf16[32,1152]{1,0:T(8,128)(2,1)} async-done(((bf16[128,1152]{1,0:T(8,128)(2,1)}), bf16[32,1152]{1,0:T(8,128)(2,1)}) %reduce-scatter.11.cloned.1.call-update) | async-done | bytes 73744 | tf_op jit(solution)/shard_map/reduce_scatter | solution.py:80
  462.9 8.8 %token_grads.1 = f32[256,1024]{1,0:T(8,128)} custom-call(bf16[8,256,256]{2,1,0:T(8,128)(2,1)} %copy-done.7, bf16[1024,3200]{1,0:T(8,128)(2,1)} %all-gather.5.cloned.1.call-done.w_ref.small_ref.router_ref, bf16[1024,3200]{1,0:T(8,128)(2,1)} %all-gather.5.cloned.1.call-done.w_ref.small_ref.router_ref, bf16[256,1024]{1,0:T(8,128)(2,1)} %bitcast.113, ...), custom_call_target="tpu_custom_call" | custom-call | flops 1073741824 | bytes 8388608 | tf_op jit(solution)/shard_map/token_grads/pallas_call | solution.py:857
  472.6 1.9 weight_sums.1
  (231 shorter events, 81.2 us)
Async XLA Ops:
  7.2 133.3 %all-gather.5.cloned.1.call-start = ((), (), s32[]{:S(2)}) async-start(), calls=%async_computation.8 | async-start | bytes 6758400 | tf_op jit(solution)/shard_map/all_gather | solution.py:76
  14.4 24.3 %collective-permute-start = (bf16[256,1024]{1,0:T(8,128)(2,1)S(1)}, bf16[256,1024]{1,0:T(8,128)(2,1)}, u32[]{:S(2)}, u32[]{:S(2)}) collective-permute-start(bf16[256,1024]{1,0:T(8,128)(2,1)S(1)} %bitcast.114), channel_id=1, source_target_pairs={{0,8},{8,16},{16,24},{1,9},{9,17},{17,25},{2,10},{10,18},{18,26},{... | collective-permute-start | bytes 1572872 | tf_op jit(solution)/shard_map/ppermute | solution.py:96
  20.2 23.2 %collective-permute-start.1 = (bf16[256,1024]{1,0:T(8,128)(2,1)S(1)}, bf16[256,1024]{1,0:T(8,128)(2,1)}, u32[]{:S(2)}, u32[]{:S(2)}) collective-permute-start(bf16[256,1024]{1,0:T(8,128)(2,1)S(1)} %bitcast.115), channel_id=1, source_target_pairs={{8,0},{16,8},{24,16},{9,1},{17,9},{25,17},{10,2},{18,10},{26,18},{... | collective-permute-start | bytes 1572872 | tf_op jit(solution)/shard_map/ppermute | solution.py:97
  22.4 25.0 %all-to-all-start = ((bf16[8,32,640]{2,1,0:T(8,128)(2,1)}), bf16[8,32,640]{2,1,0:T(8,128)(2,1)}, u32[]{:S(2)}, u32[]{:S(2)}) async-start(bf16[8,32,640]{2,1,0:T(8,128)(2,1)} %bitcast.7), calls=%async_computation | async-start | bytes 655360 | tf_op jit(solution)/shard_map/all_to_all | solution.py:916
  29.3 121.5 %all-gather.7.cloned.1.call-start = ((), (), s32[]{:S(2)}) async-start(), calls=%async_computation.9 | async-start | bytes 2949120 | tf_op jit(solution)/shard_map/all_gather | solution.py:76
  30.4 188.9 %all-gather.9.cloned.1.call-start = ((), (), s32[]{:S(2)}) async-start(), calls=%async_computation.14 | async-start | bytes 2621440 | tf_op jit(solution)/shard_map/all_gather | solution.py:1068
  32.3 252.3 %copy-start.26 = (s32[2048]{0:T(1024)}, s32[2048]{0:T(1024)S(1)}, u32[]{:S(2)}) copy-start(s32[2048]{0:T(1024)S(1)} %convert_reduce_fusion) | copy-start | bytes 24580
  32.3 40.2 %copy-start.18 = (f32[512,512]{1,0:T(8,128)S(1)}, f32[512,512]{1,0:T(8,128)}, u32[]{:S(2)}) copy-start(f32[512,512]{1,0:T(8,128)} %param.25) | copy-start | bytes 3145732
  38.7 23.5 %collective-permute-start.2 = (bf16[256,1024]{1,0:T(8,128)(2,1)}, bf16[256,1024]{1,0:T(8,128)(2,1)}, u32[]{:S(2)}, u32[]{:S(2)}) collective-permute-start(bf16[256,1024]{1,0:T(8,128)(2,1)} %collective-permute-done.refs_1_), channel_id=1, source_target_pairs={{0,8},{8,16},{16,24},{1,9},{9,17},{17,25},{2,10},{10,18},{18,26},{... | collective-permute-start | bytes 1572872 | tf_op jit(solution)/shard_map/ppermute | solution.py:96
  43.4 24.0 %collective-permute-start.3 = (bf16[256,1024]{1,0:T(8,128)(2,1)}, bf16[256,1024]{1,0:T(8,128)(2,1)}, u32[]{:S(2)}, u32[]{:S(2)}) collective-permute-start(bf16[256,1024]{1,0:T(8,128)(2,1)} %collective-permute-done.1.refs_2_), channel_id=1, source_target_pairs={{8,0},{16,8},{24,16},{9,1},{17,9},{25,17},{10,2},{18,10},{26,18},{... | collective-permute-start | bytes 1572872 | tf_op jit(solution)/shard_map/ppermute | solution.py:97
  45.3 28.1 %copy-start.13 = (f32[512,1024]{1,0:T(8,128)S(1)}, f32[512,1024]{1,0:T(8,128)}, u32[]{:S(2)}) copy-start(f32[512,1024]{1,0:T(8,128)} %param.24) | copy-start | bytes 6291460
  47.4 24.0 %collective-permute-start.7 = (bf16[8,32,640]{2,1,0:T(8,128)(2,1)}, bf16[8,32,640]{2,1,0:T(8,128)(2,1)S(1)}, u32[]{:S(2)}, u32[]{:S(2)}) collective-permute-start(bf16[8,32,640]{2,1,0:T(8,128)(2,1)} %all-to-all-done.refs_7_), channel_id=1, source_target_pairs={{0,2},{2,0},{1,3},{3,1},{4,6},{6,4},{5,7},{7,5},{8,10},{10,8},{9,1... | collective-permute-start | bytes 983048 | tf_op jit(solution)/shard_map/ppermute | solution.py:1006
  62.2 17.4 %collective-permute-start.4 = (bf16[256,1024]{1,0:T(8,128)(2,1)}, bf16[256,1024]{1,0:T(8,128)(2,1)}, u32[]{:S(2)}, u32[]{:S(2)}) collective-permute-start(bf16[256,1024]{1,0:T(8,128)(2,1)} %collective-permute-done.2.refs_3_), channel_id=1, source_target_pairs={{0,8},{8,16},{16,24},{1,9},{9,17},{17,25},{2,10},{10,18},{18,26},{... | collective-permute-start | bytes 1572872 | tf_op jit(solution)/shard_map/ppermute | solution.py:96
  67.4 32.4 %collective-permute-start.5 = (bf16[256,1024]{1,0:T(8,128)(2,1)}, bf16[256,1024]{1,0:T(8,128)(2,1)}, u32[]{:S(2)}, u32[]{:S(2)}) collective-permute-start(bf16[256,1024]{1,0:T(8,128)(2,1)} %collective-permute-done.3.refs_4_), channel_id=1, source_target_pairs={{8,0},{16,8},{24,16},{9,1},{17,9},{25,17},{10,2},{18,10},{26,18},{... | collective-permute-start | bytes 1572872 | tf_op jit(solution)/shard_map/ppermute | solution.py:97
  71.4 8.1 %collective-permute-start.6 = (bf16[8,32,640]{2,1,0:T(8,128)(2,1)}, bf16[8,32,640]{2,1,0:T(8,128)(2,1)}, u32[]{:S(2)}, u32[]{:S(2)}) collective-permute-start(bf16[8,32,640]{2,1,0:T(8,128)(2,1)} %all-to-all-done.refs_7_), channel_id=1, source_target_pairs={{0,1},{1,0},{2,3},{3,2},{4,5},{5,4},{6,7},{7,6},{8,9},{9,8},{10,11... | collective-permute-start | bytes 983048 | tf_op jit(solution)/shard_map/ppermute | solution.py:1009
  71.4 8.1 %collective-permute-start.8 = (bf16[8,32,640]{2,1,0:T(8,128)(2,1)S(1)}, bf16[8,32,640]{2,1,0:T(8,128)(2,1)}, u32[]{:S(2)}, u32[]{:S(2)}) collective-permute-start(bf16[8,32,640]{2,1,0:T(8,128)(2,1)S(1)} %collective-permute-done.7.refs_9_), channel_id=1, source_target_pairs={{0,1},{1,0},{2,3},{3,2},{4,5},{5,4},{6,7},{7,6},{8,9},{9,8},{10,11... | collective-permute-start | bytes 983048 | tf_op jit(solution)/shard_map/ppermute | solution.py:1009
  107.6 15.1 %collective-permute-start.9 = (bf16[1024,256]{1,0:T(8,128)(2,1)}, bf16[1024,256]{1,0:T(8,128)(2,1)S(1)}, u32[]{:S(2)}, u32[]{:S(2)}) collective-permute-start(bf16[1024,256]{1,0:T(8,128)(2,1)} %get-tuple-element.110), channel_id=1, source_target_pairs={{0,4},{4,0},{1,5},{5,1},{2,6},{6,2},{3,7},{7,3},{8,12},{12,8},{9,1... | collective-permute-start | bytes 1572872 | tf_op jit(solution)/shard_map/ppermute | solution.py:1058
  109.0 42.1 %collective-permute-start.11 = (bf16[512,1536]{1,0:T(8,128)(2,1)}, bf16[512,1536]{1,0:T(8,128)(2,1)}, u32[]{:S(2)}, u32[]{:S(2)}) collective-permute-start(bf16[512,1536]{1,0:T(8,128)(2,1)} %pad_maximum_fusion.3.refs_0_), channel_id=1, source_target_pairs={{0,2},{2,0},{1,3},{3,1},{4,6},{6,4},{5,7},{7,5},{8,10},{10,8},{9,1... | collective-permute-start | bytes 4718600 | tf_op jit(solution)/shard_map/ppermute | solution.py:108
  110.6 41.4 %collective-permute-start.13 = (bf16[512,1536]{1,0:T(8,128)(2,1)}, bf16[512,1536]{1,0:T(8,128)(2,1)}, u32[]{:S(2)}, u32[]{:S(2)}) collective-permute-start(bf16[512,1536]{1,0:T(8,128)(2,1)} %pad_maximum_fusion.3.refs_0_), channel_id=1, source_target_pairs={{0,4},{4,0},{1,5},{5,1},{2,6},{6,2},{3,7},{7,3},{8,12},{12,8},{9,1... | collective-permute-start | bytes 4718600 | tf_op jit(solution)/shard_map/ppermute | solution.py:108
  140.4 34.6 %copy-start = (bf16[1024,1024]{1,0:T(8,128)(2,1)S(1)}, bf16[1024,1024]{1,0:T(8,128)(2,1)}, u32[]{:S(2)}) copy-start(bf16[1024,1024]{1,0:T(8,128)(2,1)} %get-tuple-element.118.x_ref.own_ref) | copy-start | bytes 6291460
  150.9 151.8 %reduce-scatter.5.cloned.1.call-start = ((), (), s32[]{:S(2)}) async-start(), calls=%async_computation.10 | async-start | bytes 2949120 | tf_op jit(solution)/shard_map/reduce_scatter | solution.py:80
  151.1 25.4 %collective-permute-start.10 = (bf16[512,1536]{1,0:T(8,128)(2,1)}, bf16[512,1536]{1,0:T(8,128)(2,1)}, u32[]{:S(2)}, u32[]{:S(2)}) collective-permute-start(bf16[512,1536]{1,0:T(8,128)(2,1)} %pad_maximum_fusion.3.refs_0_), channel_id=1, source_target_pairs={{0,1},{1,0},{2,3},{3,2},{4,5},{5,4},{6,7},{7,6},{8,9},{9,8},{10,11... | collective-permute-start | bytes 4718600 | tf_op jit(solution)/shard_map/ppermute | solution.py:115
  151.2 30.1 %collective-permute-start.12 = (bf16[512,1536]{1,0:T(8,128)(2,1)}, bf16[512,1536]{1,0:T(8,128)(2,1)}, u32[]{:S(2)}, u32[]{:S(2)}) collective-permute-start(bf16[512,1536]{1,0:T(8,128)(2,1)} %collective-permute-done.11.refs_2_), channel_id=1, source_target_pairs={{0,1},{1,0},{2,3},{3,2},{4,5},{5,4},{6,7},{7,6},{8,9},{9,8},{10,11... | collective-permute-start | bytes 4718600 | tf_op jit(solution)/shard_map/ppermute | solution.py:115
  153.2 19.3 %collective-permute-start.15 = (bf16[256,1536]{1,0:T(8,128)(2,1)S(1)}, bf16[256,1536]{1,0:T(8,128)(2,1)}, u32[]{:S(2)}, u32[]{:S(2)}) collective-permute-start(bf16[256,1536]{1,0:T(8,128)(2,1)S(1)} %slice.86), channel_id=1, source_target_pairs={{0,2},{2,0},{1,3},{3,1},{4,6},{6,4},{5,7},{7,5},{8,10},{10,8},{9,1... | collective-permute-start | bytes 2359304 | tf_op jit(solution)/shard_map/ppermute | solution.py:113
  156.3 18.7 %collective-permute-start.17 = (bf16[256,1536]{1,0:T(8,128)(2,1)S(1)}, bf16[256,1536]{1,0:T(8,128)(2,1)}, u32[]{:S(2)}, u32[]{:S(2)}) collective-permute-start(bf16[256,1536]{1,0:T(8,128)(2,1)S(1)} %slice.87), channel_id=1, source_target_pairs={{0,4},{4,0},{1,5},{5,1},{2,6},{6,2},{3,7},{7,3},{8,12},{12,8},{9,1... | collective-permute-start | bytes 2359304 | tf_op jit(solution)/shard_map/ppermute | solution.py:114
  157.5 26.5 %collective-permute-start.14 = (bf16[512,1536]{1,0:T(8,128)(2,1)}, bf16[512,1536]{1,0:T(8,128)(2,1)}, u32[]{:S(2)}, u32[]{:S(2)}) collective-permute-start(bf16[512,1536]{1,0:T(8,128)(2,1)} %collective-permute-done.13.refs_4_), channel_id=1, source_target_pairs={{0,1},{1,0},{2,3},{3,2},{4,5},{5,4},{6,7},{7,6},{8,9},{9,8},{10,11... | collective-permute-start | bytes 4718600 | tf_op jit(solution)/shard_map/ppermute | solution.py:115
  172.5 12.9 %collective-permute-start.16 = (bf16[256,1536]{1,0:T(8,128)(2,1)}, bf16[256,1536]{1,0:T(8,128)(2,1)}, u32[]{:S(2)}, u32[]{:S(2)}) collective-permute-start(bf16[256,1536]{1,0:T(8,128)(2,1)} %collective-permute-done.15.refs_6_), channel_id=1, source_target_pairs={{0,1},{1,0},{2,3},{3,2},{4,5},{5,4},{6,7},{7,6},{8,9},{9,8},{10,11... | collective-permute-start | bytes 2359304 | tf_op jit(solution)/shard_map/ppermute | solution.py:115
  175.0 11.0 %collective-permute-start.18 = (bf16[256,1536]{1,0:T(8,128)(2,1)}, bf16[256,1536]{1,0:T(8,128)(2,1)}, u32[]{:S(2)}, u32[]{:S(2)}) collective-permute-start(bf16[256,1536]{1,0:T(8,128)(2,1)} %collective-permute-done.17.refs_8_), channel_id=1, source_target_pairs={{0,1},{1,0},{2,3},{3,2},{4,5},{5,4},{6,7},{7,6},{8,9},{9,8},{10,11... | collective-permute-start | bytes 2359304 | tf_op jit(solution)/shard_map/ppermute | solution.py:115
  176.5 42.8 %collective-permute-start.19 = (bf16[512,1024]{1,0:T(8,128)(2,1)}, bf16[512,1024]{1,0:T(8,128)(2,1)}, u32[]{:S(2)}, u32[]{:S(2)}) collective-permute-start(bf16[512,1024]{1,0:T(8,128)(2,1)} %get-tuple-element.239), channel_id=1, source_target_pairs={{0,4},{4,0},{1,5},{5,1},{2,6},{6,2},{3,7},{7,3},{8,12},{12,8},{9,1... | collective-permute-start | bytes 3145736 | tf_op jit(solution)/shard_map/ppermute | solution.py:1082
  181.3 38.0 %collective-permute-start.21 = (f32[1024,128]{1,0:T(8,128)S(1)}, f32[1024,128]{1,0:T(8,128)}, u32[]{:S(2)}, u32[]{:S(2)}) collective-permute-start(f32[1024,128]{1,0:T(8,128)S(1)} %bitcast.132), channel_id=1, source_target_pairs={{0,4},{4,0},{1,5},{5,1},{2,6},{6,2},{3,7},{7,3},{8,12},{12,8},{9,1... | collective-permute-start | bytes 1572872 | tf_op jit(solution)/shard_map/ppermute | solution.py:1079
  183.9 35.3 %collective-permute-start.20 = (bf16[1024,128]{1,0:T(8,128)(2,1)S(1)}, bf16[1024,128]{1,0:T(8,128)(2,1)S(1)}, u32[]{:S(2)}, u32[]{:S(2)}) collective-permute-start(bf16[1024,128]{1,0:T(8,128)(2,1)S(1)} %bitcast.133), channel_id=1, source_target_pairs={{0,4},{4,0},{1,5},{5,1},{2,6},{6,2},{3,7},{7,3},{8,12},{12,8},{9,1... | collective-permute-start | bytes 786440 | tf_op jit(solution)/shard_map/ppermute | solution.py:1079
  185.5 33.8 %collective-permute-start.22 = (f32[2,1,1024]{2,0,1:T(2,128)S(1)}, f32[2,1,1024]{2,0,1:T(2,128)S(1)}, u32[]{:S(2)}, u32[]{:S(2)}) collective-permute-start(f32[2,1,1024]{2,0,1:T(2,128)S(1)} %bitcast.140), channel_id=1, source_target_pairs={{0,4},{4,0},{1,5},{5,1},{2,6},{6,2},{3,7},{7,3},{8,12},{12,8},{9,1... | collective-permute-start | bytes 24584 | tf_op jit(solution)/shard_map/ppermute | solution.py:1079
  256.7 141.1 %reduce-scatter.7.cloned.1.call-start = ((), (), s32[]{:S(2)}) async-start(), calls=%async_computation.11 | async-start | bytes 2621440 | tf_op jit(solution)/shard_map/reduce_scatter | solution.py:80
  256.9 30.4 %copy-start.1 = (f32[256,1024]{1,0:T(8,128)S(1)}, f32[256,1024]{1,0:T(8,128)}, u32[]{:S(2)}) copy-start(f32[256,1024]{1,0:T(8,128)} %get-tuple-element.162) | copy-start | bytes 3145732
  284.1 28.6 %collective-permute-start.23 = (bf16[4,512,768]{2,1,0:T(8,128)(2,1)}, bf16[4,512,768]{2,1,0:T(8,128)(2,1)}, u32[]{:S(2)}, u32[]{:S(2)}) collective-permute-start(bf16[4,512,768]{2,1,0:T(8,128)(2,1)} %get-tuple-element.138), channel_id=1, source_target_pairs={{0,1},{1,0},{2,3},{3,2},{4,5},{5,4},{6,7},{7,6},{8,9},{9,8},{10,11... | collective-permute-start | bytes 9437192 | tf_op jit(solution)/shard_map/ppermute | solution.py:1127
  284.1 28.6 %collective-permute-start.24 = (bf16[4,512,768]{2,1,0:T(8,128)(2,1)}, bf16[4,512,768]{2,1,0:T(8,128)(2,1)}, u32[]{:S(2)}, u32[]{:S(2)}) collective-permute-start(bf16[4,512,768]{2,1,0:T(8,128)(2,1)} %get-tuple-element.139), channel_id=1, source_target_pairs={{0,1},{1,0},{2,3},{3,2},{4,5},{5,4},{6,7},{7,6},{8,9},{9,8},{10,11... | collective-permute-start | bytes 9437192 | tf_op jit(solution)/shard_map/ppermute | solution.py:1127
  284.8 27.9 %collective-permute-start.25 = (bf16[512,1024]{1,0:T(8,128)(2,1)}, bf16[512,1024]{1,0:T(8,128)(2,1)}, u32[]{:S(2)}, u32[]{:S(2)}) collective-permute-start(bf16[512,1024]{1,0:T(8,128)(2,1)} %get-tuple-element.238), channel_id=1, source_target_pairs={{0,4},{4,0},{1,5},{5,1},{2,6},{6,2},{3,7},{7,3},{8,12},{12,8},{9,1... | collective-permute-start | bytes 3145736 | tf_op jit(solution)/shard_map/ppermute | solution.py:1125
  308.8 26.7 %copy-start.6 = (f32[256,1024]{1,0:T(8,128)}, f32[256,1024]{1,0:T(8,128)S(1)}, u32[]{:S(2)}) copy-start(f32[256,1024]{1,0:T(8,128)S(1)} %subtract_add_fusion.resid_ref) | copy-start | bytes 3145732
  316.8 40.9 %collective-permute-start.27 = (bf16[2,512,768]{2,1,0:T(8,128)(2,1)}, bf16[2,512,768]{2,1,0:T(8,128)(2,1)}, u32[]{:S(2)}, u32[]{:S(2)}) collective-permute-start(bf16[2,512,768]{2,1,0:T(8,128)(2,1)} %dynamic-slice_bitcast_fusion), channel_id=1, source_target_pairs={{0,4},{4,0},{1,5},{5,1},{2,6},{6,2},{3,7},{7,3},{8,12},{12,8},{9,1... | collective-permute-start | bytes 4718600 | tf_op jit(solution)/shard_map/ppermute | solution.py:120
  324.8 36.0 %collective-permute-start.26 = (bf16[2,512,768]{2,1,0:T(8,128)(2,1)}, bf16[2,512,768]{2,1,0:T(8,128)(2,1)}, u32[]{:S(2)}, u32[]{:S(2)}) collective-permute-start(bf16[2,512,768]{2,1,0:T(8,128)(2,1)} %dynamic-slice_bitcast_fusion.1), channel_id=1, source_target_pairs={{0,2},{2,0},{1,3},{3,1},{4,6},{6,4},{5,7},{7,5},{8,10},{10,8},{9,1... | collective-permute-start | bytes 4718600 | tf_op jit(solution)/shard_map/ppermute | solution.py:120
  331.0 32.8 %all-to-all-start.1 = ((bf16[8,256,128]{2,1,0:T(8,128)(2,1)}), bf16[8,256,128]{2,1,0:T(8,128)(2,1)}, u32[]{:S(2)}, u32[]{:S(2)}) async-start(bf16[8,256,128]{2,1,0:T(8,128)(2,1)} %bitcast_bitcast_fusion), calls=%async_computation.2 | async-start | bytes 1048576 | tf_op jit(solution)/shard_map/all_to_all | solution.py:916
  335.1 82.1 %reduce-scatter.9.cloned.1.call-start = ((), (), s32[]{:S(2)}) async-start(), calls=%async_computation.12 | async-start | bytes 2654208 | tf_op jit(solution)/shard_map/reduce_scatter | solution.py:80
  339.1 21.7 %copy-start.5 = (bf16[4,512,768]{2,1,0:T(8,128)(2,1)S(1)}, bf16[4,512,768]{2,1,0:T(8,128)(2,1)}, u32[]{:S(2)}) copy-start(bf16[4,512,768]{2,1,0:T(8,128)(2,1)} %copy-done.4) | copy-start | bytes 9437188
  370.9 26.3 %collective-permute-start.28 = (bf16[512,768]{1,0:T(8,128)(2,1)}, bf16[512,768]{1,0:T(8,128)(2,1)S(1)}, u32[]{:S(2)}, u32[]{:S(2)}) collective-permute-start(bf16[512,768]{1,0:T(8,128)(2,1)} %get-tuple-element.242), channel_id=1, source_target_pairs={{0,4},{4,0},{1,5},{5,1},{2,6},{6,2},{3,7},{7,3},{8,12},{12,8},{9,1... | collective-permute-start | bytes 2359304 | tf_op jit(solution)/shard_map/ppermute | solution.py:120
  373.4 24.3 %collective-permute-start.29 = (bf16[512,768]{1,0:T(8,128)(2,1)}, bf16[512,768]{1,0:T(8,128)(2,1)S(1)}, u32[]{:S(2)}, u32[]{:S(2)}) collective-permute-start(bf16[512,768]{1,0:T(8,128)(2,1)} %get-tuple-element.240), channel_id=1, source_target_pairs={{0,2},{2,0},{1,3},{3,1},{4,6},{6,4},{5,7},{7,5},{8,10},{10,8},{9,1... | collective-permute-start | bytes 2359304 | tf_op jit(solution)/shard_map/ppermute | solution.py:120
  398.6 31.3 %all-to-all-start.2 = ((bf16[8,256,256]{2,1,0:T(8,128)(2,1)}), bf16[8,256,256]{2,1,0:T(8,128)(2,1)S(1)}, u32[]{:S(2)}, u32[]{:S(2)}) async-start(bf16[8,256,256]{2,1,0:T(8,128)(2,1)} %bitcast.108), calls=%async_computation.4 | async-start | bytes 2097152 | tf_op jit(solution)/shard_map/all_to_all | solution.py:916
  430.0 41.7 %all-to-all-start.3 = ((bf16[32,32,384]{2,1,0:T(8,128)(2,1)}), bf16[32,32,384]{2,1,0:T(8,128)(2,1)S(1)}, u32[]{:S(2)}, u32[]{:S(2)}) async-start(bf16[32,32,384]{2,1,0:T(8,128)(2,1)} %bitcast.109), calls=%async_computation.6 | async-start | bytes 1572864 | tf_op jit(solution)/shard_map/all_to_all | solution.py:916
  432.6 25.9 %reduce-scatter.11.cloned.1.call-start = ((), (), s32[]{:S(2)}) async-start(), calls=%async_computation.13 | async-start | bytes 368640 | tf_op jit(solution)/shard_map/reduce_scatter | solution.py:80
  (25 other events, 172.7 us)
Sparse Core Ops, SparseCore 0:
  14.5 85.8 all-gather.4
  102.0 48.7 all-gather.6
  153.0 44.7 all-gather.8
  256.8 45.8 reduce-scatter.4
  304.8 50.7 reduce-scatter.6
  364.0 53.2 reduce-scatter.8
  435.7 22.7 reduce-scatter.10

commit v4 on v3

--- a/solution.py
+++ b/solution.py
@@ -88,15 +88,28 @@
     return [(i, i + step) for i in range(n) if 0 <= i + step < n]
 
 
-def line_gather(x, axis):
-    n = lax.axis_size(axis)
+def hop(up, down):
+    n = lax.axis_size("a")
+    return lax.ppermute(up, "a", line_pairs(n, 1)), lax.ppermute(down, "a", line_pairs(n, -1))
+
+
+def line_gather(x):
     pieces = [(0, x)]
     up = down = x
-    for k in range(1, n):
-        up = lax.ppermute(up, axis, line_pairs(n, 1))
-        down = lax.ppermute(down, axis, line_pairs(n, -1))
+    for k in range(1, lax.axis_size("a")):
+        up, down = hop(up, down)
         pieces += [(-k, up), (k, down)]
     return pieces
+
+
+def in_line(own, ups, downs, me):
+    n = lax.axis_size("a")
+    out = jnp.zeros((n,) + own.shape, own.dtype)
+    out = lax.dynamic_update_index_in_dim(out, own, me, 0)
+    for k in range(1, n):
+        piece = jnp.where(me >= k, ups[k - 1], downs[n - k - 1])
+        out = lax.dynamic_update_index_in_dim(out, piece, (me - k) % n, 0)
+    return out.reshape((n * own.shape[0],) + own.shape[1:])
 
 
 def by_columns(own, other, member):
@@ -849,7 +862,7 @@
         out_ref[...] = resid_ref[...] + (inverse * scaled - x * inverse**3 * mean)
 
 
-def token_grads(grads, packed, x, resid):
+def token_grads(grads, weights, packed, x, resid):
     heads, rows, pack = grads.shape
     width = x.shape[1]
     small_at = packed.shape[1] // LANES - 1
@@ -872,7 +885,7 @@
             flops=2 * rows * width * heads * pack, bytes_accessed=8 * 2**20, transcendentals=0
         ),
         name="token_grads",
-    )(grads, packed, packed, x, resid)
+    )(grads, weights, packed, x, resid)
 
 
 def weight_sums_kernel(sums_ref, q_ref, k_ref, v_ref, gain_ref):
@@ -976,10 +989,9 @@
         axis=2,
     ).reshape(own_rows, KEY_VALUE_HEADS * HEAD_PACK)
     qkv_width = KEY_VALUE_HEADS * HEAD_PACK
-    first_all = gather(
+    second_all = gather(
         jnp.concatenate(
             [
-                by_head,
                 w_output.astype(bf16),
                 pad_lanes(
                     jnp.concatenate(
@@ -997,6 +1009,7 @@
         ),
         ALL,
     )
+    qkv_all = gather(by_head, ALL)
     experts_low = jnp.concatenate([expert_in.astype(bf16), expert_out.astype(bf16)], axis=1)
     if by_column:
         two = by_head.reshape(own_rows, GROUPS, 2 * HEAD_PACK).transpose(1, 0, 2)
@@ -1008,17 +1021,16 @@
         weights = (
             columns, lax.ppermute(columns, "c", SWAP), from_y, lax.ppermute(from_y, "c", SWAP)
         )
-        pieces = line_gather(tokens[0], "a")
+        pieces = line_gather(tokens[0])
         places = [piece[0] for piece in pieces]
         blocks = tuple(piece[1] for piece in pieces)
     else:
         at = lax.axis_index(head_axes) * HEAD_PACK
-        gain_at = qkv_width + width + E
-        gains = pad_lanes(first_all[:, gain_at : gain_at + 1], LANES)
+        gains = pad_lanes(second_all[:, width + E : width + E + 1], LANES)
         spots, places = None, None
         weights = (
             jnp.concatenate(
-                [lax.dynamic_slice_in_dim(first_all, at, HEAD_PACK, 1), gains], axis=1
+                [lax.dynamic_slice_in_dim(qkv_all, at, HEAD_PACK, 1), gains], axis=1
             ),
         )
         blocks = (gather(tokens[0], "b").reshape((-1,) + tokens.shape[1:]),)
@@ -1030,15 +1042,9 @@
             )
         )
     )
-    output_w = first_all[:, qkv_width : qkv_width + width]
-    small_at = qkv_width + width
-    router_w = first_all[:, small_at : small_at + E]
-    gain_two_f = first_all[:, small_at + E + 1].astype(f32)
-
     expert_ids = jnp.arange(E, dtype=jnp.int32)
     routed_own = jnp.any(routes[0][:, :, None] == expert_ids[None, None, :], axis=1)
     early = jnp.concatenate([cotangent[0], pad_lanes(routed_own.astype(bf16), LANES)], axis=1)
-    early_all = gather(early, "a")
     if by_column:
         beside = neighbours(experts_low)
     else:
@@ -1051,20 +1057,29 @@
     own_weights = own_weights.reshape(width, own_weights.shape[-1])
     if by_column:
         columns = (GROUPS, token_count)
+        early, q = lax.optimization_barrier((early, q))
+        up, down = hop(early, early)
+        ups, downs = [up], [down]
 
         def in_row(own, other, shape):
             return by_columns(own.reshape(shape), other.reshape(shape), member)
 
         kv_other = lax.ppermute(kv, "b", SWAP)
         kv = in_row(kv, kv_other, columns + (2 * PAIR,)).reshape(span, 2 * PAIR)
+        kv, up, down = lax.optimization_barrier((kv, up, down))
+        up, down = hop(up, down)
+        ups, downs = ups + [up], downs + [down]
     else:
         kv = gather(kv, "a")
+        early_all = gather(early, "a")
     attention_result, attended, log_total = attend(
         bounds_ahead, q, kv, docs_ahead, 2 if by_column else 1
     )
     if by_column:
-        attended, first_all = lax.optimization_barrier((attended, first_all))
-        attended, early_all = lax.optimization_barrier((attended, early_all))
+        attended, second_all, up, down = lax.optimization_barrier((attended, second_all, up, down))
+        up, down = hop(up, down)
+        early_all = in_line(early, ups + [up], downs + [down], group)
+        attended, qkv_all = lax.optimization_barrier((attended, qkv_all))
         outs = lax.all_gather(attended, "a", axis=0, tiled=False)
         parts = plane_gather(experts_low, *beside)
 
@@ -1078,14 +1093,12 @@
         q_other, out_other, log_other = (
             lax.ppermute(x, "b", SWAP) for x in (q_sent, out_sent, log_sent)
         )
-        cut = 2 * token_count
-        x_other = [lax.ppermute(x_span[:cut], "b", SWAP)]
         home = jnp.stack([member * 2 + lax.axis_index("y"), lax.axis_index("c")])
         experts_all, grad_hidden = place_experts(home, parts, early_all, width)
-        outs, experts_all, x_other[0], q_other, out_other, log_other = lax.optimization_barrier(
-            (outs, experts_all, x_other[0], q_other, out_other, log_other)
+        outs, experts_all, q_other, out_other, log_other = lax.optimization_barrier(
+            (outs, experts_all, q_other, out_other, log_other)
         )
-        normed_all, resid, attended_low = join(place, outs, first_all, qkv_width // width, x_span)
+        normed_all, resid, attended_low = join(place, outs, second_all, 0, x_span)
         normed_two = lax.dynamic_slice_in_dim(normed_all, group * token_count, token_count)
     else:
         attended_low = (
@@ -1093,9 +1106,10 @@
             .transpose(1, 0, 2)
             .reshape(token_count, QUERY_HEADS * HEAD_SIZE)
         )
-        attn_out = jnp.dot(attended_low, output_w, preferred_element_type=f32)
+        attn_out = jnp.dot(attended_low, second_all[:, :width], preferred_element_type=f32)
         resid = x_local + RESIDUAL_SCALE * attn_out
-        normed_two = rms_scale(resid, gain_two_f).astype(bf16)
+        gain_two = second_all[:, width + E + 1].astype(f32)
+        normed_two = rms_scale(resid, gain_two).astype(bf16)
         normed_all = gather(normed_two, "a")
         experts_all = parts.reshape(EXPERTS_HERE, width, 3 * F)
         grad_hidden = jnp.einsum(
@@ -1105,7 +1119,7 @@
             preferred_element_type=f32,
         )
     back_part, gates_all, gated_hidden, grad_pre = experts(
-        group.reshape(1), normed_all, early_all, first_all, experts_all, grad_hidden
+        group.reshape(1), normed_all, early_all, second_all, experts_all, grad_hidden
     )
     if by_column:
         q = in_row(q, q_other, columns + (PAIR,)).reshape(span, PAIR)
@@ -1122,10 +1136,12 @@
     inputs = (normed_all, early_all, experts_all, gated_hidden, grad_pre)
     if by_column:
         core = lax.axis_index("c")
-        x_other.append(lax.ppermute(x_span[cut:], "b", SWAP))
+        x_other = lax.ppermute(x_span, "b", SWAP)
         moe_part, *keep, send_left, send_right = expert_grads(core.reshape(1), 2, *inputs)
         arrived = [lax.ppermute(x, "c", SWAP) for x in (send_left, send_right)]
-        back_own, moe_part, keep = lax.optimization_barrier((back_own, moe_part, keep))
+        back_own, moe_part, keep, x_other = lax.optimization_barrier(
+            (back_own, moe_part, keep, x_other)
+        )
     else:
         moe_part, *grads = expert_grads(jnp.zeros((1,), jnp.int32), 1, *inputs)
         grad_experts = jnp.concatenate(grads, axis=2)
@@ -1136,6 +1152,9 @@
     back_own = back_own.astype(f32)
     moe_sum = scatter_sum(moe_part, "a")
 
+    output_w = second_all[:, :width]
+    router_w = second_all[:, width : width + E]
+    gain_two_f = second_all[:, width + E + 1].astype(f32)
     grad_out = cotangent[0].astype(f32)
     gates = lax.dynamic_slice_in_dim(gates_all, group * token_count, token_count)[:, :E]
     gate_grads_own = back_own[:, width : width + E] + back_own[:, width + E : width + 2 * E]
@@ -1151,27 +1170,20 @@
     grad_mixed = exchange(
         grad_heads.reshape(token_count, KEY_VALUE_HEADS, PAIR).transpose(1, 0, 2), head_axes
     ).reshape(span, PAIR)
-    if by_column:
-        keep, arrived, x_other, grad_heads = lax.optimization_barrier(
-            (keep, arrived, tuple(x_other), grad_heads)
-        )
-        x_other = jnp.concatenate(x_other)
-        left, right = (
-            halve_add(terms).reshape((2, 2) + terms[0].shape[1:]) for terms in zip(keep, arrived)
-        )
-        left, right = halve_send(left, "y", 1), halve_send(right, "b", 0)
     small = jnp.concatenate([grad_router, grad_gain_two[:, None]], axis=1)
     second_part = jnp.concatenate(
         [contract_rows(attended_low, grad_attn_low), pad_lanes(small, LANES)], axis=1
     ).astype(bf16)
     cols = second_part.shape[1]
+    if by_column:
+        keep, arrived, second_part = lax.optimization_barrier((keep, arrived, second_part))
+        left, right = (
+            halve_add(terms).reshape((2, 2) + terms[0].shape[1:]) for terms in zip(keep, arrived)
+        )
+        left, right = halve_send(left, "y", 1), halve_send(right, "b", 0)
     second_part = second_part.reshape(GROUPS, -1, own_rows, cols).transpose(1, 0, 2, 3)
     if by_column:
-        left, right = halve_add(left), halve_add(right)
-        second_part, left, right, grad_mixed = lax.optimization_barrier(
-            (second_part, left, right, grad_mixed)
-        )
-        left, right = halve_send(left, "b", 0), halve_send(right, "y", 0)
+        second_part, grad_mixed = lax.optimization_barrier((second_part, grad_mixed))
     rest = scatter_sum(second_part.reshape(-1, cols), PLANE)
     grads = attend_back(
         bounds, q, kv, doc_rows, grad_mixed, attention_result, log_total, wide_cos, wide_sin,
@@ -1179,6 +1191,8 @@
     )
     if by_column:
         left, right, moe_sum, grad_pack = lax.optimization_barrier((left, right, moe_sum, grads))
+        left, right = halve_add(left), halve_add(right)
+        left, right = halve_send(left, "b", 0), halve_send(right, "y", 0)
         first_part = head_grads(
             x_span, x_other, member, 1 - member, 2, member, own_weights, grad_pack
         )
@@ -1192,14 +1206,14 @@
     rest, first_part = lax.optimization_barrier((rest, first_part))
     rest = scatter_sum(rest, "a")
     by_tokens = exchange(grad_pack.reshape(KEY_VALUE_HEADS, token_count, HEAD_PACK), head_axes)
-    by_tokens, first_part = lax.optimization_barrier((by_tokens, first_part))
+    by_tokens, first_part, rest = lax.optimization_barrier((by_tokens, first_part, rest))
     sums = exchange(first_part.reshape(-1, own_rows, first_part.shape[1]), ALL)
-    sums, moe_sum, resid = lax.optimization_barrier((sums, moe_sum, resid))
+    grad_input = token_grads(by_tokens, qkv_all, second_all, tokens[0], grad_resid)
+    sums, moe_sum, resid, grad_input = lax.optimization_barrier((sums, moe_sum, resid, grad_input))
     grad_q_w, grad_k_w, grad_v_w, grad_gain_one = weight_sums(
         sums.reshape(-1, KEY_VALUE_HEADS, lax.axis_size(("y", "c")), own_rows, first_part.shape[1])
     )
     rest = rest.astype(f32)
-    grad_input = token_grads(by_tokens, first_all, tokens[0], grad_resid)
     layer_sum = resid + RESIDUAL_SCALE * moe_sum.astype(f32)
     if by_column:
         grad_experts = jnp.concatenate(

time: 494 us -> 520 us (1.053)
  starting transfers between devices: 58.5 us -> 73.6 us
  waiting for transfers between devices: 161 us -> 174 us
  other arithmetic: 51 us -> 43 us
  local copies, waits for them, and re-layouts: 36.1 us -> 42 us
  matrix products: 9.46 us -> 3.79 us
    ppermute x8 -> x13, waiting for transfers between devices: 33.3 us -> 68.9 us  [the longest x6 26.4 us: hop(): lax.ppermute(up, 'a', line_pairs(n, 1))]
    reduce_scatter x4, waiting for transfers between devices: 36.7 us -> 21.5 us  [scatter_sum(): return lax.psum_scatter(x, axes, scatter_dimension=0, tiled=True)]
    ppermute x1, waiting for transfers between devices: 15.1 us -> 0.01 us  [plane_gather(): upper = lax.ppermute(from_b[:half], 'y', SWAP)]
    ppermute x3, waiting for transfers between devices: 14.8 us -> 0.01 us  [body(): lax.ppermute(x, 'b', SWAP)]
    ppermute x8 -> x13, starting transfers between devices: 22.3 us -> 36.4 us  [the longest x6 27.4 us: hop(): lax.ppermute(up, 'a', line_pairs(n, 1))]
    ppermute x4, waiting for transfers between devices: 20.5 us -> 32.8 us  [halve_send(): lax.ppermute(lax.dynamic_index_in_dim(v, 1 - me, at, False), axis, SWAP)]
    all_to_all x4, waiting for transfers between devices: 14.8 us -> 25.7 us  [exchange(): return lax.all_to_all(x, axes, 0, 0, tiled=True)]
    all_gather x2, waiting for transfers between devices: 10.4 us -> 18.1 us  [gather(): return lax.all_gather(x, axes, axis=0, tiled=True)]
  transfers between devices with their start and end apart: 41 -> 46, of which waited for: 18 -> 19; matrix products, arithmetic and copies ran while one was open for 17% -> 16% of each run, Pallas kernels for 24% -> 23%
where the time goes in v4:
time: 520 us; the launch traced here: 510 us
  waiting for transfers between devices  174 us (33%)
  Pallas kernels  158 us (30%)
  starting transfers between devices  73.6 us (14%)
  other arithmetic  43 us (8%)
  local copies, waits for them, and re-layouts  42 us (8%)
  between operations  15.6 us (3%)
    ppermute x4, waiting for transfers between devices, halve_send(): lax.ppermute(lax.dynamic_index_in_dim(v, 1 - me, at, False), axis, SWAP)  32.8 us
    pallas_call x1, Pallas kernels, experts(): pl.pallas_call(experts_kernel, grid_spec=pltpu.PrefetchScalarGridSpec(num...  29 us
    ppermute x6, starting transfers between devices, hop(): lax.ppermute(up, 'a', line_pairs(n, 1))  27.4 us
    pallas_call x1, Pallas kernels, expert_grads(): pl.pallas_call(expert_grads_kernel, grid_spec=pltpu.PrefetchScalarGridSpe...  26.7 us
    ppermute x6, waiting for transfers between devices, hop(): lax.ppermute(up, 'a', line_pairs(n, 1))  26.4 us
    all_to_all x4, waiting for transfers between devices, exchange(): return lax.all_to_all(x, axes, 0, 0, tiled=True)  25.7 us
    pallas_call x1, Pallas kernels, attend_back(): pl.pallas_call(functools.partial(attend_back_kernel, fold), grid_spec=plt...  25 us
    ppermute x6, waiting for transfers between devices, hop(): lax.ppermute(down, 'a', line_pairs(n, -1))  24.5 us
  transfers between devices with their start and end apart: 46, of which 19 were waited for; matrix products, arithmetic and copies ran while one was open for 16% of the time, Pallas kernels for 23%

profile of v4, /device:TPU:0, one launch (start us, length us, event | category | flops | bytes accessed | tf_op | source)
XLA Modules:
  0.0 509.8 jit_solution(9692477272061975744)
XLA Ops:
  14.9 5.7 %collective-permute-start = (bf16[256,1024]{1,0:T(8,128)(2,1)}, bf16[256,1024]{1,0:T(8,128)(2,1)}, u32[]{:S(2)}, u32[]{:S(2)}) collective-permute-start(bf16[256,1024]{1,0:T(8,128)(2,1)} %bitcast.121), channel_id=1, source_target_pairs={{0,8},{8,16},{16,24},{1,9},{9,17},{17,25},{2,10},{10,18},{18,26},{... | collective-permute-start | bytes 1572872 | tf_op jit(solution)/shard_map/ppermute | solution.py:93
  22.9 6.9 %all-to-all-start = ((bf16[8,32,640]{2,1,0:T(8,128)(2,1)}), bf16[8,32,640]{2,1,0:T(8,128)(2,1)S(1)}, u32[]{:S(2)}, u32[]{:S(2)}) async-start(bf16[8,32,640]{2,1,0:T(8,128)(2,1)} %bitcast.7), calls=%async_computation | async-start | bytes 655360 | tf_op jit(solution)/shard_map/all_to_all | solution.py:929
  31.7 5.5 %multiply_sine_fusion = (f32[2048,32]{1,0:T(8,128)}, f32[2048,32]{1,0:T(8,128)}) fusion(f32[2048]{0:T(1024)S(1)} %subtract_convert_fusion, f32[32]{0:T(128)S(1)} %multiply_power_fusion), kind=kLoop, calls=%fused_computation.17 | loop fusion | flops 65536 | bytes 532608 | tf_op jit(solution)/shard_map/sin | solution.py:44
  38.1 4.7 collective-permute-start.2
  48.1 6.3 %collective-permute-done.2.refs_3_ = bf16[256,1024]{1,0:T(8,128)(2,1)} collective-permute-done((bf16[256,1024]{1,0:T(8,128)(2,1)}, bf16[256,1024]{1,0:T(8,128)(2,1)}, u32[]{:S(2)}, u32[]{:S(2)}) %collective-permute-start.2) | collective-permute-done | bytes 524320 | tf_op jit(solution)/shard_map/ppermute | solution.py:93
  54.4 5.2 %collective-permute-start.4 = (bf16[256,1024]{1,0:T(8,128)(2,1)}, bf16[256,1024]{1,0:T(8,128)(2,1)}, u32[]{:S(2)}, u32[]{:S(2)}) collective-permute-start(bf16[256,1024]{1,0:T(8,128)(2,1)} %collective-permute-done.2.refs_3_), channel_id=1, source_target_pairs={{0,8},{8,16},{16,24},{1,9},{9,17},{17,25},{2,10},{10,18},{18,26},{... | collective-permute-start | bytes 1572872 | tf_op jit(solution)/shard_map/ppermute | solution.py:93
  60.9 2.7 dynamic-slice_sine_fusion
  65.9 4.5 spread.1
  71.8 2.9 collective-permute-done.4.refs_5_
  74.6 3.7 collective-permute-done.5.refs_6_
  78.4 7.9 %project.1 = (bf16[1024,256]{1,0:T(8,128)(2,1)}, bf16[1024,256]{1,0:T(8,128)(2,1)}, bf16[1024,1024]{1,0:T(8,128)(2,1)}, bf16[8,4,32,640]{3,2,1,0:T(8,128)(2,1)}) custom-call(s32[4]{0:T(128)} %pad_add_fusion.place_ref, bf16[256,1024]{1,0:T(8,128)(2,1)} %bitcast.123, bf16[256,1024]{1,0:T(8,128)(2,1)} %collective-permute-done.refs_1_, ...), custom_call_target="tpu_custom_call" | custom-call | flops 1073741824 | bytes 8388608 | tf_op jit(solution)/shard_map/project/pallas_call | solution.py:228
  88.1 2.9 collective-permute-start.10
  94.4 7.0 %collective-permute-done.9 = bf16[1024,256]{1,0:T(8,128)(2,1)S(1)} collective-permute-done((bf16[1024,256]{1,0:T(8,128)(2,1)}, bf16[1024,256]{1,0:T(8,128)(2,1)S(1)}, u32[]{:S(2)}, u32[]{:S(2)}) %collective-permute-start.9) | collective-permute-done | bytes 524320 | tf_op jit(solution)/shard_map/ppermute | solution.py:1067
  103.6 1.9 collective-permute-done.10
  105.6 3.5 collective-permute-done.11
  109.0 3.0 collective-permute-start.12
  113.5 17.0 %attend.1 = (f32[1024,256]{1,0:T(8,128)}, bf16[1024,256]{1,0:T(8,128)(2,1)}, f32[2,2,1,1024]{3,2,1,0:T(1,128)}) custom-call(s32[5]{0:T(128)} %pad_add_fusion.1.bounds_ref, bf16[1024,256]{1,0:T(8,128)(2,1)} %get-tuple-element.116.q_ref, bf16[2048,256]{1,0:T(8,128)(2,1)} %bitcast.133, s32[2,1,512]{2,1,0:T(1,128)} %bitcast.149), custom_call_target="tpu_custom_call" | custom-call | flops 2147483648 | bytes 6291456 | tf_op jit(solution)/shard_map/attend/pallas_call | solution.py:419
  131.7 18.1 %all-gather.7.cloned.1.call-done.w_ref = bf16[1024,2048]{1,0:T(8,128)(2,1)} async-done(((bf16[32,2048]{1,0:T(8,128)(2,1)}), bf16[1024,2048]{1,0:T(8,128)(2,1)}) %all-gather.7.cloned.1.call-update) | async-done | bytes 4194320 | tf_op jit(solution)/shard_map/all_gather | solution.py:76
  153.4 2.1 slice.78
  157.0 2.1 slice.79
  166.3 16.0 %collective-permute-done.23 = bf16[256,1152]{1,0:T(8,128)(2,1)} collective-permute-done((bf16[256,1152]{1,0:T(8,128)(2,1)}, bf16[256,1152]{1,0:T(8,128)(2,1)}, u32[]{:S(2)}, u32[]{:S(2)}) %collective-permute-start.23) | collective-permute-done | bytes 589856 | tf_op jit(solution)/shard_map/ppermute | solution.py:93
  182.4 5.8 %collective-permute-start.24 = (bf16[256,1152]{1,0:T(8,128)(2,1)}, bf16[256,1152]{1,0:T(8,128)(2,1)S(1)}, u32[]{:S(2)}, u32[]{:S(2)}) collective-permute-start(bf16[256,1152]{1,0:T(8,128)(2,1)} %copy-done.24), channel_id=1, source_target_pairs={{0,8},{8,16},{16,24},{1,9},{9,17},{17,25},{2,10},{10,18},{18,26},{... | collective-permute-start | bytes 1769480 | tf_op jit(solution)/shard_map/ppermute | solution.py:93
  191.3 15.2 %collective-permute-done.24 = bf16[256,1152]{1,0:T(8,128)(2,1)S(1)} collective-permute-done((bf16[256,1152]{1,0:T(8,128)(2,1)}, bf16[256,1152]{1,0:T(8,128)(2,1)S(1)}, u32[]{:S(2)}, u32[]{:S(2)}) %collective-permute-start.24) | collective-permute-done | bytes 589856 | tf_op jit(solution)/shard_map/ppermute | solution.py:93
  211.8 18.5 %place_experts.1 = (bf16[4,1024,1536]{2,1,0:T(8,128)(2,1)}, f32[4,1024,512]{2,1,0:T(8,128)}) custom-call(s32[2]{0:T(128)} %pad_add_fusion.2.place_ref, bf16[512,1536]{1,0:T(8,128)(2,1)} %pad_maximum_fusion.2.refs_0_, bf16[512,1536]{1,0:T(8,128)(2,1)} %collective-permute-done.14.refs_1_, bf16[512,1536]{1,0:T(8,128)(2,1)} %collective-permute-done.15.refs_2_, ...), custom_call_target="tpu_custom_call" | custom-call | flops 4294967296 | bytes 37748736 | tf_op jit(solution)/shard_map/place_experts/pallas_call | solution.py:614
  230.3 8.2 %join.1 = (bf16[1024,1024]{1,0:T(8,128)(2,1)}, f32[256,1024]{1,0:T(8,128)}, bf16[256,1024]{1,0:T(8,128)(2,1)}) custom-call(s32[4]{0:T(128)} %pad_add_fusion.place_ref, bf16[4,1024,256]{2,1,0:T(8,128)(2,1)} %bitcast.120, bf16[1024,1152]{1,0:T(8,128)(2,1)} %all-gather.5.cloned.1.call-done.w_ref.small_ref.router_ref, ...), custom_call_target="tpu_custom_call" | custom-call | flops 2147483648 | bytes 12582912 | tf_op jit(solution)/shard_map/join/pallas_call | solution.py:816
  238.5 29.0 %experts.1 = (bf16[1024,1152]{1,0:T(8,128)(2,1)}, f32[1024,128]{1,0:T(8,128)}, bf16[4,1024,512]{2,1,0:T(8,128)(2,1)}, bf16[4,1024,1024]{2,1,0:T(8,128)(2,1)}) custom-call(s32[1]{0:T(128)} %bitcast.group_ref, bf16[1024,1024]{1,0:T(8,128)(2,1)} %get-tuple-element.135.n_ref, bf16[1024,1152]{1,0:T(8,128)(2,1)} %bitcast.118, ...), custom_call_target="tpu_custom_call" | custom-call | flops 17179869184 | bytes 41943040 | tf_op jit(solution)/shard_map/experts/pallas_call | solution.py:696
  269.0 26.7 %expert_grads.1 = (bf16[1024,1024]{1,0:T(8,128)(2,1)}, bf16[4,512,768]{2,1,0:T(8,128)(2,1)}, bf16[4,512,768]{2,1,0:T(8,128)(2,1)}, bf16[4,512,768]{2,1,0:T(8,128)(2,1)}, bf16[4,512,768]{2,1,0:T(8,128)(2,1)}) custom-call(s32[1]{0:T(128)} %bitcast.3.half_ref, bf16[1024,1024]{1,0:T(8,128)(2,1)} %get-tuple-element.135.n_ref, bf16[1024,1152]{1,0:T(8,128)(2,1)} %bitcast.119, ...), custom_call_target="tpu_custom_call" | custom-call | flops 17179869184 | bytes 41943040 | tf_op jit(solution)/shard_map/expert_grads/pallas_call | solution.py:762
  295.8 18.1 %collective-permute-done.28.other_ref = bf16[1024,1024]{1,0:T(8,128)(2,1)} collective-permute-done((bf16[1024,1024]{1,0:T(8,128)(2,1)}, bf16[1024,1024]{1,0:T(8,128)(2,1)}, u32[]{:S(2)}, u32[]{:S(2)}) %collective-permute-start.28) | collective-permute-done | bytes 2097184 | tf_op jit(solution)/shard_map/ppermute | solution.py:1139
  313.8 2.9 reduce-scatter.5.cloned.1.call-done
  324.8 4.3 all-to-all-start.1
  331.9 2.5 copy.105
  334.4 24.4 %all-to-all-done.1 = bf16[8,256,128]{2,1,0:T(8,128)(2,1)} async-done(((bf16[8,256,128]{2,1,0:T(8,128)(2,1)}), bf16[8,256,128]{2,1,0:T(8,128)(2,1)}, u32[]{:S(2)}, u32[]{:S(2)}) %all-to-all-start.1) | async-done | bytes 524320 | tf_op jit(solution)/shard_map/all_to_all | solution.py:929
  358.7 3.3 copy.111
  362.1 3.6 add_convert_fusion.1
  369.0 2.8 add_convert_fusion
  371.8 1.9 dynamic-slice_bitcast_fusion
  379.1 25.0 %attend_back.1.grad_ref = bf16[2048,256]{1,0:T(8,128)(2,1)} custom-call(s32[10]{0:T(128)} %pad_add_fusion.3.bounds_ref, bf16[2048,128]{1,0:T(8,128)(2,1)} %bitcast.137, bf16[2048,256]{1,0:T(8,128)(2,1)} %bitcast.134, s32[4,1,512]{2,1,0:T(1,128)} %bitcast.144, bf16[2048,128]{1,0:T(8,128)(2,1)} %bitcast.42.do_ref, f32[2048,128]{1,0:T(8,128)} %bitcast.135, ...), custom_call_target="tpu_custom_call" | custom-call | flops 5368709120 | bytes 8388608 | tf_op jit(solution)/shard_map/attend_back/pallas_call | solution.py:539
  404.1 4.1 collective-permute-done.31
  408.2 6.0 %collective-permute-done.32 = bf16[2,512,768]{2,1,0:T(8,128)(2,1)} collective-permute-done((bf16[2,512,768]{2,1,0:T(8,128)(2,1)}, bf16[2,512,768]{2,1,0:T(8,128)(2,1)}, u32[]{:S(2)}, u32[]{:S(2)}) %collective-permute-start.32) | collective-permute-done | bytes 1572896 | tf_op jit(solution)/shard_map/ppermute | solution.py:133
  414.2 4.3 all-to-all-start.2
  419.1 10.1 %head_grads.1 = bf16[1024,384]{1,0:T(8,128)(2,1)} custom-call(s32[3]{0:T(128)} %pad_add_fusion.4.place_ref, bf16[1024,1024]{1,0:T(8,128)(2,1)} %get-tuple-element.134.x_ref.own_ref, bf16[1024,1024]{1,0:T(8,128)(2,1)} %collective-permute-done.28.other_ref, bf16[1024,640]{1,0:T(8,128)(2,1)} %bitcast.113, bf16[1024,640]{1,0:T(8,128)(2,1)} %bitcast.114, ...), custom_call_target="tpu_custom_call" | custom-call | flops 2147483648 | bytes 8388608 | tf_op jit(solution)/shard_map/head_grads/pallas_call | solution.py:317
  429.2 2.9 reduce-scatter.9.cloned.1.call-done
  432.2 2.4 add_convert_fusion.2
  438.1 15.6 %reduce-scatter.11.cloned.1.call-done = bf16[32,1152]{1,0:T(8,128)(2,1)} async-done(((bf16[128,1152]{1,0:T(8,128)(2,1)}), bf16[32,1152]{1,0:T(8,128)(2,1)}) %reduce-scatter.11.cloned.1.call-update) | async-done | bytes 73744 | tf_op jit(solution)/shard_map/reduce_scatter | solution.py:80
  453.8 2.8 all-to-all-start.3
  462.1 22.7 %collective-permute-done.33 = bf16[512,768]{1,0:T(8,128)(2,1)S(1)} collective-permute-done((bf16[512,768]{1,0:T(8,128)(2,1)S(1)}, bf16[512,768]{1,0:T(8,128)(2,1)S(1)}, u32[]{:S(2)}, u32[]{:S(2)}) %collective-permute-start.33) | collective-permute-done | bytes 786464 | tf_op jit(solution)/shard_map/ppermute | solution.py:133
  488.0 8.8 %token_grads.1 = f32[256,1024]{1,0:T(8,128)} custom-call(bf16[8,256,256]{2,1,0:T(8,128)(2,1)} %all-to-all-done.2.grad_ref, bf16[1024,2048]{1,0:T(8,128)(2,1)} %all-gather.7.cloned.1.call-done.w_ref, bf16[1024,1152]{1,0:T(8,128)(2,1)} %all-gather.5.cloned.1.call-done.w_ref.small_ref.router_ref, bf16[256,1024]{1,0:T(8,128)(2,1)} %bitcast.124, ...), custom_call_target="tpu_custom_call" | custom-call | flops 1073741824 | bytes 8388608 | tf_op jit(solution)/shard_map/token_grads/pallas_call | solution.py:870
  498.3 1.9 weight_sums.1
  (264 shorter events, 90.6 us)
Async XLA Ops:
  7.2 124.5 %all-gather.5.cloned.1.call-start = ((), (), s32[]{:S(2)}) async-start(), calls=%async_computation.8 | async-start | bytes 2433024 | tf_op jit(solution)/shard_map/all_gather | solution.py:76
  11.2 138.6 %all-gather.7.cloned.1.call-start = ((), (), s32[]{:S(2)}) async-start(), calls=%async_computation.9 | async-start | bytes 4325376 | tf_op jit(solution)/shard_map/all_gather | solution.py:76
  14.9 23.2 %collective-permute-start = (bf16[256,1024]{1,0:T(8,128)(2,1)}, bf16[256,1024]{1,0:T(8,128)(2,1)}, u32[]{:S(2)}, u32[]{:S(2)}) collective-permute-start(bf16[256,1024]{1,0:T(8,128)(2,1)} %bitcast.121), channel_id=1, source_target_pairs={{0,8},{8,16},{16,24},{1,9},{9,17},{17,25},{2,10},{10,18},{18,26},{... | collective-permute-start | bytes 1572872 | tf_op jit(solution)/shard_map/ppermute | solution.py:93
  20.7 22.1 %collective-permute-start.1 = (bf16[256,1024]{1,0:T(8,128)(2,1)}, bf16[256,1024]{1,0:T(8,128)(2,1)}, u32[]{:S(2)}, u32[]{:S(2)}) collective-permute-start(bf16[256,1024]{1,0:T(8,128)(2,1)} %bitcast.122), channel_id=1, source_target_pairs={{8,0},{16,8},{24,16},{9,1},{17,9},{25,17},{10,2},{18,10},{26,18},{... | collective-permute-start | bytes 1572872 | tf_op jit(solution)/shard_map/ppermute | solution.py:93
  22.9 23.1 %all-to-all-start = ((bf16[8,32,640]{2,1,0:T(8,128)(2,1)}), bf16[8,32,640]{2,1,0:T(8,128)(2,1)S(1)}, u32[]{:S(2)}, u32[]{:S(2)}) async-start(bf16[8,32,640]{2,1,0:T(8,128)(2,1)} %bitcast.7), calls=%async_computation | async-start | bytes 655360 | tf_op jit(solution)/shard_map/all_to_all | solution.py:929
  29.8 200.5 %all-gather.9.cloned.1.call-start = ((), (), s32[]{:S(2)}) async-start(), calls=%async_computation.14 | async-start | bytes 2621440 | tf_op jit(solution)/shard_map/all_gather | solution.py:1083
  31.7 285.1 %copy-start.32 = (s32[2048]{0:T(1024)}, s32[2048]{0:T(1024)S(1)}, u32[]{:S(2)}) copy-start(s32[2048]{0:T(1024)S(1)} %convert_reduce_fusion) | copy-start | bytes 24580
  38.1 16.4 %collective-permute-start.2 = (bf16[256,1024]{1,0:T(8,128)(2,1)}, bf16[256,1024]{1,0:T(8,128)(2,1)}, u32[]{:S(2)}, u32[]{:S(2)}) collective-permute-start(bf16[256,1024]{1,0:T(8,128)(2,1)} %collective-permute-done.refs_1_), channel_id=1, source_target_pairs={{0,8},{8,16},{16,24},{1,9},{9,17},{17,25},{2,10},{10,18},{18,26},{... | collective-permute-start | bytes 1572872 | tf_op jit(solution)/shard_map/ppermute | solution.py:93
  42.8 16.9 %collective-permute-start.3 = (bf16[256,1024]{1,0:T(8,128)(2,1)}, bf16[256,1024]{1,0:T(8,128)(2,1)}, u32[]{:S(2)}, u32[]{:S(2)}) collective-permute-start(bf16[256,1024]{1,0:T(8,128)(2,1)} %collective-permute-done.1.refs_2_), channel_id=1, source_target_pairs={{8,0},{16,8},{24,16},{9,1},{17,9},{25,17},{10,2},{18,10},{26,18},{... | collective-permute-start | bytes 1572872 | tf_op jit(solution)/shard_map/ppermute | solution.py:93
  46.1 17.5 %collective-permute-start.7 = (bf16[8,32,640]{2,1,0:T(8,128)(2,1)S(1)}, bf16[8,32,640]{2,1,0:T(8,128)(2,1)}, u32[]{:S(2)}, u32[]{:S(2)}) collective-permute-start(bf16[8,32,640]{2,1,0:T(8,128)(2,1)S(1)} %all-to-all-done.refs_7_), channel_id=1, source_target_pairs={{0,2},{2,0},{1,3},{3,1},{4,6},{6,4},{5,7},{7,5},{8,10},{10,8},{9,1... | collective-permute-start | bytes 983048 | tf_op jit(solution)/shard_map/ppermute | solution.py:1019
  54.4 20.2 %collective-permute-start.4 = (bf16[256,1024]{1,0:T(8,128)(2,1)}, bf16[256,1024]{1,0:T(8,128)(2,1)}, u32[]{:S(2)}, u32[]{:S(2)}) collective-permute-start(bf16[256,1024]{1,0:T(8,128)(2,1)} %collective-permute-done.2.refs_3_), channel_id=1, source_target_pairs={{0,8},{8,16},{16,24},{1,9},{9,17},{17,25},{2,10},{10,18},{18,26},{... | collective-permute-start | bytes 1572872 | tf_op jit(solution)/shard_map/ppermute | solution.py:93
  59.7 18.7 %collective-permute-start.5 = (bf16[256,1024]{1,0:T(8,128)(2,1)}, bf16[256,1024]{1,0:T(8,128)(2,1)}, u32[]{:S(2)}, u32[]{:S(2)}) collective-permute-start(bf16[256,1024]{1,0:T(8,128)(2,1)} %collective-permute-done.3.refs_4_), channel_id=1, source_target_pairs={{8,0},{16,8},{24,16},{9,1},{17,9},{25,17},{10,2},{18,10},{26,18},{... | collective-permute-start | bytes 1572872 | tf_op jit(solution)/shard_map/ppermute | solution.py:93
  63.6 8.2 %collective-permute-start.6 = (bf16[8,32,640]{2,1,0:T(8,128)(2,1)S(1)}, bf16[8,32,640]{2,1,0:T(8,128)(2,1)}, u32[]{:S(2)}, u32[]{:S(2)}) collective-permute-start(bf16[8,32,640]{2,1,0:T(8,128)(2,1)S(1)} %all-to-all-done.refs_7_), channel_id=1, source_target_pairs={{0,1},{1,0},{2,3},{3,2},{4,5},{5,4},{6,7},{7,6},{8,9},{9,8},{10,11... | collective-permute-start | bytes 983048 | tf_op jit(solution)/shard_map/ppermute | solution.py:1022
  63.6 8.1 %collective-permute-start.8 = (bf16[8,32,640]{2,1,0:T(8,128)(2,1)}, bf16[8,32,640]{2,1,0:T(8,128)(2,1)}, u32[]{:S(2)}, u32[]{:S(2)}) collective-permute-start(bf16[8,32,640]{2,1,0:T(8,128)(2,1)} %collective-permute-done.7.refs_9_), channel_id=1, source_target_pairs={{0,1},{1,0},{2,3},{3,2},{4,5},{5,4},{6,7},{7,6},{8,9},{9,8},{10,11... | collective-permute-start | bytes 983048 | tf_op jit(solution)/shard_map/ppermute | solution.py:1022
  86.3 15.1 %collective-permute-start.9 = (bf16[1024,256]{1,0:T(8,128)(2,1)}, bf16[1024,256]{1,0:T(8,128)(2,1)S(1)}, u32[]{:S(2)}, u32[]{:S(2)}) collective-permute-start(bf16[1024,256]{1,0:T(8,128)(2,1)} %get-tuple-element.117), channel_id=1, source_target_pairs={{0,4},{4,0},{1,5},{5,1},{2,6},{6,2},{3,7},{7,3},{8,12},{12,8},{9,1... | collective-permute-start | bytes 1572872 | tf_op jit(solution)/shard_map/ppermute | solution.py:1067
  88.1 17.5 %collective-permute-start.10 = (bf16[256,1152]{1,0:T(8,128)(2,1)S(1)}, bf16[256,1152]{1,0:T(8,128)(2,1)S(1)}, u32[]{:S(2)}, u32[]{:S(2)}) collective-permute-start(bf16[256,1152]{1,0:T(8,128)(2,1)S(1)} %pad_maximum_fusion.5), channel_id=1, source_target_pairs={{0,8},{8,16},{16,24},{1,9},{9,17},{17,25},{2,10},{10,18},{18,26},{... | collective-permute-start | bytes 1769480 | tf_op jit(solution)/shard_map/ppermute | solution.py:93
  91.0 18.0 %collective-permute-start.11 = (bf16[256,1152]{1,0:T(8,128)(2,1)S(1)}, bf16[256,1152]{1,0:T(8,128)(2,1)S(1)}, u32[]{:S(2)}, u32[]{:S(2)}) collective-permute-start(bf16[256,1152]{1,0:T(8,128)(2,1)S(1)} %pad_maximum_fusion.5), channel_id=1, source_target_pairs={{8,0},{16,8},{24,16},{9,1},{17,9},{25,17},{10,2},{18,10},{26,18},{... | collective-permute-start | bytes 1769480 | tf_op jit(solution)/shard_map/ppermute | solution.py:93
  92.3 64.7 %collective-permute-start.15 = (bf16[512,1536]{1,0:T(8,128)(2,1)}, bf16[512,1536]{1,0:T(8,128)(2,1)}, u32[]{:S(2)}, u32[]{:S(2)}) collective-permute-start(bf16[512,1536]{1,0:T(8,128)(2,1)} %pad_maximum_fusion.2.refs_0_), channel_id=1, source_target_pairs={{0,2},{2,0},{1,3},{3,1},{4,6},{6,4},{5,7},{7,5},{8,10},{10,8},{9,1... | collective-permute-start | bytes 4718600 | tf_op jit(solution)/shard_map/ppermute | solution.py:121
  93.9 59.5 %collective-permute-start.17 = (bf16[512,1536]{1,0:T(8,128)(2,1)}, bf16[512,1536]{1,0:T(8,128)(2,1)}, u32[]{:S(2)}, u32[]{:S(2)}) collective-permute-start(bf16[512,1536]{1,0:T(8,128)(2,1)} %pad_maximum_fusion.2.refs_0_), channel_id=1, source_target_pairs={{0,4},{4,0},{1,5},{5,1},{2,6},{6,2},{3,7},{7,3},{8,12},{12,8},{9,1... | collective-permute-start | bytes 4718600 | tf_op jit(solution)/shard_map/ppermute | solution.py:121
  109.0 21.4 %collective-permute-start.12 = (bf16[256,1152]{1,0:T(8,128)(2,1)S(1)}, bf16[256,1152]{1,0:T(8,128)(2,1)S(1)}, u32[]{:S(2)}, u32[]{:S(2)}) collective-permute-start(bf16[256,1152]{1,0:T(8,128)(2,1)S(1)} %collective-permute-done.10), channel_id=1, source_target_pairs={{0,8},{8,16},{16,24},{1,9},{9,17},{17,25},{2,10},{10,18},{18,26},{... | collective-permute-start | bytes 1769480 | tf_op jit(solution)/shard_map/ppermute | solution.py:93
  112.1 19.6 %collective-permute-start.13 = (bf16[256,1152]{1,0:T(8,128)(2,1)S(1)}, bf16[256,1152]{1,0:T(8,128)(2,1)}, u32[]{:S(2)}, u32[]{:S(2)}) collective-permute-start(bf16[256,1152]{1,0:T(8,128)(2,1)S(1)} %collective-permute-done.11), channel_id=1, source_target_pairs={{8,0},{16,8},{24,16},{9,1},{17,9},{25,17},{10,2},{18,10},{26,18},{... | collective-permute-start | bytes 1769480 | tf_op jit(solution)/shard_map/ppermute | solution.py:93
  113.4 52.4 %collective-permute-start.14 = (bf16[512,1536]{1,0:T(8,128)(2,1)}, bf16[512,1536]{1,0:T(8,128)(2,1)}, u32[]{:S(2)}, u32[]{:S(2)}) collective-permute-start(bf16[512,1536]{1,0:T(8,128)(2,1)} %pad_maximum_fusion.2.refs_0_), channel_id=1, source_target_pairs={{0,1},{1,0},{2,3},{3,2},{4,5},{5,4},{6,7},{7,6},{8,9},{9,8},{10,11... | collective-permute-start | bytes 4718600 | tf_op jit(solution)/shard_map/ppermute | solution.py:128
  149.8 166.9 %reduce-scatter.5.cloned.1.call-start = ((), (), s32[]{:S(2)}) async-start(), calls=%async_computation.10 | async-start | bytes 2949120 | tf_op jit(solution)/shard_map/reduce_scatter | solution.py:80
  150.5 31.8 %collective-permute-start.23 = (bf16[256,1152]{1,0:T(8,128)(2,1)}, bf16[256,1152]{1,0:T(8,128)(2,1)}, u32[]{:S(2)}, u32[]{:S(2)}) collective-permute-start(bf16[256,1152]{1,0:T(8,128)(2,1)} %collective-permute-done.13), channel_id=1, source_target_pairs={{8,0},{16,8},{24,16},{9,1},{17,9},{25,17},{10,2},{18,10},{26,18},{... | collective-permute-start | bytes 1769480 | tf_op jit(solution)/shard_map/ppermute | solution.py:93
  155.5 33.9 %collective-permute-start.19 = (bf16[256,1536]{1,0:T(8,128)(2,1)}, bf16[256,1536]{1,0:T(8,128)(2,1)}, u32[]{:S(2)}, u32[]{:S(2)}) collective-permute-start(bf16[256,1536]{1,0:T(8,128)(2,1)} %slice.78), channel_id=1, source_target_pairs={{0,2},{2,0},{1,3},{3,1},{4,6},{6,4},{5,7},{7,5},{8,10},{10,8},{9,1... | collective-permute-start | bytes 2359304 | tf_op jit(solution)/shard_map/ppermute | solution.py:126
  159.1 30.4 %collective-permute-start.21 = (bf16[256,1536]{1,0:T(8,128)(2,1)}, bf16[256,1536]{1,0:T(8,128)(2,1)}, u32[]{:S(2)}, u32[]{:S(2)}) collective-permute-start(bf16[256,1536]{1,0:T(8,128)(2,1)} %slice.79), channel_id=1, source_target_pairs={{0,4},{4,0},{1,5},{5,1},{2,6},{6,2},{3,7},{7,3},{8,12},{12,8},{9,1... | collective-permute-start | bytes 2359304 | tf_op jit(solution)/shard_map/ppermute | solution.py:127
  165.8 41.6 %collective-permute-start.16 = (bf16[512,1536]{1,0:T(8,128)(2,1)}, bf16[512,1536]{1,0:T(8,128)(2,1)S(1)}, u32[]{:S(2)}, u32[]{:S(2)}) collective-permute-start(bf16[512,1536]{1,0:T(8,128)(2,1)} %collective-permute-done.15.refs_2_), channel_id=1, source_target_pairs={{0,1},{1,0},{2,3},{3,2},{4,5},{5,4},{6,7},{7,6},{8,9},{9,8},{10,11... | collective-permute-start | bytes 4718600 | tf_op jit(solution)/shard_map/ppermute | solution.py:128
  165.8 43.0 %collective-permute-start.18 = (bf16[512,1536]{1,0:T(8,128)(2,1)}, bf16[512,1536]{1,0:T(8,128)(2,1)S(1)}, u32[]{:S(2)}, u32[]{:S(2)}) collective-permute-start(bf16[512,1536]{1,0:T(8,128)(2,1)} %collective-permute-done.17.refs_4_), channel_id=1, source_target_pairs={{0,1},{1,0},{2,3},{3,2},{4,5},{5,4},{6,7},{7,6},{8,9},{9,8},{10,11... | collective-permute-start | bytes 4718600 | tf_op jit(solution)/shard_map/ppermute | solution.py:128
  182.4 24.1 %collective-permute-start.24 = (bf16[256,1152]{1,0:T(8,128)(2,1)}, bf16[256,1152]{1,0:T(8,128)(2,1)S(1)}, u32[]{:S(2)}, u32[]{:S(2)}) collective-permute-start(bf16[256,1152]{1,0:T(8,128)(2,1)} %copy-done.24), channel_id=1, source_target_pairs={{0,8},{8,16},{16,24},{1,9},{9,17},{17,25},{2,10},{10,18},{18,26},{... | collective-permute-start | bytes 1769480 | tf_op jit(solution)/shard_map/ppermute | solution.py:93
  189.4 20.1 %collective-permute-start.20 = (bf16[256,1536]{1,0:T(8,128)(2,1)}, bf16[256,1536]{1,0:T(8,128)(2,1)S(1)}, u32[]{:S(2)}, u32[]{:S(2)}) collective-permute-start(bf16[256,1536]{1,0:T(8,128)(2,1)} %collective-permute-done.19.refs_6_), channel_id=1, source_target_pairs={{0,1},{1,0},{2,3},{3,2},{4,5},{5,4},{6,7},{7,6},{8,9},{9,8},{10,11... | collective-permute-start | bytes 2359304 | tf_op jit(solution)/shard_map/ppermute | solution.py:128
  189.5 20.5 %collective-permute-start.22 = (bf16[256,1536]{1,0:T(8,128)(2,1)}, bf16[256,1536]{1,0:T(8,128)(2,1)S(1)}, u32[]{:S(2)}, u32[]{:S(2)}) collective-permute-start(bf16[256,1536]{1,0:T(8,128)(2,1)} %collective-permute-done.21.refs_8_), channel_id=1, source_target_pairs={{0,1},{1,0},{2,3},{3,2},{4,5},{5,4},{6,7},{7,6},{8,9},{9,8},{10,11... | collective-permute-start | bytes 2359304 | tf_op jit(solution)/shard_map/ppermute | solution.py:128
  206.5 23.8 %collective-permute-start.26 = (f32[1024,128]{1,0:T(8,128)S(1)}, f32[1024,128]{1,0:T(8,128)}, u32[]{:S(2)}, u32[]{:S(2)}) collective-permute-start(f32[1024,128]{1,0:T(8,128)S(1)} %bitcast.140), channel_id=1, source_target_pairs={{0,4},{4,0},{1,5},{5,1},{2,6},{6,2},{3,7},{7,3},{8,12},{12,8},{9,1... | collective-permute-start | bytes 1572872 | tf_op jit(solution)/shard_map/ppermute | solution.py:1094
  207.4 22.8 %collective-permute-start.25 = (bf16[1024,128]{1,0:T(8,128)(2,1)S(1)}, bf16[1024,128]{1,0:T(8,128)(2,1)S(1)}, u32[]{:S(2)}, u32[]{:S(2)}) collective-permute-start(bf16[1024,128]{1,0:T(8,128)(2,1)S(1)} %bitcast.141), channel_id=1, source_target_pairs={{0,4},{4,0},{1,5},{5,1},{2,6},{6,2},{3,7},{7,3},{8,12},{12,8},{9,1... | collective-permute-start | bytes 786440 | tf_op jit(solution)/shard_map/ppermute | solution.py:1094
  208.8 21.4 %collective-permute-start.27 = (f32[2,1,1024]{2,0,1:T(2,128)S(1)}, f32[2,1,1024]{2,0,1:T(2,128)S(1)}, u32[]{:S(2)}, u32[]{:S(2)}) collective-permute-start(f32[2,1,1024]{2,0,1:T(2,128)S(1)} %bitcast.148), channel_id=1, source_target_pairs={{0,4},{4,0},{1,5},{5,1},{2,6},{6,2},{3,7},{7,3},{8,12},{12,8},{9,1... | collective-permute-start | bytes 24584 | tf_op jit(solution)/shard_map/ppermute | solution.py:1094
  267.6 146.6 %reduce-scatter.7.cloned.1.call-start = ((), (), s32[]{:S(2)}) async-start(), calls=%async_computation.11 | async-start | bytes 2621440 | tf_op jit(solution)/shard_map/reduce_scatter | solution.py:80
  267.8 46.0 %collective-permute-start.28 = (bf16[1024,1024]{1,0:T(8,128)(2,1)}, bf16[1024,1024]{1,0:T(8,128)(2,1)}, u32[]{:S(2)}, u32[]{:S(2)}) collective-permute-start(bf16[1024,1024]{1,0:T(8,128)(2,1)} %get-tuple-element.134.x_ref.own_ref), channel_id=1, source_target_pairs={{0,4},{4,0},{1,5},{5,1},{2,6},{6,2},{3,7},{7,3},{8,12},{12,8},{9,1... | collective-permute-start | bytes 6291464 | tf_op jit(solution)/shard_map/ppermute | solution.py:1139
  269.0 51.2 %copy-start.1 = (f32[256,1024]{1,0:T(8,128)S(1)}, f32[256,1024]{1,0:T(8,128)}, u32[]{:S(2)}) copy-start(f32[256,1024]{1,0:T(8,128)} %get-tuple-element.174) | copy-start | bytes 3145732
  317.0 14.9 %collective-permute-start.29 = (bf16[4,512,768]{2,1,0:T(8,128)(2,1)}, bf16[4,512,768]{2,1,0:T(8,128)(2,1)}, u32[]{:S(2)}, u32[]{:S(2)}) collective-permute-start(bf16[4,512,768]{2,1,0:T(8,128)(2,1)} %get-tuple-element.146), channel_id=1, source_target_pairs={{0,1},{1,0},{2,3},{3,2},{4,5},{5,4},{6,7},{7,6},{8,9},{9,8},{10,11... | collective-permute-start | bytes 9437192 | tf_op jit(solution)/shard_map/ppermute | solution.py:1141
  317.1 14.8 %collective-permute-start.30 = (bf16[4,512,768]{2,1,0:T(8,128)(2,1)}, bf16[4,512,768]{2,1,0:T(8,128)(2,1)}, u32[]{:S(2)}, u32[]{:S(2)}) collective-permute-start(bf16[4,512,768]{2,1,0:T(8,128)(2,1)} %get-tuple-element.147), channel_id=1, source_target_pairs={{0,1},{1,0},{2,3},{3,2},{4,5},{5,4},{6,7},{7,6},{8,9},{9,8},{10,11... | collective-permute-start | bytes 9437192 | tf_op jit(solution)/shard_map/ppermute | solution.py:1141
  324.8 33.9 %all-to-all-start.1 = ((bf16[8,256,128]{2,1,0:T(8,128)(2,1)}), bf16[8,256,128]{2,1,0:T(8,128)(2,1)}, u32[]{:S(2)}, u32[]{:S(2)}) async-start(bf16[8,256,128]{2,1,0:T(8,128)(2,1)} %bitcast.106), calls=%async_computation.3 | async-start | bytes 1048576 | tf_op jit(solution)/shard_map/all_to_all | solution.py:929
  329.1 103.1 %reduce-scatter.9.cloned.1.call-start = ((), (), s32[]{:S(2)}) async-start(), calls=%async_computation.12 | async-start | bytes 2654208 | tf_op jit(solution)/shard_map/reduce_scatter | solution.py:80
  367.5 40.7 %collective-permute-start.31 = (bf16[2,512,768]{2,1,0:T(8,128)(2,1)}, bf16[2,512,768]{2,1,0:T(8,128)(2,1)S(1)}, u32[]{:S(2)}, u32[]{:S(2)}) collective-permute-start(bf16[2,512,768]{2,1,0:T(8,128)(2,1)} %get-tuple-element.252), channel_id=1, source_target_pairs={{0,2},{2,0},{1,3},{3,1},{4,6},{6,4},{5,7},{7,5},{8,10},{10,8},{9,1... | collective-permute-start | bytes 4718600 | tf_op jit(solution)/shard_map/ppermute | solution.py:133
  373.7 40.5 %collective-permute-start.32 = (bf16[2,512,768]{2,1,0:T(8,128)(2,1)}, bf16[2,512,768]{2,1,0:T(8,128)(2,1)}, u32[]{:S(2)}, u32[]{:S(2)}) collective-permute-start(bf16[2,512,768]{2,1,0:T(8,128)(2,1)} %get-tuple-element.250), channel_id=1, source_target_pairs={{0,4},{4,0},{1,5},{5,1},{2,6},{6,2},{3,7},{7,3},{8,12},{12,8},{9,1... | collective-permute-start | bytes 4718600 | tf_op jit(solution)/shard_map/ppermute | solution.py:133
  414.2 39.6 %all-to-all-start.2 = ((bf16[8,256,256]{2,1,0:T(8,128)(2,1)}), bf16[8,256,256]{2,1,0:T(8,128)(2,1)}, u32[]{:S(2)}, u32[]{:S(2)}) async-start(bf16[8,256,256]{2,1,0:T(8,128)(2,1)} %bitcast.115), calls=%async_computation.4 | async-start | bytes 2097152 | tf_op jit(solution)/shard_map/all_to_all | solution.py:929
  418.5 35.3 %reduce-scatter.11.cloned.1.call-start = ((), (), s32[]{:S(2)}) async-start(), calls=%async_computation.13 | async-start | bytes 368640 | tf_op jit(solution)/shard_map/reduce_scatter | solution.py:80
  435.6 24.1 %collective-permute-start.34 = (bf16[512,768]{1,0:T(8,128)(2,1)}, bf16[512,768]{1,0:T(8,128)(2,1)}, u32[]{:S(2)}, u32[]{:S(2)}) collective-permute-start(bf16[512,768]{1,0:T(8,128)(2,1)} %dynamic-slice_bitcast_fusion.4), channel_id=1, source_target_pairs={{0,2},{2,0},{1,3},{3,1},{4,6},{6,4},{5,7},{7,5},{8,10},{10,8},{9,1... | collective-permute-start | bytes 2359304 | tf_op jit(solution)/shard_map/ppermute | solution.py:133
  453.8 43.6 %all-to-all-start.3 = ((bf16[32,32,384]{2,1,0:T(8,128)(2,1)}), bf16[32,32,384]{2,1,0:T(8,128)(2,1)S(1)}, u32[]{:S(2)}, u32[]{:S(2)}) async-start(bf16[32,32,384]{2,1,0:T(8,128)(2,1)} %bitcast.55), calls=%async_computation.7 | async-start | bytes 1572864 | tf_op jit(solution)/shard_map/all_to_all | solution.py:929
  457.8 26.9 %collective-permute-start.33 = (bf16[512,768]{1,0:T(8,128)(2,1)S(1)}, bf16[512,768]{1,0:T(8,128)(2,1)S(1)}, u32[]{:S(2)}, u32[]{:S(2)}) collective-permute-start(bf16[512,768]{1,0:T(8,128)(2,1)S(1)} %dynamic-slice_bitcast_fusion.5), channel_id=1, source_target_pairs={{0,4},{4,0},{1,5},{5,1},{2,6},{6,2},{3,7},{7,3},{8,12},{12,8},{9,1... | collective-permute-start | bytes 2359304 | tf_op jit(solution)/shard_map/ppermute | solution.py:133
  (40 other events, 508.8 us)
Sparse Core Ops, SparseCore 0:
  11.5 62.7 all-gather.4
  77.8 72.0 all-gather.6
  152.0 51.7 all-gather.8
  267.7 49.0 reduce-scatter.4
  318.9 51.6 reduce-scatter.6
  374.2 57.9 reduce-scatter.8
  434.4 19.2 reduce-scatter.10

commit v5 on v4

--- a/solution.py
+++ b/solution.py
@@ -100,16 +100,6 @@
         up, down = hop(up, down)
         pieces += [(-k, up), (k, down)]
     return pieces
-
-
-def in_line(own, ups, downs, me):
-    n = lax.axis_size("a")
-    out = jnp.zeros((n,) + own.shape, own.dtype)
-    out = lax.dynamic_update_index_in_dim(out, own, me, 0)
-    for k in range(1, n):
-        piece = jnp.where(me >= k, ups[k - 1], downs[n - k - 1])
-        out = lax.dynamic_update_index_in_dim(out, piece, (me - k) % n, 0)
-    return out.reshape((n * own.shape[0],) + own.shape[1:])
 
 
 def by_columns(own, other, member):
@@ -727,26 +717,29 @@
     )(group, normed, early, packed, w_all, z)
 
 
-def expert_grads_kernel(half_ref, n_ref, ct_ref, w_ref, hidden_ref, pre_ref, y_ref, *refs):
-    grad_refs, (n_t, ct_t, acc) = refs[:-3], refs[-3:]
+def expert_grads_kernel(with_y, half_ref, n_ref, ct_ref, w_ref, hidden_ref, pre_ref, *refs):
+    if with_y:
+        left_ref, right_ref, y_ref, n_t, ct_t, acc = refs
+    else:
+        left_ref, right_ref, n_t, ct_t = refs
     e = pl.program_id(0)
+    cut = left_ref.shape[2]
 
     @pl.when(e == 0)
     def _():
         n_t[...] = jnp.transpose(n_ref[...])
         ct_t[...] = jnp.transpose(ct_ref[...])
-        acc[...] = jnp.zeros_like(acc)
-
-    for part in range(len(grad_refs) // 2):
-        left_ref, right_ref = grad_refs[2 * part : 2 * part + 2]
-        rows, cut = left_ref.shape[1:]
-        at = pl.ds(pl.multiple_of((half_ref[0] ^ part) * rows, rows), rows)
-        grads = jnp.dot(n_t[at, :], pre_ref[0], preferred_element_type=f32).astype(bf16)
-        left_ref[0] = grads[:, :cut]
-        right_ref[0, :, : 2 * F - cut] = grads[:, cut:]
-        right_ref[0, :, 2 * F - cut :] = (
-            RESIDUAL_SCALE * jnp.dot(ct_t[at, :], hidden_ref[0], preferred_element_type=f32)
-        ).astype(bf16)
+        if with_y:
+            acc[...] = jnp.zeros_like(acc)
+
+    grads = jnp.dot(n_t[...], pre_ref[0], preferred_element_type=f32).astype(bf16)
+    left_ref[0] = grads[:, :cut]
+    right_ref[0, :, : 2 * F - cut] = grads[:, cut:]
+    right_ref[0, :, 2 * F - cut :] = (
+        RESIDUAL_SCALE * jnp.dot(ct_t[...], hidden_ref[0], preferred_element_type=f32)
+    ).astype(bf16)
+    if not with_y:
+        return
     acc[...] += contract_cols(hidden_ref[0], w_ref[0, :, 2 * F :])
 
     @pl.when(e == pl.num_programs(0) - 1)
@@ -754,35 +747,39 @@
         y_ref[...] = acc[...].astype(bf16)
 
 
-def expert_grads(half, parts, normed, early, w_all, hidden, pre):
+def expert_grads(half, halves, normed, early, w_all, hidden, pre, with_y):
     rows, width = normed.shape
     count = w_all.shape[0]
-    own, cut = width // parts, 3 * F // 2
-    whole = pl.BlockSpec((rows, width), lambda e, h: (0, 0))
+    own, cut = width // halves, 3 * F // 2
+    feature = pl.BlockSpec((rows, own), lambda e, h: (0, h[0]))
+    out_specs = [pl.BlockSpec((1, own, cut), lambda e, h: (e, 0, 0))] * 2
+    out_shape = [jax.ShapeDtypeStruct((count, own, cut), bf16)] * 2
+    scratch = [pltpu.VMEM((own, rows), bf16), pltpu.VMEM((own, rows), bf16)]
+    if with_y:
+        out_specs.append(pl.BlockSpec((rows, width), lambda e, h: (0, 0)))
+        out_shape.append(jax.ShapeDtypeStruct((rows, width), bf16))
+        scratch.append(pltpu.VMEM((rows, width), f32))
     return pl.pallas_call(
-        expert_grads_kernel,
+        functools.partial(expert_grads_kernel, with_y),
         grid_spec=pltpu.PrefetchScalarGridSpec(
             num_scalar_prefetch=1,
             grid=(count,),
             in_specs=[
-                whole,
-                whole,
+                feature,
+                feature,
                 pl.BlockSpec((1, width, 3 * F), lambda e, h: (e, 0, 0)),
                 pl.BlockSpec((1, rows, F), lambda e, h: (e, 0, 0)),
                 pl.BlockSpec((1, rows, 2 * F), lambda e, h: (e, 0, 0)),
             ],
-            out_specs=[whole] + [pl.BlockSpec((1, own, cut), lambda e, h: (e, 0, 0))] * (2 * parts),
-            scratch_shapes=[
-                pltpu.VMEM((width, rows), bf16),
-                pltpu.VMEM((width, rows), bf16),
-                pltpu.VMEM((rows, width), f32),
-            ],
-        ),
-        out_shape=[jax.ShapeDtypeStruct((rows, width), bf16)]
-        + [jax.ShapeDtypeStruct((count, own, cut), bf16)] * (2 * parts),
+            out_specs=out_specs,
+            scratch_shapes=scratch,
+        ),
+        out_shape=out_shape,
         compiler_params=pltpu.CompilerParams(vmem_limit_bytes=VMEM_LIMIT),
         cost_estimate=pl.CostEstimate(
-            flops=2 * count * rows * width * 4 * F, bytes_accessed=40 * 2**20, transcendentals=0
+            flops=2 * count * rows * width * 3 * F // halves + 2 * with_y * count * rows * width * F,
+            bytes_accessed=30 * 2**20,
+            transcendentals=0,
         ),
         name="expert_grads",
     )(half, normed, early, w_all, hidden, pre)
@@ -989,28 +986,24 @@
         axis=2,
     ).reshape(own_rows, KEY_VALUE_HEADS * HEAD_PACK)
     qkv_width = KEY_VALUE_HEADS * HEAD_PACK
-    second_all = gather(
-        jnp.concatenate(
-            [
-                w_output.astype(bf16),
-                pad_lanes(
-                    jnp.concatenate(
-                        [
-                            w_router.astype(bf16),
-                            norm_attn.astype(bf16)[:, None],
-                            norm_moe.astype(bf16)[:, None],
-                        ],
-                        axis=1,
-                    ),
-                    LANES,
-                ),
-            ],
-            axis=1,
-        ),
-        ALL,
-    )
-    qkv_all = gather(by_head, ALL)
-    experts_low = jnp.concatenate([expert_in.astype(bf16), expert_out.astype(bf16)], axis=1)
+    expert_ids = jnp.arange(E, dtype=jnp.int32)
+    routed_own = jnp.any(routes[0][:, :, None] == expert_ids[None, None, :], axis=1)
+    small = jnp.concatenate(
+        [
+            w_router.astype(bf16),
+            norm_attn.astype(bf16)[:, None],
+            norm_moe.astype(bf16)[:, None],
+        ],
+        axis=1,
+    )
+    wide = width + LANES
+    packed = (
+        jnp.concatenate([cotangent[0], pad_lanes(routed_own.astype(bf16), LANES)], axis=1),
+        jnp.concatenate([w_output.astype(bf16), pad_lanes(small, LANES)], axis=1),
+        by_head[:, :wide],
+        pad_lanes(by_head[:, wide:], wide),
+    )
+    lines = gather(jnp.concatenate(packed), "a").reshape(GROUPS, -1, wide)
     if by_column:
         two = by_head.reshape(own_rows, GROUPS, 2 * HEAD_PACK).transpose(1, 0, 2)
         gains = pad_lanes(norm_attn.astype(bf16)[:, None], LANES)
@@ -1024,13 +1017,26 @@
         pieces = line_gather(tokens[0])
         places = [piece[0] for piece in pieces]
         blocks = tuple(piece[1] for piece in pieces)
-    else:
+        lines, blocks, weights = lax.optimization_barrier((lines, blocks, weights))
+    ends = [token_count + k * own_rows for k in range(4)]
+    early_all = lines[:, : ends[0]].reshape(-1, wide)
+
+    def across(x):
+        x = gather(x.reshape(-1, x.shape[2]), PLANE).reshape(-1, GROUPS, own_rows, x.shape[2])
+        return x.transpose(1, 0, 2, 3).reshape(-1, x.shape[3])
+
+    second_all = across(lines[:, ends[0] : ends[1]])
+    qkv_lines = jnp.concatenate(
+        [lines[:, ends[1] : ends[2]], lines[:, ends[2] : ends[3], : qkv_width - wide]], axis=2
+    )
+    experts_low = jnp.concatenate([expert_in.astype(bf16), expert_out.astype(bf16)], axis=1)
+    if not by_column:
         at = lax.axis_index(head_axes) * HEAD_PACK
         gains = pad_lanes(second_all[:, width + E : width + E + 1], LANES)
         spots, places = None, None
         weights = (
             jnp.concatenate(
-                [lax.dynamic_slice_in_dim(qkv_all, at, HEAD_PACK, 1), gains], axis=1
+                [lax.dynamic_slice_in_dim(across(qkv_lines), at, HEAD_PACK, 1), gains], axis=1
             ),
         )
         blocks = (gather(tokens[0], "b").reshape((-1,) + tokens.shape[1:]),)
@@ -1042,9 +1048,6 @@
             )
         )
     )
-    expert_ids = jnp.arange(E, dtype=jnp.int32)
-    routed_own = jnp.any(routes[0][:, :, None] == expert_ids[None, None, :], axis=1)
-    early = jnp.concatenate([cotangent[0], pad_lanes(routed_own.astype(bf16), LANES)], axis=1)
     if by_column:
         beside = neighbours(experts_low)
     else:
@@ -1057,29 +1060,20 @@
     own_weights = own_weights.reshape(width, own_weights.shape[-1])
     if by_column:
         columns = (GROUPS, token_count)
-        early, q = lax.optimization_barrier((early, q))
-        up, down = hop(early, early)
-        ups, downs = [up], [down]
 
         def in_row(own, other, shape):
             return by_columns(own.reshape(shape), other.reshape(shape), member)
 
         kv_other = lax.ppermute(kv, "b", SWAP)
         kv = in_row(kv, kv_other, columns + (2 * PAIR,)).reshape(span, 2 * PAIR)
-        kv, up, down = lax.optimization_barrier((kv, up, down))
-        up, down = hop(up, down)
-        ups, downs = ups + [up], downs + [down]
     else:
         kv = gather(kv, "a")
-        early_all = gather(early, "a")
     attention_result, attended, log_total = attend(
         bounds_ahead, q, kv, docs_ahead, 2 if by_column else 1
     )
     if by_column:
-        attended, second_all, up, down = lax.optimization_barrier((attended, second_all, up, down))
-        up, down = hop(up, down)
-        early_all = in_line(early, ups + [up], downs + [down], group)
-        attended, qkv_all = lax.optimization_barrier((attended, qkv_all))
+        attended, second_all = lax.optimization_barrier((attended, second_all))
+        attended, early_all = lax.optimization_barrier((attended, early_all))
         outs = lax.all_gather(attended, "a", axis=0, tiled=False)
         parts = plane_gather(experts_low, *beside)
 
@@ -1099,6 +1093,7 @@
             (outs, experts_all, q_other, out_other, log_other)
         )
         normed_all, resid, attended_low = join(place, outs, second_all, 0, x_span)
+        qkv_lines, outs = lax.optimization_barrier((qkv_lines, outs))
         normed_two = lax.dynamic_slice_in_dim(normed_all, group * token_count, token_count)
     else:
         attended_low = (
@@ -1132,18 +1127,26 @@
         log_total = in_row(by_block(log_total), by_block(log_other), (GROUPS, 2, BLOCK))
         log_total = log_total.transpose(0, 2, 1, 3)
     log_total = log_total.reshape(-1, 1, 2 * QUERY_BLOCK)
+    qkv_all = across(qkv_lines)
+    if by_column:
+        back_part, qkv_all = lax.optimization_barrier((back_part, qkv_all))
     back_own = scatter_sum(back_part, "a")
     inputs = (normed_all, early_all, experts_all, gated_hidden, grad_pre)
     if by_column:
         core = lax.axis_index("c")
         x_other = lax.ppermute(x_span, "b", SWAP)
-        moe_part, *keep, send_left, send_right = expert_grads(core.reshape(1), 2, *inputs)
-        arrived = [lax.ppermute(x, "c", SWAP) for x in (send_left, send_right)]
-        back_own, moe_part, keep, x_other = lax.optimization_barrier(
-            (back_own, moe_part, keep, x_other)
-        )
+        send = expert_grads((1 - core).reshape(1), 2, *inputs, False)
+        arrived = [lax.ppermute(x, "c", SWAP) for x in send]
+        *keep, moe_part = expert_grads(core.reshape(1), 2, *inputs, True)
+        left, right = (
+            halve_add(terms).reshape((2, 2) + terms[0].shape[1:]) for terms in zip(keep, arrived)
+        )
+        back_own, moe_part, left, right, x_other = lax.optimization_barrier(
+            (back_own, moe_part, left, right, x_other)
+        )
+        left, right = halve_send(left, "y", 1), halve_send(right, "b", 0)
     else:
-        moe_part, *grads = expert_grads(jnp.zeros((1,), jnp.int32), 1, *inputs)
+        *grads, moe_part = expert_grads(jnp.zeros((1,), jnp.int32), 1, *inputs, True)
         grad_experts = jnp.concatenate(grads, axis=2)
         back_own, moe_part, grad_experts = lax.optimization_barrier(
             (back_own, moe_part, grad_experts)
@@ -1175,15 +1178,13 @@
         [contract_rows(attended_low, grad_attn_low), pad_lanes(small, LANES)], axis=1
     ).astype(bf16)
     cols = second_part.shape[1]
-    if by_column:
-        keep, arrived, second_part = lax.optimization_barrier((keep, arrived, second_part))
-        left, right = (
-            halve_add(terms).reshape((2, 2) + terms[0].shape[1:]) for terms in zip(keep, arrived)
-        )
-        left, right = halve_send(left, "y", 1), halve_send(right, "b", 0)
     second_part = second_part.reshape(GROUPS, -1, own_rows, cols).transpose(1, 0, 2, 3)
     if by_column:
-        second_part, grad_mixed = lax.optimization_barrier((second_part, grad_mixed))
+        left, right = halve_add(left), halve_add(right)
+        second_part, left, right, grad_mixed = lax.optimization_barrier(
+            (second_part, left, right, grad_mixed)
+        )
+        left, right = halve_send(left, "b", 0), halve_send(right, "y", 0)
     rest = scatter_sum(second_part.reshape(-1, cols), PLANE)
     grads = attend_back(
         bounds, q, kv, doc_rows, grad_mixed, attention_result, log_total, wide_cos, wide_sin,
@@ -1191,8 +1192,6 @@
     )
     if by_column:
         left, right, moe_sum, grad_pack = lax.optimization_barrier((left, right, moe_sum, grads))
-        left, right = halve_add(left), halve_add(right)
-        left, right = halve_send(left, "b", 0), halve_send(right, "y", 0)
         first_part = head_grads(
             x_span, x_other, member, 1 - member, 2, member, own_weights, grad_pack
         )
@@ -1206,7 +1205,7 @@
     rest, first_part = lax.optimization_barrier((rest, first_part))
     rest = scatter_sum(rest, "a")
     by_tokens = exchange(grad_pack.reshape(KEY_VALUE_HEADS, token_count, HEAD_PACK), head_axes)
-    by_tokens, first_part, rest = lax.optimization_barrier((by_tokens, first_part, rest))
+    by_tokens, first_part = lax.optimization_barrier((by_tokens, first_part))
     sums = exchange(first_part.reshape(-1, own_rows, first_part.shape[1]), ALL)
     grad_input = token_grads(by_tokens, qkv_all, second_all, tokens[0], grad_resid)
     sums, moe_sum, resid, grad_input = lax.optimization_barrier((sums, moe_sum, resid, grad_input))

time: 520 us -> 538 us (1.035)
  waiting for transfers between devices: 174 us -> 157 us
  Pallas kernels: 158 us -> 169 us
  other arithmetic: 43 us -> 53 us
  starting transfers between devices: 73.6 us -> 83 us
  local copies, waits for them, and re-layouts: 42 us -> 47.9 us
    all_gather x2 -> x3, waiting for transfers between devices: 18.1 us -> 0.01 us  [gather(): return lax.all_gather(x, axes, axis=0, tiled=True)]
    ppermute x1, waiting for transfers between devices: 0.01 us -> 15.8 us  [plane_gather(): upper = lax.ppermute(from_b[:half], 'y', SWAP)]
    ppermute x6 -> x3, starting transfers between devices: 27.4 us -> 41.9 us  [hop(): lax.ppermute(up, 'a', line_pairs(n, 1))]
    ppermute x6 -> x3, waiting for transfers between devices: 24.5 us -> 13.6 us  [hop(): lax.ppermute(down, 'a', line_pairs(n, -1))]
    transpose x0 -> x2, local copies, waits for them, and re-layouts: none -> 7.99 us  [across(): return x.transpose(1, 0, 2, 3).reshape(-1, x.shape[3])]
    all_to_all x4, waiting for transfers between devices: 25.7 us -> 18.9 us  [exchange(): return lax.all_to_all(x, axes, 0, 0, tiled=True)]
    ppermute x2, waiting for transfers between devices: 0.01 us -> 6.41 us  [neighbours(): return (lax.ppermute(x, 'y', SWAP), lax.ppermute(x, 'b', SWAP))]
    pallas_call x1 -> x2, Pallas kernels: 26.7 us -> 33 us  [expert_grads(): pl.pallas_call(functools.partial(expert_grads_kernel, with_y), grid_spec=...]
  transfers between devices with their start and end apart: 46 -> 41, of which waited for: 19 -> 16; matrix products, arithmetic and copies ran while one was open for 16% -> 16% of each run, Pallas kernels for 23% -> 31%
where the time goes in v5:
time: 538 us; the launch traced here: 530 us
  Pallas kernels  169 us (31%)
  waiting for transfers between devices  157 us (29%)
  starting transfers between devices  83 us (15%)
  other arithmetic  53 us (10%)
  local copies, waits for them, and re-layouts  47.9 us (9%)
  between operations  15.4 us (3%)
    ppermute x3, starting transfers between devices, hop(): lax.ppermute(up, 'a', line_pairs(n, 1))  41.9 us
    pallas_call x2, Pallas kernels, expert_grads(): pl.pallas_call(functools.partial(expert_grads_kernel, with_y), grid_spec=...  33 us
    pallas_call x1, Pallas kernels, experts(): pl.pallas_call(experts_kernel, grid_spec=pltpu.PrefetchScalarGridSpec(num...  29.1 us
    pallas_call x1, Pallas kernels, attend_back(): pl.pallas_call(functools.partial(attend_back_kernel, fold), grid_spec=plt...  27.9 us
    ppermute x4, waiting for transfers between devices, halve_send(): lax.ppermute(lax.dynamic_index_in_dim(v, 1 - me, at, False), axis, SWAP)  26.7 us
    ppermute x3, waiting for transfers between devices, hop(): lax.ppermute(up, 'a', line_pairs(n, 1))  23.2 us
    reduce_scatter x4, waiting for transfers between devices, scatter_sum(): return lax.psum_scatter(x, axes, scatter_dimension=0, tiled=True)  20.4 us
    all_to_all x4, starting transfers between devices, exchange(): return lax.all_to_all(x, axes, 0, 0, tiled=True)  19 us
  transfers between devices with their start and end apart: 41, of which 16 were waited for; matrix products, arithmetic and copies ran while one was open for 16% of the time, Pallas kernels for 31%

profile of v5, /device:TPU:0, one launch (start us, length us, event | category | flops | bytes accessed | tf_op | source)
XLA Modules:
  0.0 529.6 jit_solution(685910369596456672)
XLA Ops:
  15.5 5.8 %collective-permute-start = (bf16[256,1024]{1,0:T(8,128)(2,1)S(1)}, bf16[256,1024]{1,0:T(8,128)(2,1)}, u32[]{:S(2)}, u32[]{:S(2)}) collective-permute-start(bf16[256,1024]{1,0:T(8,128)(2,1)S(1)} %bitcast.145), channel_id=1, source_target_pairs={{0,8},{8,16},{16,24},{1,9},{9,17},{17,25},{2,10},{10,18},{18,26},{... | collective-permute-start | bytes 1572872 | tf_op jit(solution)/shard_map/ppermute | solution.py:93
  23.6 7.0 %all-to-all-start = ((bf16[8,32,640]{2,1,0:T(8,128)(2,1)}), bf16[8,32,640]{2,1,0:T(8,128)(2,1)S(1)}, u32[]{:S(2)}, u32[]{:S(2)}) async-start(bf16[8,32,640]{2,1,0:T(8,128)(2,1)} %bitcast.11), calls=%async_computation | async-start | bytes 655360 | tf_op jit(solution)/shard_map/all_to_all | solution.py:926
  30.6 7.9 %collective-permute-done.refs_1_ = bf16[256,1024]{1,0:T(8,128)(2,1)} collective-permute-done((bf16[256,1024]{1,0:T(8,128)(2,1)S(1)}, bf16[256,1024]{1,0:T(8,128)(2,1)}, u32[]{:S(2)}, u32[]{:S(2)}) %collective-permute-start) | collective-permute-done | bytes 524320 | tf_op jit(solution)/shard_map/ppermute | solution.py:93
  38.6 10.5 %collective-permute-start.2 = (bf16[256,1024]{1,0:T(8,128)(2,1)}, bf16[256,1024]{1,0:T(8,128)(2,1)}, u32[]{:S(2)}, u32[]{:S(2)}) collective-permute-start(bf16[256,1024]{1,0:T(8,128)(2,1)} %collective-permute-done.refs_1_), channel_id=1, source_target_pairs={{0,8},{8,16},{16,24},{1,9},{9,17},{17,25},{2,10},{10,18},{18,26},{... | collective-permute-start | bytes 1572872 | tf_op jit(solution)/shard_map/ppermute | solution.py:93
  49.1 8.9 %collective-permute-done.1.refs_2_ = bf16[256,1024]{1,0:T(8,128)(2,1)} collective-permute-done((bf16[256,1024]{1,0:T(8,128)(2,1)S(1)}, bf16[256,1024]{1,0:T(8,128)(2,1)}, u32[]{:S(2)}, u32[]{:S(2)}) %collective-permute-start.1) | collective-permute-done | bytes 524320 | tf_op jit(solution)/shard_map/ppermute | solution.py:93
  59.3 6.2 %all-to-all-done.refs_7_ = bf16[8,32,640]{2,1,0:T(8,128)(2,1)S(1)} async-done(((bf16[8,32,640]{2,1,0:T(8,128)(2,1)}), bf16[8,32,640]{2,1,0:T(8,128)(2,1)S(1)}, u32[]{:S(2)}, u32[]{:S(2)}) %all-to-all-start) | async-done | bytes 327712 | tf_op jit(solution)/shard_map/all_to_all | solution.py:926
  67.2 3.6 collective-permute-done.2.refs_3_
  70.8 25.6 %collective-permute-start.4 = (bf16[256,1024]{1,0:T(8,128)(2,1)}, bf16[256,1024]{1,0:T(8,128)(2,1)}, u32[]{:S(2)}, u32[]{:S(2)}) collective-permute-start(bf16[256,1024]{1,0:T(8,128)(2,1)} %collective-permute-done.2.refs_3_), channel_id=1, source_target_pairs={{0,8},{8,16},{16,24},{1,9},{9,17},{17,25},{2,10},{10,18},{18,26},{... | collective-permute-start | bytes 1572872 | tf_op jit(solution)/shard_map/ppermute | solution.py:93
  100.1 11.7 %collective-permute-done.4.refs_5_ = bf16[256,1024]{1,0:T(8,128)(2,1)} collective-permute-done((bf16[256,1024]{1,0:T(8,128)(2,1)}, bf16[256,1024]{1,0:T(8,128)(2,1)}, u32[]{:S(2)}, u32[]{:S(2)}) %collective-permute-start.4) | collective-permute-done | bytes 524320 | tf_op jit(solution)/shard_map/ppermute | solution.py:93
  111.8 4.7 collective-permute-done.5.refs_6_
  116.5 1.8 fusion.30
  118.5 2.1 convert_element_type.142
  120.7 1.8 convert_reduce_fusion
  123.2 5.5 %multiply_sine_fusion = (f32[2048,32]{1,0:T(8,128)}, f32[2048,32]{1,0:T(8,128)}) fusion(f32[2048]{0:T(1024)S(1)} %subtract_convert_fusion, f32[32]{0:T(128)S(1)} %multiply_power_fusion), kind=kLoop, calls=%fused_computation.20 | loop fusion | flops 65536 | bytes 532608 | tf_op jit(solution)/shard_map/sin | solution.py:44
  128.8 4.5 spread.1
  135.1 2.7 dynamic-slice_sine_fusion
  139.0 8.1 %project.1 = (bf16[1024,256]{1,0:T(8,128)(2,1)}, bf16[1024,256]{1,0:T(8,128)(2,1)}, bf16[1024,1024]{1,0:T(8,128)(2,1)}, bf16[8,4,32,640]{3,2,1,0:T(8,128)(2,1)}) custom-call(s32[4]{0:T(128)} %pad_add_fusion.place_ref, bf16[256,1024]{1,0:T(8,128)(2,1)} %bitcast.143, bf16[256,1024]{1,0:T(8,128)(2,1)} %collective-permute-done.refs_1_, ...), custom_call_target="tpu_custom_call" | custom-call | flops 1073741824 | bytes 8388608 | tf_op jit(solution)/shard_map/project/pallas_call | solution.py:218
  152.4 10.1 %collective-permute-done.9 = bf16[1024,256]{1,0:T(8,128)(2,1)} collective-permute-done((bf16[1024,256]{1,0:T(8,128)(2,1)}, bf16[1024,256]{1,0:T(8,128)(2,1)}, u32[]{:S(2)}, u32[]{:S(2)}) %collective-permute-start.9) | collective-permute-done | bytes 524320 | tf_op jit(solution)/shard_map/ppermute | solution.py:1067
  164.6 18.6 %attend.1 = (f32[1024,256]{1,0:T(8,128)}, bf16[1024,256]{1,0:T(8,128)(2,1)}, f32[2,2,1,1024]{3,2,1,0:T(1,128)}) custom-call(s32[5]{0:T(128)} %pad_add_fusion.1.bounds_ref, bf16[1024,256]{1,0:T(8,128)(2,1)} %get-tuple-element.130.q_ref, bf16[2048,256]{1,0:T(8,128)(2,1)} %bitcast.158, s32[2,1,512]{2,1,0:T(1,128)} %bitcast.176), custom_call_target="tpu_custom_call" | custom-call | flops 2147483648 | bytes 6291456 | tf_op jit(solution)/shard_map/attend/pallas_call | solution.py:409
  183.2 3.3 copy.112
  187.3 6.4 %collective-permute-done.13.refs_4_ = bf16[512,1536]{1,0:T(8,128)(2,1)} collective-permute-done((bf16[512,1536]{1,0:T(8,128)(2,1)}, bf16[512,1536]{1,0:T(8,128)(2,1)}, u32[]{:S(2)}, u32[]{:S(2)}) %collective-permute-start.13) | collective-permute-done | bytes 1572896 | tf_op jit(solution)/shard_map/ppermute | solution.py:111
  199.2 15.8 %collective-permute-done.15.refs_6_ = bf16[256,1536]{1,0:T(8,128)(2,1)} collective-permute-done((bf16[256,1536]{1,0:T(8,128)(2,1)S(1)}, bf16[256,1536]{1,0:T(8,128)(2,1)}, u32[]{:S(2)}, u32[]{:S(2)}) %collective-permute-start.15) | collective-permute-done | bytes 786464 | tf_op jit(solution)/shard_map/ppermute | solution.py:116
  215.1 2.5 collective-permute-done.17.refs_8_
  223.9 1.9 constant_dynamic-slice_fusion.1
  228.0 18.5 %place_experts.1 = (bf16[4,1024,1536]{2,1,0:T(8,128)(2,1)}, f32[4,1024,512]{2,1,0:T(8,128)}) custom-call(s32[2]{0:T(128)} %pad_add_fusion.2.place_ref, bf16[512,1536]{1,0:T(8,128)(2,1)} %pad_maximum_fusion.2.refs_0_, bf16[512,1536]{1,0:T(8,128)(2,1)} %collective-permute-done.10.refs_1_, bf16[512,1536]{1,0:T(8,128)(2,1)} %collective-permute-done.11.refs_2_, ...), custom_call_target="tpu_custom_call" | custom-call | flops 4294967296 | bytes 37748736 | tf_op jit(solution)/shard_map/place_experts/pallas_call | solution.py:604
  246.6 8.3 %join.1 = (bf16[1024,1024]{1,0:T(8,128)(2,1)}, f32[256,1024]{1,0:T(8,128)}, bf16[256,1024]{1,0:T(8,128)(2,1)}) custom-call(s32[4]{0:T(128)} %pad_add_fusion.place_ref, bf16[4,1024,256]{2,1,0:T(8,128)(2,1)} %bitcast.142, bf16[1024,1152]{1,0:T(8,128)(2,1)} %bitcast.114, bf16[1024,1152]{1,0:T(8,128)(2,1)} %bitcast.115, ...), custom_call_target="tpu_custom_call" | custom-call | flops 2147483648 | bytes 12582912 | tf_op jit(solution)/shard_map/join/pallas_call | solution.py:813
  254.9 29.1 %experts.1 = (bf16[1024,1152]{1,0:T(8,128)(2,1)}, f32[1024,128]{1,0:T(8,128)}, bf16[4,1024,512]{2,1,0:T(8,128)(2,1)}, bf16[4,1024,1024]{2,1,0:T(8,128)(2,1)}) custom-call(s32[1]{0:T(128)} %bitcast.group_ref, bf16[1024,1024]{1,0:T(8,128)(2,1)} %get-tuple-element.147.n_ref, bf16[1024,1152]{1,0:T(8,128)(2,1)} %bitcast.128, bf16[1024,1152]{1,0:T(8,128)(2,1)} %bitcast.116, ...), custom_call_target="tpu_custom_call" | custom-call | flops 17179869184 | bytes 41943040 | tf_op jit(solution)/shard_map/experts/pallas_call | solution.py:686
  284.0 4.7 copy.114
  289.0 14.4 %expert_grads.3 = (bf16[4,512,768]{2,1,0:T(8,128)(2,1)}, bf16[4,512,768]{2,1,0:T(8,128)(2,1)}) custom-call(s32[1]{0:T(128)} %bitcast.34.half_ref, bf16[1024,1024]{1,0:T(8,128)(2,1)} %get-tuple-element.147.n_ref, bf16[1024,1152]{1,0:T(8,128)(2,1)} %bitcast.129, bf16[4,1024,1536]{2,1,0:T(8,128)(2,1)} %get-tuple-element.148.w_ref, ...), custom_call_target="tpu_custom_call" | custom-call | flops 6442450944 | bytes 31457280 | tf_op jit(solution)/shard_map/expert_grads/pallas_call | solution.py:762
  304.6 18.6 %expert_grads.2 = (bf16[4,512,768]{2,1,0:T(8,128)(2,1)}, bf16[4,512,768]{2,1,0:T(8,128)(2,1)}, bf16[1024,1024]{1,0:T(8,128)(2,1)}) custom-call(s32[1]{0:T(128)} %bitcast.3.half_ref, bf16[1024,1024]{1,0:T(8,128)(2,1)} %get-tuple-element.147.n_ref, bf16[1024,1152]{1,0:T(8,128)(2,1)} %bitcast.130, bf16[4,1024,1536]{2,1,0:T(8,128)(2,1)} %get-tuple-element.148.w_ref, ...), custom_call_target="tpu_custom_call" | custom-call | flops 10737418240 | bytes 31457280 | tf_op jit(solution)/shard_map/expert_grads/pallas_call | solution.py:762
  323.2 5.4 %add_convert_fusion.1 = bf16[4,512,768]{2,1,0:T(8,128)(2,1)} fusion(bf16[4,512,768]{2,1,0:T(8,128)(2,1)} %collective-permute-done.22, bf16[4,512,768]{2,1,0:T(8,128)(2,1)} %get-tuple-element.156), kind=kLoop, calls=%fused_computation.2 | loop fusion | flops 6291456 | bytes 9437184 | tf_op jit(solution)/shard_map/convert_element_type | solution.py:129
  330.3 4.5 add_convert_fusion
  334.9 16.9 %collective-permute-done.24.other_ref = bf16[1024,1024]{1,0:T(8,128)(2,1)} collective-permute-done((bf16[1024,1024]{1,0:T(8,128)(2,1)}, bf16[1024,1024]{1,0:T(8,128)(2,1)}, u32[]{:S(2)}, u32[]{:S(2)}) %collective-permute-start.24) | collective-permute-done | bytes 2097184 | tf_op jit(solution)/shard_map/ppermute | solution.py:1137
  352.4 1.8 copy.129
  367.7 4.8 all-to-all-start.1
  373.6 1.8 copy_bitcast_fusion
  375.4 26.7 %collective-permute-done.26 = bf16[2,512,768]{2,1,0:T(8,128)(2,1)} collective-permute-done((bf16[2,512,768]{2,1,0:T(8,128)(2,1)}, bf16[2,512,768]{2,1,0:T(8,128)(2,1)}, u32[]{:S(2)}, u32[]{:S(2)}) %collective-permute-start.26) | collective-permute-done | bytes 1572896 | tf_op jit(solution)/shard_map/ppermute | solution.py:123
  402.1 1.8 fusion
  404.0 3.0 fusion.1
  412.2 2.7 dynamic-slice_bitcast_fusion.4
  418.8 27.9 %attend_back.1.grad_ref = bf16[2048,256]{1,0:T(8,128)(2,1)} custom-call(s32[10]{0:T(128)} %pad_add_fusion.3.bounds_ref, bf16[2048,128]{1,0:T(8,128)(2,1)} %bitcast.163, bf16[2048,256]{1,0:T(8,128)(2,1)} %bitcast.159, s32[4,1,512]{2,1,0:T(1,128)} %bitcast.171, bf16[2048,128]{1,0:T(8,128)(2,1)} %bitcast.162, f32[2048,128]{1,0:T(8,128)} %bitcast.160, ...), custom_call_target="tpu_custom_call" | custom-call | flops 5368709120 | bytes 8388608 | tf_op jit(solution)/shard_map/attend_back/pallas_call | solution.py:529
  447.6 4.5 all-to-all-start.2
  452.7 10.1 %head_grads.1 = bf16[1024,384]{1,0:T(8,128)(2,1)} custom-call(s32[3]{0:T(128)} %pad_add_fusion.4.place_ref, bf16[1024,1024]{1,0:T(8,128)(2,1)} %get-tuple-element.144.x_ref.own_ref, bf16[1024,1024]{1,0:T(8,128)(2,1)} %collective-permute-done.24.other_ref, bf16[1024,640]{1,0:T(8,128)(2,1)} %bitcast.132, bf16[1024,640]{1,0:T(8,128)(2,1)} %bitcast.133, ...), custom_call_target="tpu_custom_call" | custom-call | flops 2147483648 | bytes 8388608 | tf_op jit(solution)/shard_map/head_grads/pallas_call | solution.py:307
  462.9 12.7 %all-to-all-done.2.grad_ref = bf16[8,256,256]{2,1,0:T(8,128)(2,1)S(1)} async-done(((bf16[8,256,256]{2,1,0:T(8,128)(2,1)}), bf16[8,256,256]{2,1,0:T(8,128)(2,1)S(1)}, u32[]{:S(2)}, u32[]{:S(2)}) %all-to-all-start.2) | async-done | bytes 1048608 | tf_op jit(solution)/shard_map/all_to_all | solution.py:926
  475.6 2.6 all-to-all-start.3
  483.6 20.4 %reduce-scatter.11.cloned.1.call-done = bf16[32,1152]{1,0:T(8,128)(2,1)} async-done(((bf16[128,1152]{1,0:T(8,128)(2,1)}), bf16[32,1152]{1,0:T(8,128)(2,1)}) %reduce-scatter.11.cloned.1.call-update) | async-done | bytes 73744 | tf_op jit(solution)/shard_map/reduce_scatter | solution.py:80
  508.4 8.8 %token_grads.1 = f32[256,1024]{1,0:T(8,128)} custom-call(bf16[8,256,256]{2,1,0:T(8,128)(2,1)} %copy-done.8, bf16[1024,2048]{1,0:T(8,128)(2,1)} %bitcast.121, bf16[1024,1152]{1,0:T(8,128)(2,1)} %bitcast.117, bf16[256,1024]{1,0:T(8,128)(2,1)} %bitcast.144, f32[256,1024]{1,0:T(8,128)} %copy-done.6), custom_call_target="tpu_custom_call" | custom-call | flops 1073741824 | bytes 8388608 | tf_op jit(solution)/shard_map/token_grads/pallas_call | solution.py:867
  518.1 1.9 weight_sums.1
  (254 shorter events, 85.3 us)
Async XLA Ops:
  7.2 109.3 %all-gather.6.cloned.1.call-start = ((), (), s32[]{:S(2)}) async-start(), calls=%async_computation.8 | async-start | bytes 4055040 | tf_op jit(solution)/shard_map/all_gather | solution.py:76
  15.5 23.0 %collective-permute-start = (bf16[256,1024]{1,0:T(8,128)(2,1)S(1)}, bf16[256,1024]{1,0:T(8,128)(2,1)}, u32[]{:S(2)}, u32[]{:S(2)}) collective-permute-start(bf16[256,1024]{1,0:T(8,128)(2,1)S(1)} %bitcast.145), channel_id=1, source_target_pairs={{0,8},{8,16},{16,24},{1,9},{9,17},{17,25},{2,10},{10,18},{18,26},{... | collective-permute-start | bytes 1572872 | tf_op jit(solution)/shard_map/ppermute | solution.py:93
  21.3 36.7 %collective-permute-start.1 = (bf16[256,1024]{1,0:T(8,128)(2,1)S(1)}, bf16[256,1024]{1,0:T(8,128)(2,1)}, u32[]{:S(2)}, u32[]{:S(2)}) collective-permute-start(bf16[256,1024]{1,0:T(8,128)(2,1)S(1)} %bitcast.146), channel_id=1, source_target_pairs={{8,0},{16,8},{24,16},{9,1},{17,9},{25,17},{10,2},{18,10},{26,18},{... | collective-permute-start | bytes 1572872 | tf_op jit(solution)/shard_map/ppermute | solution.py:93
  22.8 97.8 %copy-start.15 = (f32[512,1024]{1,0:T(8,128)S(1)}, f32[512,1024]{1,0:T(8,128)}, u32[]{:S(2)}) copy-start(f32[512,1024]{1,0:T(8,128)} %param.24) | copy-start | bytes 6291460
  23.6 41.9 %all-to-all-start = ((bf16[8,32,640]{2,1,0:T(8,128)(2,1)}), bf16[8,32,640]{2,1,0:T(8,128)(2,1)S(1)}, u32[]{:S(2)}, u32[]{:S(2)}) async-start(bf16[8,32,640]{2,1,0:T(8,128)(2,1)} %bitcast.11), calls=%async_computation | async-start | bytes 655360 | tf_op jit(solution)/shard_map/all_to_all | solution.py:926
  30.6 152.6 %all-gather.8.cloned.1.call-start = ((), (), s32[]{:S(2)}) async-start(), calls=%async_computation.9 | async-start | bytes 2654208 | tf_op jit(solution)/shard_map/all_gather | solution.py:76
  38.6 32.2 %collective-permute-start.2 = (bf16[256,1024]{1,0:T(8,128)(2,1)}, bf16[256,1024]{1,0:T(8,128)(2,1)}, u32[]{:S(2)}, u32[]{:S(2)}) collective-permute-start(bf16[256,1024]{1,0:T(8,128)(2,1)} %collective-permute-done.refs_1_), channel_id=1, source_target_pairs={{0,8},{8,16},{16,24},{1,9},{9,17},{17,25},{2,10},{10,18},{18,26},{... | collective-permute-start | bytes 1572872 | tf_op jit(solution)/shard_map/ppermute | solution.py:93
  58.0 38.4 %collective-permute-start.3 = (bf16[256,1024]{1,0:T(8,128)(2,1)}, bf16[256,1024]{1,0:T(8,128)(2,1)S(1)}, u32[]{:S(2)}, u32[]{:S(2)}) collective-permute-start(bf16[256,1024]{1,0:T(8,128)(2,1)} %collective-permute-done.1.refs_2_), channel_id=1, source_target_pairs={{8,0},{16,8},{24,16},{9,1},{17,9},{25,17},{10,2},{18,10},{26,18},{... | collective-permute-start | bytes 1572872 | tf_op jit(solution)/shard_map/ppermute | solution.py:93
  65.5 52.9 %copy-start.19 = (bf16[8,32,640]{2,1,0:T(8,128)(2,1)}, bf16[8,32,640]{2,1,0:T(8,128)(2,1)S(1)}, u32[]{:S(2)}) copy-start(bf16[8,32,640]{2,1,0:T(8,128)(2,1)S(1)} %all-to-all-done.refs_7_) | copy-start | bytes 983044
  65.5 32.3 %collective-permute-start.7 = (bf16[8,32,640]{2,1,0:T(8,128)(2,1)S(1)}, bf16[8,32,640]{2,1,0:T(8,128)(2,1)S(1)}, u32[]{:S(2)}, u32[]{:S(2)}) collective-permute-start(bf16[8,32,640]{2,1,0:T(8,128)(2,1)S(1)} %all-to-all-done.refs_7_), channel_id=1, source_target_pairs={{0,2},{2,0},{1,3},{3,1},{4,6},{6,4},{5,7},{7,5},{8,10},{10,8},{9,1... | collective-permute-start | bytes 983048 | tf_op jit(solution)/shard_map/ppermute | solution.py:1012
  70.8 41.0 %collective-permute-start.4 = (bf16[256,1024]{1,0:T(8,128)(2,1)}, bf16[256,1024]{1,0:T(8,128)(2,1)}, u32[]{:S(2)}, u32[]{:S(2)}) collective-permute-start(bf16[256,1024]{1,0:T(8,128)(2,1)} %collective-permute-done.2.refs_3_), channel_id=1, source_target_pairs={{0,8},{8,16},{16,24},{1,9},{9,17},{17,25},{2,10},{10,18},{18,26},{... | collective-permute-start | bytes 1572872 | tf_op jit(solution)/shard_map/ppermute | solution.py:93
  96.4 20.1 %collective-permute-start.5 = (bf16[256,1024]{1,0:T(8,128)(2,1)S(1)}, bf16[256,1024]{1,0:T(8,128)(2,1)}, u32[]{:S(2)}, u32[]{:S(2)}) collective-permute-start(bf16[256,1024]{1,0:T(8,128)(2,1)S(1)} %collective-permute-done.3.refs_4_), channel_id=1, source_target_pairs={{8,0},{16,8},{24,16},{9,1},{17,9},{25,17},{10,2},{18,10},{26,18},{... | collective-permute-start | bytes 1572872 | tf_op jit(solution)/shard_map/ppermute | solution.py:93
  97.7 1.7 collective-permute-start.6
  97.8 2.1 collective-permute-start.8
  118.4 128.1 %all-gather.12.cloned.1.call-start = ((), (), s32[]{:S(2)}) async-start(), calls=%async_computation.15 | async-start | bytes 2621440 | tf_op jit(solution)/shard_map/all_gather | solution.py:1077
  122.5 181.8 %copy-start.37 = (s32[2048]{0:T(1024)}, s32[2048]{0:T(1024)S(1)}, u32[]{:S(2)}) copy-start(s32[2048]{0:T(1024)S(1)} %convert_reduce_fusion) | copy-start | bytes 24580
  147.2 15.2 %collective-permute-start.9 = (bf16[1024,256]{1,0:T(8,128)(2,1)}, bf16[1024,256]{1,0:T(8,128)(2,1)}, u32[]{:S(2)}, u32[]{:S(2)}) collective-permute-start(bf16[1024,256]{1,0:T(8,128)(2,1)} %get-tuple-element.131), channel_id=1, source_target_pairs={{0,4},{4,0},{1,5},{5,1},{2,6},{6,2},{3,7},{7,3},{8,12},{12,8},{9,1... | collective-permute-start | bytes 1572872 | tf_op jit(solution)/shard_map/ppermute | solution.py:1067
  150.3 36.5 %collective-permute-start.11 = (bf16[512,1536]{1,0:T(8,128)(2,1)}, bf16[512,1536]{1,0:T(8,128)(2,1)}, u32[]{:S(2)}, u32[]{:S(2)}) collective-permute-start(bf16[512,1536]{1,0:T(8,128)(2,1)} %pad_maximum_fusion.2.refs_0_), channel_id=1, source_target_pairs={{0,2},{2,0},{1,3},{3,1},{4,6},{6,4},{5,7},{7,5},{8,10},{10,8},{9,1... | collective-permute-start | bytes 4718600 | tf_op jit(solution)/shard_map/ppermute | solution.py:111
  151.8 41.9 %collective-permute-start.13 = (bf16[512,1536]{1,0:T(8,128)(2,1)}, bf16[512,1536]{1,0:T(8,128)(2,1)}, u32[]{:S(2)}, u32[]{:S(2)}) collective-permute-start(bf16[512,1536]{1,0:T(8,128)(2,1)} %pad_maximum_fusion.2.refs_0_), channel_id=1, source_target_pairs={{0,4},{4,0},{1,5},{5,1},{2,6},{6,2},{3,7},{7,3},{8,12},{12,8},{9,1... | collective-permute-start | bytes 4718600 | tf_op jit(solution)/shard_map/ppermute | solution.py:111
  186.5 31.7 %copy-start.29 = (bf16[1024,256]{1,0:T(8,128)(2,1)S(1)}, bf16[1024,256]{1,0:T(8,128)(2,1)}, u32[]{:S(2)}) copy-start(bf16[1024,256]{1,0:T(8,128)(2,1)} %get-tuple-element.130.q_ref) | copy-start | bytes 1572868
  186.5 97.5 %all-gather.10.cloned.1.call-start = ((), (), s32[]{:S(2)}) async-start(), calls=%async_computation.10 | async-start | bytes 4718592 | tf_op jit(solution)/shard_map/all_gather | solution.py:76
  186.7 35.7 %collective-permute-start.10 = (bf16[512,1536]{1,0:T(8,128)(2,1)}, bf16[512,1536]{1,0:T(8,128)(2,1)}, u32[]{:S(2)}, u32[]{:S(2)}) collective-permute-start(bf16[512,1536]{1,0:T(8,128)(2,1)} %pad_maximum_fusion.2.refs_0_), channel_id=1, source_target_pairs={{0,1},{1,0},{2,3},{3,2},{4,5},{5,4},{6,7},{7,6},{8,9},{9,8},{10,11... | collective-permute-start | bytes 4718600 | tf_op jit(solution)/shard_map/ppermute | solution.py:118
  186.8 39.0 %collective-permute-start.12 = (bf16[512,1536]{1,0:T(8,128)(2,1)}, bf16[512,1536]{1,0:T(8,128)(2,1)}, u32[]{:S(2)}, u32[]{:S(2)}) collective-permute-start(bf16[512,1536]{1,0:T(8,128)(2,1)} %collective-permute-done.11.refs_2_), channel_id=1, source_target_pairs={{0,1},{1,0},{2,3},{3,2},{4,5},{5,4},{6,7},{7,6},{8,9},{9,8},{10,11... | collective-permute-start | bytes 4718600 | tf_op jit(solution)/shard_map/ppermute | solution.py:118
  193.7 32.8 %collective-permute-start.14 = (bf16[512,1536]{1,0:T(8,128)(2,1)}, bf16[512,1536]{1,0:T(8,128)(2,1)}, u32[]{:S(2)}, u32[]{:S(2)}) collective-permute-start(bf16[512,1536]{1,0:T(8,128)(2,1)} %collective-permute-done.13.refs_4_), channel_id=1, source_target_pairs={{0,1},{1,0},{2,3},{3,2},{4,5},{5,4},{6,7},{7,6},{8,9},{9,8},{10,11... | collective-permute-start | bytes 4718600 | tf_op jit(solution)/shard_map/ppermute | solution.py:118
  194.9 25.3 %copy-start.21 = (f32[1024,256]{1,0:T(8,128)S(1)}, f32[1024,256]{1,0:T(8,128)}, u32[]{:S(2)}) copy-start(f32[1024,256]{1,0:T(8,128)} %get-tuple-element.140) | copy-start | bytes 3145732
  194.9 20.1 %collective-permute-start.15 = (bf16[256,1536]{1,0:T(8,128)(2,1)S(1)}, bf16[256,1536]{1,0:T(8,128)(2,1)}, u32[]{:S(2)}, u32[]{:S(2)}) collective-permute-start(bf16[256,1536]{1,0:T(8,128)(2,1)S(1)} %slice.104), channel_id=1, source_target_pairs={{0,2},{2,0},{1,3},{3,1},{4,6},{6,4},{5,7},{7,5},{8,10},{10,8},{9,1... | collective-permute-start | bytes 2359304 | tf_op jit(solution)/shard_map/ppermute | solution.py:116
  197.7 19.8 %collective-permute-start.17 = (bf16[256,1536]{1,0:T(8,128)(2,1)S(1)}, bf16[256,1536]{1,0:T(8,128)(2,1)}, u32[]{:S(2)}, u32[]{:S(2)}) collective-permute-start(bf16[256,1536]{1,0:T(8,128)(2,1)S(1)} %slice.105), channel_id=1, source_target_pairs={{0,4},{4,0},{1,5},{5,1},{2,6},{6,2},{3,7},{7,3},{8,12},{12,8},{9,1... | collective-permute-start | bytes 2359304 | tf_op jit(solution)/shard_map/ppermute | solution.py:117
  215.1 12.9 %collective-permute-start.16 = (bf16[256,1536]{1,0:T(8,128)(2,1)}, bf16[256,1536]{1,0:T(8,128)(2,1)}, u32[]{:S(2)}, u32[]{:S(2)}) collective-permute-start(bf16[256,1536]{1,0:T(8,128)(2,1)} %collective-permute-done.15.refs_6_), channel_id=1, source_target_pairs={{0,1},{1,0},{2,3},{3,2},{4,5},{5,4},{6,7},{7,6},{8,9},{9,8},{10,11... | collective-permute-start | bytes 2359304 | tf_op jit(solution)/shard_map/ppermute | solution.py:118
  217.6 10.4 %collective-permute-start.18 = (bf16[256,1536]{1,0:T(8,128)(2,1)}, bf16[256,1536]{1,0:T(8,128)(2,1)}, u32[]{:S(2)}, u32[]{:S(2)}) collective-permute-start(bf16[256,1536]{1,0:T(8,128)(2,1)} %collective-permute-done.17.refs_8_), channel_id=1, source_target_pairs={{0,1},{1,0},{2,3},{3,2},{4,5},{5,4},{6,7},{7,6},{8,9},{9,8},{10,11... | collective-permute-start | bytes 2359304 | tf_op jit(solution)/shard_map/ppermute | solution.py:118
  222.5 24.0 %collective-permute-start.20 = (f32[1024,128]{1,0:T(8,128)S(1)}, f32[1024,128]{1,0:T(8,128)}, u32[]{:S(2)}, u32[]{:S(2)}) collective-permute-start(f32[1024,128]{1,0:T(8,128)S(1)} %bitcast.167), channel_id=1, source_target_pairs={{0,4},{4,0},{1,5},{5,1},{2,6},{6,2},{3,7},{7,3},{8,12},{12,8},{9,1... | collective-permute-start | bytes 1572872 | tf_op jit(solution)/shard_map/ppermute | solution.py:1088
  225.9 20.6 %collective-permute-start.19 = (bf16[1024,128]{1,0:T(8,128)(2,1)S(1)}, bf16[1024,128]{1,0:T(8,128)(2,1)S(1)}, u32[]{:S(2)}, u32[]{:S(2)}) collective-permute-start(bf16[1024,128]{1,0:T(8,128)(2,1)S(1)} %bitcast.168), channel_id=1, source_target_pairs={{0,4},{4,0},{1,5},{5,1},{2,6},{6,2},{3,7},{7,3},{8,12},{12,8},{9,1... | collective-permute-start | bytes 786440 | tf_op jit(solution)/shard_map/ppermute | solution.py:1088
  226.6 19.9 %collective-permute-start.21 = (f32[2,1,1024]{2,0,1:T(2,128)S(1)}, f32[2,1,1024]{2,0,1:T(2,128)S(1)}, u32[]{:S(2)}, u32[]{:S(2)}) collective-permute-start(f32[2,1,1024]{2,0,1:T(2,128)S(1)} %bitcast.175), channel_id=1, source_target_pairs={{0,4},{4,0},{1,5},{5,1},{2,6},{6,2},{3,7},{7,3},{8,12},{12,8},{9,1... | collective-permute-start | bytes 24584 | tf_op jit(solution)/shard_map/ppermute | solution.py:1088
  246.6 105.2 %reduce-scatter.5.cloned.1.call-start = ((), (), s32[]{:S(2)}) async-start(), calls=%async_computation.11 | async-start | bytes 2949120 | tf_op jit(solution)/shard_map/reduce_scatter | solution.py:80
  288.7 158.0 %reduce-scatter.7.cloned.1.call-start = ((), (), s32[]{:S(2)}) async-start(), calls=%async_computation.12 | async-start | bytes 2621440 | tf_op jit(solution)/shard_map/reduce_scatter | solution.py:80
  303.3 19.8 %collective-permute-start.22 = (bf16[4,512,768]{2,1,0:T(8,128)(2,1)}, bf16[4,512,768]{2,1,0:T(8,128)(2,1)}, u32[]{:S(2)}, u32[]{:S(2)}) collective-permute-start(bf16[4,512,768]{2,1,0:T(8,128)(2,1)} %get-tuple-element.157), channel_id=1, source_target_pairs={{0,1},{1,0},{2,3},{3,2},{4,5},{5,4},{6,7},{7,6},{8,9},{9,8},{10,11... | collective-permute-start | bytes 9437192 | tf_op jit(solution)/shard_map/ppermute | solution.py:1139
  303.4 25.2 %collective-permute-start.23 = (bf16[4,512,768]{2,1,0:T(8,128)(2,1)}, bf16[4,512,768]{2,1,0:T(8,128)(2,1)S(1)}, u32[]{:S(2)}, u32[]{:S(2)}) collective-permute-start(bf16[4,512,768]{2,1,0:T(8,128)(2,1)} %get-tuple-element.159), channel_id=1, source_target_pairs={{0,1},{1,0},{2,3},{3,2},{4,5},{5,4},{6,7},{7,6},{8,9},{9,8},{10,11... | collective-permute-start | bytes 9437192 | tf_op jit(solution)/shard_map/ppermute | solution.py:1139
  303.9 47.9 %collective-permute-start.24 = (bf16[1024,1024]{1,0:T(8,128)(2,1)}, bf16[1024,1024]{1,0:T(8,128)(2,1)}, u32[]{:S(2)}, u32[]{:S(2)}) collective-permute-start(bf16[1024,1024]{1,0:T(8,128)(2,1)} %get-tuple-element.144.x_ref.own_ref), channel_id=1, source_target_pairs={{0,4},{4,0},{1,5},{5,1},{2,6},{6,2},{3,7},{7,3},{8,12},{12,8},{9,1... | collective-permute-start | bytes 6291464 | tf_op jit(solution)/shard_map/ppermute | solution.py:1137
  359.3 44.6 %collective-permute-start.25 = (bf16[2,512,768]{2,1,0:T(8,128)(2,1)}, bf16[2,512,768]{2,1,0:T(8,128)(2,1)}, u32[]{:S(2)}, u32[]{:S(2)}) collective-permute-start(bf16[2,512,768]{2,1,0:T(8,128)(2,1)} %dynamic-slice_bitcast_fusion.1), channel_id=1, source_target_pairs={{0,2},{2,0},{1,3},{3,1},{4,6},{6,4},{5,7},{7,5},{8,10},{10,8},{9,1... | collective-permute-start | bytes 4718600 | tf_op jit(solution)/shard_map/ppermute | solution.py:123
  361.9 40.2 %collective-permute-start.26 = (bf16[2,512,768]{2,1,0:T(8,128)(2,1)}, bf16[2,512,768]{2,1,0:T(8,128)(2,1)}, u32[]{:S(2)}, u32[]{:S(2)}) collective-permute-start(bf16[2,512,768]{2,1,0:T(8,128)(2,1)} %dynamic-slice_bitcast_fusion), channel_id=1, source_target_pairs={{0,4},{4,0},{1,5},{5,1},{2,6},{6,2},{3,7},{7,3},{8,12},{12,8},{9,1... | collective-permute-start | bytes 4718600 | tf_op jit(solution)/shard_map/ppermute | solution.py:123
  367.7 39.3 %all-to-all-start.1 = ((bf16[8,256,128]{2,1,0:T(8,128)(2,1)}), bf16[8,256,128]{2,1,0:T(8,128)(2,1)S(1)}, u32[]{:S(2)}, u32[]{:S(2)}) async-start(bf16[8,256,128]{2,1,0:T(8,128)(2,1)} %bitcast.111), calls=%async_computation.2 | async-start | bytes 1048576 | tf_op jit(solution)/shard_map/all_to_all | solution.py:926
  372.5 90.4 %reduce-scatter.9.cloned.1.call-start = ((), (), s32[]{:S(2)}) async-start(), calls=%async_computation.13 | async-start | bytes 2654208 | tf_op jit(solution)/shard_map/reduce_scatter | solution.py:80
  373.6 28.5 %copy-start.5 = (bf16[4,512,768]{2,1,0:T(8,128)(2,1)S(1)}, bf16[4,512,768]{2,1,0:T(8,128)(2,1)}, u32[]{:S(2)}) copy-start(bf16[4,512,768]{2,1,0:T(8,128)(2,1)} %add_convert_fusion) | copy-start | bytes 9437188
  375.4 28.5 %copy-start.3 = (bf16[4,512,768]{2,1,0:T(8,128)(2,1)S(1)}, bf16[4,512,768]{2,1,0:T(8,128)(2,1)}, u32[]{:S(2)}) copy-start(bf16[4,512,768]{2,1,0:T(8,128)(2,1)} %add_convert_fusion.1) | copy-start | bytes 9437188
  414.9 31.7 %collective-permute-start.27 = (bf16[512,768]{1,0:T(8,128)(2,1)}, bf16[512,768]{1,0:T(8,128)(2,1)S(1)}, u32[]{:S(2)}, u32[]{:S(2)}) collective-permute-start(bf16[512,768]{1,0:T(8,128)(2,1)} %get-tuple-element.262), channel_id=1, source_target_pairs={{0,4},{4,0},{1,5},{5,1},{2,6},{6,2},{3,7},{7,3},{8,12},{12,8},{9,1... | collective-permute-start | bytes 2359304 | tf_op jit(solution)/shard_map/ppermute | solution.py:123
  417.3 29.4 %collective-permute-start.28 = (bf16[512,768]{1,0:T(8,128)(2,1)}, bf16[512,768]{1,0:T(8,128)(2,1)S(1)}, u32[]{:S(2)}, u32[]{:S(2)}) collective-permute-start(bf16[512,768]{1,0:T(8,128)(2,1)} %get-tuple-element.260), channel_id=1, source_target_pairs={{0,2},{2,0},{1,3},{3,1},{4,6},{6,4},{5,7},{7,5},{8,10},{10,8},{9,1... | collective-permute-start | bytes 2359304 | tf_op jit(solution)/shard_map/ppermute | solution.py:123
  447.6 28.0 %all-to-all-start.2 = ((bf16[8,256,256]{2,1,0:T(8,128)(2,1)}), bf16[8,256,256]{2,1,0:T(8,128)(2,1)S(1)}, u32[]{:S(2)}, u32[]{:S(2)}) async-start(bf16[8,256,256]{2,1,0:T(8,128)(2,1)} %bitcast.134), calls=%async_computation.4 | async-start | bytes 2097152 | tf_op jit(solution)/shard_map/all_to_all | solution.py:926
  475.6 41.6 %all-to-all-start.3 = ((bf16[32,32,384]{2,1,0:T(8,128)(2,1)}), bf16[32,32,384]{2,1,0:T(8,128)(2,1)S(1)}, u32[]{:S(2)}, u32[]{:S(2)}) async-start(bf16[32,32,384]{2,1,0:T(8,128)(2,1)} %bitcast.136), calls=%async_computation.6 | async-start | bytes 1572864 | tf_op jit(solution)/shard_map/all_to_all | solution.py:926
  478.2 25.8 %reduce-scatter.11.cloned.1.call-start = ((), (), s32[]{:S(2)}) async-start(), calls=%async_computation.14 | async-start | bytes 368640 | tf_op jit(solution)/shard_map/reduce_scatter | solution.py:80
  (33 other events, 224.4 us)
Sparse Core Ops, SparseCore 0:
  15.7 94.2 all-gather.5
  118.5 29.2 all-gather.7
  186.6 49.2 all-gather.11
  246.7 34.6 all-gather.9
  288.8 45.9 reduce-scatter.4
  351.9 50.1 reduce-scatter.6
  407.1 45.2 reduce-scatter.8
  481.3 22.5 reduce-scatter.10

commit v6 on v2

--- a/solution.py
+++ b/solution.py
@@ -31,7 +31,6 @@
 PLANE = ("b", "y", "c")
 SEQ = ("a", "b")
 ALL = ("a", "b", "y", "c")
-SWAP = [(0, 1), (1, 0)]
 
 f32 = jnp.float32
 bf16 = jnp.bfloat16
@@ -106,20 +105,21 @@
     return pieces
 
 
-def neighbours(x):
-    return lax.ppermute(x, "y", SWAP), lax.ppermute(x, "b", SWAP)
-
-
-def plane_gather(x, from_y, from_b):
+def plane_gather(x):
+    swap = [(0, 1), (1, 0)]
     half = x.shape[0] // 2
-    upper = lax.ppermute(from_b[:half], "y", SWAP)
-    lower = lax.ppermute(from_y[half:], "b", SWAP)
-    return [(block, lax.ppermute(block, "c", SWAP)) for block in (x, from_y, from_b, upper, lower)]
+    from_y = lax.ppermute(x, "y", swap)
+    from_b = lax.ppermute(x, "b", swap)
+    upper = lax.ppermute(from_b[:half], "y", swap)
+    lower = lax.ppermute(from_y[half:], "b", swap)
+    return [
+        (block, lax.ppermute(block, "c", swap)) for block in (x, from_y, from_b, upper, lower)
+    ]
 
 
 def halve_send(v, axis, at):
     me = lax.axis_index(axis)
-    other = lax.ppermute(lax.dynamic_index_in_dim(v, 1 - me, at, False), axis, SWAP)
+    other = lax.ppermute(lax.dynamic_index_in_dim(v, 1 - me, at, False), axis, [(0, 1), (1, 0)])
     return lax.dynamic_index_in_dim(v, me, at, False), other
 
 
@@ -148,29 +148,16 @@
     return jnp.where(low, cos, 1.0), jnp.where(low, sin, 0.0)
 
 
-def project_kernel(places, spots, place_ref, *refs):
+def project_kernel(places, place_ref, *refs):
     count = 1 if places is None else len(places)
     blocks, refs = refs[:count], refs[count:]
-    count = 1 if spots is None else len(spots)
-    weights, refs = refs[:count], refs[count:]
-    cos_ref, sin_ref, qkv_ref, normed_ref, x_ref, w_ref, wide_cos_ref, wide_sin_ref = refs[:8]
-    gain, held, sems = refs[8:]
+    small_ref, w_ref, cos_ref, sin_ref, qkv_ref, normed_ref, x_ref = refs[:7]
+    wide_cos_ref, wide_sin_ref, gain, held, sems = refs[7:]
     i = pl.program_id(0)
     slots = held.shape[0]
 
     @pl.when(i == 0)
     def _():
-        copies = []
-        if spots is None:
-            copies.append(pltpu.make_async_copy(weights[0], w_ref, sems.at[slots]))
-        else:
-            for at, ((y, c), block) in enumerate(zip(spots, weights)):
-                row = 2 * (place_ref[3] ^ y) + (place_ref[4] ^ c)
-                copies.append(
-                    pltpu.make_async_copy(block, w_ref.at[:, row], sems.at[slots + at])
-                )
-        for copy in copies:
-            copy.start()
         if places is None:
             for slot in range(slots):
                 pltpu.make_async_copy(blocks[0].at[slot], held.at[slot], sems.at[slot]).start()
@@ -183,10 +170,7 @@
                 def _(block=block, slot=2 * at + member):
                     pltpu.make_async_copy(block, held.at[slot], sems.at[slot]).start()
 
-        for copy in copies:
-            copy.wait()
-        small = w_ref[..., HEAD_PACK:].reshape(held.shape[2], LANES)
-        gain[...] = jnp.transpose(small.astype(f32))[:8, :]
+        gain[...] = jnp.transpose(small_ref[...].astype(f32))[E : E + 8, :]
 
     arrived = blocks[0].at[0] if places is None else blocks[0]
     pltpu.make_async_copy(arrived, held.at[i], sems.at[i]).wait()
@@ -194,8 +178,7 @@
     x_ref[...] = x
     normed = rms_scale(x.astype(f32), gain[0:1, :]).astype(bf16)
     normed_ref[...] = normed
-    w = w_ref[..., :HEAD_PACK].reshape(held.shape[2], HEAD_PACK)
-    pre = jnp.dot(normed, w, preferred_element_type=f32)
+    pre = jnp.dot(normed, w_ref[...], preferred_element_type=f32)
     cos, sin = spread_tables(cos_ref[...], sin_ref[...])
     wide_cos_ref[...] = cos
     wide_sin_ref[...] = sin
@@ -203,40 +186,41 @@
     qkv_ref[:, PAIR:] = rotate_lanes(pre[:, PAIR:], *key_tables(cos, sin)).astype(bf16)
 
 
-def project(place, places, blocks, spots, weights, rows, width, cos, sin):
+def project(place, places, blocks, rows, packed, cos, sin):
+    width = packed.shape[0]
+    small_at = packed.shape[1] // LANES - 1
     span = cos.shape[0]
     table = pl.BlockSpec((rows, HEAD_SIZE // 2), lambda i, h: (i, 0))
     token_rows = pl.BlockSpec((rows, width), lambda i, h: (i, 0))
-    cols = HEAD_PACK + LANES
-    shape = weights[0].shape if spots is None else (
-        weights[0].shape[0], len(spots), weights[0].shape[1], cols
-    )
     return pl.pallas_call(
-        functools.partial(project_kernel, places, spots),
+        functools.partial(project_kernel, places),
         grid_spec=pltpu.PrefetchScalarGridSpec(
             num_scalar_prefetch=1,
             grid=(span // rows,),
-            in_specs=[pl.BlockSpec(memory_space=pl.ANY)] * (len(blocks) + len(weights))
-            + [table, table],
+            in_specs=[pl.BlockSpec(memory_space=pl.ANY)] * len(blocks)
+            + [
+                pl.BlockSpec((width, LANES), lambda i, h: (0, small_at)),
+                pl.BlockSpec((width, HEAD_PACK), lambda i, h: (0, h[0])),
+                table,
+                table,
+            ],
             out_specs=[
                 pl.BlockSpec((rows, HEAD_PACK), lambda i, h: (i, 0)),
                 token_rows,
                 token_rows,
-                pl.BlockSpec(shape, lambda i, h: (0,) * len(shape)),
                 pl.BlockSpec((rows, PAIR), lambda i, h: (i, 0)),
                 pl.BlockSpec((rows, PAIR), lambda i, h: (i, 0)),
             ],
             scratch_shapes=[
                 pltpu.VMEM((8, width), f32),
                 pltpu.VMEM((span // rows, rows, width), bf16),
-                pltpu.SemaphoreType.DMA((span // rows + len(weights),)),
+                pltpu.SemaphoreType.DMA((span // rows,)),
             ],
         ),
         out_shape=[
             jax.ShapeDtypeStruct((span, HEAD_PACK), bf16),
             jax.ShapeDtypeStruct((span, width), bf16),
             jax.ShapeDtypeStruct((span, width), bf16),
-            jax.ShapeDtypeStruct(shape, bf16),
             jax.ShapeDtypeStruct((span, PAIR), f32),
             jax.ShapeDtypeStruct((span, PAIR), f32),
         ],
@@ -245,10 +229,10 @@
             flops=2 * span * width * HEAD_PACK, bytes_accessed=18 * 2**20, transcendentals=0
         ),
         name="project",
-    )(place, *blocks, *weights, cos, sin)
-
-
-def head_grads_kernel(x_ref, normed_ref, w_ref, grad_ref, out_ref, acc, gain):
+    )(place, *blocks, packed, packed, cos, sin)
+
+
+def head_grads_kernel(head_ref, x_ref, normed_ref, w_ref, grad_ref, out_ref, acc, gain):
     i = pl.program_id(0)
 
     @pl.when(i == 0)
@@ -273,28 +257,31 @@
         ).astype(bf16)
 
 
-def head_grads(x, normed, weights, grads):
+def head_grads(head, x, normed, packed, grads):
     span, width = x.shape
     rows = 2 * BLOCK
-    token_rows = pl.BlockSpec((rows, width), lambda i: (i, 0))
+    token_rows = pl.BlockSpec((rows, width), lambda i, h: (i, 0))
     return pl.pallas_call(
         head_grads_kernel,
-        grid=(span // rows,),
-        in_specs=[
-            token_rows,
-            token_rows,
-            pl.BlockSpec((width, HEAD_PACK), lambda i: (0, 0)),
-            pl.BlockSpec((rows, HEAD_PACK), lambda i: (i, 0)),
-        ],
-        out_specs=pl.BlockSpec((width, HEAD_PACK + LANES), lambda i: (0, 0)),
-        scratch_shapes=[pltpu.VMEM((HEAD_PACK, width), f32), pltpu.VMEM((8, width), f32)],
+        grid_spec=pltpu.PrefetchScalarGridSpec(
+            num_scalar_prefetch=1,
+            grid=(span // rows,),
+            in_specs=[
+                token_rows,
+                token_rows,
+                pl.BlockSpec((width, HEAD_PACK), lambda i, h: (0, h[0])),
+                pl.BlockSpec((rows, HEAD_PACK), lambda i, h: (i, 0)),
+            ],
+            out_specs=pl.BlockSpec((width, HEAD_PACK + LANES), lambda i, h: (0, 0)),
+            scratch_shapes=[pltpu.VMEM((HEAD_PACK, width), f32), pltpu.VMEM((8, width), f32)],
+        ),
         out_shape=jax.ShapeDtypeStruct((width, HEAD_PACK + LANES), bf16),
         compiler_params=pltpu.CompilerParams(vmem_limit_bytes=VMEM_LIMIT),
         cost_estimate=pl.CostEstimate(
             flops=4 * span * width * HEAD_PACK, bytes_accessed=12 * 2**20, transcendentals=0
         ),
         name="head_grads",
-    )(x, normed, weights, grads)
+    )(head, x, normed, packed, grads)
 
 
 def lower_lanes(shape):
@@ -798,54 +785,6 @@
         ),
         name="join",
     )(place, outs, packed, packed, x)
-
-
-def token_grads_kernel(grad_ref, w_ref, small_ref, x_ref, resid_ref, out_ref, acc):
-    h = pl.program_id(0)
-    part = contract_cols(grad_ref[0], w_ref[...])
-
-    @pl.when(h == 0)
-    def _():
-        acc[...] = part
-
-    @pl.when(h > 0)
-    def _():
-        acc[...] += part
-
-    @pl.when(h == pl.num_programs(0) - 1)
-    def _():
-        gain = jnp.transpose(small_ref[...].astype(f32))[E : E + 1, :]
-        x = x_ref[...].astype(f32)
-        inverse = lax.rsqrt(jnp.mean(x * x, axis=-1, keepdims=True) + NORM_EPS)
-        scaled = acc[...] * gain
-        mean = jnp.mean(x * scaled, axis=-1, keepdims=True)
-        out_ref[...] = resid_ref[...] + (inverse * scaled - x * inverse**3 * mean)
-
-
-def token_grads(grads, packed, x, resid):
-    heads, rows, pack = grads.shape
-    width = x.shape[1]
-    small_at = packed.shape[1] // LANES - 1
-    whole = pl.BlockSpec((rows, width), lambda h: (0, 0))
-    return pl.pallas_call(
-        token_grads_kernel,
-        grid=(heads,),
-        in_specs=[
-            pl.BlockSpec((1, rows, pack), lambda h: (h, 0, 0)),
-            pl.BlockSpec((width, pack), lambda h: (0, h)),
-            pl.BlockSpec((width, LANES), lambda h: (0, small_at)),
-            whole,
-            whole,
-        ],
-        out_specs=whole,
-        out_shape=jax.ShapeDtypeStruct((rows, width), f32),
-        scratch_shapes=[pltpu.VMEM((rows, width), f32)],
-        compiler_params=pltpu.CompilerParams(vmem_limit_bytes=VMEM_LIMIT),
-        cost_estimate=pl.CostEstimate(
-            flops=2 * rows * width * heads * pack, bytes_accessed=8 * 2**20, transcendentals=0
-        ),
-        name="token_grads",
-    )(grads, packed, packed, x, resid)
 
 
 def weight_sums_kernel(sums_ref, q_ref, k_ref, v_ref, gain_ref):
@@ -963,36 +902,6 @@
         ALL,
     )
     experts_low = jnp.concatenate([expert_in.astype(bf16), expert_out.astype(bf16)], axis=1)
-    small_plane = lax.axis_size("b") == 2 and lax.axis_size("y") == 2 and lax.axis_size("c") == 2
-    if small_plane:
-        gains = jnp.broadcast_to(
-            pad_lanes(norm_attn.astype(bf16)[:, None], LANES), (KEY_VALUE_HEADS, own_rows, LANES)
-        )
-        columns = exchange(
-            jnp.concatenate(
-                [by_head.reshape(own_rows, KEY_VALUE_HEADS, HEAD_PACK).transpose(1, 0, 2), gains],
-                axis=2,
-            ),
-            SEQ,
-        )
-        from_y = lax.ppermute(columns, "y", SWAP)
-        spots = ((0, 0), (0, 1), (1, 0), (1, 1))
-        weights = (
-            columns, lax.ppermute(columns, "c", SWAP), from_y, lax.ppermute(from_y, "c", SWAP)
-        )
-    else:
-        spots = None
-        at = lax.axis_index(head_axes) * HEAD_PACK
-        gain_at = qkv_width + width + E
-        weights = (
-            jnp.concatenate(
-                [
-                    lax.dynamic_slice_in_dim(first_all, at, HEAD_PACK, 1),
-                    pad_lanes(first_all[:, gain_at : gain_at + 1], LANES),
-                ],
-                axis=1,
-            ),
-        )
     if whole_rows:
         pieces = grid_gather(tokens[0])
         places = [piece[:2] for piece in pieces]
@@ -1000,32 +909,32 @@
     else:
         places = None
         blocks = (gather(tokens[0], "b").reshape((-1,) + tokens.shape[1:]),)
-    experts_low, blocks, weights, cos_span, sin_span, bounds, doc_rows = (
+    first_all, experts_low, blocks, cos_span, sin_span, bounds, doc_rows = (
         lax.optimization_barrier(
-            (experts_low, blocks, weights, cos_span, sin_span, bounds, doc_rows)
+            (first_all, experts_low, blocks, cos_span, sin_span, bounds, doc_rows)
         )
     )
     output_w = first_all[:, qkv_width : qkv_width + width]
     small_at = qkv_width + width
     router_w = first_all[:, small_at : small_at + E]
+    gain_one_f = first_all[:, small_at + E].astype(f32)
     gain_two_f = first_all[:, small_at + E + 1].astype(f32)
 
     expert_ids = jnp.arange(E, dtype=jnp.int32)
     routed_own = jnp.any(routes[0][:, :, None] == expert_ids[None, None, :], axis=1)
     early = jnp.concatenate([cotangent[0], pad_lanes(routed_own.astype(bf16), LANES)], axis=1)
+    early, first_all = lax.optimization_barrier((early, first_all))
     early_all = gather(early, "a")
+    small_plane = lax.axis_size("b") == 2 and lax.axis_size("y") == 2
     if small_plane:
-        beside = neighbours(experts_low)
+        parts = plane_gather(experts_low)
     else:
         parts = gather(experts_low, PLANE)
 
-    place = jnp.stack(
-        [lax.axis_index(axis) for axis in (head_axes, "a", "b", "y", "c")]
-    )
-    qkv, normed_span, x_span, own_weights, wide_cos, wide_sin = project(
-        place, places, blocks, spots, weights, token_count, width, cos_span, sin_span
-    )
-    own_weights = own_weights.reshape(width, HEAD_PACK + LANES)
+    place = jnp.stack([lax.axis_index(head_axes), group, lax.axis_index("b")])
+    qkv, normed_span, x_span, wide_cos, wide_sin = project(
+        place, places, blocks, token_count, first_all, cos_span, sin_span
+    )
     if whole_rows:
         kv, kv_at = qkv, 1
     else:
@@ -1033,11 +942,9 @@
     attention_result, attended, log_total = attend(bounds, qkv, kv, kv_at, doc_rows)
     if small_plane:
         member = lax.axis_index("b")
-        attended, beside, first_all = lax.optimization_barrier((attended, beside, first_all))
-        parts = plane_gather(experts_low, *beside)
         by_column = attended.reshape(GROUPS, 2, token_count, PAIR)
         other = lax.ppermute(
-            lax.dynamic_index_in_dim(by_column, 1 - member, 1, False), "b", SWAP
+            lax.dynamic_index_in_dim(by_column, 1 - member, 1, False), "b", [(0, 1), (1, 0)]
         )
         own = lax.dynamic_index_in_dim(by_column, member, 1, False)
         pair, early_all = lax.optimization_barrier((jnp.stack([own, other]), early_all))
@@ -1071,7 +978,7 @@
     if small_plane:
         core = lax.axis_index("c")
         (send,) = expert_grads((1 - core).reshape(1), 2, *inputs, False)
-        arrived = lax.ppermute(send, "c", SWAP)
+        arrived = lax.ppermute(send, "c", [(0, 1), (1, 0)])
         moe_part, keep = expert_grads(core.reshape(1), 2, *inputs, True)
         back_own, moe_part, keep = lax.optimization_barrier((back_own, moe_part, keep))
     else:
@@ -1129,7 +1036,7 @@
         )
         left, right = halve_add(left), halve_add(right)
         left, right = halve_send(left, "b", 0), halve_send(right, "y", 0)
-    first_part = head_grads(x_span, normed_span, own_weights, grad_pack)
+    first_part = head_grads(place, x_span, normed_span, first_all, grad_pack)
     rest, first_part = lax.optimization_barrier((rest, first_part))
     rest = scatter_sum(rest, "a")
     by_tokens = exchange(grad_pack.reshape(KEY_VALUE_HEADS, token_count, HEAD_PACK), head_axes)
@@ -1140,7 +1047,10 @@
         sums.reshape(-1, KEY_VALUE_HEADS, lax.axis_size(("y", "c")), own_rows, first_part.shape[1])
     )
     rest = rest.astype(f32)
-    grad_input = token_grads(by_tokens, first_all, tokens[0], grad_resid)
+    grad_qkv = by_tokens.transpose(1, 0, 2).reshape(token_count, qkv_width)
+    grad_normed_one = contract_cols(grad_qkv, first_all[:, :qkv_width])
+    grad_x_norm, _ = rms_back(x_local, gain_one_f, grad_normed_one)
+    grad_input = grad_resid + grad_x_norm
     layer_sum = resid + RESIDUAL_SCALE * moe_sum.astype(f32)
     if small_plane:
         grad_experts = jnp.concatenate(

time: 486 us -> 467 us (0.961)
  Pallas kernels: 160 us -> 151 us
  waiting for transfers between devices: 152 us -> 143 us
  starting transfers between devices: 69.9 us -> 64.2 us
    ppermute x17 -> x14, waiting for transfers between devices: 70.6 us -> 42 us  [the longest x4 22.2 us: halve_send(): lax.ppermute(lax.dynamic_index_in_dim(v, 1 - me, at, False), axis, [(0, 1...]
    all_gather x2, waiting for transfers between devices: 0.01 us -> 9.64 us  [gather(): return lax.all_gather(x, axes, axis=0, tiled=True)]
    pallas_call x3 -> x2, Pallas kernels: 27.2 us -> 18.6 us  [the longest x1 10.8 us: project(): pl.pallas_call(functools.partial(project_kernel, places), grid_spec=pltpu...]
    ppermute x17 -> x14, starting transfers between devices: 11.2 us -> 16.7 us  [the longest x4 7.13 us: halve_send(): lax.ppermute(lax.dynamic_index_in_dim(v, 1 - me, at, False), axis, [(0, 1...]
    squeeze x4, local copies, waits for them, and re-layouts: 8.71 us -> 3.34 us  [halve_send(): lax.dynamic_index_in_dim(v, 1 - me, at, False)]
    all_to_all x4 -> x3, starting transfers between devices: 17.6 us -> 13.1 us  [exchange(): return lax.all_to_all(x, axes, 0, 0, tiled=True)]
    all_to_all x4 -> x3, waiting for transfers between devices: 24.8 us -> 23.6 us  [exchange(): return lax.all_to_all(x, axes, 0, 0, tiled=True)]
  transfers between devices with their start and end apart: 42 -> 38, of which waited for: 20 -> 20; matrix products, arithmetic and copies ran while one was open for 15% -> 15% of each run, Pallas kernels for 25% -> 24%
where the time goes in v6:
time: 467 us; the launch traced here: 459 us
  Pallas kernels  151 us (32%)
  waiting for transfers between devices  143 us (31%)
  starting transfers between devices  64.2 us (14%)
  other arithmetic  50 us (11%)
  local copies, waits for them, and re-layouts  24.1 us (5%)
  between operations  15.2 us (3%)
  matrix products  10.8 us (2%)
    pallas_call x2, Pallas kernels, expert_grads(): pl.pallas_call(functools.partial(expert_grads_kernel, with_y), grid_spec=...  33.5 us
    pallas_call x1, Pallas kernels, experts(): pl.pallas_call(experts_kernel, grid_spec=pltpu.PrefetchScalarGridSpec(num...  29 us
    pallas_call x1, Pallas kernels, attend_back(): pl.pallas_call(functools.partial(attend_back_kernel, fold), grid_spec=plt...  25 us
    all_to_all x3, waiting for transfers between devices, exchange(): return lax.all_to_all(x, axes, 0, 0, tiled=True)  23.6 us
    ppermute x4, waiting for transfers between devices, halve_send(): lax.ppermute(lax.dynamic_index_in_dim(v, 1 - me, at, False), axis, [(0, 1...  22.2 us
    ppermute x7, waiting for transfers between devices, cross(): lax.ppermute(block, SEQ, [(2 * i + j, 2 * i + 1 - j) for i in range(n) if...  20.8 us
    ppermute x3, waiting for transfers between devices, grid_gather(): up = lax.ppermute(up, 'a', line_pairs(n, 1))  19.3 us
    pallas_call x1, Pallas kernels, place_experts(): pl.pallas_call(place_experts_kernel, grid_spec=pltpu.PrefetchScalarGridSp...  18.6 us
  transfers between devices with their start and end apart: 38, of which 20 were waited for; matrix products, arithmetic and copies ran while one was open for 15% of the time, Pallas kernels for 24%

profile of v6, /device:TPU:0, one launch (start us, length us, event | category | flops | bytes accessed | tf_op | source)
XLA Modules:
  0.0 459.0 jit_solution(398555425235755579)
XLA Ops:
  14.5 5.8 %collective-permute-start.1 = (bf16[256,1024]{1,0:T(8,128)(2,1)}, bf16[256,1024]{1,0:T(8,128)(2,1)}, u32[]{:S(2)}, u32[]{:S(2)}) collective-permute-start(bf16[256,1024]{1,0:T(8,128)(2,1)} %bitcast.83), channel_id=1, source_target_pairs={{0,8},{8,16},{16,24},{1,9},{9,17},{17,25},{2,10},{10,18},{18,26},{... | collective-permute-start | bytes 1572872 | tf_op jit(solution)/shard_map/ppermute | solution.py:101
  26.9 6.9 %collective-permute-done.1.refs_2_ = bf16[256,1024]{1,0:T(8,128)(2,1)} collective-permute-done((bf16[256,1024]{1,0:T(8,128)(2,1)}, bf16[256,1024]{1,0:T(8,128)(2,1)}, u32[]{:S(2)}, u32[]{:S(2)}) %collective-permute-start.1) | collective-permute-done | bytes 524320 | tf_op jit(solution)/shard_map/ppermute | solution.py:101
  33.8 4.4 collective-permute-start.5
  42.9 12.4 %collective-permute-done.5.refs_6_ = bf16[256,1024]{1,0:T(8,128)(2,1)S(1)} collective-permute-done((bf16[256,1024]{1,0:T(8,128)(2,1)}, bf16[256,1024]{1,0:T(8,128)(2,1)S(1)}, u32[]{:S(2)}, u32[]{:S(2)}) %collective-permute-start.5) | collective-permute-done | bytes 524320 | tf_op jit(solution)/shard_map/ppermute | solution.py:101
  55.3 5.1 %collective-permute-start.9 = (bf16[256,1024]{1,0:T(8,128)(2,1)S(1)}, bf16[256,1024]{1,0:T(8,128)(2,1)}, u32[]{:S(2)}, u32[]{:S(2)}) collective-permute-start(bf16[256,1024]{1,0:T(8,128)(2,1)S(1)} %collective-permute-done.5.refs_6_), channel_id=1, source_target_pairs={{0,8},{8,16},{16,24},{1,9},{9,17},{17,25},{2,10},{10,18},{18,26},{... | collective-permute-start | bytes 1572872 | tf_op jit(solution)/shard_map/ppermute | solution.py:101
  63.8 4.0 collective-permute-start.4
  68.5 2.0 collective-permute-start.8
  71.2 6.5 %collective-permute-done.11.refs_12_ = bf16[256,1024]{1,0:T(8,128)(2,1)} collective-permute-done((bf16[256,1024]{1,0:T(8,128)(2,1)S(1)}, bf16[256,1024]{1,0:T(8,128)(2,1)}, u32[]{:S(2)}, u32[]{:S(2)}) %collective-permute-start.11) | collective-permute-done | bytes 524320 | tf_op jit(solution)/shard_map/ppermute | solution.py:102
  77.7 3.8 collective-permute-start.12
  82.1 5.5 %multiply_sine_fusion = (f32[2048,32]{1,0:T(8,128)}, f32[2048,32]{1,0:T(8,128)}) fusion(f32[32]{0:T(128)S(1)} %multiply_power_fusion, f32[2048]{0:T(1024)S(1)} %subtract_convert_fusion), kind=kLoop, calls=%fused_computation.22 | loop fusion | flops 65536 | bytes 532608 | tf_op jit(solution)/shard_map/sin | solution.py:43
  87.6 2.2 collective-permute-done.4.refs_5_
  89.8 14.1 %collective-permute-done.8.refs_9_ = bf16[256,1024]{1,0:T(8,128)(2,1)S(1)} collective-permute-done((bf16[256,1024]{1,0:T(8,128)(2,1)S(1)}, bf16[256,1024]{1,0:T(8,128)(2,1)S(1)}, u32[]{:S(2)}, u32[]{:S(2)}) %collective-permute-start.8) | collective-permute-done | bytes 524320 | tf_op jit(solution)/shard_map/ppermute | solution.py:94
  105.5 4.6 collective-permute-done.12.refs_13_
  110.7 2.5 collective-permute-start.17
  113.2 3.4 collective-permute-start.15
  116.6 10.8 %project.1 = (bf16[2048,256]{1,0:T(8,128)(2,1)}, bf16[2048,1024]{1,0:T(8,128)(2,1)}, bf16[2048,1024]{1,0:T(8,128)(2,1)}, f32[2048,128]{1,0:T(8,128)}, f32[2048,128]{1,0:T(8,128)}) custom-call(s32[3]{0:T(128)} %pad_add_fusion.place_ref.head_ref, bf16[256,1024]{1,0:T(8,128)(2,1)} %bitcast.86, bf16[256,1024]{1,0:T(8,128)(2,1)} %collective-permute-done.refs_1_, ...), custom_call_target="tpu_custom_call" | custom-call | flops 1073741824 | bytes 18874368 | tf_op jit(solution)/shard_map/project/pallas_call | solution.py:195
  127.4 16.4 %attend.1 = (f32[2048,128]{1,0:T(8,128)}, bf16[2048,128]{1,0:T(8,128)(2,1)}, f32[4,1,1024]{2,1,0:T(1,128)}) custom-call(s32[9]{0:T(128)} %pad_add_fusion.1.bounds_ref, bf16[2048,256]{1,0:T(8,128)(2,1)} %get-tuple-element.100.q_ref.kv_ref, bf16[2048,256]{1,0:T(8,128)(2,1)} %get-tuple-element.100.q_ref.kv_ref, s32[4,1,512]{2,1,0:T(1,128)} %bitcast.95), custom_call_target="tpu_custom_call" | custom-call | flops 2147483648 | bytes 6291456 | tf_op jit(solution)/shard_map/attend/pallas_call | solution.py:370
  145.1 6.2 %collective-permute-done.13 = bf16[4,256,128]{2,1,0:T(8,128)(2,1)S(1)} collective-permute-done((bf16[4,256,128]{2,1,0:T(8,128)(2,1)S(1)}, bf16[4,256,128]{2,1,0:T(8,128)(2,1)S(1)}, u32[]{:S(2)}, u32[]{:S(2)}) %collective-permute-start.13) | collective-permute-done | bytes 262176 | tf_op jit(solution)/shard_map/ppermute | solution.py:946
  152.2 9.6 %all-gather.7.cloned.1.call-done.refs_10_.routed_ref.ct_ref = bf16[1024,1152]{1,0:T(8,128)(2,1)} async-done(((bf16[256,1152]{1,0:T(8,128)(2,1)}), bf16[1024,1152]{1,0:T(8,128)(2,1)}) %all-gather.7.cloned.1.call-update) | async-done | bytes 2359312 | tf_op jit(solution)/shard_map/all_gather | solution.py:75
  168.1 15.2 %collective-permute-done.19.refs_6_ = bf16[256,1536]{1,0:T(8,128)(2,1)S(1)} collective-permute-done((bf16[256,1536]{1,0:T(8,128)(2,1)S(1)}, bf16[256,1536]{1,0:T(8,128)(2,1)S(1)}, u32[]{:S(2)}, u32[]{:S(2)}) %collective-permute-start.19) | collective-permute-done | bytes 786464 | tf_op jit(solution)/shard_map/ppermute | solution.py:113
  183.4 2.6 collective-permute-done.21.refs_8_
  186.6 2.0 collective-permute-done.22.refs_9_
  188.6 18.6 %place_experts.1 = (bf16[4,1024,1536]{2,1,0:T(8,128)(2,1)}, f32[4,1024,512]{2,1,0:T(8,128)}) custom-call(s32[2]{0:T(128)} %pad_add_fusion.2.place_ref, bf16[512,1536]{1,0:T(8,128)(2,1)} %pad_maximum_fusion.2.refs_0_, bf16[512,1536]{1,0:T(8,128)(2,1)} %collective-permute-done.14.refs_1_, bf16[512,1536]{1,0:T(8,128)(2,1)} %collective-permute-done.15.refs_2_, ...), custom_call_target="tpu_custom_call" | custom-call | flops 4294967296 | bytes 37748736 | tf_op jit(solution)/shard_map/place_experts/pallas_call | solution.py:552
  208.8 8.2 %join.1 = (bf16[1024,1024]{1,0:T(8,128)(2,1)}, f32[256,1024]{1,0:T(8,128)}, bf16[256,1024]{1,0:T(8,128)(2,1)}) custom-call(s32[3]{0:T(128)} %pad_add_fusion.place_ref.head_ref, bf16[4,2,4,256,128]{4,3,2,1,0:T(8,128)(2,1)} %bitcast.87, bf16[1024,3200]{1,0:T(8,128)(2,1)} %all-gather.5.cloned.1.call-done.refs_14_.refs_15_.w_ref.small_ref.router_ref, ...), custom_call_target="tpu_custom_call" | custom-call | flops 2147483648 | bytes 12582912 | tf_op jit(solution)/shard_map/join/pallas_call | solution.py:763
  217.0 29.0 %experts.1 = (bf16[1024,1152]{1,0:T(8,128)(2,1)}, f32[1024,128]{1,0:T(8,128)}, bf16[4,1024,512]{2,1,0:T(8,128)(2,1)}, bf16[4,1024,1024]{2,1,0:T(8,128)(2,1)}) custom-call(s32[1]{0:T(128)} %bitcast.group_ref, bf16[1024,1024]{1,0:T(8,128)(2,1)} %get-tuple-element.106.n_ref, bf16[1024,1152]{1,0:T(8,128)(2,1)} %all-gather.7.cloned.1.call-done.refs_10_.routed_ref.ct_ref, ...), custom_call_target="tpu_custom_call" | custom-call | flops 17179869184 | bytes 41943040 | tf_op jit(solution)/shard_map/experts/pallas_call | solution.py:634
  246.3 14.9 %expert_grads.3 = bf16[4,512,1536]{2,1,0:T(8,128)(2,1)} custom-call(s32[1]{0:T(128)} %bitcast.17.half_ref, bf16[1024,1024]{1,0:T(8,128)(2,1)} %get-tuple-element.106.n_ref, bf16[1024,1152]{1,0:T(8,128)(2,1)} %all-gather.7.cloned.1.call-done.refs_10_.routed_ref.ct_ref, bf16[4,1024,1536]{2,1,0:T(8,128)(2,1)} %get-tuple-element.109.w_ref, ...), custom_call_target="tpu_custom_call" | custom-call | flops 6442450944 | bytes 31457280 | tf_op jit(solution)/shard_map/expert_grads/pallas_call | solution.py:707
  262.6 18.7 %expert_grads.2 = (bf16[1024,1024]{1,0:T(8,128)(2,1)}, bf16[4,512,1536]{2,1,0:T(8,128)(2,1)}) custom-call(s32[1]{0:T(128)} %bitcast.16.half_ref, bf16[1024,1024]{1,0:T(8,128)(2,1)} %get-tuple-element.106.n_ref, bf16[1024,1152]{1,0:T(8,128)(2,1)} %all-gather.7.cloned.1.call-done.refs_10_.routed_ref.ct_ref, bf16[4,1024,1536]{2,1,0:T(8,128)(2,1)} %get-tuple-element.109.w_ref, ...), custom_call_target="tpu_custom_call" | custom-call | flops 10737418240 | bytes 31457280 | tf_op jit(solution)/shard_map/expert_grads/pallas_call | solution.py:707
  281.3 11.7 %reduce-scatter.5.cloned.1.call-done = bf16[256,1152]{1,0:T(8,128)(2,1)} async-done(((bf16[1024,1152]{1,0:T(8,128)(2,1)}), bf16[256,1152]{1,0:T(8,128)(2,1)}) %reduce-scatter.5.cloned.1.call-update) | async-done | bytes 589840 | tf_op jit(solution)/shard_map/reduce_scatter | solution.py:79
  296.9 2.7 fusion.7
  300.5 4.1 all-to-all-start
  306.3 9.3 %add_convert_fusion = bf16[4,512,1536]{2,1,0:T(8,128)(2,1)} fusion(bf16[4,512,1536]{2,1,0:T(8,128)(2,1)} %collective-permute-done.23, bf16[4,512,1536]{2,1,0:T(8,128)(2,1)} %get-tuple-element.120), kind=kLoop, calls=%fused_computation.1 | loop fusion | flops 12582912 | bytes 18874368 | tf_op jit(solution)/shard_map/convert_element_type | solution.py:1010
  318.4 16.0 %all-to-all-done = bf16[8,256,128]{2,1,0:T(8,128)(2,1)S(1)} async-done(((bf16[8,256,128]{2,1,0:T(8,128)(2,1)}), bf16[8,256,128]{2,1,0:T(8,128)(2,1)S(1)}, u32[]{:S(2)}, u32[]{:S(2)}) %all-to-all-start) | async-done | bytes 524320 | tf_op jit(solution)/shard_map/all_to_all | solution.py:828
  334.4 3.4 fusion.30
  343.8 25.0 %attend_back.1.grad_ref = bf16[2048,256]{1,0:T(8,128)(2,1)} custom-call(s32[9]{0:T(128)} %pad_add_fusion.1.bounds_ref, bf16[2048,256]{1,0:T(8,128)(2,1)} %get-tuple-element.100.q_ref.kv_ref, bf16[2048,256]{1,0:T(8,128)(2,1)} %get-tuple-element.100.q_ref.kv_ref, s32[4,1,512]{2,1,0:T(1,128)} %bitcast.96, bf16[2048,128]{1,0:T(8,128)(2,1)} %bitcast.91, ...), custom_call_target="tpu_custom_call" | custom-call | flops 5368709120 | bytes 8388608 | tf_op jit(solution)/shard_map/attend_back/pallas_call | solution.py:477
  368.8 5.6 %collective-permute-done.25 = bf16[2,512,768]{2,1,0:T(8,128)(2,1)} collective-permute-done((bf16[2,512,768]{2,1,0:T(8,128)(2,1)}, bf16[2,512,768]{2,1,0:T(8,128)(2,1)}, u32[]{:S(2)}, u32[]{:S(2)}) %collective-permute-start.25) | collective-permute-done | bytes 1572896 | tf_op jit(solution)/shard_map/ppermute | solution.py:122
  374.4 8.1 %collective-permute-done.24 = bf16[2,512,768]{2,1,0:T(8,128)(2,1)} collective-permute-done((bf16[2,512,768]{2,1,0:T(8,128)(2,1)}, bf16[2,512,768]{2,1,0:T(8,128)(2,1)}, u32[]{:S(2)}, u32[]{:S(2)}) %collective-permute-start.24) | collective-permute-done | bytes 1572896 | tf_op jit(solution)/shard_map/ppermute | solution.py:122
  382.6 2.3 copy.80
  384.9 4.3 all-to-all-start.1
  389.2 1.9 add_convert_fusion.1
  391.2 2.5 collective-permute-start.27
  398.6 7.8 %head_grads.1 = bf16[1024,384]{1,0:T(8,128)(2,1)} custom-call(s32[3]{0:T(128)} %pad_add_fusion.place_ref.head_ref, bf16[2048,1024]{1,0:T(8,128)(2,1)} %get-tuple-element.105.x_ref, bf16[2048,1024]{1,0:T(8,128)(2,1)} %get-tuple-element.134.normed_ref, bf16[1024,3200]{1,0:T(8,128)(2,1)} %all-gather.5.cloned.1.call-done.refs_14_.refs_15_.w_ref.small_ref.router_ref, ...), custom_call_target="tpu_custom_call" | custom-call | flops 2147483648 | bytes 12582912 | tf_op jit(solution)/shard_map/head_grads/pallas_call | solution.py:264
  409.6 8.0 %collective-permute-done.26 = bf16[512,768]{1,0:T(8,128)(2,1)} collective-permute-done((bf16[512,768]{1,0:T(8,128)(2,1)S(1)}, bf16[512,768]{1,0:T(8,128)(2,1)}, u32[]{:S(2)}, u32[]{:S(2)}) %collective-permute-start.26) | collective-permute-done | bytes 786464 | tf_op jit(solution)/shard_map/ppermute | solution.py:122
  417.6 2.5 convert_add_fusion.1
  420.2 4.7 %all-to-all-start.2 = ((bf16[32,32,384]{2,1,0:T(8,128)(2,1)}), bf16[32,32,384]{2,1,0:T(8,128)(2,1)S(1)}, u32[]{:S(2)}, u32[]{:S(2)}) async-start(bf16[32,32,384]{2,1,0:T(8,128)(2,1)} %bitcast.30), calls=%async_computation.5 | async-start | bytes 1572864 | tf_op jit(solution)/shard_map/all_to_all | solution.py:828
  424.9 3.0 pad_maximum_fusion.1
  432.4 4.1 fusion.10
  437.9 7.7 %all-to-all-done.2 = bf16[32,32,384]{2,1,0:T(8,128)(2,1)S(1)} async-done(((bf16[32,32,384]{2,1,0:T(8,128)(2,1)}), bf16[32,32,384]{2,1,0:T(8,128)(2,1)S(1)}, u32[]{:S(2)}, u32[]{:S(2)}) %all-to-all-start.2) | async-done | bytes 786464 | tf_op jit(solution)/shard_map/all_to_all | solution.py:828
  449.7 2.0 fusion.16
  (175 shorter events, 71.6 us)
Async XLA Ops:
  7.2 15.9 %copy-start.24 = (s32[1,2048]{1,0:T(1,128)S(1)}, s32[1,2048]{1,0:T(1,128)}, u32[]{:S(2)}) copy-start(s32[1,2048]{1,0:T(1,128)} %param.15) | copy-start | bytes 24580
  7.2 17.7 %copy-start.8 = (f32[512,1024]{1,0:T(8,128)S(1)}, f32[512,1024]{1,0:T(8,128)}, u32[]{:S(2)}) copy-start(f32[512,1024]{1,0:T(8,128)} %param.24) | copy-start | bytes 6291460
  7.2 102.8 %all-gather.5.cloned.1.call-start = ((), (), s32[]{:S(2)}) async-start(), calls=%async_computation.7 | async-start | bytes 6758400 | tf_op jit(solution)/shard_map/all_gather | solution.py:75
  14.4 147.4 %all-gather.7.cloned.1.call-start = ((), (), s32[]{:S(2)}) async-start(), calls=%async_computation.8 | async-start | bytes 2949120 | tf_op jit(solution)/shard_map/all_gather | solution.py:75
  14.5 19.3 %collective-permute-start.1 = (bf16[256,1024]{1,0:T(8,128)(2,1)}, bf16[256,1024]{1,0:T(8,128)(2,1)}, u32[]{:S(2)}, u32[]{:S(2)}) collective-permute-start(bf16[256,1024]{1,0:T(8,128)(2,1)} %bitcast.83), channel_id=1, source_target_pairs={{0,8},{8,16},{16,24},{1,9},{9,17},{17,25},{2,10},{10,18},{18,26},{... | collective-permute-start | bytes 1572872 | tf_op jit(solution)/shard_map/ppermute | solution.py:101
  20.2 19.8 %collective-permute-start.3 = (bf16[256,1024]{1,0:T(8,128)(2,1)}, bf16[256,1024]{1,0:T(8,128)(2,1)}, u32[]{:S(2)}, u32[]{:S(2)}) collective-permute-start(bf16[256,1024]{1,0:T(8,128)(2,1)} %bitcast.84), channel_id=1, source_target_pairs={{8,0},{16,8},{24,16},{9,1},{17,9},{25,17},{10,2},{18,10},{26,18},{... | collective-permute-start | bytes 1572872 | tf_op jit(solution)/shard_map/ppermute | solution.py:102
  21.5 46.2 %collective-permute-start = (bf16[256,1024]{1,0:T(8,128)(2,1)}, bf16[256,1024]{1,0:T(8,128)(2,1)}, u32[]{:S(2)}, u32[]{:S(2)}) collective-permute-start(bf16[256,1024]{1,0:T(8,128)(2,1)} %bitcast.85), channel_id=1, source_target_pairs={{0,4},{4,0},{8,12},{12,8},{16,20},{20,16},{24,28},{28,24},{1,5},{5... | collective-permute-start | bytes 1572872 | tf_op jit(solution)/shard_map/ppermute | solution.py:94
  24.9 16.5 %copy-start.21 = (s32[2048]{0:T(1024)}, s32[2048]{0:T(1024)S(1)}, u32[]{:S(2)}) copy-start(s32[2048]{0:T(1024)S(1)} %convert_reduce_fusion) | copy-start | bytes 24580
  25.1 36.6 %copy-start.9 = (bf16[1,256,1024]{2,1,0:T(8,128)(2,1)S(1)}, bf16[1,256,1024]{2,1,0:T(8,128)(2,1)}, u32[]{:S(2)}) copy-start(bf16[1,256,1024]{2,1,0:T(8,128)(2,1)} %param.14) | copy-start | bytes 1572868
  33.8 21.5 %collective-permute-start.5 = (bf16[256,1024]{1,0:T(8,128)(2,1)}, bf16[256,1024]{1,0:T(8,128)(2,1)S(1)}, u32[]{:S(2)}, u32[]{:S(2)}) collective-permute-start(bf16[256,1024]{1,0:T(8,128)(2,1)} %collective-permute-done.1.refs_2_), channel_id=1, source_target_pairs={{0,8},{8,16},{16,24},{1,9},{9,17},{17,25},{2,10},{10,18},{18,26},{... | collective-permute-start | bytes 1572872 | tf_op jit(solution)/shard_map/ppermute | solution.py:101
  40.1 20.3 %collective-permute-start.7 = (bf16[256,1024]{1,0:T(8,128)(2,1)}, bf16[256,1024]{1,0:T(8,128)(2,1)S(1)}, u32[]{:S(2)}, u32[]{:S(2)}) collective-permute-start(bf16[256,1024]{1,0:T(8,128)(2,1)} %collective-permute-done.3.refs_4_), channel_id=1, source_target_pairs={{8,0},{16,8},{24,16},{9,1},{17,9},{25,17},{10,2},{18,10},{26,18},{... | collective-permute-start | bytes 1572872 | tf_op jit(solution)/shard_map/ppermute | solution.py:102
  41.4 27.1 %collective-permute-start.2 = (bf16[256,1024]{1,0:T(8,128)(2,1)}, bf16[256,1024]{1,0:T(8,128)(2,1)}, u32[]{:S(2)}, u32[]{:S(2)}) collective-permute-start(bf16[256,1024]{1,0:T(8,128)(2,1)} %collective-permute-done.1.refs_2_), channel_id=1, source_target_pairs={{8,12},{12,8},{16,20},{20,16},{24,28},{28,24},{9,13},{13,9},{17,21... | collective-permute-start | bytes 1572872 | tf_op jit(solution)/shard_map/ppermute | solution.py:94
  55.3 15.2 %collective-permute-start.9 = (bf16[256,1024]{1,0:T(8,128)(2,1)S(1)}, bf16[256,1024]{1,0:T(8,128)(2,1)}, u32[]{:S(2)}, u32[]{:S(2)}) collective-permute-start(bf16[256,1024]{1,0:T(8,128)(2,1)S(1)} %collective-permute-done.5.refs_6_), channel_id=1, source_target_pairs={{0,8},{8,16},{16,24},{1,9},{9,17},{17,25},{2,10},{10,18},{18,26},{... | collective-permute-start | bytes 1572872 | tf_op jit(solution)/shard_map/ppermute | solution.py:101
  60.4 17.4 %collective-permute-start.11 = (bf16[256,1024]{1,0:T(8,128)(2,1)S(1)}, bf16[256,1024]{1,0:T(8,128)(2,1)}, u32[]{:S(2)}, u32[]{:S(2)}) collective-permute-start(bf16[256,1024]{1,0:T(8,128)(2,1)S(1)} %collective-permute-done.7.refs_8_), channel_id=1, source_target_pairs={{8,0},{16,8},{24,16},{9,1},{17,9},{25,17},{10,2},{18,10},{26,18},{... | collective-permute-start | bytes 1572872 | tf_op jit(solution)/shard_map/ppermute | solution.py:102
  63.8 47.0 %copy-start.11 = (bf16[512,1536]{1,0:T(8,128)(2,1)S(1)}, bf16[512,1536]{1,0:T(8,128)(2,1)}, u32[]{:S(2)}) copy-start(bf16[512,1536]{1,0:T(8,128)(2,1)} %pad_maximum_fusion.2.refs_0_) | copy-start | bytes 4718596
  63.8 26.0 %collective-permute-start.4 = (bf16[256,1024]{1,0:T(8,128)(2,1)}, bf16[256,1024]{1,0:T(8,128)(2,1)S(1)}, u32[]{:S(2)}, u32[]{:S(2)}) collective-permute-start(bf16[256,1024]{1,0:T(8,128)(2,1)} %collective-permute-done.3.refs_4_), channel_id=1, source_target_pairs={{0,4},{4,0},{8,12},{12,8},{16,20},{20,16},{1,5},{5,1},{9,13},{13,9... | collective-permute-start | bytes 1572872 | tf_op jit(solution)/shard_map/ppermute | solution.py:94
  67.8 22.0 %collective-permute-start.6 = (bf16[256,1024]{1,0:T(8,128)(2,1)S(1)}, bf16[256,1024]{1,0:T(8,128)(2,1)S(1)}, u32[]{:S(2)}, u32[]{:S(2)}) collective-permute-start(bf16[256,1024]{1,0:T(8,128)(2,1)S(1)} %collective-permute-done.5.refs_6_), channel_id=1, source_target_pairs={{16,20},{20,16},{24,28},{28,24},{17,21},{21,17},{25,29},{29,25},{1... | collective-permute-start | bytes 1572872 | tf_op jit(solution)/shard_map/ppermute | solution.py:94
  68.5 35.3 %collective-permute-start.8 = (bf16[256,1024]{1,0:T(8,128)(2,1)S(1)}, bf16[256,1024]{1,0:T(8,128)(2,1)S(1)}, u32[]{:S(2)}, u32[]{:S(2)}) collective-permute-start(bf16[256,1024]{1,0:T(8,128)(2,1)S(1)} %collective-permute-done.7.refs_8_), channel_id=1, source_target_pairs={{0,4},{4,0},{8,12},{12,8},{1,5},{5,1},{9,13},{13,9},{2,6},{6,2},{1... | collective-permute-start | bytes 1572872 | tf_op jit(solution)/shard_map/ppermute | solution.py:94
  70.5 33.4 %collective-permute-start.10 = (bf16[256,1024]{1,0:T(8,128)(2,1)}, bf16[256,1024]{1,0:T(8,128)(2,1)S(1)}, u32[]{:S(2)}, u32[]{:S(2)}) collective-permute-start(bf16[256,1024]{1,0:T(8,128)(2,1)} %collective-permute-done.9.refs_10_), channel_id=1, source_target_pairs={{24,28},{28,24},{25,29},{29,25},{26,30},{30,26},{27,31},{31,27}} | collective-permute-start | bytes 1572872 | tf_op jit(solution)/shard_map/ppermute | solution.py:94
  77.7 32.3 %collective-permute-start.12 = (bf16[256,1024]{1,0:T(8,128)(2,1)}, bf16[256,1024]{1,0:T(8,128)(2,1)}, u32[]{:S(2)}, u32[]{:S(2)}) collective-permute-start(bf16[256,1024]{1,0:T(8,128)(2,1)} %collective-permute-done.11.refs_12_), channel_id=1, source_target_pairs={{0,4},{4,0},{1,5},{5,1},{2,6},{6,2},{3,7},{7,3}} | collective-permute-start | bytes 1572872 | tf_op jit(solution)/shard_map/ppermute | solution.py:94
  89.8 14.1 %copy-start.15 = (bf16[256,1024]{1,0:T(8,128)(2,1)}, bf16[256,1024]{1,0:T(8,128)(2,1)S(1)}, u32[]{:S(2)}) copy-start(bf16[256,1024]{1,0:T(8,128)(2,1)S(1)} %collective-permute-done.4.refs_5_) | copy-start | bytes 1572868
  89.8 14.1 %copy-start.16 = (bf16[256,1024]{1,0:T(8,128)(2,1)}, bf16[256,1024]{1,0:T(8,128)(2,1)S(1)}, u32[]{:S(2)}) copy-start(bf16[256,1024]{1,0:T(8,128)(2,1)S(1)} %collective-permute-done.6.refs_7_) | copy-start | bytes 1572868
  110.1 98.7 %all-gather.9.cloned.1.call-start = ((), (), s32[]{:S(2)}) async-start(), calls=%async_computation.13 | async-start | bytes 2621440 | tf_op jit(solution)/shard_map/all_gather | solution.py:951
  110.7 51.4 %collective-permute-start.17 = (bf16[512,1536]{1,0:T(8,128)(2,1)S(1)}, bf16[512,1536]{1,0:T(8,128)(2,1)}, u32[]{:S(2)}, u32[]{:S(2)}) collective-permute-start(bf16[512,1536]{1,0:T(8,128)(2,1)S(1)} %copy-done.11), channel_id=1, source_target_pairs={{0,4},{4,0},{1,5},{5,1},{2,6},{6,2},{3,7},{7,3},{8,12},{12,8},{9,1... | collective-permute-start | bytes 4718600 | tf_op jit(solution)/shard_map/ppermute | solution.py:112
  113.2 51.7 %collective-permute-start.15 = (bf16[512,1536]{1,0:T(8,128)(2,1)S(1)}, bf16[512,1536]{1,0:T(8,128)(2,1)}, u32[]{:S(2)}, u32[]{:S(2)}) collective-permute-start(bf16[512,1536]{1,0:T(8,128)(2,1)S(1)} %copy-done.11), channel_id=1, source_target_pairs={{0,2},{2,0},{1,3},{3,1},{4,6},{6,4},{5,7},{7,5},{8,10},{10,8},{9,1... | collective-permute-start | bytes 4718600 | tf_op jit(solution)/shard_map/ppermute | solution.py:111
  144.9 6.4 %collective-permute-start.13 = (bf16[4,256,128]{2,1,0:T(8,128)(2,1)S(1)}, bf16[4,256,128]{2,1,0:T(8,128)(2,1)S(1)}, u32[]{:S(2)}, u32[]{:S(2)}) collective-permute-start(bf16[4,256,128]{2,1,0:T(8,128)(2,1)S(1)} %get-tuple-element.232), channel_id=1, source_target_pairs={{0,4},{4,0},{1,5},{5,1},{2,6},{6,2},{3,7},{7,3},{8,12},{12,8},{9,1... | collective-permute-start | bytes 786440 | tf_op jit(solution)/shard_map/ppermute | solution.py:946
  161.9 131.1 %reduce-scatter.5.cloned.1.call-start = ((), (), s32[]{:S(2)}) async-start(), calls=%async_computation.9 | async-start | bytes 2949120 | tf_op jit(solution)/shard_map/reduce_scatter | solution.py:79
  162.1 24.5 %collective-permute-start.14 = (bf16[512,1536]{1,0:T(8,128)(2,1)S(1)}, bf16[512,1536]{1,0:T(8,128)(2,1)}, u32[]{:S(2)}, u32[]{:S(2)}) collective-permute-start(bf16[512,1536]{1,0:T(8,128)(2,1)S(1)} %copy-done.11), channel_id=1, source_target_pairs={{0,1},{1,0},{2,3},{3,2},{4,5},{5,4},{6,7},{7,6},{8,9},{9,8},{10,11... | collective-permute-start | bytes 4718600 | tf_op jit(solution)/shard_map/ppermute | solution.py:116
  163.4 20.0 %collective-permute-start.19 = (bf16[256,1536]{1,0:T(8,128)(2,1)S(1)}, bf16[256,1536]{1,0:T(8,128)(2,1)S(1)}, u32[]{:S(2)}, u32[]{:S(2)}) collective-permute-start(bf16[256,1536]{1,0:T(8,128)(2,1)S(1)} %slice.86), channel_id=1, source_target_pairs={{0,2},{2,0},{1,3},{3,1},{4,6},{6,4},{5,7},{7,5},{8,10},{10,8},{9,1... | collective-permute-start | bytes 2359304 | tf_op jit(solution)/shard_map/ppermute | solution.py:113
  166.1 19.8 %collective-permute-start.21 = (bf16[256,1536]{1,0:T(8,128)(2,1)S(1)}, bf16[256,1536]{1,0:T(8,128)(2,1)}, u32[]{:S(2)}, u32[]{:S(2)}) collective-permute-start(bf16[256,1536]{1,0:T(8,128)(2,1)S(1)} %slice.87), channel_id=1, source_target_pairs={{0,4},{4,0},{1,5},{5,1},{2,6},{6,2},{3,7},{7,3},{8,12},{12,8},{9,1... | collective-permute-start | bytes 2359304 | tf_op jit(solution)/shard_map/ppermute | solution.py:114
  167.6 20.9 %collective-permute-start.16 = (bf16[512,1536]{1,0:T(8,128)(2,1)}, bf16[512,1536]{1,0:T(8,128)(2,1)}, u32[]{:S(2)}, u32[]{:S(2)}) collective-permute-start(bf16[512,1536]{1,0:T(8,128)(2,1)} %collective-permute-done.15.refs_2_), channel_id=1, source_target_pairs={{0,1},{1,0},{2,3},{3,2},{4,5},{5,4},{6,7},{7,6},{8,9},{9,8},{10,11... | collective-permute-start | bytes 4718600 | tf_op jit(solution)/shard_map/ppermute | solution.py:116
  167.6 20.9 %collective-permute-start.18 = (bf16[512,1536]{1,0:T(8,128)(2,1)}, bf16[512,1536]{1,0:T(8,128)(2,1)}, u32[]{:S(2)}, u32[]{:S(2)}) collective-permute-start(bf16[512,1536]{1,0:T(8,128)(2,1)} %collective-permute-done.17.refs_4_), channel_id=1, source_target_pairs={{0,1},{1,0},{2,3},{3,2},{4,5},{5,4},{6,7},{7,6},{8,9},{9,8},{10,11... | collective-permute-start | bytes 4718600 | tf_op jit(solution)/shard_map/ppermute | solution.py:116
  183.4 3.2 collective-permute-start.20
  185.9 2.6 collective-permute-start.22
  246.1 136.5 %reduce-scatter.7.cloned.1.call-start = ((), (), s32[]{:S(2)}) async-start(), calls=%async_computation.10 | async-start | bytes 2621440 | tf_op jit(solution)/shard_map/reduce_scatter | solution.py:79
  261.2 45.1 %collective-permute-start.23 = (bf16[4,512,1536]{2,1,0:T(8,128)(2,1)}, bf16[4,512,1536]{2,1,0:T(8,128)(2,1)}, u32[]{:S(2)}, u32[]{:S(2)}) collective-permute-start(bf16[4,512,1536]{2,1,0:T(8,128)(2,1)} %expert_grads.3), channel_id=1, source_target_pairs={{0,1},{1,0},{2,3},{3,2},{4,5},{5,4},{6,7},{7,6},{8,9},{9,8},{10,11... | collective-permute-start | bytes 18874376 | tf_op jit(solution)/shard_map/ppermute | solution.py:981
  281.3 12.9 %copy-start = (f32[256,1024]{1,0:T(8,128)S(1)}, f32[256,1024]{1,0:T(8,128)}, u32[]{:S(2)}) copy-start(f32[256,1024]{1,0:T(8,128)} %get-tuple-element.138) | copy-start | bytes 3145732
  281.3 13.0 %copy-start.20 = (f32[1024,128]{1,0:T(8,128)S(1)}, f32[1024,128]{1,0:T(8,128)}, u32[]{:S(2)}) copy-start(f32[1024,128]{1,0:T(8,128)} %get-tuple-element.119) | copy-start | bytes 1572868
  296.8 19.0 %copy-start.1 = (f32[256,1024]{1,0:T(8,128)}, f32[256,1024]{1,0:T(8,128)S(1)}, u32[]{:S(2)}) copy-start(f32[256,1024]{1,0:T(8,128)S(1)} %subtract_add_fusion) | copy-start | bytes 3145732
  300.5 33.9 %all-to-all-start = ((bf16[8,256,128]{2,1,0:T(8,128)(2,1)}), bf16[8,256,128]{2,1,0:T(8,128)(2,1)S(1)}, u32[]{:S(2)}, u32[]{:S(2)}) async-start(bf16[8,256,128]{2,1,0:T(8,128)(2,1)} %bitcast_bitcast_fusion), calls=%async_computation.2 | async-start | bytes 1048576 | tf_op jit(solution)/shard_map/all_to_all | solution.py:828
  304.6 101.8 %reduce-scatter.9.cloned.1.call-start = ((), (), s32[]{:S(2)}) async-start(), calls=%async_computation.11 | async-start | bytes 2654208 | tf_op jit(solution)/shard_map/reduce_scatter | solution.py:79
  339.2 35.3 %collective-permute-start.25 = (bf16[2,512,768]{2,1,0:T(8,128)(2,1)}, bf16[2,512,768]{2,1,0:T(8,128)(2,1)}, u32[]{:S(2)}, u32[]{:S(2)}) collective-permute-start(bf16[2,512,768]{2,1,0:T(8,128)(2,1)} %get-tuple-element.227), channel_id=1, source_target_pairs={{0,4},{4,0},{1,5},{5,1},{2,6},{6,2},{3,7},{7,3},{8,12},{12,8},{9,1... | collective-permute-start | bytes 4718600 | tf_op jit(solution)/shard_map/ppermute | solution.py:122
  342.3 40.3 %collective-permute-start.24 = (bf16[2,512,768]{2,1,0:T(8,128)(2,1)}, bf16[2,512,768]{2,1,0:T(8,128)(2,1)}, u32[]{:S(2)}, u32[]{:S(2)}) collective-permute-start(bf16[2,512,768]{2,1,0:T(8,128)(2,1)} %get-tuple-element.229), channel_id=1, source_target_pairs={{0,2},{2,0},{1,3},{3,1},{4,6},{6,4},{5,7},{7,5},{8,10},{10,8},{9,1... | collective-permute-start | bytes 4718600 | tf_op jit(solution)/shard_map/ppermute | solution.py:122
  384.9 35.3 %all-to-all-start.1 = ((bf16[8,256,256]{1,2,0:T(8,128)(2,1)}), bf16[8,256,256]{1,2,0:T(8,128)(2,1)}, u32[]{:S(2)}, u32[]{:S(2)}) async-start(bf16[8,256,256]{1,2,0:T(8,128)(2,1)} %copy.80), calls=%async_computation.3 | async-start | bytes 2097152 | tf_op jit(solution)/shard_map/all_to_all | solution.py:828
  389.1 38.8 %reduce-scatter.11.cloned.1.call-start = ((), (), s32[]{:S(2)}) async-start(), calls=%async_computation.12 | async-start | bytes 368640 | tf_op jit(solution)/shard_map/reduce_scatter | solution.py:79
  391.2 15.7 %collective-permute-start.27 = (bf16[512,768]{1,0:T(8,128)(2,1)S(1)}, bf16[512,768]{1,0:T(8,128)(2,1)}, u32[]{:S(2)}, u32[]{:S(2)}) collective-permute-start(bf16[512,768]{1,0:T(8,128)(2,1)S(1)} %dynamic-slice_bitcast_fusion.4), channel_id=1, source_target_pairs={{0,2},{2,0},{1,3},{3,1},{4,6},{6,4},{5,7},{7,5},{8,10},{10,8},{9,1... | collective-permute-start | bytes 2359304 | tf_op jit(solution)/shard_map/ppermute | solution.py:122
  396.8 20.9 %collective-permute-start.26 = (bf16[512,768]{1,0:T(8,128)(2,1)S(1)}, bf16[512,768]{1,0:T(8,128)(2,1)}, u32[]{:S(2)}, u32[]{:S(2)}) collective-permute-start(bf16[512,768]{1,0:T(8,128)(2,1)S(1)} %dynamic-slice_bitcast_fusion.5), channel_id=1, source_target_pairs={{0,4},{4,0},{1,5},{5,1},{2,6},{6,2},{3,7},{7,3},{8,12},{12,8},{9,1... | collective-permute-start | bytes 2359304 | tf_op jit(solution)/shard_map/ppermute | solution.py:122
  420.2 25.4 %all-to-all-start.2 = ((bf16[32,32,384]{2,1,0:T(8,128)(2,1)}), bf16[32,32,384]{2,1,0:T(8,128)(2,1)S(1)}, u32[]{:S(2)}, u32[]{:S(2)}) async-start(bf16[32,32,384]{2,1,0:T(8,128)(2,1)} %bitcast.30), calls=%async_computation.5 | async-start | bytes 1572864 | tf_op jit(solution)/shard_map/all_to_all | solution.py:828
  (15 other events, 72.7 us)
Sparse Core Ops, SparseCore 0:
  14.5 91.7 all-gather.4
  110.2 51.5 all-gather.6
  164.0 44.7 all-gather.8
  246.2 46.7 reduce-scatter.4
  295.1 51.6 reduce-scatter.6
  350.4 50.4 reduce-scatter.8
  406.6 18.9 reduce-scatter.10

commit v7 on v6

--- a/solution.py
+++ b/solution.py
@@ -31,6 +31,7 @@
 PLANE = ("b", "y", "c")
 SEQ = ("a", "b")
 ALL = ("a", "b", "y", "c")
+SWAP = [(0, 1), (1, 0)]
 
 f32 = jnp.float32
 bf16 = jnp.bfloat16
@@ -106,20 +107,20 @@
 
 
 def plane_gather(x):
-    swap = [(0, 1), (1, 0)]
+    swap = SWAP
     half = x.shape[0] // 2
-    from_y = lax.ppermute(x, "y", swap)
-    from_b = lax.ppermute(x, "b", swap)
-    upper = lax.ppermute(from_b[:half], "y", swap)
-    lower = lax.ppermute(from_y[half:], "b", swap)
+    from_y = lax.ppermute(x, "y", SWAP)
+    from_b = lax.ppermute(x, "b", SWAP)
+    upper = lax.ppermute(from_b[:half], "y", SWAP)
+    lower = lax.ppermute(from_y[half:], "b", SWAP)
     return [
-        (block, lax.ppermute(block, "c", swap)) for block in (x, from_y, from_b, upper, lower)
+        (block, lax.ppermute(block, "c", SWAP)) for block in (x, from_y, from_b, upper, lower)
     ]
 
 
 def halve_send(v, axis, at):
     me = lax.axis_index(axis)
-    other = lax.ppermute(lax.dynamic_index_in_dim(v, 1 - me, at, False), axis, [(0, 1), (1, 0)])
+    other = lax.ppermute(lax.dynamic_index_in_dim(v, 1 - me, at, False), axis, SWAP)
     return lax.dynamic_index_in_dim(v, me, at, False), other
 
 
@@ -667,10 +668,11 @@
 
 def expert_grads_kernel(with_y, half_ref, n_ref, ct_ref, w_ref, hidden_ref, pre_ref, *refs):
     if with_y:
-        y_ref, grad_ref, n_t, ct_t, acc = refs
+        left_ref, right_ref, y_ref, n_t, ct_t, acc = refs
     else:
-        grad_ref, n_t, ct_t = refs
+        left_ref, right_ref, n_t, ct_t = refs
     e = pl.program_id(0)
+    cut = left_ref.shape[2]
 
     @pl.when(e == 0)
     def _():
@@ -679,8 +681,10 @@
         if with_y:
             acc[...] = jnp.zeros_like(acc)
 
-    grad_ref[0, :, : 2 * F] = jnp.dot(n_t[...], pre_ref[0], preferred_element_type=f32).astype(bf16)
-    grad_ref[0, :, 2 * F :] = (
+    grads = jnp.dot(n_t[...], pre_ref[0], preferred_element_type=f32).astype(bf16)
+    left_ref[0] = grads[:, :cut]
+    right_ref[0, :, : 2 * F - cut] = grads[:, cut:]
+    right_ref[0, :, 2 * F - cut :] = (
         RESIDUAL_SCALE * jnp.dot(ct_t[...], hidden_ref[0], preferred_element_type=f32)
     ).astype(bf16)
     if not with_y:
@@ -695,14 +699,14 @@
 def expert_grads(half, halves, normed, early, w_all, hidden, pre, with_y):
     rows, width = normed.shape
     count = w_all.shape[0]
-    own = width // halves
+    own, cut = width // halves, 3 * F // 2
     feature = pl.BlockSpec((rows, own), lambda e, h: (0, h[0]))
-    out_specs = [pl.BlockSpec((1, own, 3 * F), lambda e, h: (e, 0, 0))]
-    out_shape = [jax.ShapeDtypeStruct((count, own, 3 * F), bf16)]
+    out_specs = [pl.BlockSpec((1, own, cut), lambda e, h: (e, 0, 0))] * 2
+    out_shape = [jax.ShapeDtypeStruct((count, own, cut), bf16)] * 2
     scratch = [pltpu.VMEM((own, rows), bf16), pltpu.VMEM((own, rows), bf16)]
     if with_y:
-        out_specs.insert(0, pl.BlockSpec((rows, width), lambda e, h: (0, 0)))
-        out_shape.insert(0, jax.ShapeDtypeStruct((rows, width), bf16))
+        out_specs.append(pl.BlockSpec((rows, width), lambda e, h: (0, 0)))
+        out_shape.append(jax.ShapeDtypeStruct((rows, width), bf16))
         scratch.append(pltpu.VMEM((rows, width), f32))
     return pl.pallas_call(
         functools.partial(expert_grads_kernel, with_y),
@@ -944,7 +948,7 @@
         member = lax.axis_index("b")
         by_column = attended.reshape(GROUPS, 2, token_count, PAIR)
         other = lax.ppermute(
-            lax.dynamic_index_in_dim(by_column, 1 - member, 1, False), "b", [(0, 1), (1, 0)]
+            lax.dynamic_index_in_dim(by_column, 1 - member, 1, False), "b", SWAP
         )
         own = lax.dynamic_index_in_dim(by_column, member, 1, False)
         pair, early_all = lax.optimization_barrier((jnp.stack([own, other]), early_all))
@@ -977,12 +981,19 @@
     inputs = (normed_all, early_all, experts_all, gated_hidden, grad_pre)
     if small_plane:
         core = lax.axis_index("c")
-        (send,) = expert_grads((1 - core).reshape(1), 2, *inputs, False)
-        arrived = lax.ppermute(send, "c", [(0, 1), (1, 0)])
-        moe_part, keep = expert_grads(core.reshape(1), 2, *inputs, True)
-        back_own, moe_part, keep = lax.optimization_barrier((back_own, moe_part, keep))
+        send = expert_grads((1 - core).reshape(1), 2, *inputs, False)
+        arrived = [lax.ppermute(x, "c", SWAP) for x in send]
+        *keep, moe_part = expert_grads(core.reshape(1), 2, *inputs, True)
+        left, right = (
+            halve_add(terms).reshape((2, 2) + terms[0].shape[1:]) for terms in zip(keep, arrived)
+        )
+        back_own, moe_part, left, right = lax.optimization_barrier(
+            (back_own, moe_part, left, right)
+        )
+        left, right = halve_send(left, "y", 1), halve_send(right, "b", 0)
     else:
-        moe_part, grad_experts = expert_grads(jnp.zeros((1,), jnp.int32), 1, *inputs, True)
+        *grads, moe_part = expert_grads(jnp.zeros((1,), jnp.int32), 1, *inputs, True)
+        grad_experts = jnp.concatenate(grads, axis=2)
         back_own, moe_part, grad_experts = lax.optimization_barrier(
             (back_own, moe_part, grad_experts)
         )
@@ -1004,22 +1015,18 @@
     grad_mixed = exchange(
         grad_heads.reshape(token_count, KEY_VALUE_HEADS, PAIR).transpose(1, 0, 2), head_axes
     ).reshape(span, PAIR)
-    if small_plane:
-        keep, arrived, grad_heads = lax.optimization_barrier((keep, arrived, grad_heads))
-        total = keep.astype(f32) + arrived.astype(f32)
-        total = total.astype(bf16).reshape((2, 2) + keep.shape[1:])
-        total, attended_low, grad_router = lax.optimization_barrier(
-            (total, attended_low, grad_router)
-        )
-        wide = 3 * F // 2
-        left, right = halve_send(total[..., :wide], "y", 1), halve_send(total[..., wide:], "b", 0)
     small = jnp.concatenate([grad_router, grad_gain_two[:, None]], axis=1)
     second_part = jnp.concatenate(
         [contract_rows(attended_low, grad_attn_low), pad_lanes(small, LANES)], axis=1
     ).astype(bf16)
     cols = second_part.shape[1]
     second_part = second_part.reshape(GROUPS, -1, own_rows, cols).transpose(1, 0, 2, 3)
-    second_part, grad_mixed = lax.optimization_barrier((second_part, grad_mixed))
+    if small_plane:
+        left, right = halve_add(left), halve_add(right)
+        second_part, left, right, grad_mixed = lax.optimization_barrier(
+            (second_part, left, right, grad_mixed)
+        )
+        left, right = halve_send(left, "b", 0), halve_send(right, "y", 0)
     rest = scatter_sum(second_part.reshape(-1, cols), PLANE)
     grads = attend_back(
         bounds, qkv, kv, kv_at, doc_rows, grad_mixed, attention_result, log_total,
@@ -1034,8 +1041,6 @@
         left, right, moe_sum, grad_pack = lax.optimization_barrier(
             (left, right, moe_sum, grad_pack)
         )
-        left, right = halve_add(left), halve_add(right)
-        left, right = halve_send(left, "b", 0), halve_send(right, "y", 0)
     first_part = head_grads(place, x_span, normed_span, first_all, grad_pack)
     rest, first_part = lax.optimization_barrier((rest, first_part))
     rest = scatter_sum(rest, "a")

time: 467 us -> 459 us (0.983)
  starting transfers between devices: 64.2 us -> 58.8 us
  Pallas kernels: 151 us -> 156 us
    all_to_all x3, waiting for transfers between devices: 23.6 us -> 12.5 us  [exchange(): return lax.all_to_all(x, axes, 0, 0, tiled=True)]
    convert_element_type x1 -> x0, other arithmetic: 9.27 us -> none  [body(): total = total.astype(bf16).reshape((2, 2) + keep.shape[1:])]
    convert_element_type x2 -> x4, other arithmetic: 3.74 us -> 12.7 us  [halve_add(): return (own.astype(f32) + other.astype(f32)).astype(own.dtype)]
    ppermute x14 -> x15, waiting for transfers between devices: 42 us -> 46.2 us  [the longest x4 26.4 us: halve_send(): lax.ppermute(lax.dynamic_index_in_dim(v, 1 - me, at, False), axis, SWAP)]
    ppermute x14 -> x15, starting transfers between devices: 16.7 us -> 13.5 us  [the longest x4 5.88 us: halve_send(): lax.ppermute(lax.dynamic_index_in_dim(v, 1 - me, at, False), axis, SWAP)]
  transfers between devices with their start and end apart: 38 -> 39, of which waited for: 20 -> 20; matrix products, arithmetic and copies ran while one was open for 15% -> 16% of each run, Pallas kernels for 24% -> 26%
where the time goes in v7:
time: 459 us; the launch traced here: 452 us
  Pallas kernels  156 us (34%)
  waiting for transfers between devices  140 us (31%)
  starting transfers between devices  58.8 us (13%)
  other arithmetic  49 us (11%)
  local copies, waits for them, and re-layouts  21.6 us (5%)
  between operations  15.3 us (3%)
  matrix products  11 us (2%)
    pallas_call x2, Pallas kernels, expert_grads(): pl.pallas_call(functools.partial(expert_grads_kernel, with_y), grid_spec=...  32.9 us
    pallas_call x1, Pallas kernels, experts(): pl.pallas_call(experts_kernel, grid_spec=pltpu.PrefetchScalarGridSpec(num...  29.2 us
    pallas_call x1, Pallas kernels, attend_back(): pl.pallas_call(functools.partial(attend_back_kernel, fold), grid_spec=plt...  28 us
    ppermute x4, waiting for transfers between devices, halve_send(): lax.ppermute(lax.dynamic_index_in_dim(v, 1 - me, at, False), axis, SWAP)  26.4 us
    ppermute x3, waiting for transfers between devices, grid_gather(): up = lax.ppermute(up, 'a', line_pairs(n, 1))  23.3 us
    ppermute x7, waiting for transfers between devices, cross(): lax.ppermute(block, SEQ, [(2 * i + j, 2 * i + 1 - j) for i in range(n) if...  20.3 us
    pallas_call x1, Pallas kernels, place_experts(): pl.pallas_call(place_experts_kernel, grid_spec=pltpu.PrefetchScalarGridSp...  18.5 us
    pallas_call x1, Pallas kernels, attend(): pl.pallas_call(attend_kernel, grid_spec=pltpu.PrefetchScalarGridSpec(num_...  18.4 us
  transfers between devices with their start and end apart: 39, of which 20 were waited for; matrix products, arithmetic and copies ran while one was open for 16% of the time, Pallas kernels for 26%

profile of v7, /device:TPU:0, one launch (start us, length us, event | category | flops | bytes accessed | tf_op | source)
XLA Modules:
  0.0 452.0 jit_solution(14485843696981326072)
XLA Ops:
  14.5 3.0 collective-permute-start
  17.5 4.3 collective-permute-start.1
  26.3 9.0 %collective-permute-done.1.refs_2_ = bf16[256,1024]{1,0:T(8,128)(2,1)} collective-permute-done((bf16[256,1024]{1,0:T(8,128)(2,1)}, bf16[256,1024]{1,0:T(8,128)(2,1)}, u32[]{:S(2)}, u32[]{:S(2)}) %collective-permute-start.1) | collective-permute-done | bytes 524320 | tf_op jit(solution)/shard_map/ppermute | solution.py:102
  35.3 4.4 collective-permute-start.5
  44.2 14.2 %collective-permute-done.5.refs_6_ = bf16[256,1024]{1,0:T(8,128)(2,1)S(1)} collective-permute-done((bf16[256,1024]{1,0:T(8,128)(2,1)}, bf16[256,1024]{1,0:T(8,128)(2,1)S(1)}, u32[]{:S(2)}, u32[]{:S(2)}) %collective-permute-start.5) | collective-permute-done | bytes 524320 | tf_op jit(solution)/shard_map/ppermute | solution.py:102
  58.5 5.1 %collective-permute-start.9 = (bf16[256,1024]{1,0:T(8,128)(2,1)S(1)}, bf16[256,1024]{1,0:T(8,128)(2,1)}, u32[]{:S(2)}, u32[]{:S(2)}) collective-permute-start(bf16[256,1024]{1,0:T(8,128)(2,1)S(1)} %collective-permute-done.5.refs_6_), channel_id=1, source_target_pairs={{0,8},{8,16},{16,24},{1,9},{9,17},{17,25},{2,10},{10,18},{18,26},{... | collective-permute-start | bytes 1572872 | tf_op jit(solution)/shard_map/ppermute | solution.py:102
  66.1 1.9 pad_maximum_fusion.3
  69.2 1.9 collective-permute-start.4
  71.8 3.9 collective-permute-start.8
  77.2 7.8 %collective-permute-done.11.refs_12_ = bf16[256,1024]{1,0:T(8,128)(2,1)} collective-permute-done((bf16[256,1024]{1,0:T(8,128)(2,1)}, bf16[256,1024]{1,0:T(8,128)(2,1)}, u32[]{:S(2)}, u32[]{:S(2)}) %collective-permute-start.11) | collective-permute-done | bytes 524320 | tf_op jit(solution)/shard_map/ppermute | solution.py:103
  85.1 1.9 collective-permute-start.12
  87.6 5.5 %multiply_sine_fusion = (f32[2048,32]{1,0:T(8,128)}, f32[2048,32]{1,0:T(8,128)}) fusion(f32[32]{0:T(128)S(1)} %multiply_power_fusion, f32[2048]{0:T(1024)S(1)} %subtract_convert_fusion), kind=kLoop, calls=%fused_computation.23 | loop fusion | flops 65536 | bytes 532608 | tf_op jit(solution)/shard_map/sin | solution.py:44
  93.1 3.0 collective-permute-done.4.refs_5_
  96.1 11.3 %collective-permute-done.8.refs_9_ = bf16[256,1024]{1,0:T(8,128)(2,1)} collective-permute-done((bf16[256,1024]{1,0:T(8,128)(2,1)}, bf16[256,1024]{1,0:T(8,128)(2,1)}, u32[]{:S(2)}, u32[]{:S(2)}) %collective-permute-start.8) | collective-permute-done | bytes 524320 | tf_op jit(solution)/shard_map/ppermute | solution.py:95
  107.4 6.0 %collective-permute-done.12.refs_13_ = bf16[256,1024]{1,0:T(8,128)(2,1)} collective-permute-done((bf16[256,1024]{1,0:T(8,128)(2,1)}, bf16[256,1024]{1,0:T(8,128)(2,1)}, u32[]{:S(2)}, u32[]{:S(2)}) %collective-permute-start.12) | collective-permute-done | bytes 524320 | tf_op jit(solution)/shard_map/ppermute | solution.py:95
  114.1 3.2 collective-permute-start.15
  117.6 11.0 %project.1 = (bf16[2048,256]{1,0:T(8,128)(2,1)}, bf16[2048,1024]{1,0:T(8,128)(2,1)}, bf16[2048,1024]{1,0:T(8,128)(2,1)}, f32[2048,128]{1,0:T(8,128)}, f32[2048,128]{1,0:T(8,128)}) custom-call(s32[3]{0:T(128)} %pad_add_fusion.place_ref.head_ref, bf16[256,1024]{1,0:T(8,128)(2,1)} %bitcast.91, bf16[256,1024]{1,0:T(8,128)(2,1)} %collective-permute-done.refs_1_, ...), custom_call_target="tpu_custom_call" | custom-call | flops 1073741824 | bytes 18874368 | tf_op jit(solution)/shard_map/project/pallas_call | solution.py:196
  128.5 18.4 %attend.1 = (f32[2048,128]{1,0:T(8,128)}, bf16[2048,128]{1,0:T(8,128)(2,1)}, f32[4,1,1024]{2,1,0:T(1,128)}) custom-call(s32[9]{0:T(128)} %pad_add_fusion.1.bounds_ref, bf16[2048,256]{1,0:T(8,128)(2,1)} %get-tuple-element.101.q_ref.kv_ref, bf16[2048,256]{1,0:T(8,128)(2,1)} %get-tuple-element.101.q_ref.kv_ref, s32[4,1,512]{2,1,0:T(1,128)} %bitcast.100), custom_call_target="tpu_custom_call" | custom-call | flops 2147483648 | bytes 6291456 | tf_op jit(solution)/shard_map/attend/pallas_call | solution.py:371
  148.0 2.0 collective-permute-start.13
  150.0 4.5 collective-permute-done.13
  155.3 7.7 %all-gather.7.cloned.1.call-done.refs_10_.routed_ref.ct_ref = bf16[1024,1152]{1,0:T(8,128)(2,1)} async-done(((bf16[256,1152]{1,0:T(8,128)(2,1)}), bf16[1024,1152]{1,0:T(8,128)(2,1)}) %all-gather.7.cloned.1.call-update) | async-done | bytes 2359312 | tf_op jit(solution)/shard_map/all_gather | solution.py:76
  169.3 15.2 %collective-permute-done.19.refs_6_ = bf16[256,1536]{1,0:T(8,128)(2,1)S(1)} collective-permute-done((bf16[256,1536]{1,0:T(8,128)(2,1)S(1)}, bf16[256,1536]{1,0:T(8,128)(2,1)S(1)}, u32[]{:S(2)}, u32[]{:S(2)}) %collective-permute-start.19) | collective-permute-done | bytes 786464 | tf_op jit(solution)/shard_map/ppermute | solution.py:114
  184.6 3.0 collective-permute-done.21.refs_8_
  189.9 18.5 %place_experts.1 = (bf16[4,1024,1536]{2,1,0:T(8,128)(2,1)}, f32[4,1024,512]{2,1,0:T(8,128)}) custom-call(s32[2]{0:T(128)} %pad_add_fusion.2.place_ref, bf16[512,1536]{1,0:T(8,128)(2,1)} %copy-done.12, bf16[512,1536]{1,0:T(8,128)(2,1)} %collective-permute-done.14.refs_1_, bf16[512,1536]{1,0:T(8,128)(2,1)} %collective-permute-done.15.refs_2_, ...), custom_call_target="tpu_custom_call" | custom-call | flops 4294967296 | bytes 37748736 | tf_op jit(solution)/shard_map/place_experts/pallas_call | solution.py:553
  210.0 8.2 %join.1 = (bf16[1024,1024]{1,0:T(8,128)(2,1)}, f32[256,1024]{1,0:T(8,128)}, bf16[256,1024]{1,0:T(8,128)(2,1)}) custom-call(s32[3]{0:T(128)} %pad_add_fusion.place_ref.head_ref, bf16[4,2,4,256,128]{4,3,2,1,0:T(8,128)(2,1)} %bitcast.92, bf16[1024,3200]{1,0:T(8,128)(2,1)} %all-gather.5.cloned.1.call-done.refs_14_.refs_15_.w_ref.small_ref.router_ref, ...), custom_call_target="tpu_custom_call" | custom-call | flops 2147483648 | bytes 12582912 | tf_op jit(solution)/shard_map/join/pallas_call | solution.py:767
  218.2 29.2 %experts.1 = (bf16[1024,1152]{1,0:T(8,128)(2,1)}, f32[1024,128]{1,0:T(8,128)}, bf16[4,1024,512]{2,1,0:T(8,128)(2,1)}, bf16[4,1024,1024]{2,1,0:T(8,128)(2,1)}) custom-call(s32[1]{0:T(128)} %bitcast.1.group_ref, bf16[1024,1024]{1,0:T(8,128)(2,1)} %get-tuple-element.109.n_ref, bf16[1024,1152]{1,0:T(8,128)(2,1)} %all-gather.7.cloned.1.call-done.refs_10_.routed_ref.ct_ref, ...), custom_call_target="tpu_custom_call" | custom-call | flops 17179869184 | bytes 41943040 | tf_op jit(solution)/shard_map/experts/pallas_call | solution.py:635
  247.7 14.3 %expert_grads.3 = (bf16[4,512,768]{2,1,0:T(8,128)(2,1)}, bf16[4,512,768]{2,1,0:T(8,128)(2,1)}) custom-call(s32[1]{0:T(128)} %bitcast.17.half_ref, bf16[1024,1024]{1,0:T(8,128)(2,1)} %get-tuple-element.109.n_ref, bf16[1024,1152]{1,0:T(8,128)(2,1)} %all-gather.7.cloned.1.call-done.refs_10_.routed_ref.ct_ref, bf16[4,1024,1536]{2,1,0:T(8,128)(2,1)} %get-tuple-element.112.w_ref, ...), custom_call_target="tpu_custom_call" | custom-call | flops 6442450944 | bytes 31457280 | tf_op jit(solution)/shard_map/expert_grads/pallas_call | solution.py:711
  262.6 18.6 %expert_grads.2 = (bf16[4,512,768]{2,1,0:T(8,128)(2,1)}, bf16[4,512,768]{2,1,0:T(8,128)(2,1)}, bf16[1024,1024]{1,0:T(8,128)(2,1)}) custom-call(s32[1]{0:T(128)} %bitcast.16.half_ref, bf16[1024,1024]{1,0:T(8,128)(2,1)} %get-tuple-element.109.n_ref, bf16[1024,1152]{1,0:T(8,128)(2,1)} %all-gather.7.cloned.1.call-done.refs_10_.routed_ref.ct_ref, ...), custom_call_target="tpu_custom_call" | custom-call | flops 10737418240 | bytes 31457280 | tf_op jit(solution)/shard_map/expert_grads/pallas_call | solution.py:711
  281.2 5.3 %add_convert_fusion.1 = bf16[4,512,768]{2,1,0:T(8,128)(2,1)} fusion(bf16[4,512,768]{2,1,0:T(8,128)(2,1)} %collective-permute-done.23, bf16[4,512,768]{2,1,0:T(8,128)(2,1)} %get-tuple-element.118), kind=kLoop, calls=%fused_computation.2 | loop fusion | flops 6291456 | bytes 9437184 | tf_op jit(solution)/shard_map/convert_element_type | solution.py:129
  286.5 2.5 add_convert_fusion
  289.1 5.3 %reduce-scatter.5.cloned.1.call-done = bf16[256,1152]{1,0:T(8,128)(2,1)} async-done(((bf16[1024,1152]{1,0:T(8,128)(2,1)}), bf16[256,1152]{1,0:T(8,128)(2,1)}) %reduce-scatter.5.cloned.1.call-update) | async-done | bytes 589840 | tf_op jit(solution)/shard_map/reduce_scatter | solution.py:80
  297.5 2.0 multiply_reduce_fusion.1
  308.0 2.7 fusion.12
  311.6 3.5 all-to-all-start
  318.1 26.4 %collective-permute-done.26 = bf16[2,512,768]{2,1,0:T(8,128)(2,1)} collective-permute-done((bf16[2,512,768]{2,1,0:T(8,128)(2,1)}, bf16[2,512,768]{2,1,0:T(8,128)(2,1)}, u32[]{:S(2)}, u32[]{:S(2)}) %collective-permute-start.26) | collective-permute-done | bytes 1572896 | tf_op jit(solution)/shard_map/ppermute | solution.py:123
  344.4 1.9 fusion.2
  346.3 3.0 fusion.3
  349.3 2.8 dynamic-slice_bitcast_fusion.4
  356.3 28.0 %attend_back.1.grad_ref = bf16[2048,256]{1,0:T(8,128)(2,1)} custom-call(s32[9]{0:T(128)} %pad_add_fusion.1.bounds_ref, bf16[2048,256]{1,0:T(8,128)(2,1)} %get-tuple-element.101.q_ref.kv_ref, bf16[2048,256]{1,0:T(8,128)(2,1)} %get-tuple-element.101.q_ref.kv_ref, s32[4,1,512]{2,1,0:T(1,128)} %bitcast.101, bf16[2048,128]{1,0:T(8,128)(2,1)} %bitcast.96, ...), custom_call_target="tpu_custom_call" | custom-call | flops 5368709120 | bytes 8388608 | tf_op jit(solution)/shard_map/attend_back/pallas_call | solution.py:478
  384.4 2.7 copy.80
  387.2 4.2 all-to-all-start.1
  391.5 7.8 %head_grads.1 = bf16[1024,384]{1,0:T(8,128)(2,1)} custom-call(s32[3]{0:T(128)} %pad_add_fusion.place_ref.head_ref, bf16[2048,1024]{1,0:T(8,128)(2,1)} %get-tuple-element.106.x_ref, bf16[2048,1024]{1,0:T(8,128)(2,1)} %get-tuple-element.136.normed_ref, bf16[1024,3200]{1,0:T(8,128)(2,1)} %all-gather.5.cloned.1.call-done.refs_14_.refs_15_.w_ref.small_ref.router_ref, ...), custom_call_target="tpu_custom_call" | custom-call | flops 2147483648 | bytes 12582912 | tf_op jit(solution)/shard_map/head_grads/pallas_call | solution.py:265
  404.3 10.9 %all-to-all-done.1 = bf16[8,256,256]{1,2,0:T(8,128)(2,1)} async-done(((bf16[8,256,256]{1,2,0:T(8,128)(2,1)}), bf16[8,256,256]{1,2,0:T(8,128)(2,1)}, u32[]{:S(2)}, u32[]{:S(2)}) %all-to-all-start.1) | async-done | bytes 1048608 | tf_op jit(solution)/shard_map/all_to_all | solution.py:832
  415.2 2.6 all-to-all-start.2
  417.8 3.0 pad_maximum_fusion.1
  420.9 7.2 %reduce-scatter.11.cloned.1.call-done = bf16[32,1152]{1,0:T(8,128)(2,1)} async-done(((bf16[128,1152]{1,0:T(8,128)(2,1)}), bf16[32,1152]{1,0:T(8,128)(2,1)}) %reduce-scatter.11.cloned.1.call-update) | async-done | bytes 73744 | tf_op jit(solution)/shard_map/reduce_scatter | solution.py:80
  432.6 4.1 fusion.15
  440.5 1.9 weight_sums.1
  (185 shorter events, 71.5 us)
Async XLA Ops:
  7.2 15.9 %copy-start.13 = (f32[512,512]{1,0:T(8,128)S(1)}, f32[512,512]{1,0:T(8,128)}, u32[]{:S(2)}) copy-start(f32[512,512]{1,0:T(8,128)} %param.25) | copy-start | bytes 3145732
  7.2 16.8 %copy-start.10 = (f32[512,1024]{1,0:T(8,128)S(1)}, f32[512,1024]{1,0:T(8,128)}, u32[]{:S(2)}) copy-start(f32[512,1024]{1,0:T(8,128)} %param.24) | copy-start | bytes 6291460
  7.2 106.2 %all-gather.5.cloned.1.call-start = ((), (), s32[]{:S(2)}) async-start(), calls=%async_computation.7 | async-start | bytes 6758400 | tf_op jit(solution)/shard_map/all_gather | solution.py:76
  14.4 148.6 %all-gather.7.cloned.1.call-start = ((), (), s32[]{:S(2)}) async-start(), calls=%async_computation.8 | async-start | bytes 2949120 | tf_op jit(solution)/shard_map/all_gather | solution.py:76
  14.5 56.6 %collective-permute-start = (bf16[256,1024]{1,0:T(8,128)(2,1)}, bf16[256,1024]{1,0:T(8,128)(2,1)}, u32[]{:S(2)}, u32[]{:S(2)}) collective-permute-start(bf16[256,1024]{1,0:T(8,128)(2,1)} %bitcast.88), channel_id=1, source_target_pairs={{0,4},{4,0},{8,12},{12,8},{16,20},{20,16},{24,28},{28,24},{1,5},{5... | collective-permute-start | bytes 1572872 | tf_op jit(solution)/shard_map/ppermute | solution.py:95
  17.5 17.9 %collective-permute-start.1 = (bf16[256,1024]{1,0:T(8,128)(2,1)}, bf16[256,1024]{1,0:T(8,128)(2,1)}, u32[]{:S(2)}, u32[]{:S(2)}) collective-permute-start(bf16[256,1024]{1,0:T(8,128)(2,1)} %bitcast.89), channel_id=1, source_target_pairs={{0,8},{8,16},{16,24},{1,9},{9,17},{17,25},{2,10},{10,18},{18,26},{... | collective-permute-start | bytes 1572872 | tf_op jit(solution)/shard_map/ppermute | solution.py:102
  21.8 19.6 %collective-permute-start.3 = (bf16[256,1024]{1,0:T(8,128)(2,1)}, bf16[256,1024]{1,0:T(8,128)(2,1)}, u32[]{:S(2)}, u32[]{:S(2)}) collective-permute-start(bf16[256,1024]{1,0:T(8,128)(2,1)} %bitcast.90), channel_id=1, source_target_pairs={{8,0},{16,8},{24,16},{9,1},{17,9},{25,17},{10,2},{18,10},{26,18},{... | collective-permute-start | bytes 1572872 | tf_op jit(solution)/shard_map/ppermute | solution.py:103
  25.9 67.2 %copy-start.24 = (s32[2048]{0:T(1024)}, s32[2048]{0:T(1024)S(1)}, u32[]{:S(2)}) copy-start(s32[2048]{0:T(1024)S(1)} %convert_reduce_fusion) | copy-start | bytes 24580
  35.3 23.1 %collective-permute-start.5 = (bf16[256,1024]{1,0:T(8,128)(2,1)}, bf16[256,1024]{1,0:T(8,128)(2,1)S(1)}, u32[]{:S(2)}, u32[]{:S(2)}) collective-permute-start(bf16[256,1024]{1,0:T(8,128)(2,1)} %collective-permute-done.1.refs_2_), channel_id=1, source_target_pairs={{0,8},{8,16},{16,24},{1,9},{9,17},{17,25},{2,10},{10,18},{18,26},{... | collective-permute-start | bytes 1572872 | tf_op jit(solution)/shard_map/ppermute | solution.py:102
  41.4 23.4 %collective-permute-start.7 = (bf16[256,1024]{1,0:T(8,128)(2,1)}, bf16[256,1024]{1,0:T(8,128)(2,1)}, u32[]{:S(2)}, u32[]{:S(2)}) collective-permute-start(bf16[256,1024]{1,0:T(8,128)(2,1)} %collective-permute-done.3.refs_4_), channel_id=1, source_target_pairs={{8,0},{16,8},{24,16},{9,1},{17,9},{25,17},{10,2},{18,10},{26,18},{... | collective-permute-start | bytes 1572872 | tf_op jit(solution)/shard_map/ppermute | solution.py:103
  42.8 29.1 %collective-permute-start.2 = (bf16[256,1024]{1,0:T(8,128)(2,1)}, bf16[256,1024]{1,0:T(8,128)(2,1)}, u32[]{:S(2)}, u32[]{:S(2)}) collective-permute-start(bf16[256,1024]{1,0:T(8,128)(2,1)} %collective-permute-done.1.refs_2_), channel_id=1, source_target_pairs={{8,12},{12,8},{16,20},{20,16},{24,28},{28,24},{9,13},{13,9},{17,21... | collective-permute-start | bytes 1572872 | tf_op jit(solution)/shard_map/ppermute | solution.py:95
  58.5 34.6 %copy-start.18 = (bf16[256,1024]{1,0:T(8,128)(2,1)}, bf16[256,1024]{1,0:T(8,128)(2,1)S(1)}, u32[]{:S(2)}) copy-start(bf16[256,1024]{1,0:T(8,128)(2,1)S(1)} %collective-permute-done.5.refs_6_) | copy-start | bytes 1572868
  58.5 17.3 %collective-permute-start.9 = (bf16[256,1024]{1,0:T(8,128)(2,1)S(1)}, bf16[256,1024]{1,0:T(8,128)(2,1)}, u32[]{:S(2)}, u32[]{:S(2)}) collective-permute-start(bf16[256,1024]{1,0:T(8,128)(2,1)S(1)} %collective-permute-done.5.refs_6_), channel_id=1, source_target_pairs={{0,8},{8,16},{16,24},{1,9},{9,17},{17,25},{2,10},{10,18},{18,26},{... | collective-permute-start | bytes 1572872 | tf_op jit(solution)/shard_map/ppermute | solution.py:102
  64.8 20.2 %collective-permute-start.11 = (bf16[256,1024]{1,0:T(8,128)(2,1)}, bf16[256,1024]{1,0:T(8,128)(2,1)}, u32[]{:S(2)}, u32[]{:S(2)}) collective-permute-start(bf16[256,1024]{1,0:T(8,128)(2,1)} %collective-permute-done.7.refs_8_), channel_id=1, source_target_pairs={{8,0},{16,8},{24,16},{9,1},{17,9},{25,17},{10,2},{18,10},{26,18},{... | collective-permute-start | bytes 1572872 | tf_op jit(solution)/shard_map/ppermute | solution.py:103
  69.2 94.1 %copy-start.12 = (bf16[512,1536]{1,0:T(8,128)(2,1)}, bf16[512,1536]{1,0:T(8,128)(2,1)S(1)}, u32[]{:S(2)}) copy-start(bf16[512,1536]{1,0:T(8,128)(2,1)S(1)} %pad_maximum_fusion.2.refs_0_) | copy-start | bytes 4718596
  69.2 26.9 %collective-permute-start.4 = (bf16[256,1024]{1,0:T(8,128)(2,1)}, bf16[256,1024]{1,0:T(8,128)(2,1)S(1)}, u32[]{:S(2)}, u32[]{:S(2)}) collective-permute-start(bf16[256,1024]{1,0:T(8,128)(2,1)} %collective-permute-done.3.refs_4_), channel_id=1, source_target_pairs={{0,4},{4,0},{8,12},{12,8},{16,20},{20,16},{1,5},{5,1},{9,13},{13,9... | collective-permute-start | bytes 1572872 | tf_op jit(solution)/shard_map/ppermute | solution.py:95
  71.1 24.9 %collective-permute-start.6 = (bf16[256,1024]{1,0:T(8,128)(2,1)S(1)}, bf16[256,1024]{1,0:T(8,128)(2,1)S(1)}, u32[]{:S(2)}, u32[]{:S(2)}) collective-permute-start(bf16[256,1024]{1,0:T(8,128)(2,1)S(1)} %collective-permute-done.5.refs_6_), channel_id=1, source_target_pairs={{16,20},{20,16},{24,28},{28,24},{17,21},{21,17},{25,29},{29,25},{1... | collective-permute-start | bytes 1572872 | tf_op jit(solution)/shard_map/ppermute | solution.py:95
  71.8 35.6 %collective-permute-start.8 = (bf16[256,1024]{1,0:T(8,128)(2,1)}, bf16[256,1024]{1,0:T(8,128)(2,1)}, u32[]{:S(2)}, u32[]{:S(2)}) collective-permute-start(bf16[256,1024]{1,0:T(8,128)(2,1)} %collective-permute-done.7.refs_8_), channel_id=1, source_target_pairs={{0,4},{4,0},{8,12},{12,8},{1,5},{5,1},{9,13},{13,9},{2,6},{6,2},{1... | collective-permute-start | bytes 1572872 | tf_op jit(solution)/shard_map/ppermute | solution.py:95
  75.8 31.6 %collective-permute-start.10 = (bf16[256,1024]{1,0:T(8,128)(2,1)}, bf16[256,1024]{1,0:T(8,128)(2,1)}, u32[]{:S(2)}, u32[]{:S(2)}) collective-permute-start(bf16[256,1024]{1,0:T(8,128)(2,1)} %collective-permute-done.9.refs_10_), channel_id=1, source_target_pairs={{24,28},{28,24},{25,29},{29,25},{26,30},{30,26},{27,31},{31,27}} | collective-permute-start | bytes 1572872 | tf_op jit(solution)/shard_map/ppermute | solution.py:95
  85.1 28.3 %collective-permute-start.12 = (bf16[256,1024]{1,0:T(8,128)(2,1)}, bf16[256,1024]{1,0:T(8,128)(2,1)}, u32[]{:S(2)}, u32[]{:S(2)}) collective-permute-start(bf16[256,1024]{1,0:T(8,128)(2,1)} %collective-permute-done.11.refs_12_), channel_id=1, source_target_pairs={{0,4},{4,0},{1,5},{5,1},{2,6},{6,2},{3,7},{7,3}} | collective-permute-start | bytes 1572872 | tf_op jit(solution)/shard_map/ppermute | solution.py:95
  96.1 21.5 %copy-start.19 = (bf16[256,1024]{1,0:T(8,128)(2,1)}, bf16[256,1024]{1,0:T(8,128)(2,1)S(1)}, u32[]{:S(2)}) copy-start(bf16[256,1024]{1,0:T(8,128)(2,1)S(1)} %collective-permute-done.4.refs_5_) | copy-start | bytes 1572868
  96.1 21.5 %copy-start.20 = (bf16[256,1024]{1,0:T(8,128)(2,1)}, bf16[256,1024]{1,0:T(8,128)(2,1)S(1)}, u32[]{:S(2)}) copy-start(bf16[256,1024]{1,0:T(8,128)(2,1)S(1)} %collective-permute-done.6.refs_7_) | copy-start | bytes 1572868
  113.4 96.5 %all-gather.9.cloned.1.call-start = ((), (), s32[]{:S(2)}) async-start(), calls=%async_computation.13 | async-start | bytes 2621440 | tf_op jit(solution)/shard_map/all_gather | solution.py:955
  114.1 52.2 %collective-permute-start.15 = (bf16[512,1536]{1,0:T(8,128)(2,1)S(1)}, bf16[512,1536]{1,0:T(8,128)(2,1)}, u32[]{:S(2)}, u32[]{:S(2)}) collective-permute-start(bf16[512,1536]{1,0:T(8,128)(2,1)S(1)} %pad_maximum_fusion.2.refs_0_), channel_id=1, source_target_pairs={{0,2},{2,0},{1,3},{3,1},{4,6},{6,4},{5,7},{7,5},{8,10},{10,8},{9,1... | collective-permute-start | bytes 4718600 | tf_op jit(solution)/shard_map/ppermute | solution.py:112
  117.3 46.1 %collective-permute-start.17 = (bf16[512,1536]{1,0:T(8,128)(2,1)S(1)}, bf16[512,1536]{1,0:T(8,128)(2,1)}, u32[]{:S(2)}, u32[]{:S(2)}) collective-permute-start(bf16[512,1536]{1,0:T(8,128)(2,1)S(1)} %pad_maximum_fusion.2.refs_0_), channel_id=1, source_target_pairs={{0,4},{4,0},{1,5},{5,1},{2,6},{6,2},{3,7},{7,3},{8,12},{12,8},{9,1... | collective-permute-start | bytes 4718600 | tf_op jit(solution)/shard_map/ppermute | solution.py:113
  148.0 6.4 %collective-permute-start.13 = (bf16[4,256,128]{2,1,0:T(8,128)(2,1)S(1)}, bf16[4,256,128]{2,1,0:T(8,128)(2,1)S(1)}, u32[]{:S(2)}, u32[]{:S(2)}) collective-permute-start(bf16[4,256,128]{2,1,0:T(8,128)(2,1)S(1)} %get-tuple-element.232), channel_id=1, source_target_pairs={{0,4},{4,0},{1,5},{5,1},{2,6},{6,2},{3,7},{7,3},{8,12},{12,8},{9,1... | collective-permute-start | bytes 786440 | tf_op jit(solution)/shard_map/ppermute | solution.py:950
  163.0 131.3 %reduce-scatter.5.cloned.1.call-start = ((), (), s32[]{:S(2)}) async-start(), calls=%async_computation.9 | async-start | bytes 2949120 | tf_op jit(solution)/shard_map/reduce_scatter | solution.py:80
  163.3 25.0 %collective-permute-start.14 = (bf16[512,1536]{1,0:T(8,128)(2,1)S(1)}, bf16[512,1536]{1,0:T(8,128)(2,1)}, u32[]{:S(2)}, u32[]{:S(2)}) collective-permute-start(bf16[512,1536]{1,0:T(8,128)(2,1)S(1)} %pad_maximum_fusion.2.refs_0_), channel_id=1, source_target_pairs={{0,1},{1,0},{2,3},{3,2},{4,5},{5,4},{6,7},{7,6},{8,9},{9,8},{10,11... | collective-permute-start | bytes 4718600 | tf_op jit(solution)/shard_map/ppermute | solution.py:117
  164.6 20.0 %collective-permute-start.19 = (bf16[256,1536]{1,0:T(8,128)(2,1)S(1)}, bf16[256,1536]{1,0:T(8,128)(2,1)S(1)}, u32[]{:S(2)}, u32[]{:S(2)}) collective-permute-start(bf16[256,1536]{1,0:T(8,128)(2,1)S(1)} %slice.78), channel_id=1, source_target_pairs={{0,2},{2,0},{1,3},{3,1},{4,6},{6,4},{5,7},{7,5},{8,10},{10,8},{9,1... | collective-permute-start | bytes 2359304 | tf_op jit(solution)/shard_map/ppermute | solution.py:114
  166.1 22.2 %collective-permute-start.18 = (bf16[512,1536]{1,0:T(8,128)(2,1)}, bf16[512,1536]{1,0:T(8,128)(2,1)}, u32[]{:S(2)}, u32[]{:S(2)}) collective-permute-start(bf16[512,1536]{1,0:T(8,128)(2,1)} %collective-permute-done.17.refs_4_), channel_id=1, source_target_pairs={{0,1},{1,0},{2,3},{3,2},{4,5},{5,4},{6,7},{7,6},{8,9},{9,8},{10,11... | collective-permute-start | bytes 4718600 | tf_op jit(solution)/shard_map/ppermute | solution.py:117
  166.3 22.0 %collective-permute-start.16 = (bf16[512,1536]{1,0:T(8,128)(2,1)}, bf16[512,1536]{1,0:T(8,128)(2,1)}, u32[]{:S(2)}, u32[]{:S(2)}) collective-permute-start(bf16[512,1536]{1,0:T(8,128)(2,1)} %collective-permute-done.15.refs_2_), channel_id=1, source_target_pairs={{0,1},{1,0},{2,3},{3,2},{4,5},{5,4},{6,7},{7,6},{8,9},{9,8},{10,11... | collective-permute-start | bytes 4718600 | tf_op jit(solution)/shard_map/ppermute | solution.py:117
  167.8 19.7 %collective-permute-start.21 = (bf16[256,1536]{1,0:T(8,128)(2,1)S(1)}, bf16[256,1536]{1,0:T(8,128)(2,1)S(1)}, u32[]{:S(2)}, u32[]{:S(2)}) collective-permute-start(bf16[256,1536]{1,0:T(8,128)(2,1)S(1)} %slice.79), channel_id=1, source_target_pairs={{0,4},{4,0},{1,5},{5,1},{2,6},{6,2},{3,7},{7,3},{8,12},{12,8},{9,1... | collective-permute-start | bytes 2359304 | tf_op jit(solution)/shard_map/ppermute | solution.py:115
  184.6 3.7 collective-permute-start.20
  187.5 2.4 collective-permute-start.22
  247.4 137.0 %reduce-scatter.7.cloned.1.call-start = ((), (), s32[]{:S(2)}) async-start(), calls=%async_computation.10 | async-start | bytes 2621440 | tf_op jit(solution)/shard_map/reduce_scatter | solution.py:80
  262.0 19.1 %collective-permute-start.23 = (bf16[4,512,768]{2,1,0:T(8,128)(2,1)}, bf16[4,512,768]{2,1,0:T(8,128)(2,1)}, u32[]{:S(2)}, u32[]{:S(2)}) collective-permute-start(bf16[4,512,768]{2,1,0:T(8,128)(2,1)} %get-tuple-element.119), channel_id=1, source_target_pairs={{0,1},{1,0},{2,3},{3,2},{4,5},{5,4},{6,7},{7,6},{8,9},{9,8},{10,11... | collective-permute-start | bytes 9437192 | tf_op jit(solution)/shard_map/ppermute | solution.py:985
  262.0 24.5 %collective-permute-start.24 = (bf16[4,512,768]{2,1,0:T(8,128)(2,1)}, bf16[4,512,768]{2,1,0:T(8,128)(2,1)S(1)}, u32[]{:S(2)}, u32[]{:S(2)}) collective-permute-start(bf16[4,512,768]{2,1,0:T(8,128)(2,1)} %get-tuple-element.121), channel_id=1, source_target_pairs={{0,1},{1,0},{2,3},{3,2},{4,5},{5,4},{6,7},{7,6},{8,9},{9,8},{10,11... | collective-permute-start | bytes 9437192 | tf_op jit(solution)/shard_map/ppermute | solution.py:985
  300.8 45.5 %collective-permute-start.25 = (bf16[2,512,768]{2,1,0:T(8,128)(2,1)}, bf16[2,512,768]{2,1,0:T(8,128)(2,1)}, u32[]{:S(2)}, u32[]{:S(2)}) collective-permute-start(bf16[2,512,768]{2,1,0:T(8,128)(2,1)} %dynamic-slice_bitcast_fusion.1), channel_id=1, source_target_pairs={{0,2},{2,0},{1,3},{3,1},{4,6},{6,4},{5,7},{7,5},{8,10},{10,8},{9,1... | collective-permute-start | bytes 4718600 | tf_op jit(solution)/shard_map/ppermute | solution.py:123
  303.5 40.9 %collective-permute-start.26 = (bf16[2,512,768]{2,1,0:T(8,128)(2,1)}, bf16[2,512,768]{2,1,0:T(8,128)(2,1)}, u32[]{:S(2)}, u32[]{:S(2)}) collective-permute-start(bf16[2,512,768]{2,1,0:T(8,128)(2,1)} %dynamic-slice_bitcast_fusion), channel_id=1, source_target_pairs={{0,4},{4,0},{1,5},{5,1},{2,6},{6,2},{3,7},{7,3},{8,12},{12,8},{9,1... | collective-permute-start | bytes 4718600 | tf_op jit(solution)/shard_map/ppermute | solution.py:123
  311.6 37.7 %all-to-all-start = ((bf16[8,256,128]{2,1,0:T(8,128)(2,1)}), bf16[8,256,128]{2,1,0:T(8,128)(2,1)S(1)}, u32[]{:S(2)}, u32[]{:S(2)}) async-start(bf16[8,256,128]{2,1,0:T(8,128)(2,1)} %bitcast.78), calls=%async_computation.1 | async-start | bytes 1048576 | tf_op jit(solution)/shard_map/all_to_all | solution.py:832
  315.1 85.0 %reduce-scatter.9.cloned.1.call-start = ((), (), s32[]{:S(2)}) async-start(), calls=%async_computation.11 | async-start | bytes 2654208 | tf_op jit(solution)/shard_map/reduce_scatter | solution.py:80
  316.3 28.2 %copy-start.4 = (bf16[4,512,768]{2,1,0:T(8,128)(2,1)S(1)}, bf16[4,512,768]{2,1,0:T(8,128)(2,1)}, u32[]{:S(2)}) copy-start(bf16[4,512,768]{2,1,0:T(8,128)(2,1)} %add_convert_fusion) | copy-start | bytes 9437188
  318.1 28.3 %copy-start.2 = (bf16[4,512,768]{2,1,0:T(8,128)(2,1)S(1)}, bf16[4,512,768]{2,1,0:T(8,128)(2,1)}, u32[]{:S(2)}) copy-start(bf16[4,512,768]{2,1,0:T(8,128)(2,1)} %add_convert_fusion.1) | copy-start | bytes 9437188
  352.2 32.2 %collective-permute-start.27 = (bf16[512,768]{1,0:T(8,128)(2,1)}, bf16[512,768]{1,0:T(8,128)(2,1)S(1)}, u32[]{:S(2)}, u32[]{:S(2)}) collective-permute-start(bf16[512,768]{1,0:T(8,128)(2,1)} %get-tuple-element.229), channel_id=1, source_target_pairs={{0,4},{4,0},{1,5},{5,1},{2,6},{6,2},{3,7},{7,3},{8,12},{12,8},{9,1... | collective-permute-start | bytes 2359304 | tf_op jit(solution)/shard_map/ppermute | solution.py:123
  354.9 29.5 %collective-permute-start.28 = (bf16[512,768]{1,0:T(8,128)(2,1)}, bf16[512,768]{1,0:T(8,128)(2,1)S(1)}, u32[]{:S(2)}, u32[]{:S(2)}) collective-permute-start(bf16[512,768]{1,0:T(8,128)(2,1)} %get-tuple-element.227), channel_id=1, source_target_pairs={{0,2},{2,0},{1,3},{3,1},{4,6},{6,4},{5,7},{7,5},{8,10},{10,8},{9,1... | collective-permute-start | bytes 2359304 | tf_op jit(solution)/shard_map/ppermute | solution.py:123
  387.2 28.0 %all-to-all-start.1 = ((bf16[8,256,256]{1,2,0:T(8,128)(2,1)}), bf16[8,256,256]{1,2,0:T(8,128)(2,1)}, u32[]{:S(2)}, u32[]{:S(2)}) async-start(bf16[8,256,256]{1,2,0:T(8,128)(2,1)} %copy.80), calls=%async_computation.3 | async-start | bytes 2097152 | tf_op jit(solution)/shard_map/all_to_all | solution.py:832
  391.4 36.7 %reduce-scatter.11.cloned.1.call-start = ((), (), s32[]{:S(2)}) async-start(), calls=%async_computation.12 | async-start | bytes 368640 | tf_op jit(solution)/shard_map/reduce_scatter | solution.py:80
  415.2 24.4 %all-to-all-start.2 = ((bf16[32,32,384]{2,1,0:T(8,128)(2,1)}), bf16[32,32,384]{2,1,0:T(8,128)(2,1)S(1)}, u32[]{:S(2)}, u32[]{:S(2)}) async-start(bf16[32,32,384]{2,1,0:T(8,128)(2,1)} %bitcast.35), calls=%async_computation.5 | async-start | bytes 1572864 | tf_op jit(solution)/shard_map/all_to_all | solution.py:832
  (20 other events, 125.2 us)
Sparse Core Ops, SparseCore 0:
  14.5 92.1 all-gather.4
  113.6 49.4 all-gather.6
  165.2 44.7 all-gather.8
  247.6 46.7 reduce-scatter.4
  296.5 51.6 reduce-scatter.6
  351.8 48.3 reduce-scatter.8
  402.4 25.6 reduce-scatter.10

commit v8 on v7

--- a/solution.py
+++ b/solution.py
@@ -118,10 +118,8 @@
     ]
 
 
-def halve_send(v, axis, at):
-    me = lax.axis_index(axis)
-    other = lax.ppermute(lax.dynamic_index_in_dim(v, 1 - me, at, False), axis, SWAP)
-    return lax.dynamic_index_in_dim(v, me, at, False), other
+def quarter(v, b, y):
+    return lax.dynamic_index_in_dim(lax.dynamic_index_in_dim(v, b, 0, False), y, 0, False)
 
 
 def halve_add(terms):
@@ -990,7 +988,9 @@
         back_own, moe_part, left, right = lax.optimization_barrier(
             (back_own, moe_part, left, right)
         )
-        left, right = halve_send(left, "y", 1), halve_send(right, "b", 0)
+        b, y = lax.axis_index("b"), lax.axis_index("y")
+        left_on = quarter(left, 1 - b, y), lax.ppermute(quarter(left, 1 - b, 1 - y), "y", SWAP)
+        right_on = quarter(right, b, 1 - y), lax.ppermute(quarter(right, 1 - b, 1 - y), "b", SWAP)
     else:
         *grads, moe_part = expert_grads(jnp.zeros((1,), jnp.int32), 1, *inputs, True)
         grad_experts = jnp.concatenate(grads, axis=2)
@@ -1015,6 +1015,11 @@
     grad_mixed = exchange(
         grad_heads.reshape(token_count, KEY_VALUE_HEADS, PAIR).transpose(1, 0, 2), head_axes
     ).reshape(span, PAIR)
+    if small_plane:
+        left_on, right_on = halve_add(left_on), halve_add(right_on)
+        left_on, right_on, attended_low, grad_router = lax.optimization_barrier(
+            (left_on, right_on, attended_low, grad_router)
+        )
     small = jnp.concatenate([grad_router, grad_gain_two[:, None]], axis=1)
     second_part = jnp.concatenate(
         [contract_rows(attended_low, grad_attn_low), pad_lanes(small, LANES)], axis=1
@@ -1022,11 +1027,10 @@
     cols = second_part.shape[1]
     second_part = second_part.reshape(GROUPS, -1, own_rows, cols).transpose(1, 0, 2, 3)
     if small_plane:
-        left, right = halve_add(left), halve_add(right)
-        second_part, left, right, grad_mixed = lax.optimization_barrier(
-            (second_part, left, right, grad_mixed)
+        second_part, left_on, right_on, grad_mixed = lax.optimization_barrier(
+            (second_part, left_on, right_on, grad_mixed)
         )
-        left, right = halve_send(left, "b", 0), halve_send(right, "y", 0)
+        left_on, right_on = lax.ppermute(left_on, "b", SWAP), lax.ppermute(right_on, "y", SWAP)
     rest = scatter_sum(second_part.reshape(-1, cols), PLANE)
     grads = attend_back(
         bounds, qkv, kv, kv_at, doc_rows, grad_mixed, attention_result, log_total,
@@ -1038,9 +1042,11 @@
         grad_kv = scatter_sum(grads[1].astype(bf16), "a").astype(f32)
         grad_pack = unrotate(grads[0], grad_kv, wide_cos, wide_sin)
     if small_plane:
-        left, right, moe_sum, grad_pack = lax.optimization_barrier(
-            (left, right, moe_sum, grad_pack)
+        left_on, right_on, left, right, moe_sum, grad_pack = lax.optimization_barrier(
+            (left_on, right_on, left, right, moe_sum, grad_pack)
         )
+        left_last = lax.ppermute(quarter(left, b, 1 - y), "y", SWAP)
+        right_last = lax.ppermute(quarter(right, 1 - b, y), "b", SWAP)
     first_part = head_grads(place, x_span, normed_span, first_all, grad_pack)
     rest, first_part = lax.optimization_barrier((rest, first_part))
     rest = scatter_sum(rest, "a")
@@ -1059,7 +1065,11 @@
     layer_sum = resid + RESIDUAL_SCALE * moe_sum.astype(f32)
     if small_plane:
         grad_experts = jnp.concatenate(
-            [own.astype(f32) + other.astype(f32) for own, other in (left, right)], axis=1
+            [
+                quarter(left, b, y).astype(f32) + left_last.astype(f32) + left_on.astype(f32),
+                quarter(right, b, y).astype(f32) + right_last.astype(f32) + right_on.astype(f32),
+            ],
+            axis=1,
         )
     else:
         grad_experts = grad_experts.astype(f32)

time: 459 us -> 467 us (1.017)
  starting transfers between devices: 58.8 us -> 63.7 us
    ppermute x4 -> x6, waiting for transfers between devices: 26.4 us -> 13.4 us  [the longest x1 5.18 us: body(): right_last = lax.ppermute(quarter(right, 1 - b, y), 'b', SWAP)]
    reduce_scatter x4, waiting for transfers between devices: 13.4 us -> 23.4 us  [scatter_sum(): return lax.psum_scatter(x, axes, scatter_dimension=0, tiled=True)]
  transfers between devices with their start and end apart: 39 -> 41, of which waited for: 20 -> 22; matrix products, arithmetic and copies ran while one was open for 16% -> 16% of each run, Pallas kernels for 26% -> 25%
where the time goes in v8:
time: 467 us; the launch traced here: 459 us
  Pallas kernels  156 us (33%)
  waiting for transfers between devices  139 us (30%)
  starting transfers between devices  63.7 us (14%)
  other arithmetic  50.5 us (11%)
  local copies, waits for them, and re-layouts  22.3 us (5%)
  between operations  15.2 us (3%)
  matrix products  11.9 us (3%)
    pallas_call x2, Pallas kernels, expert_grads(): pl.pallas_call(functools.partial(expert_grads_kernel, with_y), grid_spec=...  32.9 us
    pallas_call x1, Pallas kernels, experts(): pl.pallas_call(experts_kernel, grid_spec=pltpu.PrefetchScalarGridSpec(num...  29 us
    pallas_call x1, Pallas kernels, attend_back(): pl.pallas_call(functools.partial(attend_back_kernel, fold), grid_spec=plt...  27.9 us
    reduce_scatter x4, waiting for transfers between devices, scatter_sum(): return lax.psum_scatter(x, axes, scatter_dimension=0, tiled=True)  23.4 us
    ppermute x3, waiting for transfers between devices, grid_gather(): up = lax.ppermute(up, 'a', line_pairs(n, 1))  23.2 us
    ppermute x7, waiting for transfers between devices, cross(): lax.ppermute(block, SEQ, [(2 * i + j, 2 * i + 1 - j) for i in range(n) if...  20.3 us
    pallas_call x1, Pallas kernels, place_experts(): pl.pallas_call(place_experts_kernel, grid_spec=pltpu.PrefetchScalarGridSp...  18.5 us
    pallas_call x1, Pallas kernels, attend(): pl.pallas_call(attend_kernel, grid_spec=pltpu.PrefetchScalarGridSpec(num_...  18.4 us
  transfers between devices with their start and end apart: 41, of which 22 were waited for; matrix products, arithmetic and copies ran while one was open for 16% of the time, Pallas kernels for 25%

profile of v8, /device:TPU:0, one launch (start us, length us, event | category | flops | bytes accessed | tf_op | source)
XLA Modules:
  0.0 458.6 jit_solution(988492228852483110)
XLA Ops:
  14.5 3.0 collective-permute-start
  17.5 4.3 collective-permute-start.1
  26.3 9.0 %collective-permute-done.1.refs_2_ = bf16[256,1024]{1,0:T(8,128)(2,1)} collective-permute-done((bf16[256,1024]{1,0:T(8,128)(2,1)}, bf16[256,1024]{1,0:T(8,128)(2,1)}, u32[]{:S(2)}, u32[]{:S(2)}) %collective-permute-start.1) | collective-permute-done | bytes 524320 | tf_op jit(solution)/shard_map/ppermute | solution.py:102
  35.3 4.4 collective-permute-start.5
  44.2 14.2 %collective-permute-done.5.refs_6_ = bf16[256,1024]{1,0:T(8,128)(2,1)S(1)} collective-permute-done((bf16[256,1024]{1,0:T(8,128)(2,1)}, bf16[256,1024]{1,0:T(8,128)(2,1)S(1)}, u32[]{:S(2)}, u32[]{:S(2)}) %collective-permute-start.5) | collective-permute-done | bytes 524320 | tf_op jit(solution)/shard_map/ppermute | solution.py:102
  58.5 5.1 %collective-permute-start.9 = (bf16[256,1024]{1,0:T(8,128)(2,1)S(1)}, bf16[256,1024]{1,0:T(8,128)(2,1)}, u32[]{:S(2)}, u32[]{:S(2)}) collective-permute-start(bf16[256,1024]{1,0:T(8,128)(2,1)S(1)} %collective-permute-done.5.refs_6_), channel_id=1, source_target_pairs={{0,8},{8,16},{16,24},{1,9},{9,17},{17,25},{2,10},{10,18},{18,26},{... | collective-permute-start | bytes 1572872 | tf_op jit(solution)/shard_map/ppermute | solution.py:102
  71.8 3.9 collective-permute-start.8
  77.3 7.8 %collective-permute-done.11.refs_12_ = bf16[256,1024]{1,0:T(8,128)(2,1)} collective-permute-done((bf16[256,1024]{1,0:T(8,128)(2,1)}, bf16[256,1024]{1,0:T(8,128)(2,1)}, u32[]{:S(2)}, u32[]{:S(2)}) %collective-permute-start.11) | collective-permute-done | bytes 524320 | tf_op jit(solution)/shard_map/ppermute | solution.py:103
  87.6 5.5 %multiply_sine_fusion = (f32[2048,32]{1,0:T(8,128)}, f32[2048,32]{1,0:T(8,128)}) fusion(f32[32]{0:T(128)S(1)} %multiply_power_fusion, f32[2048]{0:T(1024)S(1)} %subtract_convert_fusion), kind=kLoop, calls=%fused_computation.23 | loop fusion | flops 65536 | bytes 532608 | tf_op jit(solution)/shard_map/sin | solution.py:44
  93.1 3.0 collective-permute-done.4.refs_5_
  96.1 11.3 %collective-permute-done.8.refs_9_ = bf16[256,1024]{1,0:T(8,128)(2,1)} collective-permute-done((bf16[256,1024]{1,0:T(8,128)(2,1)}, bf16[256,1024]{1,0:T(8,128)(2,1)}, u32[]{:S(2)}, u32[]{:S(2)}) %collective-permute-start.8) | collective-permute-done | bytes 524320 | tf_op jit(solution)/shard_map/ppermute | solution.py:95
  107.4 6.0 %collective-permute-done.12.refs_13_ = bf16[256,1024]{1,0:T(8,128)(2,1)} collective-permute-done((bf16[256,1024]{1,0:T(8,128)(2,1)}, bf16[256,1024]{1,0:T(8,128)(2,1)}, u32[]{:S(2)}, u32[]{:S(2)}) %collective-permute-start.12) | collective-permute-done | bytes 524320 | tf_op jit(solution)/shard_map/ppermute | solution.py:95
  114.1 3.2 collective-permute-start.15
  117.6 10.9 %project.1 = (bf16[2048,256]{1,0:T(8,128)(2,1)}, bf16[2048,1024]{1,0:T(8,128)(2,1)}, bf16[2048,1024]{1,0:T(8,128)(2,1)}, f32[2048,128]{1,0:T(8,128)}, f32[2048,128]{1,0:T(8,128)}) custom-call(s32[3]{0:T(128)} %pad_add_fusion.place_ref.head_ref, bf16[256,1024]{1,0:T(8,128)(2,1)} %bitcast.97, bf16[256,1024]{1,0:T(8,128)(2,1)} %collective-permute-done.refs_1_, ...), custom_call_target="tpu_custom_call" | custom-call | flops 1073741824 | bytes 18874368 | tf_op jit(solution)/shard_map/project/pallas_call | solution.py:194
  128.5 18.4 %attend.1 = (f32[2048,128]{1,0:T(8,128)}, bf16[2048,128]{1,0:T(8,128)(2,1)}, f32[4,1,1024]{2,1,0:T(1,128)}) custom-call(s32[9]{0:T(128)} %pad_add_fusion.1.bounds_ref, bf16[2048,256]{1,0:T(8,128)(2,1)} %get-tuple-element.105.q_ref.kv_ref, bf16[2048,256]{1,0:T(8,128)(2,1)} %get-tuple-element.105.q_ref.kv_ref, s32[4,1,512]{2,1,0:T(1,128)} %bitcast.105), custom_call_target="tpu_custom_call" | custom-call | flops 2147483648 | bytes 6291456 | tf_op jit(solution)/shard_map/attend/pallas_call | solution.py:369
  150.0 4.5 collective-permute-done.13
  155.3 7.7 %all-gather.7.cloned.1.call-done.refs_10_.routed_ref.ct_ref = bf16[1024,1152]{1,0:T(8,128)(2,1)} async-done(((bf16[256,1152]{1,0:T(8,128)(2,1)}), bf16[1024,1152]{1,0:T(8,128)(2,1)}) %all-gather.7.cloned.1.call-update) | async-done | bytes 2359312 | tf_op jit(solution)/shard_map/all_gather | solution.py:76
  169.3 15.2 %collective-permute-done.19.refs_6_ = bf16[256,1536]{1,0:T(8,128)(2,1)S(1)} collective-permute-done((bf16[256,1536]{1,0:T(8,128)(2,1)S(1)}, bf16[256,1536]{1,0:T(8,128)(2,1)S(1)}, u32[]{:S(2)}, u32[]{:S(2)}) %collective-permute-start.19) | collective-permute-done | bytes 786464 | tf_op jit(solution)/shard_map/ppermute | solution.py:114
  184.6 3.0 collective-permute-done.21.refs_8_
  189.9 18.5 %place_experts.1 = (bf16[4,1024,1536]{2,1,0:T(8,128)(2,1)}, f32[4,1024,512]{2,1,0:T(8,128)}) custom-call(s32[2]{0:T(128)} %pad_add_fusion.2.place_ref, bf16[512,1536]{1,0:T(8,128)(2,1)} %copy-done.8, bf16[512,1536]{1,0:T(8,128)(2,1)} %collective-permute-done.14.refs_1_, bf16[512,1536]{1,0:T(8,128)(2,1)} %collective-permute-done.15.refs_2_, ...), custom_call_target="tpu_custom_call" | custom-call | flops 4294967296 | bytes 37748736 | tf_op jit(solution)/shard_map/place_experts/pallas_call | solution.py:551
  210.0 8.2 %join.1 = (bf16[1024,1024]{1,0:T(8,128)(2,1)}, f32[256,1024]{1,0:T(8,128)}, bf16[256,1024]{1,0:T(8,128)(2,1)}) custom-call(s32[3]{0:T(128)} %pad_add_fusion.place_ref.head_ref, bf16[4,2,4,256,128]{4,3,2,1,0:T(8,128)(2,1)} %bitcast.98, bf16[1024,3200]{1,0:T(8,128)(2,1)} %all-gather.5.cloned.1.call-done.refs_14_.refs_15_.w_ref.small_ref.router_ref, ...), custom_call_target="tpu_custom_call" | custom-call | flops 2147483648 | bytes 12582912 | tf_op jit(solution)/shard_map/join/pallas_call | solution.py:765
  218.2 29.0 %experts.1 = (bf16[1024,1152]{1,0:T(8,128)(2,1)}, f32[1024,128]{1,0:T(8,128)}, bf16[4,1024,512]{2,1,0:T(8,128)(2,1)}, bf16[4,1024,1024]{2,1,0:T(8,128)(2,1)}) custom-call(s32[1]{0:T(128)} %bitcast.group_ref, bf16[1024,1024]{1,0:T(8,128)(2,1)} %get-tuple-element.111.n_ref, bf16[1024,1152]{1,0:T(8,128)(2,1)} %all-gather.7.cloned.1.call-done.refs_10_.routed_ref.ct_ref, ...), custom_call_target="tpu_custom_call" | custom-call | flops 17179869184 | bytes 41943040 | tf_op jit(solution)/shard_map/experts/pallas_call | solution.py:633
  247.5 14.3 %expert_grads.3 = (bf16[4,512,768]{2,1,0:T(8,128)(2,1)}, bf16[4,512,768]{2,1,0:T(8,128)(2,1)}) custom-call(s32[1]{0:T(128)} %bitcast.17.half_ref, bf16[1024,1024]{1,0:T(8,128)(2,1)} %get-tuple-element.111.n_ref, bf16[1024,1152]{1,0:T(8,128)(2,1)} %all-gather.7.cloned.1.call-done.refs_10_.routed_ref.ct_ref, bf16[4,1024,1536]{2,1,0:T(8,128)(2,1)} %get-tuple-element.114.w_ref, ...), custom_call_target="tpu_custom_call" | custom-call | flops 6442450944 | bytes 31457280 | tf_op jit(solution)/shard_map/expert_grads/pallas_call | solution.py:709
  262.4 18.6 %expert_grads.2 = (bf16[4,512,768]{2,1,0:T(8,128)(2,1)}, bf16[4,512,768]{2,1,0:T(8,128)(2,1)}, bf16[1024,1024]{1,0:T(8,128)(2,1)}) custom-call(s32[1]{0:T(128)} %bitcast.16.half_ref, bf16[1024,1024]{1,0:T(8,128)(2,1)} %get-tuple-element.111.n_ref, bf16[1024,1152]{1,0:T(8,128)(2,1)} %all-gather.7.cloned.1.call-done.refs_10_.routed_ref.ct_ref, ...), custom_call_target="tpu_custom_call" | custom-call | flops 10737418240 | bytes 31457280 | tf_op jit(solution)/shard_map/expert_grads/pallas_call | solution.py:709
  281.0 5.4 %add_convert_fusion.1 = bf16[4,512,768]{2,1,0:T(8,128)(2,1)} fusion(bf16[4,512,768]{2,1,0:T(8,128)(2,1)} %collective-permute-done.23, bf16[4,512,768]{2,1,0:T(8,128)(2,1)} %get-tuple-element.120), kind=kLoop, calls=%fused_computation.2 | loop fusion | flops 6291456 | bytes 9437184 | tf_op jit(solution)/shard_map/convert_element_type | solution.py:127
  286.3 2.5 add_convert_fusion
  288.9 5.3 %reduce-scatter.5.cloned.1.call-done = bf16[256,1152]{1,0:T(8,128)(2,1)} async-done(((bf16[1024,1152]{1,0:T(8,128)(2,1)}), bf16[256,1152]{1,0:T(8,128)(2,1)}) %reduce-scatter.5.cloned.1.call-update) | async-done | bytes 589840 | tf_op jit(solution)/shard_map/reduce_scatter | solution.py:80
  299.2 2.1 dynamic-slice_bitcast_fusion.3
  302.8 2.1 dynamic-slice_bitcast_fusion.2
  306.7 2.7 fusion.14
  310.4 4.2 all-to-all-start
  316.2 4.5 collective-permute-done.25
  320.8 2.4 fusion.7
  323.2 3.6 collective-permute-done.26
  326.8 2.2 fusion.6
  332.9 11.4 %all-to-all-done = bf16[8,256,128]{2,1,0:T(8,128)(2,1)} async-done(((bf16[8,256,128]{2,1,0:T(8,128)(2,1)}), bf16[8,256,128]{2,1,0:T(8,128)(2,1)}, u32[]{:S(2)}, u32[]{:S(2)}) %all-to-all-start) | async-done | bytes 524320 | tf_op jit(solution)/shard_map/all_to_all | solution.py:830
  345.7 27.9 %attend_back.1.grad_ref = bf16[2048,256]{1,0:T(8,128)(2,1)} custom-call(s32[9]{0:T(128)} %pad_add_fusion.1.bounds_ref, bf16[2048,256]{1,0:T(8,128)(2,1)} %get-tuple-element.105.q_ref.kv_ref, bf16[2048,256]{1,0:T(8,128)(2,1)} %get-tuple-element.105.q_ref.kv_ref, s32[4,1,512]{2,1,0:T(1,128)} %bitcast.106, bf16[2048,128]{1,0:T(8,128)(2,1)} %bitcast.28.do_ref, ...), custom_call_target="tpu_custom_call" | custom-call | flops 5368709120 | bytes 8388608 | tf_op jit(solution)/shard_map/attend_back/pallas_call | solution.py:476
  373.6 2.6 copy.80
  376.2 4.3 all-to-all-start.1
  387.7 7.8 %head_grads.1 = bf16[1024,384]{1,0:T(8,128)(2,1)} custom-call(s32[3]{0:T(128)} %pad_add_fusion.place_ref.head_ref, bf16[2048,1024]{1,0:T(8,128)(2,1)} %get-tuple-element.110.x_ref, bf16[2048,1024]{1,0:T(8,128)(2,1)} %get-tuple-element.144.normed_ref, bf16[1024,3200]{1,0:T(8,128)(2,1)} %all-gather.5.cloned.1.call-done.refs_14_.refs_15_.w_ref.small_ref.router_ref, ...), custom_call_target="tpu_custom_call" | custom-call | flops 2147483648 | bytes 12582912 | tf_op jit(solution)/shard_map/head_grads/pallas_call | solution.py:263
  395.5 12.7 %reduce-scatter.9.cloned.1.call-done = bf16[128,1152]{1,0:T(8,128)(2,1)} async-done(((bf16[1024,1152]{1,0:T(8,128)(2,1)}), bf16[128,1152]{1,0:T(8,128)(2,1)}) %reduce-scatter.9.cloned.1.call-update) | async-done | bytes 294928 | tf_op jit(solution)/shard_map/reduce_scatter | solution.py:80
  408.3 5.2 %collective-permute-done.30 = bf16[512,768]{1,0:T(8,128)(2,1)} collective-permute-done((bf16[512,768]{1,0:T(8,128)(2,1)S(1)}, bf16[512,768]{1,0:T(8,128)(2,1)}, u32[]{:S(2)}, u32[]{:S(2)}) %collective-permute-start.30) | collective-permute-done | bytes 786464 | tf_op jit(solution)/shard_map/ppermute | solution.py:1049
  416.5 2.8 fusion.5
  419.3 4.6 all-to-all-start.2
  423.8 3.0 pad_maximum_fusion.1
  426.9 5.4 %reduce-scatter.11.cloned.1.call-done = bf16[32,1152]{1,0:T(8,128)(2,1)} async-done(((bf16[128,1152]{1,0:T(8,128)(2,1)}), bf16[32,1152]{1,0:T(8,128)(2,1)}) %reduce-scatter.11.cloned.1.call-update) | async-done | bytes 73744 | tf_op jit(solution)/shard_map/reduce_scatter | solution.py:80
  436.8 4.1 fusion.17
  442.2 2.9 all-to-all-done.2
  (173 shorter events, 82.3 us)
Async XLA Ops:
  7.2 16.8 %copy-start.5 = (f32[512,1024]{1,0:T(8,128)S(1)}, f32[512,1024]{1,0:T(8,128)}, u32[]{:S(2)}) copy-start(f32[512,1024]{1,0:T(8,128)} %param.24) | copy-start | bytes 6291460
  7.2 106.2 %all-gather.5.cloned.1.call-start = ((), (), s32[]{:S(2)}) async-start(), calls=%async_computation.7 | async-start | bytes 6758400 | tf_op jit(solution)/shard_map/all_gather | solution.py:76
  14.4 148.6 %all-gather.7.cloned.1.call-start = ((), (), s32[]{:S(2)}) async-start(), calls=%async_computation.8 | async-start | bytes 2949120 | tf_op jit(solution)/shard_map/all_gather | solution.py:76
  14.5 56.6 %collective-permute-start = (bf16[256,1024]{1,0:T(8,128)(2,1)}, bf16[256,1024]{1,0:T(8,128)(2,1)}, u32[]{:S(2)}, u32[]{:S(2)}) collective-permute-start(bf16[256,1024]{1,0:T(8,128)(2,1)} %bitcast.94), channel_id=1, source_target_pairs={{0,4},{4,0},{8,12},{12,8},{16,20},{20,16},{24,28},{28,24},{1,5},{5... | collective-permute-start | bytes 1572872 | tf_op jit(solution)/shard_map/ppermute | solution.py:95
  17.5 17.8 %collective-permute-start.1 = (bf16[256,1024]{1,0:T(8,128)(2,1)}, bf16[256,1024]{1,0:T(8,128)(2,1)}, u32[]{:S(2)}, u32[]{:S(2)}) collective-permute-start(bf16[256,1024]{1,0:T(8,128)(2,1)} %bitcast.95), channel_id=1, source_target_pairs={{0,8},{8,16},{16,24},{1,9},{9,17},{17,25},{2,10},{10,18},{18,26},{... | collective-permute-start | bytes 1572872 | tf_op jit(solution)/shard_map/ppermute | solution.py:102
  21.8 19.6 %collective-permute-start.3 = (bf16[256,1024]{1,0:T(8,128)(2,1)}, bf16[256,1024]{1,0:T(8,128)(2,1)}, u32[]{:S(2)}, u32[]{:S(2)}) collective-permute-start(bf16[256,1024]{1,0:T(8,128)(2,1)} %bitcast.96), channel_id=1, source_target_pairs={{8,0},{16,8},{24,16},{9,1},{17,9},{25,17},{10,2},{18,10},{26,18},{... | collective-permute-start | bytes 1572872 | tf_op jit(solution)/shard_map/ppermute | solution.py:103
  25.9 67.2 %copy-start.16 = (s32[2048]{0:T(1024)}, s32[2048]{0:T(1024)S(1)}, u32[]{:S(2)}) copy-start(s32[2048]{0:T(1024)S(1)} %convert_reduce_fusion) | copy-start | bytes 24580
  35.3 23.1 %collective-permute-start.5 = (bf16[256,1024]{1,0:T(8,128)(2,1)}, bf16[256,1024]{1,0:T(8,128)(2,1)S(1)}, u32[]{:S(2)}, u32[]{:S(2)}) collective-permute-start(bf16[256,1024]{1,0:T(8,128)(2,1)} %collective-permute-done.1.refs_2_), channel_id=1, source_target_pairs={{0,8},{8,16},{16,24},{1,9},{9,17},{17,25},{2,10},{10,18},{18,26},{... | collective-permute-start | bytes 1572872 | tf_op jit(solution)/shard_map/ppermute | solution.py:102
  41.4 23.4 %collective-permute-start.7 = (bf16[256,1024]{1,0:T(8,128)(2,1)}, bf16[256,1024]{1,0:T(8,128)(2,1)}, u32[]{:S(2)}, u32[]{:S(2)}) collective-permute-start(bf16[256,1024]{1,0:T(8,128)(2,1)} %collective-permute-done.3.refs_4_), channel_id=1, source_target_pairs={{8,0},{16,8},{24,16},{9,1},{17,9},{25,17},{10,2},{18,10},{26,18},{... | collective-permute-start | bytes 1572872 | tf_op jit(solution)/shard_map/ppermute | solution.py:103
  42.8 29.1 %collective-permute-start.2 = (bf16[256,1024]{1,0:T(8,128)(2,1)}, bf16[256,1024]{1,0:T(8,128)(2,1)}, u32[]{:S(2)}, u32[]{:S(2)}) collective-permute-start(bf16[256,1024]{1,0:T(8,128)(2,1)} %collective-permute-done.1.refs_2_), channel_id=1, source_target_pairs={{8,12},{12,8},{16,20},{20,16},{24,28},{28,24},{9,13},{13,9},{17,21... | collective-permute-start | bytes 1572872 | tf_op jit(solution)/shard_map/ppermute | solution.py:95
  58.5 34.6 %copy-start.12 = (bf16[256,1024]{1,0:T(8,128)(2,1)}, bf16[256,1024]{1,0:T(8,128)(2,1)S(1)}, u32[]{:S(2)}) copy-start(bf16[256,1024]{1,0:T(8,128)(2,1)S(1)} %collective-permute-done.5.refs_6_) | copy-start | bytes 1572868
  58.5 17.3 %collective-permute-start.9 = (bf16[256,1024]{1,0:T(8,128)(2,1)S(1)}, bf16[256,1024]{1,0:T(8,128)(2,1)}, u32[]{:S(2)}, u32[]{:S(2)}) collective-permute-start(bf16[256,1024]{1,0:T(8,128)(2,1)S(1)} %collective-permute-done.5.refs_6_), channel_id=1, source_target_pairs={{0,8},{8,16},{16,24},{1,9},{9,17},{17,25},{2,10},{10,18},{18,26},{... | collective-permute-start | bytes 1572872 | tf_op jit(solution)/shard_map/ppermute | solution.py:102
  64.8 20.2 %collective-permute-start.11 = (bf16[256,1024]{1,0:T(8,128)(2,1)}, bf16[256,1024]{1,0:T(8,128)(2,1)}, u32[]{:S(2)}, u32[]{:S(2)}) collective-permute-start(bf16[256,1024]{1,0:T(8,128)(2,1)} %collective-permute-done.7.refs_8_), channel_id=1, source_target_pairs={{8,0},{16,8},{24,16},{9,1},{17,9},{25,17},{10,2},{18,10},{26,18},{... | collective-permute-start | bytes 1572872 | tf_op jit(solution)/shard_map/ppermute | solution.py:103
  69.2 94.1 %copy-start.8 = (bf16[512,1536]{1,0:T(8,128)(2,1)}, bf16[512,1536]{1,0:T(8,128)(2,1)S(1)}, u32[]{:S(2)}) copy-start(bf16[512,1536]{1,0:T(8,128)(2,1)S(1)} %pad_maximum_fusion.2.refs_0_) | copy-start | bytes 4718596
  69.2 26.9 %collective-permute-start.4 = (bf16[256,1024]{1,0:T(8,128)(2,1)}, bf16[256,1024]{1,0:T(8,128)(2,1)S(1)}, u32[]{:S(2)}, u32[]{:S(2)}) collective-permute-start(bf16[256,1024]{1,0:T(8,128)(2,1)} %collective-permute-done.3.refs_4_), channel_id=1, source_target_pairs={{0,4},{4,0},{8,12},{12,8},{16,20},{20,16},{1,5},{5,1},{9,13},{13,9... | collective-permute-start | bytes 1572872 | tf_op jit(solution)/shard_map/ppermute | solution.py:95
  71.1 24.9 %collective-permute-start.6 = (bf16[256,1024]{1,0:T(8,128)(2,1)S(1)}, bf16[256,1024]{1,0:T(8,128)(2,1)S(1)}, u32[]{:S(2)}, u32[]{:S(2)}) collective-permute-start(bf16[256,1024]{1,0:T(8,128)(2,1)S(1)} %collective-permute-done.5.refs_6_), channel_id=1, source_target_pairs={{16,20},{20,16},{24,28},{28,24},{17,21},{21,17},{25,29},{29,25},{1... | collective-permute-start | bytes 1572872 | tf_op jit(solution)/shard_map/ppermute | solution.py:95
  71.8 35.6 %collective-permute-start.8 = (bf16[256,1024]{1,0:T(8,128)(2,1)}, bf16[256,1024]{1,0:T(8,128)(2,1)}, u32[]{:S(2)}, u32[]{:S(2)}) collective-permute-start(bf16[256,1024]{1,0:T(8,128)(2,1)} %collective-permute-done.7.refs_8_), channel_id=1, source_target_pairs={{0,4},{4,0},{8,12},{12,8},{1,5},{5,1},{9,13},{13,9},{2,6},{6,2},{1... | collective-permute-start | bytes 1572872 | tf_op jit(solution)/shard_map/ppermute | solution.py:95
  75.8 31.6 %collective-permute-start.10 = (bf16[256,1024]{1,0:T(8,128)(2,1)}, bf16[256,1024]{1,0:T(8,128)(2,1)}, u32[]{:S(2)}, u32[]{:S(2)}) collective-permute-start(bf16[256,1024]{1,0:T(8,128)(2,1)} %collective-permute-done.9.refs_10_), channel_id=1, source_target_pairs={{24,28},{28,24},{25,29},{29,25},{26,30},{30,26},{27,31},{31,27}} | collective-permute-start | bytes 1572872 | tf_op jit(solution)/shard_map/ppermute | solution.py:95
  85.1 28.3 %collective-permute-start.12 = (bf16[256,1024]{1,0:T(8,128)(2,1)}, bf16[256,1024]{1,0:T(8,128)(2,1)}, u32[]{:S(2)}, u32[]{:S(2)}) collective-permute-start(bf16[256,1024]{1,0:T(8,128)(2,1)} %collective-permute-done.11.refs_12_), channel_id=1, source_target_pairs={{0,4},{4,0},{1,5},{5,1},{2,6},{6,2},{3,7},{7,3}} | collective-permute-start | bytes 1572872 | tf_op jit(solution)/shard_map/ppermute | solution.py:95
  96.1 21.5 %copy-start.13 = (bf16[256,1024]{1,0:T(8,128)(2,1)}, bf16[256,1024]{1,0:T(8,128)(2,1)S(1)}, u32[]{:S(2)}) copy-start(bf16[256,1024]{1,0:T(8,128)(2,1)S(1)} %collective-permute-done.4.refs_5_) | copy-start | bytes 1572868
  96.1 21.5 %copy-start.14 = (bf16[256,1024]{1,0:T(8,128)(2,1)}, bf16[256,1024]{1,0:T(8,128)(2,1)S(1)}, u32[]{:S(2)}) copy-start(bf16[256,1024]{1,0:T(8,128)(2,1)S(1)} %collective-permute-done.6.refs_7_) | copy-start | bytes 1572868
  113.4 96.5 %all-gather.9.cloned.1.call-start = ((), (), s32[]{:S(2)}) async-start(), calls=%async_computation.13 | async-start | bytes 2621440 | tf_op jit(solution)/shard_map/all_gather | solution.py:953
  114.1 52.2 %collective-permute-start.15 = (bf16[512,1536]{1,0:T(8,128)(2,1)S(1)}, bf16[512,1536]{1,0:T(8,128)(2,1)}, u32[]{:S(2)}, u32[]{:S(2)}) collective-permute-start(bf16[512,1536]{1,0:T(8,128)(2,1)S(1)} %pad_maximum_fusion.2.refs_0_), channel_id=1, source_target_pairs={{0,2},{2,0},{1,3},{3,1},{4,6},{6,4},{5,7},{7,5},{8,10},{10,8},{9,1... | collective-permute-start | bytes 4718600 | tf_op jit(solution)/shard_map/ppermute | solution.py:112
  117.3 46.1 %collective-permute-start.17 = (bf16[512,1536]{1,0:T(8,128)(2,1)S(1)}, bf16[512,1536]{1,0:T(8,128)(2,1)}, u32[]{:S(2)}, u32[]{:S(2)}) collective-permute-start(bf16[512,1536]{1,0:T(8,128)(2,1)S(1)} %pad_maximum_fusion.2.refs_0_), channel_id=1, source_target_pairs={{0,4},{4,0},{1,5},{5,1},{2,6},{6,2},{3,7},{7,3},{8,12},{12,8},{9,1... | collective-permute-start | bytes 4718600 | tf_op jit(solution)/shard_map/ppermute | solution.py:113
  148.0 6.4 %collective-permute-start.13 = (bf16[4,256,128]{2,1,0:T(8,128)(2,1)S(1)}, bf16[4,256,128]{2,1,0:T(8,128)(2,1)S(1)}, u32[]{:S(2)}, u32[]{:S(2)}) collective-permute-start(bf16[4,256,128]{2,1,0:T(8,128)(2,1)S(1)} %get-tuple-element.236), channel_id=1, source_target_pairs={{0,4},{4,0},{1,5},{5,1},{2,6},{6,2},{3,7},{7,3},{8,12},{12,8},{9,1... | collective-permute-start | bytes 786440 | tf_op jit(solution)/shard_map/ppermute | solution.py:948
  163.0 131.1 %reduce-scatter.5.cloned.1.call-start = ((), (), s32[]{:S(2)}) async-start(), calls=%async_computation.9 | async-start | bytes 2949120 | tf_op jit(solution)/shard_map/reduce_scatter | solution.py:80
  163.3 24.9 %collective-permute-start.14 = (bf16[512,1536]{1,0:T(8,128)(2,1)S(1)}, bf16[512,1536]{1,0:T(8,128)(2,1)}, u32[]{:S(2)}, u32[]{:S(2)}) collective-permute-start(bf16[512,1536]{1,0:T(8,128)(2,1)S(1)} %pad_maximum_fusion.2.refs_0_), channel_id=1, source_target_pairs={{0,1},{1,0},{2,3},{3,2},{4,5},{5,4},{6,7},{7,6},{8,9},{9,8},{10,11... | collective-permute-start | bytes 4718600 | tf_op jit(solution)/shard_map/ppermute | solution.py:117
  164.6 20.0 %collective-permute-start.19 = (bf16[256,1536]{1,0:T(8,128)(2,1)S(1)}, bf16[256,1536]{1,0:T(8,128)(2,1)S(1)}, u32[]{:S(2)}, u32[]{:S(2)}) collective-permute-start(bf16[256,1536]{1,0:T(8,128)(2,1)S(1)} %slice.78), channel_id=1, source_target_pairs={{0,2},{2,0},{1,3},{3,1},{4,6},{6,4},{5,7},{7,5},{8,10},{10,8},{9,1... | collective-permute-start | bytes 2359304 | tf_op jit(solution)/shard_map/ppermute | solution.py:114
  166.1 22.1 %collective-permute-start.18 = (bf16[512,1536]{1,0:T(8,128)(2,1)}, bf16[512,1536]{1,0:T(8,128)(2,1)}, u32[]{:S(2)}, u32[]{:S(2)}) collective-permute-start(bf16[512,1536]{1,0:T(8,128)(2,1)} %collective-permute-done.17.refs_4_), channel_id=1, source_target_pairs={{0,1},{1,0},{2,3},{3,2},{4,5},{5,4},{6,7},{7,6},{8,9},{9,8},{10,11... | collective-permute-start | bytes 4718600 | tf_op jit(solution)/shard_map/ppermute | solution.py:117
  166.3 21.9 %collective-permute-start.16 = (bf16[512,1536]{1,0:T(8,128)(2,1)}, bf16[512,1536]{1,0:T(8,128)(2,1)}, u32[]{:S(2)}, u32[]{:S(2)}) collective-permute-start(bf16[512,1536]{1,0:T(8,128)(2,1)} %collective-permute-done.15.refs_2_), channel_id=1, source_target_pairs={{0,1},{1,0},{2,3},{3,2},{4,5},{5,4},{6,7},{7,6},{8,9},{9,8},{10,11... | collective-permute-start | bytes 4718600 | tf_op jit(solution)/shard_map/ppermute | solution.py:117
  167.8 19.7 %collective-permute-start.21 = (bf16[256,1536]{1,0:T(8,128)(2,1)S(1)}, bf16[256,1536]{1,0:T(8,128)(2,1)S(1)}, u32[]{:S(2)}, u32[]{:S(2)}) collective-permute-start(bf16[256,1536]{1,0:T(8,128)(2,1)S(1)} %slice.79), channel_id=1, source_target_pairs={{0,4},{4,0},{1,5},{5,1},{2,6},{6,2},{3,7},{7,3},{8,12},{12,8},{9,1... | collective-permute-start | bytes 2359304 | tf_op jit(solution)/shard_map/ppermute | solution.py:115
  184.6 3.7 collective-permute-start.20
  187.5 2.4 collective-permute-start.22
  247.2 126.4 %reduce-scatter.7.cloned.1.call-start = ((), (), s32[]{:S(2)}) async-start(), calls=%async_computation.10 | async-start | bytes 2621440 | tf_op jit(solution)/shard_map/reduce_scatter | solution.py:80
  261.8 19.1 %collective-permute-start.23 = (bf16[4,512,768]{2,1,0:T(8,128)(2,1)}, bf16[4,512,768]{2,1,0:T(8,128)(2,1)}, u32[]{:S(2)}, u32[]{:S(2)}) collective-permute-start(bf16[4,512,768]{2,1,0:T(8,128)(2,1)} %get-tuple-element.121), channel_id=1, source_target_pairs={{0,1},{1,0},{2,3},{3,2},{4,5},{5,4},{6,7},{7,6},{8,9},{9,8},{10,11... | collective-permute-start | bytes 9437192 | tf_op jit(solution)/shard_map/ppermute | solution.py:983
  261.9 24.5 %collective-permute-start.24 = (bf16[4,512,768]{2,1,0:T(8,128)(2,1)}, bf16[4,512,768]{2,1,0:T(8,128)(2,1)S(1)}, u32[]{:S(2)}, u32[]{:S(2)}) collective-permute-start(bf16[4,512,768]{2,1,0:T(8,128)(2,1)} %get-tuple-element.123), channel_id=1, source_target_pairs={{0,1},{1,0},{2,3},{3,2},{4,5},{5,4},{6,7},{7,6},{8,9},{9,8},{10,11... | collective-permute-start | bytes 9437192 | tf_op jit(solution)/shard_map/ppermute | solution.py:983
  301.3 19.4 %collective-permute-start.25 = (bf16[512,768]{1,0:T(8,128)(2,1)}, bf16[512,768]{1,0:T(8,128)(2,1)}, u32[]{:S(2)}, u32[]{:S(2)}) collective-permute-start(bf16[512,768]{1,0:T(8,128)(2,1)} %dynamic-slice_bitcast_fusion.3), channel_id=1, source_target_pairs={{0,2},{2,0},{1,3},{3,1},{4,6},{6,4},{5,7},{7,5},{8,10},{10,8},{9,1... | collective-permute-start | bytes 2359304 | tf_op jit(solution)/shard_map/ppermute | solution.py:992
  304.9 21.9 %collective-permute-start.26 = (bf16[512,768]{1,0:T(8,128)(2,1)}, bf16[512,768]{1,0:T(8,128)(2,1)S(1)}, u32[]{:S(2)}, u32[]{:S(2)}) collective-permute-start(bf16[512,768]{1,0:T(8,128)(2,1)} %dynamic-slice_bitcast_fusion.2), channel_id=1, source_target_pairs={{0,4},{4,0},{1,5},{5,1},{2,6},{6,2},{3,7},{7,3},{8,12},{12,8},{9,1... | collective-permute-start | bytes 2359304 | tf_op jit(solution)/shard_map/ppermute | solution.py:993
  306.7 22.6 %copy-start.1 = (f32[256,1024]{1,0:T(8,128)}, f32[256,1024]{1,0:T(8,128)S(1)}, u32[]{:S(2)}) copy-start(f32[256,1024]{1,0:T(8,128)S(1)} %subtract_add_fusion) | copy-start | bytes 3145732
  310.4 33.9 %all-to-all-start = ((bf16[8,256,128]{2,1,0:T(8,128)(2,1)}), bf16[8,256,128]{2,1,0:T(8,128)(2,1)}, u32[]{:S(2)}, u32[]{:S(2)}) async-start(bf16[8,256,128]{2,1,0:T(8,128)(2,1)} %bitcast.80), calls=%async_computation.1 | async-start | bytes 1048576 | tf_op jit(solution)/shard_map/all_to_all | solution.py:830
  314.5 93.7 %reduce-scatter.9.cloned.1.call-start = ((), (), s32[]{:S(2)}) async-start(), calls=%async_computation.11 | async-start | bytes 2654208 | tf_op jit(solution)/shard_map/reduce_scatter | solution.py:80
  344.3 29.2 %collective-permute-start.27 = (bf16[512,768]{1,0:T(8,128)(2,1)S(1)}, bf16[512,768]{1,0:T(8,128)(2,1)S(1)}, u32[]{:S(2)}, u32[]{:S(2)}) collective-permute-start(bf16[512,768]{1,0:T(8,128)(2,1)S(1)} %copy-done.11), channel_id=1, source_target_pairs={{0,4},{4,0},{1,5},{5,1},{2,6},{6,2},{3,7},{7,3},{8,12},{12,8},{9,1... | collective-permute-start | bytes 2359304 | tf_op jit(solution)/shard_map/ppermute | solution.py:1033
  345.7 27.9 %collective-permute-start.28 = (bf16[512,768]{1,0:T(8,128)(2,1)}, bf16[512,768]{1,0:T(8,128)(2,1)S(1)}, u32[]{:S(2)}, u32[]{:S(2)}) collective-permute-start(bf16[512,768]{1,0:T(8,128)(2,1)} %fusion.6), channel_id=1, source_target_pairs={{0,2},{2,0},{1,3},{3,1},{4,6},{6,4},{5,7},{7,5},{8,10},{10,8},{9,1... | collective-permute-start | bytes 2359304 | tf_op jit(solution)/shard_map/ppermute | solution.py:1033
  376.2 43.1 %all-to-all-start.1 = ((bf16[8,256,256]{1,2,0:T(8,128)(2,1)}), bf16[8,256,256]{1,2,0:T(8,128)(2,1)}, u32[]{:S(2)}, u32[]{:S(2)}) async-start(bf16[8,256,256]{1,2,0:T(8,128)(2,1)} %copy.80), calls=%async_computation.3 | async-start | bytes 2097152 | tf_op jit(solution)/shard_map/all_to_all | solution.py:830
  380.5 51.9 %reduce-scatter.11.cloned.1.call-start = ((), (), s32[]{:S(2)}) async-start(), calls=%async_computation.12 | async-start | bytes 368640 | tf_op jit(solution)/shard_map/reduce_scatter | solution.py:80
  381.7 31.8 %collective-permute-start.30 = (bf16[512,768]{1,0:T(8,128)(2,1)S(1)}, bf16[512,768]{1,0:T(8,128)(2,1)}, u32[]{:S(2)}, u32[]{:S(2)}) collective-permute-start(bf16[512,768]{1,0:T(8,128)(2,1)S(1)} %dynamic-slice_bitcast_fusion), channel_id=1, source_target_pairs={{0,4},{4,0},{1,5},{5,1},{2,6},{6,2},{3,7},{7,3},{8,12},{12,8},{9,1... | collective-permute-start | bytes 2359304 | tf_op jit(solution)/shard_map/ppermute | solution.py:1049
  385.7 30.8 %collective-permute-start.29 = (bf16[512,768]{1,0:T(8,128)(2,1)}, bf16[512,768]{1,0:T(8,128)(2,1)}, u32[]{:S(2)}, u32[]{:S(2)}) collective-permute-start(bf16[512,768]{1,0:T(8,128)(2,1)} %dynamic-slice_bitcast_fusion.1), channel_id=1, source_target_pairs={{0,2},{2,0},{1,3},{3,1},{4,6},{6,4},{5,7},{7,5},{8,10},{10,8},{9,1... | collective-permute-start | bytes 2359304 | tf_op jit(solution)/shard_map/ppermute | solution.py:1048
  419.3 25.9 %all-to-all-start.2 = ((bf16[32,32,384]{2,1,0:T(8,128)(2,1)}), bf16[32,32,384]{2,1,0:T(8,128)(2,1)S(1)}, u32[]{:S(2)}, u32[]{:S(2)}) async-start(bf16[32,32,384]{2,1,0:T(8,128)(2,1)} %bitcast.31), calls=%async_computation.5 | async-start | bytes 1572864 | tf_op jit(solution)/shard_map/all_to_all | solution.py:830
  (14 other events, 102.4 us)
Sparse Core Ops, SparseCore 0:
  14.5 92.1 all-gather.4
  113.6 49.4 all-gather.6
  165.2 44.7 all-gather.8
  247.4 46.7 reduce-scatter.4
  296.3 51.6 reduce-scatter.6
  351.6 56.6 reduce-scatter.8
  410.5 21.7 reduce-scatter.10

commit v9 on v8

--- a/solution.py
+++ b/solution.py
@@ -1045,15 +1045,17 @@
         left_on, right_on, left, right, moe_sum, grad_pack = lax.optimization_barrier(
             (left_on, right_on, left, right, moe_sum, grad_pack)
         )
-        left_last = lax.ppermute(quarter(left, b, 1 - y), "y", SWAP)
-        right_last = lax.ppermute(quarter(right, 1 - b, y), "b", SWAP)
     first_part = head_grads(place, x_span, normed_span, first_all, grad_pack)
     rest, first_part = lax.optimization_barrier((rest, first_part))
     rest = scatter_sum(rest, "a")
     by_tokens = exchange(grad_pack.reshape(KEY_VALUE_HEADS, token_count, HEAD_PACK), head_axes)
     by_tokens, first_part = lax.optimization_barrier((by_tokens, first_part))
+    if small_plane:
+        left, right, by_tokens = lax.optimization_barrier((left, right, by_tokens))
+        left_last = lax.ppermute(quarter(left, b, 1 - y), "y", SWAP)
+        right_last = lax.ppermute(quarter(right, 1 - b, y), "b", SWAP)
     sums = exchange(first_part.reshape(-1, own_rows, first_part.shape[1]), ALL)
-    sums, moe_sum, resid = lax.optimization_barrier((sums, moe_sum, resid))
+    sums, moe_sum, resid, rest = lax.optimization_barrier((sums, moe_sum, resid, rest))
     grad_q_w, grad_k_w, grad_v_w, grad_gain_one = weight_sums(
         sums.reshape(-1, KEY_VALUE_HEADS, lax.axis_size(("y", "c")), own_rows, first_part.shape[1])
     )

time: 467 us -> 469 us (level)
  waiting for transfers between devices: 139 us -> 158 us
  Pallas kernels: 156 us -> 145 us
    ppermute x1, waiting for transfers between devices: 5.18 us -> 17.4 us  [body(): right_last = lax.ppermute(quarter(right, 1 - b, y), 'b', SWAP)]
    reduce_scatter x4, waiting for transfers between devices: 23.4 us -> 29.9 us  [scatter_sum(): return lax.psum_scatter(x, axes, scatter_dimension=0, tiled=True)]
    pallas_call x1, Pallas kernels: 27.9 us -> 21.5 us  [attend_back(): pl.pallas_call(functools.partial(attend_back_kernel, fold), grid_spec=plt...]
  transfers between devices with their start and end apart: 41 -> 41, of which waited for: 22 -> 20; matrix products, arithmetic and copies ran while one was open for 16% -> 14% of each run, Pallas kernels for 25% -> 23%
where the time goes in v9:
time: 469 us; the launch traced here: 461 us
  waiting for transfers between devices  158 us (34%)
  Pallas kernels  145 us (31%)
  starting transfers between devices  63.4 us (14%)
  other arithmetic  46.4 us (10%)
  local copies, waits for them, and re-layouts  21.6 us (5%)
  between operations  15.2 us (3%)
  matrix products  11 us (2%)
    pallas_call x2, Pallas kernels, expert_grads(): pl.pallas_call(functools.partial(expert_grads_kernel, with_y), grid_spec=...  32.9 us
    reduce_scatter x4, waiting for transfers between devices, scatter_sum(): return lax.psum_scatter(x, axes, scatter_dimension=0, tiled=True)  29.9 us
    pallas_call x1, Pallas kernels, experts(): pl.pallas_call(experts_kernel, grid_spec=pltpu.PrefetchScalarGridSpec(num...  29 us
    ppermute x3, waiting for transfers between devices, grid_gather(): up = lax.ppermute(up, 'a', line_pairs(n, 1))  23.3 us
    pallas_call x1, Pallas kernels, attend_back(): pl.pallas_call(functools.partial(attend_back_kernel, fold), grid_spec=plt...  21.5 us
    ppermute x7, waiting for transfers between devices, cross(): lax.ppermute(block, SEQ, [(2 * i + j, 2 * i + 1 - j) for i in range(n) if...  20.4 us
    pallas_call x1, Pallas kernels, place_experts(): pl.pallas_call(place_experts_kernel, grid_spec=pltpu.PrefetchScalarGridSp...  18.5 us
    ppermute x1, waiting for transfers between devices, body(): right_last = lax.ppermute(quarter(right, 1 - b, y), 'b', SWAP)  17.4 us
  transfers between devices with their start and end apart: 41, of which 20 were waited for; matrix products, arithmetic and copies ran while one was open for 14% of the time, Pallas kernels for 23%

profile of v9, /device:TPU:0, one launch (start us, length us, event | category | flops | bytes accessed | tf_op | source)
XLA Modules:
  0.0 460.8 jit_solution(18188294997527357960)
XLA Ops:
  14.5 3.0 collective-permute-start
  17.5 4.3 collective-permute-start.1
  26.3 9.0 %collective-permute-done.1.refs_2_ = bf16[256,1024]{1,0:T(8,128)(2,1)} collective-permute-done((bf16[256,1024]{1,0:T(8,128)(2,1)}, bf16[256,1024]{1,0:T(8,128)(2,1)}, u32[]{:S(2)}, u32[]{:S(2)}) %collective-permute-start.1) | collective-permute-done | bytes 524320 | tf_op jit(solution)/shard_map/ppermute | solution.py:102
  35.3 4.4 collective-permute-start.5
  44.2 14.3 %collective-permute-done.5.refs_6_ = bf16[256,1024]{1,0:T(8,128)(2,1)S(1)} collective-permute-done((bf16[256,1024]{1,0:T(8,128)(2,1)}, bf16[256,1024]{1,0:T(8,128)(2,1)S(1)}, u32[]{:S(2)}, u32[]{:S(2)}) %collective-permute-start.5) | collective-permute-done | bytes 524320 | tf_op jit(solution)/shard_map/ppermute | solution.py:102
  58.5 5.1 %collective-permute-start.9 = (bf16[256,1024]{1,0:T(8,128)(2,1)S(1)}, bf16[256,1024]{1,0:T(8,128)(2,1)}, u32[]{:S(2)}, u32[]{:S(2)}) collective-permute-start(bf16[256,1024]{1,0:T(8,128)(2,1)S(1)} %collective-permute-done.5.refs_6_), channel_id=1, source_target_pairs={{0,8},{8,16},{16,24},{1,9},{9,17},{17,25},{2,10},{10,18},{18,26},{... | collective-permute-start | bytes 1572872 | tf_op jit(solution)/shard_map/ppermute | solution.py:102
  66.1 1.9 pad_maximum_fusion.3
  69.2 1.9 collective-permute-start.4
  71.8 3.9 collective-permute-start.8
  77.2 7.8 %collective-permute-done.11.refs_12_ = bf16[256,1024]{1,0:T(8,128)(2,1)} collective-permute-done((bf16[256,1024]{1,0:T(8,128)(2,1)}, bf16[256,1024]{1,0:T(8,128)(2,1)}, u32[]{:S(2)}, u32[]{:S(2)}) %collective-permute-start.11) | collective-permute-done | bytes 524320 | tf_op jit(solution)/shard_map/ppermute | solution.py:103
  85.1 1.9 collective-permute-start.12
  87.6 5.5 %multiply_sine_fusion = (f32[2048,32]{1,0:T(8,128)}, f32[2048,32]{1,0:T(8,128)}) fusion(f32[32]{0:T(128)S(1)} %multiply_power_fusion, f32[2048]{0:T(1024)S(1)} %subtract_convert_fusion), kind=kLoop, calls=%fused_computation.23 | loop fusion | flops 65536 | bytes 532608 | tf_op jit(solution)/shard_map/sin | solution.py:44
  93.1 3.0 collective-permute-done.4.refs_5_
  96.0 11.3 %collective-permute-done.8.refs_9_ = bf16[256,1024]{1,0:T(8,128)(2,1)} collective-permute-done((bf16[256,1024]{1,0:T(8,128)(2,1)}, bf16[256,1024]{1,0:T(8,128)(2,1)}, u32[]{:S(2)}, u32[]{:S(2)}) %collective-permute-start.8) | collective-permute-done | bytes 524320 | tf_op jit(solution)/shard_map/ppermute | solution.py:95
  107.4 6.1 %collective-permute-done.12.refs_13_ = bf16[256,1024]{1,0:T(8,128)(2,1)} collective-permute-done((bf16[256,1024]{1,0:T(8,128)(2,1)}, bf16[256,1024]{1,0:T(8,128)(2,1)}, u32[]{:S(2)}, u32[]{:S(2)}) %collective-permute-start.12) | collective-permute-done | bytes 524320 | tf_op jit(solution)/shard_map/ppermute | solution.py:95
  114.1 3.1 collective-permute-start.15
  117.5 10.9 %project.1 = (bf16[2048,256]{1,0:T(8,128)(2,1)}, bf16[2048,1024]{1,0:T(8,128)(2,1)}, bf16[2048,1024]{1,0:T(8,128)(2,1)}, f32[2048,128]{1,0:T(8,128)}, f32[2048,128]{1,0:T(8,128)}) custom-call(s32[3]{0:T(128)} %pad_add_fusion.place_ref.head_ref, bf16[256,1024]{1,0:T(8,128)(2,1)} %bitcast.98, bf16[256,1024]{1,0:T(8,128)(2,1)} %collective-permute-done.refs_1_, ...), custom_call_target="tpu_custom_call" | custom-call | flops 1073741824 | bytes 18874368 | tf_op jit(solution)/shard_map/project/pallas_call | solution.py:194
  128.4 14.0 %attend.1 = (f32[2048,128]{1,0:T(8,128)}, bf16[2048,128]{1,0:T(8,128)(2,1)}, f32[4,1,1024]{2,1,0:T(1,128)}) custom-call(s32[9]{0:T(128)} %pad_add_fusion.1.bounds_ref, bf16[2048,256]{1,0:T(8,128)(2,1)} %get-tuple-element.109.q_ref.kv_ref, bf16[2048,256]{1,0:T(8,128)(2,1)} %get-tuple-element.109.q_ref.kv_ref, s32[4,1,512]{2,1,0:T(1,128)} %bitcast.107), custom_call_target="tpu_custom_call" | custom-call | flops 2147483648 | bytes 6291456 | tf_op jit(solution)/shard_map/attend/pallas_call | solution.py:369
  143.5 2.0 collective-permute-start.13
  145.5 7.0 %collective-permute-done.13 = bf16[4,256,128]{2,1,0:T(8,128)(2,1)S(1)} collective-permute-done((bf16[4,256,128]{2,1,0:T(8,128)(2,1)S(1)}, bf16[4,256,128]{2,1,0:T(8,128)(2,1)S(1)}, u32[]{:S(2)}, u32[]{:S(2)}) %collective-permute-start.13) | collective-permute-done | bytes 262176 | tf_op jit(solution)/shard_map/ppermute | solution.py:948
  153.4 9.6 %all-gather.7.cloned.1.call-done.refs_10_.routed_ref.ct_ref = bf16[1024,1152]{1,0:T(8,128)(2,1)} async-done(((bf16[256,1152]{1,0:T(8,128)(2,1)}), bf16[1024,1152]{1,0:T(8,128)(2,1)}) %all-gather.7.cloned.1.call-update) | async-done | bytes 2359312 | tf_op jit(solution)/shard_map/all_gather | solution.py:76
  169.3 15.2 %collective-permute-done.19.refs_6_ = bf16[256,1536]{1,0:T(8,128)(2,1)S(1)} collective-permute-done((bf16[256,1536]{1,0:T(8,128)(2,1)S(1)}, bf16[256,1536]{1,0:T(8,128)(2,1)S(1)}, u32[]{:S(2)}, u32[]{:S(2)}) %collective-permute-start.19) | collective-permute-done | bytes 786464 | tf_op jit(solution)/shard_map/ppermute | solution.py:114
  184.5 3.0 collective-permute-done.21.refs_8_
  189.9 18.5 %place_experts.1 = (bf16[4,1024,1536]{2,1,0:T(8,128)(2,1)}, f32[4,1024,512]{2,1,0:T(8,128)}) custom-call(s32[2]{0:T(128)} %pad_add_fusion.2.place_ref, bf16[512,1536]{1,0:T(8,128)(2,1)} %copy-done.6, bf16[512,1536]{1,0:T(8,128)(2,1)} %collective-permute-done.14.refs_1_, bf16[512,1536]{1,0:T(8,128)(2,1)} %collective-permute-done.15.refs_2_, ...), custom_call_target="tpu_custom_call" | custom-call | flops 4294967296 | bytes 37748736 | tf_op jit(solution)/shard_map/place_experts/pallas_call | solution.py:551
  209.9 8.2 %join.1 = (bf16[1024,1024]{1,0:T(8,128)(2,1)}, f32[256,1024]{1,0:T(8,128)}, bf16[256,1024]{1,0:T(8,128)(2,1)}) custom-call(s32[3]{0:T(128)} %pad_add_fusion.place_ref.head_ref, bf16[4,2,4,256,128]{4,3,2,1,0:T(8,128)(2,1)} %bitcast.99, bf16[1024,3200]{1,0:T(8,128)(2,1)} %all-gather.5.cloned.1.call-done.refs_14_.refs_15_.w_ref.small_ref.router_ref, ...), custom_call_target="tpu_custom_call" | custom-call | flops 2147483648 | bytes 12582912 | tf_op jit(solution)/shard_map/join/pallas_call | solution.py:765
  218.2 29.0 %experts.1 = (bf16[1024,1152]{1,0:T(8,128)(2,1)}, f32[1024,128]{1,0:T(8,128)}, bf16[4,1024,512]{2,1,0:T(8,128)(2,1)}, bf16[4,1024,1024]{2,1,0:T(8,128)(2,1)}) custom-call(s32[1]{0:T(128)} %bitcast.group_ref, bf16[1024,1024]{1,0:T(8,128)(2,1)} %get-tuple-element.115.n_ref, bf16[1024,1152]{1,0:T(8,128)(2,1)} %all-gather.7.cloned.1.call-done.refs_10_.routed_ref.ct_ref, ...), custom_call_target="tpu_custom_call" | custom-call | flops 17179869184 | bytes 41943040 | tf_op jit(solution)/shard_map/experts/pallas_call | solution.py:633
  247.5 14.3 %expert_grads.3 = (bf16[4,512,768]{2,1,0:T(8,128)(2,1)}, bf16[4,512,768]{2,1,0:T(8,128)(2,1)}) custom-call(s32[1]{0:T(128)} %bitcast.17.half_ref, bf16[1024,1024]{1,0:T(8,128)(2,1)} %get-tuple-element.115.n_ref, bf16[1024,1152]{1,0:T(8,128)(2,1)} %all-gather.7.cloned.1.call-done.refs_10_.routed_ref.ct_ref, bf16[4,1024,1536]{2,1,0:T(8,128)(2,1)} %get-tuple-element.118.w_ref, ...), custom_call_target="tpu_custom_call" | custom-call | flops 6442450944 | bytes 31457280 | tf_op jit(solution)/shard_map/expert_grads/pallas_call | solution.py:709
  262.3 18.6 %expert_grads.2 = (bf16[4,512,768]{2,1,0:T(8,128)(2,1)}, bf16[4,512,768]{2,1,0:T(8,128)(2,1)}, bf16[1024,1024]{1,0:T(8,128)(2,1)}) custom-call(s32[1]{0:T(128)} %bitcast.16.half_ref, bf16[1024,1024]{1,0:T(8,128)(2,1)} %get-tuple-element.115.n_ref, bf16[1024,1152]{1,0:T(8,128)(2,1)} %all-gather.7.cloned.1.call-done.refs_10_.routed_ref.ct_ref, ...), custom_call_target="tpu_custom_call" | custom-call | flops 10737418240 | bytes 31457280 | tf_op jit(solution)/shard_map/expert_grads/pallas_call | solution.py:709
  280.9 5.4 %add_convert_fusion.1 = bf16[4,512,768]{2,1,0:T(8,128)(2,1)} fusion(bf16[4,512,768]{2,1,0:T(8,128)(2,1)} %collective-permute-done.23, bf16[4,512,768]{2,1,0:T(8,128)(2,1)} %get-tuple-element.124), kind=kLoop, calls=%fused_computation.2 | loop fusion | flops 6291456 | bytes 9437184 | tf_op jit(solution)/shard_map/convert_element_type | solution.py:127
  286.3 2.6 add_convert_fusion
  288.9 5.3 %reduce-scatter.5.cloned.1.call-done = bf16[256,1152]{1,0:T(8,128)(2,1)} async-done(((bf16[1024,1152]{1,0:T(8,128)(2,1)}), bf16[256,1152]{1,0:T(8,128)(2,1)}) %reduce-scatter.5.cloned.1.call-update) | async-done | bytes 589840 | tf_op jit(solution)/shard_map/reduce_scatter | solution.py:80
  299.1 2.1 dynamic-slice_bitcast_fusion.3
  302.7 2.1 dynamic-slice_bitcast_fusion.2
  306.6 2.3 fusion.14
  309.8 4.1 all-to-all-start
  315.7 5.0 %collective-permute-done.25 = bf16[512,768]{1,0:T(8,128)(2,1)} collective-permute-done((bf16[512,768]{1,0:T(8,128)(2,1)}, bf16[512,768]{1,0:T(8,128)(2,1)}, u32[]{:S(2)}, u32[]{:S(2)}) %collective-permute-start.25) | collective-permute-done | bytes 786464 | tf_op jit(solution)/shard_map/ppermute | solution.py:992
  320.7 2.4 fusion.7
  323.2 3.6 collective-permute-done.26
  326.7 2.2 fusion.6
  332.7 10.1 %all-to-all-done = bf16[8,256,128]{2,1,0:T(8,128)(2,1)} async-done(((bf16[8,256,128]{2,1,0:T(8,128)(2,1)}), bf16[8,256,128]{2,1,0:T(8,128)(2,1)}, u32[]{:S(2)}, u32[]{:S(2)}) %all-to-all-start) | async-done | bytes 524320 | tf_op jit(solution)/shard_map/all_to_all | solution.py:830
  345.1 21.5 %attend_back.1.grad_ref = bf16[2048,256]{1,0:T(8,128)(2,1)} custom-call(s32[9]{0:T(128)} %pad_add_fusion.1.bounds_ref, bf16[2048,256]{1,0:T(8,128)(2,1)} %get-tuple-element.109.q_ref.kv_ref, bf16[2048,256]{1,0:T(8,128)(2,1)} %get-tuple-element.109.q_ref.kv_ref, s32[4,1,512]{2,1,0:T(1,128)} %bitcast.108, bf16[2048,128]{1,0:T(8,128)(2,1)} %bitcast.28.do_ref, ...), custom_call_target="tpu_custom_call" | custom-call | flops 5368709120 | bytes 8388608 | tf_op jit(solution)/shard_map/attend_back/pallas_call | solution.py:476
  366.7 2.5 copy.80
  369.2 3.6 all-to-all-start.1
  372.8 7.9 %head_grads.1 = bf16[1024,384]{1,0:T(8,128)(2,1)} custom-call(s32[3]{0:T(128)} %pad_add_fusion.place_ref.head_ref, bf16[2048,1024]{1,0:T(8,128)(2,1)} %get-tuple-element.114.x_ref, bf16[2048,1024]{1,0:T(8,128)(2,1)} %get-tuple-element.148.normed_ref, bf16[1024,3200]{1,0:T(8,128)(2,1)} %all-gather.5.cloned.1.call-done.refs_14_.refs_15_.w_ref.small_ref.router_ref, ...), custom_call_target="tpu_custom_call" | custom-call | flops 2147483648 | bytes 12582912 | tf_op jit(solution)/shard_map/head_grads/pallas_call | solution.py:263
  380.7 24.6 %reduce-scatter.9.cloned.1.call-done = bf16[128,1152]{1,0:T(8,128)(2,1)} async-done(((bf16[1024,1152]{1,0:T(8,128)(2,1)}), bf16[128,1152]{1,0:T(8,128)(2,1)}) %reduce-scatter.9.cloned.1.call-update) | async-done | bytes 294928 | tf_op jit(solution)/shard_map/reduce_scatter | solution.py:80
  406.3 4.6 all-to-all-start.2
  416.7 3.6 fusion.17
  421.6 17.4 %collective-permute-done.30 = bf16[512,768]{1,0:T(8,128)(2,1)S(1)} collective-permute-done((bf16[512,768]{1,0:T(8,128)(2,1)S(1)}, bf16[512,768]{1,0:T(8,128)(2,1)S(1)}, u32[]{:S(2)}, u32[]{:S(2)}) %collective-permute-start.30) | collective-permute-done | bytes 786464 | tf_op jit(solution)/shard_map/ppermute | solution.py:1056
  (175 shorter events, 76.0 us)
Async XLA Ops:
  7.2 16.7 %copy-start.3 = (f32[512,1024]{1,0:T(8,128)S(1)}, f32[512,1024]{1,0:T(8,128)}, u32[]{:S(2)}) copy-start(f32[512,1024]{1,0:T(8,128)} %param.24) | copy-start | bytes 6291460
  7.2 106.3 %all-gather.5.cloned.1.call-start = ((), (), s32[]{:S(2)}) async-start(), calls=%async_computation.7 | async-start | bytes 6758400 | tf_op jit(solution)/shard_map/all_gather | solution.py:76
  14.4 148.6 %all-gather.7.cloned.1.call-start = ((), (), s32[]{:S(2)}) async-start(), calls=%async_computation.8 | async-start | bytes 2949120 | tf_op jit(solution)/shard_map/all_gather | solution.py:76
  14.5 56.6 %collective-permute-start = (bf16[256,1024]{1,0:T(8,128)(2,1)}, bf16[256,1024]{1,0:T(8,128)(2,1)}, u32[]{:S(2)}, u32[]{:S(2)}) collective-permute-start(bf16[256,1024]{1,0:T(8,128)(2,1)} %bitcast.95), channel_id=1, source_target_pairs={{0,4},{4,0},{8,12},{12,8},{16,20},{20,16},{24,28},{28,24},{1,5},{5... | collective-permute-start | bytes 1572872 | tf_op jit(solution)/shard_map/ppermute | solution.py:95
  17.5 17.9 %collective-permute-start.1 = (bf16[256,1024]{1,0:T(8,128)(2,1)}, bf16[256,1024]{1,0:T(8,128)(2,1)}, u32[]{:S(2)}, u32[]{:S(2)}) collective-permute-start(bf16[256,1024]{1,0:T(8,128)(2,1)} %bitcast.96), channel_id=1, source_target_pairs={{0,8},{8,16},{16,24},{1,9},{9,17},{17,25},{2,10},{10,18},{18,26},{... | collective-permute-start | bytes 1572872 | tf_op jit(solution)/shard_map/ppermute | solution.py:102
  21.8 19.6 %collective-permute-start.3 = (bf16[256,1024]{1,0:T(8,128)(2,1)}, bf16[256,1024]{1,0:T(8,128)(2,1)}, u32[]{:S(2)}, u32[]{:S(2)}) collective-permute-start(bf16[256,1024]{1,0:T(8,128)(2,1)} %bitcast.97), channel_id=1, source_target_pairs={{8,0},{16,8},{24,16},{9,1},{17,9},{25,17},{10,2},{18,10},{26,18},{... | collective-permute-start | bytes 1572872 | tf_op jit(solution)/shard_map/ppermute | solution.py:103
  25.9 67.2 %copy-start.17 = (s32[2048]{0:T(1024)}, s32[2048]{0:T(1024)S(1)}, u32[]{:S(2)}) copy-start(s32[2048]{0:T(1024)S(1)} %convert_reduce_fusion) | copy-start | bytes 24580
  35.3 23.1 %collective-permute-start.5 = (bf16[256,1024]{1,0:T(8,128)(2,1)}, bf16[256,1024]{1,0:T(8,128)(2,1)S(1)}, u32[]{:S(2)}, u32[]{:S(2)}) collective-permute-start(bf16[256,1024]{1,0:T(8,128)(2,1)} %collective-permute-done.1.refs_2_), channel_id=1, source_target_pairs={{0,8},{8,16},{16,24},{1,9},{9,17},{17,25},{2,10},{10,18},{18,26},{... | collective-permute-start | bytes 1572872 | tf_op jit(solution)/shard_map/ppermute | solution.py:102
  41.4 23.4 %collective-permute-start.7 = (bf16[256,1024]{1,0:T(8,128)(2,1)}, bf16[256,1024]{1,0:T(8,128)(2,1)}, u32[]{:S(2)}, u32[]{:S(2)}) collective-permute-start(bf16[256,1024]{1,0:T(8,128)(2,1)} %collective-permute-done.3.refs_4_), channel_id=1, source_target_pairs={{8,0},{16,8},{24,16},{9,1},{17,9},{25,17},{10,2},{18,10},{26,18},{... | collective-permute-start | bytes 1572872 | tf_op jit(solution)/shard_map/ppermute | solution.py:103
  42.7 29.1 %collective-permute-start.2 = (bf16[256,1024]{1,0:T(8,128)(2,1)}, bf16[256,1024]{1,0:T(8,128)(2,1)}, u32[]{:S(2)}, u32[]{:S(2)}) collective-permute-start(bf16[256,1024]{1,0:T(8,128)(2,1)} %collective-permute-done.1.refs_2_), channel_id=1, source_target_pairs={{8,12},{12,8},{16,20},{20,16},{24,28},{28,24},{9,13},{13,9},{17,21... | collective-permute-start | bytes 1572872 | tf_op jit(solution)/shard_map/ppermute | solution.py:95
  58.5 34.6 %copy-start.12 = (bf16[256,1024]{1,0:T(8,128)(2,1)}, bf16[256,1024]{1,0:T(8,128)(2,1)S(1)}, u32[]{:S(2)}) copy-start(bf16[256,1024]{1,0:T(8,128)(2,1)S(1)} %collective-permute-done.5.refs_6_) | copy-start | bytes 1572868
  58.5 17.3 %collective-permute-start.9 = (bf16[256,1024]{1,0:T(8,128)(2,1)S(1)}, bf16[256,1024]{1,0:T(8,128)(2,1)}, u32[]{:S(2)}, u32[]{:S(2)}) collective-permute-start(bf16[256,1024]{1,0:T(8,128)(2,1)S(1)} %collective-permute-done.5.refs_6_), channel_id=1, source_target_pairs={{0,8},{8,16},{16,24},{1,9},{9,17},{17,25},{2,10},{10,18},{18,26},{... | collective-permute-start | bytes 1572872 | tf_op jit(solution)/shard_map/ppermute | solution.py:102
  64.8 20.2 %collective-permute-start.11 = (bf16[256,1024]{1,0:T(8,128)(2,1)}, bf16[256,1024]{1,0:T(8,128)(2,1)}, u32[]{:S(2)}, u32[]{:S(2)}) collective-permute-start(bf16[256,1024]{1,0:T(8,128)(2,1)} %collective-permute-done.7.refs_8_), channel_id=1, source_target_pairs={{8,0},{16,8},{24,16},{9,1},{17,9},{25,17},{10,2},{18,10},{26,18},{... | collective-permute-start | bytes 1572872 | tf_op jit(solution)/shard_map/ppermute | solution.py:103
  69.2 94.1 %copy-start.6 = (bf16[512,1536]{1,0:T(8,128)(2,1)}, bf16[512,1536]{1,0:T(8,128)(2,1)S(1)}, u32[]{:S(2)}) copy-start(bf16[512,1536]{1,0:T(8,128)(2,1)S(1)} %pad_maximum_fusion.2.refs_0_) | copy-start | bytes 4718596
  69.2 26.9 %collective-permute-start.4 = (bf16[256,1024]{1,0:T(8,128)(2,1)}, bf16[256,1024]{1,0:T(8,128)(2,1)S(1)}, u32[]{:S(2)}, u32[]{:S(2)}) collective-permute-start(bf16[256,1024]{1,0:T(8,128)(2,1)} %collective-permute-done.3.refs_4_), channel_id=1, source_target_pairs={{0,4},{4,0},{8,12},{12,8},{16,20},{20,16},{1,5},{5,1},{9,13},{13,9... | collective-permute-start | bytes 1572872 | tf_op jit(solution)/shard_map/ppermute | solution.py:95
  71.1 24.9 %collective-permute-start.6 = (bf16[256,1024]{1,0:T(8,128)(2,1)S(1)}, bf16[256,1024]{1,0:T(8,128)(2,1)S(1)}, u32[]{:S(2)}, u32[]{:S(2)}) collective-permute-start(bf16[256,1024]{1,0:T(8,128)(2,1)S(1)} %collective-permute-done.5.refs_6_), channel_id=1, source_target_pairs={{16,20},{20,16},{24,28},{28,24},{17,21},{21,17},{25,29},{29,25},{1... | collective-permute-start | bytes 1572872 | tf_op jit(solution)/shard_map/ppermute | solution.py:95
  71.8 35.6 %collective-permute-start.8 = (bf16[256,1024]{1,0:T(8,128)(2,1)}, bf16[256,1024]{1,0:T(8,128)(2,1)}, u32[]{:S(2)}, u32[]{:S(2)}) collective-permute-start(bf16[256,1024]{1,0:T(8,128)(2,1)} %collective-permute-done.7.refs_8_), channel_id=1, source_target_pairs={{0,4},{4,0},{8,12},{12,8},{1,5},{5,1},{9,13},{13,9},{2,6},{6,2},{1... | collective-permute-start | bytes 1572872 | tf_op jit(solution)/shard_map/ppermute | solution.py:95
  75.8 31.6 %collective-permute-start.10 = (bf16[256,1024]{1,0:T(8,128)(2,1)}, bf16[256,1024]{1,0:T(8,128)(2,1)}, u32[]{:S(2)}, u32[]{:S(2)}) collective-permute-start(bf16[256,1024]{1,0:T(8,128)(2,1)} %collective-permute-done.9.refs_10_), channel_id=1, source_target_pairs={{24,28},{28,24},{25,29},{29,25},{26,30},{30,26},{27,31},{31,27}} | collective-permute-start | bytes 1572872 | tf_op jit(solution)/shard_map/ppermute | solution.py:95
  85.1 28.4 %collective-permute-start.12 = (bf16[256,1024]{1,0:T(8,128)(2,1)}, bf16[256,1024]{1,0:T(8,128)(2,1)}, u32[]{:S(2)}, u32[]{:S(2)}) collective-permute-start(bf16[256,1024]{1,0:T(8,128)(2,1)} %collective-permute-done.11.refs_12_), channel_id=1, source_target_pairs={{0,4},{4,0},{1,5},{5,1},{2,6},{6,2},{3,7},{7,3}} | collective-permute-start | bytes 1572872 | tf_op jit(solution)/shard_map/ppermute | solution.py:95
  96.0 21.5 %copy-start.13 = (bf16[256,1024]{1,0:T(8,128)(2,1)}, bf16[256,1024]{1,0:T(8,128)(2,1)S(1)}, u32[]{:S(2)}) copy-start(bf16[256,1024]{1,0:T(8,128)(2,1)S(1)} %collective-permute-done.4.refs_5_) | copy-start | bytes 1572868
  96.0 21.5 %copy-start.14 = (bf16[256,1024]{1,0:T(8,128)(2,1)}, bf16[256,1024]{1,0:T(8,128)(2,1)S(1)}, u32[]{:S(2)}) copy-start(bf16[256,1024]{1,0:T(8,128)(2,1)S(1)} %collective-permute-done.6.refs_7_) | copy-start | bytes 1572868
  113.5 96.4 %all-gather.9.cloned.1.call-start = ((), (), s32[]{:S(2)}) async-start(), calls=%async_computation.13 | async-start | bytes 2621440 | tf_op jit(solution)/shard_map/all_gather | solution.py:953
  114.1 52.1 %collective-permute-start.15 = (bf16[512,1536]{1,0:T(8,128)(2,1)S(1)}, bf16[512,1536]{1,0:T(8,128)(2,1)}, u32[]{:S(2)}, u32[]{:S(2)}) collective-permute-start(bf16[512,1536]{1,0:T(8,128)(2,1)S(1)} %pad_maximum_fusion.2.refs_0_), channel_id=1, source_target_pairs={{0,2},{2,0},{1,3},{3,1},{4,6},{6,4},{5,7},{7,5},{8,10},{10,8},{9,1... | collective-permute-start | bytes 4718600 | tf_op jit(solution)/shard_map/ppermute | solution.py:112
  117.2 46.1 %collective-permute-start.17 = (bf16[512,1536]{1,0:T(8,128)(2,1)S(1)}, bf16[512,1536]{1,0:T(8,128)(2,1)}, u32[]{:S(2)}, u32[]{:S(2)}) collective-permute-start(bf16[512,1536]{1,0:T(8,128)(2,1)S(1)} %pad_maximum_fusion.2.refs_0_), channel_id=1, source_target_pairs={{0,4},{4,0},{1,5},{5,1},{2,6},{6,2},{3,7},{7,3},{8,12},{12,8},{9,1... | collective-permute-start | bytes 4718600 | tf_op jit(solution)/shard_map/ppermute | solution.py:113
  143.5 9.0 %collective-permute-start.13 = (bf16[4,256,128]{2,1,0:T(8,128)(2,1)S(1)}, bf16[4,256,128]{2,1,0:T(8,128)(2,1)S(1)}, u32[]{:S(2)}, u32[]{:S(2)}) collective-permute-start(bf16[4,256,128]{2,1,0:T(8,128)(2,1)S(1)} %get-tuple-element.244), channel_id=1, source_target_pairs={{0,4},{4,0},{1,5},{5,1},{2,6},{6,2},{3,7},{7,3},{8,12},{12,8},{9,1... | collective-permute-start | bytes 786440 | tf_op jit(solution)/shard_map/ppermute | solution.py:948
  163.0 131.1 %reduce-scatter.5.cloned.1.call-start = ((), (), s32[]{:S(2)}) async-start(), calls=%async_computation.9 | async-start | bytes 2949120 | tf_op jit(solution)/shard_map/reduce_scatter | solution.py:80
  163.2 25.0 %collective-permute-start.14 = (bf16[512,1536]{1,0:T(8,128)(2,1)S(1)}, bf16[512,1536]{1,0:T(8,128)(2,1)}, u32[]{:S(2)}, u32[]{:S(2)}) collective-permute-start(bf16[512,1536]{1,0:T(8,128)(2,1)S(1)} %pad_maximum_fusion.2.refs_0_), channel_id=1, source_target_pairs={{0,1},{1,0},{2,3},{3,2},{4,5},{5,4},{6,7},{7,6},{8,9},{9,8},{10,11... | collective-permute-start | bytes 4718600 | tf_op jit(solution)/shard_map/ppermute | solution.py:117
  164.5 20.0 %collective-permute-start.19 = (bf16[256,1536]{1,0:T(8,128)(2,1)S(1)}, bf16[256,1536]{1,0:T(8,128)(2,1)S(1)}, u32[]{:S(2)}, u32[]{:S(2)}) collective-permute-start(bf16[256,1536]{1,0:T(8,128)(2,1)S(1)} %slice.78), channel_id=1, source_target_pairs={{0,2},{2,0},{1,3},{3,1},{4,6},{6,4},{5,7},{7,5},{8,10},{10,8},{9,1... | collective-permute-start | bytes 2359304 | tf_op jit(solution)/shard_map/ppermute | solution.py:114
  166.1 22.2 %collective-permute-start.18 = (bf16[512,1536]{1,0:T(8,128)(2,1)}, bf16[512,1536]{1,0:T(8,128)(2,1)}, u32[]{:S(2)}, u32[]{:S(2)}) collective-permute-start(bf16[512,1536]{1,0:T(8,128)(2,1)} %collective-permute-done.17.refs_4_), channel_id=1, source_target_pairs={{0,1},{1,0},{2,3},{3,2},{4,5},{5,4},{6,7},{7,6},{8,9},{9,8},{10,11... | collective-permute-start | bytes 4718600 | tf_op jit(solution)/shard_map/ppermute | solution.py:117
  166.3 22.0 %collective-permute-start.16 = (bf16[512,1536]{1,0:T(8,128)(2,1)}, bf16[512,1536]{1,0:T(8,128)(2,1)}, u32[]{:S(2)}, u32[]{:S(2)}) collective-permute-start(bf16[512,1536]{1,0:T(8,128)(2,1)} %collective-permute-done.15.refs_2_), channel_id=1, source_target_pairs={{0,1},{1,0},{2,3},{3,2},{4,5},{5,4},{6,7},{7,6},{8,9},{9,8},{10,11... | collective-permute-start | bytes 4718600 | tf_op jit(solution)/shard_map/ppermute | solution.py:117
  167.8 19.7 %collective-permute-start.21 = (bf16[256,1536]{1,0:T(8,128)(2,1)S(1)}, bf16[256,1536]{1,0:T(8,128)(2,1)S(1)}, u32[]{:S(2)}, u32[]{:S(2)}) collective-permute-start(bf16[256,1536]{1,0:T(8,128)(2,1)S(1)} %slice.79), channel_id=1, source_target_pairs={{0,4},{4,0},{1,5},{5,1},{2,6},{6,2},{3,7},{7,3},{8,12},{12,8},{9,1... | collective-permute-start | bytes 2359304 | tf_op jit(solution)/shard_map/ppermute | solution.py:115
  184.5 3.7 collective-permute-start.20
  187.5 2.4 collective-permute-start.22
  247.2 119.5 %reduce-scatter.7.cloned.1.call-start = ((), (), s32[]{:S(2)}) async-start(), calls=%async_computation.10 | async-start | bytes 2621440 | tf_op jit(solution)/shard_map/reduce_scatter | solution.py:80
  261.8 19.1 %collective-permute-start.23 = (bf16[4,512,768]{2,1,0:T(8,128)(2,1)}, bf16[4,512,768]{2,1,0:T(8,128)(2,1)}, u32[]{:S(2)}, u32[]{:S(2)}) collective-permute-start(bf16[4,512,768]{2,1,0:T(8,128)(2,1)} %get-tuple-element.125), channel_id=1, source_target_pairs={{0,1},{1,0},{2,3},{3,2},{4,5},{5,4},{6,7},{7,6},{8,9},{9,8},{10,11... | collective-permute-start | bytes 9437192 | tf_op jit(solution)/shard_map/ppermute | solution.py:983
  261.8 24.5 %collective-permute-start.24 = (bf16[4,512,768]{2,1,0:T(8,128)(2,1)}, bf16[4,512,768]{2,1,0:T(8,128)(2,1)S(1)}, u32[]{:S(2)}, u32[]{:S(2)}) collective-permute-start(bf16[4,512,768]{2,1,0:T(8,128)(2,1)} %get-tuple-element.127), channel_id=1, source_target_pairs={{0,1},{1,0},{2,3},{3,2},{4,5},{5,4},{6,7},{7,6},{8,9},{9,8},{10,11... | collective-permute-start | bytes 9437192 | tf_op jit(solution)/shard_map/ppermute | solution.py:983
  301.2 19.5 %collective-permute-start.25 = (bf16[512,768]{1,0:T(8,128)(2,1)}, bf16[512,768]{1,0:T(8,128)(2,1)}, u32[]{:S(2)}, u32[]{:S(2)}) collective-permute-start(bf16[512,768]{1,0:T(8,128)(2,1)} %dynamic-slice_bitcast_fusion.3), channel_id=1, source_target_pairs={{0,2},{2,0},{1,3},{3,1},{4,6},{6,4},{5,7},{7,5},{8,10},{10,8},{9,1... | collective-permute-start | bytes 2359304 | tf_op jit(solution)/shard_map/ppermute | solution.py:992
  304.8 21.9 %collective-permute-start.26 = (bf16[512,768]{1,0:T(8,128)(2,1)}, bf16[512,768]{1,0:T(8,128)(2,1)S(1)}, u32[]{:S(2)}, u32[]{:S(2)}) collective-permute-start(bf16[512,768]{1,0:T(8,128)(2,1)} %dynamic-slice_bitcast_fusion.2), channel_id=1, source_target_pairs={{0,4},{4,0},{1,5},{5,1},{2,6},{6,2},{3,7},{7,3},{8,12},{12,8},{9,1... | collective-permute-start | bytes 2359304 | tf_op jit(solution)/shard_map/ppermute | solution.py:993
  309.8 33.0 %all-to-all-start = ((bf16[8,256,128]{2,1,0:T(8,128)(2,1)}), bf16[8,256,128]{2,1,0:T(8,128)(2,1)}, u32[]{:S(2)}, u32[]{:S(2)}) async-start(bf16[8,256,128]{2,1,0:T(8,128)(2,1)} %bitcast.80), calls=%async_computation.1 | async-start | bytes 1048576 | tf_op jit(solution)/shard_map/all_to_all | solution.py:830
  314.0 91.3 %reduce-scatter.9.cloned.1.call-start = ((), (), s32[]{:S(2)}) async-start(), calls=%async_computation.11 | async-start | bytes 2654208 | tf_op jit(solution)/shard_map/reduce_scatter | solution.py:80
  342.8 23.8 %collective-permute-start.27 = (bf16[512,768]{1,0:T(8,128)(2,1)}, bf16[512,768]{1,0:T(8,128)(2,1)S(1)}, u32[]{:S(2)}, u32[]{:S(2)}) collective-permute-start(bf16[512,768]{1,0:T(8,128)(2,1)} %fusion.7), channel_id=1, source_target_pairs={{0,4},{4,0},{1,5},{5,1},{2,6},{6,2},{3,7},{7,3},{8,12},{12,8},{9,1... | collective-permute-start | bytes 2359304 | tf_op jit(solution)/shard_map/ppermute | solution.py:1033
  344.1 22.6 %collective-permute-start.28 = (bf16[512,768]{1,0:T(8,128)(2,1)}, bf16[512,768]{1,0:T(8,128)(2,1)}, u32[]{:S(2)}, u32[]{:S(2)}) collective-permute-start(bf16[512,768]{1,0:T(8,128)(2,1)} %fusion.6), channel_id=1, source_target_pairs={{0,2},{2,0},{1,3},{3,1},{4,6},{6,4},{5,7},{7,5},{8,10},{10,8},{9,1... | collective-permute-start | bytes 2359304 | tf_op jit(solution)/shard_map/ppermute | solution.py:1033
  369.2 36.1 %all-to-all-start.1 = ((bf16[8,256,256]{1,2,0:T(8,128)(2,1)}), bf16[8,256,256]{1,2,0:T(8,128)(2,1)S(1)}, u32[]{:S(2)}, u32[]{:S(2)}) async-start(bf16[8,256,256]{1,2,0:T(8,128)(2,1)} %copy.80), calls=%async_computation.3 | async-start | bytes 2097152 | tf_op jit(solution)/shard_map/all_to_all | solution.py:830
  372.8 72.0 %reduce-scatter.11.cloned.1.call-start = ((), (), s32[]{:S(2)}) async-start(), calls=%async_computation.12 | async-start | bytes 368640 | tf_op jit(solution)/shard_map/reduce_scatter | solution.py:80
  406.3 38.5 %all-to-all-start.2 = ((bf16[32,32,384]{2,1,0:T(8,128)(2,1)}), bf16[32,32,384]{2,1,0:T(8,128)(2,1)S(1)}, u32[]{:S(2)}, u32[]{:S(2)}) async-start(bf16[32,32,384]{2,1,0:T(8,128)(2,1)} %bitcast.92), calls=%async_computation.5 | async-start | bytes 1572864 | tf_op jit(solution)/shard_map/all_to_all | solution.py:830
  412.2 26.8 %collective-permute-start.30 = (bf16[512,768]{1,0:T(8,128)(2,1)S(1)}, bf16[512,768]{1,0:T(8,128)(2,1)S(1)}, u32[]{:S(2)}, u32[]{:S(2)}) collective-permute-start(bf16[512,768]{1,0:T(8,128)(2,1)S(1)} %dynamic-slice_bitcast_fusion), channel_id=1, source_target_pairs={{0,4},{4,0},{1,5},{5,1},{2,6},{6,2},{3,7},{7,3},{8,12},{12,8},{9,1... | collective-permute-start | bytes 2359304 | tf_op jit(solution)/shard_map/ppermute | solution.py:1056
  415.2 26.6 %collective-permute-start.29 = (bf16[512,768]{1,0:T(8,128)(2,1)S(1)}, bf16[512,768]{1,0:T(8,128)(2,1)S(1)}, u32[]{:S(2)}, u32[]{:S(2)}) collective-permute-start(bf16[512,768]{1,0:T(8,128)(2,1)S(1)} %dynamic-slice_bitcast_fusion.1), channel_id=1, source_target_pairs={{0,2},{2,0},{1,3},{3,1},{4,6},{6,4},{5,7},{7,5},{8,10},{10,8},{9,1... | collective-permute-start | bytes 2359304 | tf_op jit(solution)/shard_map/ppermute | solution.py:1055
  421.6 20.1 %copy-start.11 = (bf16[512,768]{1,0:T(8,128)(2,1)S(1)}, bf16[512,768]{1,0:T(8,128)(2,1)}, u32[]{:S(2)}) copy-start(bf16[512,768]{1,0:T(8,128)(2,1)} %copy-done.10) | copy-start | bytes 2359300
  (15 other events, 105.7 us)
Sparse Core Ops, SparseCore 0:
  14.5 92.1 all-gather.4
  113.6 49.3 all-gather.6
  165.1 44.7 all-gather.8
  247.4 46.7 reduce-scatter.4
  296.3 51.6 reduce-scatter.6
  351.5 53.6 reduce-scatter.8
  407.5 21.8 reduce-scatter.10
